TPU v7x, 128 devices: a whole 4x4x4 slice. The times are simulated.
128 devices in a mesh: slab: 32 (over y, x_hi, z), patch: 4 (over x_lo, core).
Axes of the slice: x: 4 (x_hi: 2, x_lo: 2; x = x_hi * 2 + x_lo), y: 4, z: 4, core: 2. Of those that a mesh axis runs over, the one named last changes fastest.
Arguments:
- fluid_state: float32 [64, 256, 256], P('slab', 'patch'), may hold values from -6 to 6
- fluid_rhs: float32 [64, 256, 256], P('slab', 'patch'), may hold values from -24 to 24
- element_scale: float32 [64, 256], P('slab', 'patch'), may hold values from 1 to 4
- element_matrix: bfloat16 [256, 256], replicated
- couple_x: bfloat16 [256, 256], replicated, may hold values from -0.09375 to 0.09375
- couple_y: bfloat16 [256, 256], replicated, may hold values from -0.09375 to 0.09375
- block_inverse: bfloat16 [256, 256], replicated
- traction_map: bfloat16 [3, 256], replicated, may hold values from -0.375 to 0.375
- slot_elem: int32 [32, 4, 1024], P('slab', 'patch'), may hold values from 0 to 127
- slot_point: int32 [32, 4, 1024], P('slab', 'patch'), may hold values from 0 to 8191
- slot_count: int32 [32, 4, 4], P('slab', 'patch'), may hold values from 0 to 256, as said below
- displacement: float32 [3, 256, 128], P(None, 'patch'), may hold values from -6 to 6
- stiffness: float32 [256, 128], P('patch'), may hold values from 0.03 to 0.3
Outputs:
- fluid_out: float32 [64, 256, 256], P('slab', 'patch')
- displacement_new: float32 [3, 256, 128], P(None, 'patch')
- wall_motion: float32 [3, 32, 4, 1024], P(None, 'slab', 'patch')
Inputs may be any that keep to these rules, and one draw needn't show every extreme that they name: For every block and owner only the first slot_count slots of that owner's 256 slots are live; the count 256 is reached for some block and owner in every draw.
All inputs are finite; a program needn't handle non-finite values.
Results may differ from a plain program's by a relative error of at most 0.0049.
Values may be sent and summed in bfloat16 or wider, within the bound.
No kernel may reach another device: no remote copies, remote signals or barrier semaphores. Data moves between devices by JAX's collectives and lax.ppermute only.
A program may use at most 128 MiB of HBM per device.

v0:
```python
import jax
import jax.numpy as jnp
from jax import lax
from jax.sharding import PartitionSpec as P

SWEEPS = 3


def extended(value, sides, width):
    edges = {}
    for axis, dim in sides:
        count, length = (lax.axis_size(axis), value.shape[dim])
        up = [(i, (i + 1) % count) for i in range(count - 1)]
        last = lax.slice_in_dim(value, length - width, length, axis=dim)
        leading = lax.slice_in_dim(value, 0, width, axis=dim)
        edges[dim] = (
            lax.ppermute(last, axis, up),
            lax.ppermute(leading, axis, [(b, a) for a, b in up]),
        )
    done = []
    for _, dim in sides:
        low, high = edges[dim]
        around = [(width, width) if d in done else (0, 0) for d in range(value.ndim)]
        value = jnp.concatenate([jnp.pad(low, around), value, jnp.pad(high, around)], axis=dim)
        done.append(dim)
    return value


def with_halo(cells, sides, width):
    for axis, dim in sides:
        count = lax.axis_size(axis)
        ends = count - 1
        head = lax.slice_in_dim(cells, 0, width, axis=dim)
        tail = lax.slice_in_dim(cells, cells.shape[dim] - width, cells.shape[dim], axis=dim)
        cells = jnp.concatenate(
            [
                lax.ppermute(tail, axis, [(i, (i + 1) % count) for i in range(ends)]),
                cells,
                lax.ppermute(head, axis, [((i + 1) % count, i) for i in range(ends)]),
            ],
            axis=dim,
        )
    return cells


def gathered_total(value, axis):
    tiles = lax.all_gather(value, axis)
    return tiles.sum(axis=0)


def copy_for_each(value, axis):
    count = lax.axis_size(axis)
    return lax.all_to_all(
        jnp.broadcast_to(value[None], (count, *value.shape)), axis, 0, 0, tiled=True
    )


def in_order(tiles, dim):
    lengths = list(tiles.shape[1:])
    lengths[dim] *= tiles.shape[0]
    return jnp.moveaxis(tiles, 0, dim).reshape(lengths)


def gather_directly(value, axis, dim):
    tiles = copy_for_each(value, axis)
    return in_order(tiles, dim)


def element_apply(rounded, scale, element_matrix, couple_x, couple_y):
    padded = extended(rounded, (("slab", 0), ("patch", 1)), 1)
    along_x = (padded[:-2, 1:-1].astype(jnp.float32) + padded[2:, 1:-1].astype(jnp.float32)).astype(
        jnp.bfloat16
    )
    along_y = (padded[1:-1, :-2].astype(jnp.float32) + padded[1:-1, 2:].astype(jnp.float32)).astype(
        jnp.bfloat16
    )
    width = rounded.shape[2]
    own = jnp.dot(rounded.reshape(-1, width), element_matrix, preferred_element_type=jnp.float32)
    side_x = jnp.dot(along_x.reshape(-1, width), couple_x, preferred_element_type=jnp.float32)
    side_y = jnp.dot(along_y.reshape(-1, width), couple_y, preferred_element_type=jnp.float32)
    return (
        scale[:, :, None] * own.reshape(rounded.shape)
        - side_x.reshape(rounded.shape)
        - side_y.reshape(rounded.shape)
    )


def laplace_net(field):
    edged = with_halo(field.astype(jnp.bfloat16), (("patch", 1),), 1).astype(field.dtype)
    edged = jnp.pad(edged, ((0, 0), (0, 0), (1, 1)))
    return 4.0 * field - (
        edged[:, 2:, 1:-1] + edged[:, :-2, 1:-1] + edged[:, 1:-1, 2:] + edged[:, 1:-1, :-2]
    )


def shards(
    fluid_state,
    fluid_rhs,
    element_scale,
    element_matrix,
    couple_x,
    couple_y,
    block_inverse,
    traction_map,
    slot_elem,
    slot_point,
    slot_count,
    displacement,
    stiffness,
):
    width = fluid_state.shape[2]
    state = fluid_state
    for sweep in range(SWEEPS):
        rounded = state.astype(jnp.bfloat16)
        applied = element_apply(rounded, element_scale, element_matrix, couple_x, couple_y)
        residue = (fluid_rhs - applied).astype(jnp.bfloat16)
        update = jnp.dot(
            residue.reshape(-1, width), block_inverse, preferred_element_type=jnp.float32
        ).reshape(state.shape)
        state = state + update / element_scale[:, :, None]
    final = state.astype(jnp.bfloat16)
    owners = lax.axis_size("patch")
    capacity = slot_elem.shape[2] // owners
    net_rows = displacement.shape[1]
    net_cols = displacement.shape[2]
    cells = net_rows * net_cols
    rows = jnp.take(final.reshape(-1, width), slot_elem.reshape(-1), axis=0).reshape(
        owners, capacity, width
    )
    pull = jnp.einsum("cd,kqd->kcq", traction_map, rows, preferred_element_type=jnp.float32)
    limits = slot_count.reshape(owners)
    live = (lax.broadcasted_iota(jnp.int32, (owners, capacity), 1) < limits[:, None]).astype(
        jnp.float32
    )
    pull = pull * live[:, None, :]
    points = slot_point.reshape(owners, capacity)
    owner_ids = lax.broadcasted_iota(jnp.int32, (owners, capacity), 0)
    got_pull, got_points = (
        lax.all_to_all(pull, "patch", split_axis=0, concat_axis=0, tiled=True),
        lax.all_to_all(points, "patch", split_axis=0, concat_axis=0, tiled=True),
    )
    local = jnp.zeros((3, cells), jnp.float32)
    local = local.at[:, got_points.reshape(-1)].add(got_pull.transpose(1, 0, 2).reshape(3, -1))
    loads = gathered_total(local, "slab")
    loads = loads.reshape(3, net_rows, net_cols)
    bend = laplace_net(displacement)
    stiff_term = stiffness[None] * (laplace_net(bend) + 4.0 * bend)
    displacement_new = displacement + (loads - stiff_term) / (36.0 * stiffness[None])
    flat_net = displacement_new.reshape(3, -1)
    whole = gather_directly(flat_net, "patch", 1)
    picked = whole[:, (owner_ids * cells + points).reshape(-1)]
    wall_motion = (picked * live.reshape(1, -1)).reshape(3, 1, 1, owners * capacity)
    return (state, displacement_new, wall_motion)


def solution(mesh):
    return jax.shard_map(
        shards,
        mesh=mesh,
        in_specs=(
            P("slab", "patch", None),
            P("slab", "patch", None),
            P("slab", "patch"),
            P(),
            P(),
            P(),
            P(),
            P(),
            P("slab", "patch", None),
            P("slab", "patch", None),
            P("slab", "patch", None),
            P(None, "patch", None),
            P("patch", None),
        ),
        out_specs=(
            P("slab", "patch", None),
            P(None, "patch", None),
            P(None, "slab", "patch", None),
        ),
        check_vma=False,
    )
```

profile of v0, /device:TPU:1, one launch (start us, length us, event | category | flops | bytes accessed | tf_op | source)
XLA Modules:
  0.0 222.4 jit_solution(11759951274872581223)
XLA Ops:
  7.2 4.8 %all-to-all-start = ((s32[4,1,256]{2,1,0:T(1,128)}), s32[4,1,256]{2,1,0:T(1,128)S(1)}, u32[]{:S(2)}, u32[]{:S(2)}) async-start(s32[4,1,256]{2,1,0:T(1,128)} %bitcast.100), calls=%async_computation | async-start | bytes 8192 | tf_op jit(solution)/shard_map/all_to_all | solution.py:140
  12.0 0.9 convert_element_type.113
  12.9 3.5 %collective-permute-start.2 = (bf16[2,1,256]{2,1,0:T(2,128)(2,1)S(1)}, bf16[2,1,256]{2,1,0:T(2,128)(2,1)S(1)}, u32[]{:S(2)}, u32[]{:S(2)}) collective-permute-start(bf16[2,1,256]{2,1,0:T(2,128)(2,1)S(1)} %get-tuple-element.22), channel_id=1, source_target_pairs={{0,1},{1,2},{2,3},{4,5},{5,6},{6,7},{8,9},{9,10},{10,11},{12,13},{... | collective-permute-start | bytes 3080 | tf_op jit(solution)/shard_map/ppermute | solution.py:17
  16.5 1.9 collective-permute-start.3
  18.4 3.6 %collective-permute-start = (bf16[1,64,256]{2,1,0:T(8,128)(2,1)S(1)}, bf16[1,64,256]{2,1,0:T(8,128)(2,1)S(1)}, u32[]{:S(2)}, u32[]{:S(2)}) collective-permute-start(bf16[1,64,256]{2,1,0:T(8,128)(2,1)S(1)} %get-tuple-element.24), channel_id=1, source_target_pairs={{0,4},{4,8},{8,12},{12,16},{16,20},{20,24},{24,28},{28,32},{32,36}... | collective-permute-start | bytes 98312 | tf_op jit(solution)/shard_map/ppermute | solution.py:17
  22.1 1.3 collective-permute-start.1
  24.6 1.3 reduce.4
  25.9 0.7 fusion.119
  26.7 1.1 convolution_multiply_fusion.2
  27.8 1.1 convolution_subtract_fusion.5
  28.9 1.3 fusion.164
  30.2 1.1 convolution_multiply_fusion.1
  31.3 4.2 %collective-permute-start.4 = (bf16[1,64,256]{2,1,0:T(8,128)(2,1)S(1)}, bf16[1,64,256]{2,1,0:T(8,128)(2,1)S(1)}, u32[]{:S(2)}, u32[]{:S(2)}) collective-permute-start(bf16[1,64,256]{2,1,0:T(8,128)(2,1)S(1)} %get-tuple-element.20), channel_id=1, source_target_pairs={{0,4},{4,8},{8,12},{12,16},{16,20},{20,24},{24,28},{28,32},{32,36}... | collective-permute-start | bytes 98312 | tf_op jit(solution)/shard_map/ppermute | solution.py:17
  35.5 1.3 collective-permute-start.5
  36.8 4.3 %collective-permute-start.6 = (bf16[2,1,256]{2,1,0:T(2,128)(2,1)S(1)}, bf16[2,1,256]{2,1,0:T(2,128)(2,1)S(1)}, u32[]{:S(2)}, u32[]{:S(2)}) collective-permute-start(bf16[2,1,256]{2,1,0:T(2,128)(2,1)S(1)} %get-tuple-element.18), channel_id=1, source_target_pairs={{0,1},{1,2},{2,3},{4,5},{5,6},{6,7},{8,9},{9,10},{10,11},{12,13},{... | collective-permute-start | bytes 3080 | tf_op jit(solution)/shard_map/ppermute | solution.py:17
  41.1 1.9 collective-permute-start.7
  43.1 1.1 convolution_subtract_fusion.3
  44.2 1.9 collective-permute-done.7
  46.0 1.3 fusion.167
  47.5 4.3 %collective-permute-start.8 = (bf16[1,64,256]{2,1,0:T(8,128)(2,1)S(1)}, bf16[1,64,256]{2,1,0:T(8,128)(2,1)S(1)}, u32[]{:S(2)}, u32[]{:S(2)}) collective-permute-start(bf16[1,64,256]{2,1,0:T(8,128)(2,1)S(1)} %get-tuple-element.16), channel_id=1, source_target_pairs={{0,4},{4,8},{8,12},{12,16},{16,20},{20,24},{24,28},{28,32},{32,36}... | collective-permute-start | bytes 98312 | tf_op jit(solution)/shard_map/ppermute | solution.py:17
  51.8 1.3 collective-permute-start.9
  53.1 2.2 %collective-permute-start.10 = (bf16[2,1,256]{2,1,0:T(2,128)(2,1)S(1)}, bf16[2,1,256]{2,1,0:T(2,128)(2,1)S(1)}, u32[]{:S(2)}, u32[]{:S(2)}) collective-permute-start(bf16[2,1,256]{2,1,0:T(2,128)(2,1)S(1)} %get-tuple-element.14), channel_id=1, source_target_pairs={{0,1},{1,2},{2,3},{4,5},{5,6},{6,7},{8,9},{9,10},{10,11},{12,13},{... | collective-permute-start | bytes 3080 | tf_op jit(solution)/shard_map/ppermute | solution.py:17
  55.4 2.1 collective-permute-start.11
  57.5 0.9 collective-permute-done.9
  58.6 1.7 collective-permute-done.11
  60.3 1.0 fusion.170
  61.2 3.9 %gather_fusion = bf16[1024,256]{1,0:T(8,128)(2,1)S(1)} fusion(bf16[128,256]{1,0:T(8,128)(2,1)S(1)} %bitcast.90, s32[1024]{0:T(1024)S(1)} %broadcast_clamp_fusion.1), kind=kCustom, calls=%fused_computation | custom fusion | bytes 1052672 | tf_op jit(solution)/shard_map/jit(_take)/gather | solution.py:127
  65.2 0.9 fusion.11
  66.1 3.2 %all-to-all-start.1 = ((f32[4,3,256]{2,1,0:T(4,128)}), f32[4,3,256]{2,1,0:T(4,128)S(1)}, u32[]{:S(2)}, u32[]{:S(2)}) async-start(f32[4,3,256]{2,1,0:T(4,128)} %fusion.11), calls=%async_computation.1 | async-start | bytes 32768 | tf_op jit(solution)/shard_map/all_to_all | solution.py:139
  69.4 1.6 all-to-all-done.1
  71.3 8.2 %scatter_custom_fusion = f32[3,8192]{0,1:T(8,128)} fusion(s32[1024]{0:T(1024)S(1)} %bitcast.105, f32[1024,3]{1,0:T(8,128)S(1)} %copy.21, f32[]{:T(128)} %constant.11.clone.1), kind=kCustom, calls=%fused_computation.3 | custom fusion | flops 3072 | bytes 98308 | tf_op jit(solution)/shard_map/scatter-add | solution.py:143
  79.5 3.5 %copy.22 = f32[1,3,8192]{2,1,0:T(4,128)} copy(f32[1,3,8192]{1,2,0:T(8,128)} %bitcast.92) | data formatting | bytes 196608
  83.0 3.5 %collective-permute-start.12 = (bf16[3,1,128]{2,1,0:T(2,128)(2,1)S(1)}, bf16[3,1,128]{2,1,0:T(2,128)(2,1)S(1)}, u32[]{:S(2)}, u32[]{:S(2)}) collective-permute-start(bf16[3,1,128]{2,1,0:T(2,128)(2,1)S(1)} %get-tuple-element.28), channel_id=1, source_target_pairs={{0,1},{1,2},{2,3},{4,5},{5,6},{6,7},{8,9},{9,10},{10,11},{12,13},{... | collective-permute-start | bytes 2312 | tf_op jit(solution)/shard_map/ppermute | solution.py:37
  86.5 1.9 collective-permute-start.13
  88.5 2.9 %collective-permute-done.13 = bf16[3,1,128]{2,1,0:T(2,128)(2,1)S(1)} collective-permute-done((bf16[3,1,128]{2,1,0:T(2,128)(2,1)S(1)}, bf16[3,1,128]{2,1,0:T(2,128)(2,1)S(1)}, u32[]{:S(2)}, u32[]{:S(2)}) %collective-permute-start.13) | collective-permute-done | bytes 800 | tf_op jit(solution)/shard_map/ppermute | solution.py:39
  91.6 2.0 collective-permute-start.14
  93.5 2.4 %collective-permute-start.15 = (bf16[3,1,128]{2,1,0:T(2,128)(2,1)S(1)}, bf16[3,1,128]{2,1,0:T(2,128)(2,1)S(1)}, u32[]{:S(2)}, u32[]{:S(2)}) collective-permute-start(bf16[3,1,128]{2,1,0:T(2,128)(2,1)S(1)} %get-tuple-element.27), channel_id=1, source_target_pairs={{1,0},{2,1},{3,2},{5,4},{6,5},{7,6},{9,8},{10,9},{11,10},{13,12},{... | collective-permute-start | bytes 2312 | tf_op jit(solution)/shard_map/ppermute | solution.py:39
  96.0 2.4 %collective-permute-done.15 = bf16[3,1,128]{2,1,0:T(2,128)(2,1)S(1)} collective-permute-done((bf16[3,1,128]{2,1,0:T(2,128)(2,1)S(1)}, bf16[3,1,128]{2,1,0:T(2,128)(2,1)S(1)}, u32[]{:S(2)}, u32[]{:S(2)}) %collective-permute-start.15) | collective-permute-done | bytes 800 | tf_op jit(solution)/shard_map/ppermute | solution.py:39
  98.5 77.0 %all-gather.4.cloned.1.call-done = f32[32,3,8192]{2,1,0:T(4,128)} async-done(((f32[1,3,8192]{2,1,0:T(4,128)}), f32[32,3,8192]{2,1,0:T(4,128)}) %all-gather.4.cloned.1.call-update) | async-done | bytes 3145744 | tf_op jit(solution)/shard_map/all_gather | solution.py:47
  175.4 2.9 %reduce_sum.9 = f32[3,8192]{1,0:T(4,128)S(1)} reduce(f32[32,3,8192]{2,1,0:T(4,128)} %all-gather.4.cloned.1.call-done, f32[]{:T(128)} %constant.11.clone.1), dimensions={0}, to_apply=%region_1.2 | reduce | flops 761856 | bytes 3244036 | tf_op jit(solution)/shard_map/reduce_sum | solution.py:48
  178.3 2.7 %copy.27 = f32[3,8192]{0,1:T(8,128)} copy(f32[3,8192]{1,0:T(4,128)S(1)} %reduce_sum.9) | data formatting | bytes 196608
  181.0 2.9 %copy.24 = f32[3,64,128]{2,1,0:T(8,128)S(1)} copy(f32[3,64,128]{0,2,1:T(8,128)} %bitcast.93) | data formatting | bytes 196608 | tf_op jit(solution)/shard_map/reshape | solution.py:145
  184.1 0.9 broadcast_in_dim.20
  184.9 4.6 %all-to-all-start.2 = ((f32[4,3,8192]{2,1,0:T(4,128)}), f32[4,3,8192]{2,1,0:T(4,128)S(1)}, u32[]{:S(2)}, u32[]{:S(2)}) async-start(f32[4,3,8192]{2,1,0:T(4,128)} %broadcast_in_dim.20), calls=%async_computation.2 | async-start | bytes 1048576 | tf_op jit(solution)/shard_map/all_to_all | solution.py:53
  189.6 7.9 %all-to-all-done.2 = f32[4,3,8192]{2,1,0:T(4,128)S(1)} async-done(((f32[4,3,8192]{2,1,0:T(4,128)}), f32[4,3,8192]{2,1,0:T(4,128)S(1)}, u32[]{:S(2)}, u32[]{:S(2)}) %all-to-all-start.2) | async-done | bytes 393248 | tf_op jit(solution)/shard_map/all_to_all | solution.py:53
  197.5 8.4 %copy.25 = f32[3,4,8192]{0,2,1:T(8,128)} copy(f32[3,4,8192]{2,0,1:T(4,128)S(1)} %bitcast.94) | data formatting | bytes 786432 | tf_op jit(solution)/shard_map/transpose | solution.py:61
  205.9 8.6 %gather_fusion.1 = f32[1024,3]{1,0:T(8,128)S(1)} fusion(f32[3,32768]{0,1:T(8,128)} %bitcast.91, s32[1024]{0:T(1024)S(1)} %broadcast_clamp_fusion), kind=kCustom, calls=%fused_computation.1 | custom fusion | bytes 28672 | tf_op jit(solution)/shard_map/gather | solution.py:151
  214.7 0.8 copy.26
  (66 shorter events, 2.7 us)
Async XLA Ops:
  7.2 21.7 %copy-start = (bf16[256,256]{1,0:T(8,128)(2,1)S(1)}, bf16[256,256]{1,0:T(8,128)(2,1)}, u32[]{:S(2)}) copy-start(bf16[256,256]{1,0:T(8,128)(2,1)} %param.19) | copy-start | bytes 393220
  7.2 40.2 %copy-start.7 = (f32[2,64]{1,0:T(2,128)S(1)}, f32[2,64]{1,0:T(2,128)}, u32[]{:S(2)}) copy-start(f32[2,64]{1,0:T(2,128)} %param.15) | copy-start | bytes 1540
  7.2 40.2 %copy-start.1 = (bf16[256,256]{1,0:T(8,128)(2,1)S(1)}, bf16[256,256]{1,0:T(8,128)(2,1)}, u32[]{:S(2)}) copy-start(bf16[256,256]{1,0:T(8,128)(2,1)} %param.16) | copy-start | bytes 393220
  7.2 51.2 %copy-start.2 = (bf16[256,256]{1,0:T(8,128)(2,1)S(1)}, bf16[256,256]{1,0:T(8,128)(2,1)}, u32[]{:S(2)}) copy-start(bf16[256,256]{1,0:T(8,128)(2,1)} %param.17) | copy-start | bytes 393220
  7.2 53.0 %copy-start.9 = (bf16[256,256]{1,0:T(8,128)(2,1)S(1)}, bf16[256,256]{1,0:T(8,128)(2,1)}, u32[]{:S(2)}) copy-start(bf16[256,256]{1,0:T(8,128)(2,1)} %param.18) | copy-start | bytes 393220
  7.2 53.0 %copy-start.8 = (f32[2,64,256]{2,1,0:T(8,128)S(1)}, f32[2,64,256]{2,1,0:T(8,128)}, u32[]{:S(2)}) copy-start(f32[2,64,256]{2,1,0:T(8,128)} %param.14) | copy-start | bytes 393220
  7.2 58.9 %all-to-all-start = ((s32[4,1,256]{2,1,0:T(1,128)}), s32[4,1,256]{2,1,0:T(1,128)S(1)}, u32[]{:S(2)}, u32[]{:S(2)}) async-start(s32[4,1,256]{2,1,0:T(1,128)} %bitcast.100), calls=%async_computation | async-start | bytes 8192 | tf_op jit(solution)/shard_map/all_to_all | solution.py:140
  12.9 15.9 %collective-permute-start.2 = (bf16[2,1,256]{2,1,0:T(2,128)(2,1)S(1)}, bf16[2,1,256]{2,1,0:T(2,128)(2,1)S(1)}, u32[]{:S(2)}, u32[]{:S(2)}) collective-permute-start(bf16[2,1,256]{2,1,0:T(2,128)(2,1)S(1)} %get-tuple-element.22), channel_id=1, source_target_pairs={{0,1},{1,2},{2,3},{4,5},{5,6},{6,7},{8,9},{9,10},{10,11},{12,13},{... | collective-permute-start | bytes 3080 | tf_op jit(solution)/shard_map/ppermute | solution.py:17
  16.5 12.4 %collective-permute-start.3 = (bf16[2,1,256]{2,1,0:T(2,128)(2,1)S(1)}, bf16[2,1,256]{2,1,0:T(2,128)(2,1)S(1)}, u32[]{:S(2)}, u32[]{:S(2)}) collective-permute-start(bf16[2,1,256]{2,1,0:T(2,128)(2,1)S(1)} %get-tuple-element.23), channel_id=1, source_target_pairs={{1,0},{2,1},{3,2},{5,4},{6,5},{7,6},{9,8},{10,9},{11,10},{13,12},{... | collective-permute-start | bytes 3080 | tf_op jit(solution)/shard_map/ppermute | solution.py:18
  18.4 9.3 %collective-permute-start = (bf16[1,64,256]{2,1,0:T(8,128)(2,1)S(1)}, bf16[1,64,256]{2,1,0:T(8,128)(2,1)S(1)}, u32[]{:S(2)}, u32[]{:S(2)}) collective-permute-start(bf16[1,64,256]{2,1,0:T(8,128)(2,1)S(1)} %get-tuple-element.24), channel_id=1, source_target_pairs={{0,4},{4,8},{8,12},{12,16},{16,20},{20,24},{24,28},{28,32},{32,36}... | collective-permute-start | bytes 98312 | tf_op jit(solution)/shard_map/ppermute | solution.py:17
  22.1 5.7 %collective-permute-start.1 = (bf16[1,64,256]{2,1,0:T(8,128)(2,1)S(1)}, bf16[1,64,256]{2,1,0:T(8,128)(2,1)S(1)}, u32[]{:S(2)}, u32[]{:S(2)}) collective-permute-start(bf16[1,64,256]{2,1,0:T(8,128)(2,1)S(1)} %get-tuple-element.25), channel_id=1, source_target_pairs={{4,0},{8,4},{12,8},{16,12},{20,16},{24,20},{28,24},{32,28},{36,32}... | collective-permute-start | bytes 98312 | tf_op jit(solution)/shard_map/ppermute | solution.py:18
  31.3 11.7 %collective-permute-start.4 = (bf16[1,64,256]{2,1,0:T(8,128)(2,1)S(1)}, bf16[1,64,256]{2,1,0:T(8,128)(2,1)S(1)}, u32[]{:S(2)}, u32[]{:S(2)}) collective-permute-start(bf16[1,64,256]{2,1,0:T(8,128)(2,1)S(1)} %get-tuple-element.20), channel_id=1, source_target_pairs={{0,4},{4,8},{8,12},{12,16},{16,20},{20,24},{24,28},{28,32},{32,36}... | collective-permute-start | bytes 98312 | tf_op jit(solution)/shard_map/ppermute | solution.py:17
  35.5 7.6 %collective-permute-start.5 = (bf16[1,64,256]{2,1,0:T(8,128)(2,1)S(1)}, bf16[1,64,256]{2,1,0:T(8,128)(2,1)S(1)}, u32[]{:S(2)}, u32[]{:S(2)}) collective-permute-start(bf16[1,64,256]{2,1,0:T(8,128)(2,1)S(1)} %get-tuple-element.21), channel_id=1, source_target_pairs={{4,0},{8,4},{12,8},{16,12},{20,16},{24,20},{28,24},{32,28},{36,32}... | collective-permute-start | bytes 98312 | tf_op jit(solution)/shard_map/ppermute | solution.py:18
  36.8 7.3 %collective-permute-start.6 = (bf16[2,1,256]{2,1,0:T(2,128)(2,1)S(1)}, bf16[2,1,256]{2,1,0:T(2,128)(2,1)S(1)}, u32[]{:S(2)}, u32[]{:S(2)}) collective-permute-start(bf16[2,1,256]{2,1,0:T(2,128)(2,1)S(1)} %get-tuple-element.18), channel_id=1, source_target_pairs={{0,1},{1,2},{2,3},{4,5},{5,6},{6,7},{8,9},{9,10},{10,11},{12,13},{... | collective-permute-start | bytes 3080 | tf_op jit(solution)/shard_map/ppermute | solution.py:17
  41.1 4.9 %collective-permute-start.7 = (bf16[2,1,256]{2,1,0:T(2,128)(2,1)S(1)}, bf16[2,1,256]{2,1,0:T(2,128)(2,1)S(1)}, u32[]{:S(2)}, u32[]{:S(2)}) collective-permute-start(bf16[2,1,256]{2,1,0:T(2,128)(2,1)S(1)} %get-tuple-element.19), channel_id=1, source_target_pairs={{1,0},{2,1},{3,2},{5,4},{6,5},{7,6},{9,8},{10,9},{11,10},{13,12},{... | collective-permute-start | bytes 3080 | tf_op jit(solution)/shard_map/ppermute | solution.py:18
  46.0 19.1 %copy-start.10 = (bf16[3,256]{1,0:T(4,128)(2,1)S(1)}, bf16[3,256]{1,0:T(4,128)(2,1)}, u32[]{:S(2)}) copy-start(bf16[3,256]{1,0:T(4,128)(2,1)} %param.20) | copy-start | bytes 4612
  47.5 9.9 %collective-permute-start.8 = (bf16[1,64,256]{2,1,0:T(8,128)(2,1)S(1)}, bf16[1,64,256]{2,1,0:T(8,128)(2,1)S(1)}, u32[]{:S(2)}, u32[]{:S(2)}) collective-permute-start(bf16[1,64,256]{2,1,0:T(8,128)(2,1)S(1)} %get-tuple-element.16), channel_id=1, source_target_pairs={{0,4},{4,8},{8,12},{12,16},{16,20},{20,24},{24,28},{28,32},{32,36}... | collective-permute-start | bytes 98312 | tf_op jit(solution)/shard_map/ppermute | solution.py:17
  51.8 6.6 %collective-permute-start.9 = (bf16[1,64,256]{2,1,0:T(8,128)(2,1)S(1)}, bf16[1,64,256]{2,1,0:T(8,128)(2,1)S(1)}, u32[]{:S(2)}, u32[]{:S(2)}) collective-permute-start(bf16[1,64,256]{2,1,0:T(8,128)(2,1)S(1)} %get-tuple-element.17), channel_id=1, source_target_pairs={{4,0},{8,4},{12,8},{16,12},{20,16},{24,20},{28,24},{32,28},{36,32}... | collective-permute-start | bytes 98312 | tf_op jit(solution)/shard_map/ppermute | solution.py:18
  53.1 5.4 %collective-permute-start.10 = (bf16[2,1,256]{2,1,0:T(2,128)(2,1)S(1)}, bf16[2,1,256]{2,1,0:T(2,128)(2,1)S(1)}, u32[]{:S(2)}, u32[]{:S(2)}) collective-permute-start(bf16[2,1,256]{2,1,0:T(2,128)(2,1)S(1)} %get-tuple-element.14), channel_id=1, source_target_pairs={{0,1},{1,2},{2,3},{4,5},{5,6},{6,7},{8,9},{9,10},{10,11},{12,13},{... | collective-permute-start | bytes 3080 | tf_op jit(solution)/shard_map/ppermute | solution.py:17
  55.4 4.9 %collective-permute-start.11 = (bf16[2,1,256]{2,1,0:T(2,128)(2,1)S(1)}, bf16[2,1,256]{2,1,0:T(2,128)(2,1)S(1)}, u32[]{:S(2)}, u32[]{:S(2)}) collective-permute-start(bf16[2,1,256]{2,1,0:T(2,128)(2,1)S(1)} %get-tuple-element.15), channel_id=1, source_target_pairs={{1,0},{2,1},{3,2},{5,4},{6,5},{7,6},{9,8},{10,9},{11,10},{13,12},{... | collective-permute-start | bytes 3080 | tf_op jit(solution)/shard_map/ppermute | solution.py:18
  66.1 4.9 %all-to-all-start.1 = ((f32[4,3,256]{2,1,0:T(4,128)}), f32[4,3,256]{2,1,0:T(4,128)S(1)}, u32[]{:S(2)}, u32[]{:S(2)}) async-start(f32[4,3,256]{2,1,0:T(4,128)} %fusion.11), calls=%async_computation.1 | async-start | bytes 32768 | tf_op jit(solution)/shard_map/all_to_all | solution.py:139
  69.4 106.1 %all-gather.4.cloned.1.call-start = ((), (), s32[]{:S(2)}) async-start(), calls=%async_computation.3 | async-start | bytes 4325376 | tf_op jit(solution)/shard_map/all_gather | solution.py:47
  71.2 11.7 %copy-start.3 = (f32[3,64,128]{2,1,0:T(8,128)S(1)}, f32[3,64,128]{2,1,0:T(8,128)}, u32[]{:S(2)}) copy-start(f32[3,64,128]{2,1,0:T(8,128)} %param.24) | copy-start | bytes 294916
  71.3 17.2 %copy-start.5 = (f32[64,128]{1,0:T(8,128)S(1)}, f32[64,128]{1,0:T(8,128)}, u32[]{:S(2)}) copy-start(f32[64,128]{1,0:T(8,128)} %param.25) | copy-start | bytes 98308
  83.0 5.4 %collective-permute-start.12 = (bf16[3,1,128]{2,1,0:T(2,128)(2,1)S(1)}, bf16[3,1,128]{2,1,0:T(2,128)(2,1)S(1)}, u32[]{:S(2)}, u32[]{:S(2)}) collective-permute-start(bf16[3,1,128]{2,1,0:T(2,128)(2,1)S(1)} %get-tuple-element.28), channel_id=1, source_target_pairs={{0,1},{1,2},{2,3},{4,5},{5,6},{6,7},{8,9},{9,10},{10,11},{12,13},{... | collective-permute-start | bytes 2312 | tf_op jit(solution)/shard_map/ppermute | solution.py:37
  86.5 4.9 %collective-permute-start.13 = (bf16[3,1,128]{2,1,0:T(2,128)(2,1)S(1)}, bf16[3,1,128]{2,1,0:T(2,128)(2,1)S(1)}, u32[]{:S(2)}, u32[]{:S(2)}) collective-permute-start(bf16[3,1,128]{2,1,0:T(2,128)(2,1)S(1)} %get-tuple-element.29), channel_id=1, source_target_pairs={{1,0},{2,1},{3,2},{5,4},{6,5},{7,6},{9,8},{10,9},{11,10},{13,12},{... | collective-permute-start | bytes 2312 | tf_op jit(solution)/shard_map/ppermute | solution.py:39
  91.6 4.4 %collective-permute-start.14 = (bf16[3,1,128]{2,1,0:T(2,128)(2,1)S(1)}, bf16[3,1,128]{2,1,0:T(2,128)(2,1)S(1)}, u32[]{:S(2)}, u32[]{:S(2)}) collective-permute-start(bf16[3,1,128]{2,1,0:T(2,128)(2,1)S(1)} %get-tuple-element.26), channel_id=1, source_target_pairs={{0,1},{1,2},{2,3},{4,5},{5,6},{6,7},{8,9},{9,10},{10,11},{12,13},{... | collective-permute-start | bytes 2312 | tf_op jit(solution)/shard_map/ppermute | solution.py:37
  93.5 4.9 %collective-permute-start.15 = (bf16[3,1,128]{2,1,0:T(2,128)(2,1)S(1)}, bf16[3,1,128]{2,1,0:T(2,128)(2,1)S(1)}, u32[]{:S(2)}, u32[]{:S(2)}) collective-permute-start(bf16[3,1,128]{2,1,0:T(2,128)(2,1)S(1)} %get-tuple-element.27), channel_id=1, source_target_pairs={{1,0},{2,1},{3,2},{5,4},{6,5},{7,6},{9,8},{10,9},{11,10},{13,12},{... | collective-permute-start | bytes 2312 | tf_op jit(solution)/shard_map/ppermute | solution.py:39
  181.0 8.6 %copy-start.6 = (s32[1,1,1024]{2,1,0:T(1,128)S(1)}, s32[1,1,1024]{2,1,0:T(1,128)}, u32[]{:S(2)}) copy-start(s32[1,1,1024]{2,1,0:T(1,128)} %param.22) | copy-start | bytes 12292
  184.0 22.0 %copy-start.4 = (f32[3,64,128]{2,1,0:T(8,128)}, f32[3,64,128]{2,1,0:T(8,128)S(1)}, u32[]{:S(2)}) copy-start(f32[3,64,128]{2,1,0:T(8,128)S(1)} %fusion.39) | copy-start | bytes 294916
  184.9 12.6 %all-to-all-start.2 = ((f32[4,3,8192]{2,1,0:T(4,128)}), f32[4,3,8192]{2,1,0:T(4,128)S(1)}, u32[]{:S(2)}, u32[]{:S(2)}) async-start(f32[4,3,8192]{2,1,0:T(4,128)} %broadcast_in_dim.20), calls=%async_computation.2 | async-start | bytes 1048576 | tf_op jit(solution)/shard_map/all_to_all | solution.py:53
Sparse Core Ops, SparseCore 0:
  83.1 92.2 all-gather.3
where the time goes:
time: 223 us; the launch traced here: 222 us
  waiting for transfers between devices  96.4 us (43%)
  starting transfers between devices  54.3 us (24%)
  local copies, waits for them, and re-layouts  32.6 us (15%)
  other arithmetic  15.3 us (7%)
  between operations  14.6 us (7%)
  matrix products  9.12 us (4%)
    all_gather x1, waiting for transfers between devices, gathered_total(): tiles = lax.all_gather(value, axis)  77 us
    ppermute x6, starting transfers between devices, extended(): lax.ppermute(last, axis, up)  22.1 us
    ppermute x6, starting transfers between devices, extended(): lax.ppermute(leading, axis, [(b, a) for a, b in up])  9.81 us
    gather x1, local copies, waits for them, and re-layouts, shards(): picked = whole[:, (owner_ids * cells + points).reshape(-1)]  8.57 us
    transpose x1, local copies, waits for them, and re-layouts, in_order(): return jnp.moveaxis(tiles, 0, dim).reshape(lengths)  8.42 us
    scatter-add x1, other arithmetic, shards(): local.at[:, got_points.reshape(-1)]  8.22 us
    all_to_all x1, waiting for transfers between devices, copy_for_each(): lax.all_to_all(jnp.broadcast_to(value[None], (count, *value.shape)), axis...  7.94 us
    unnamed x30, local copies, waits for them, and re-layouts  7.65 us
  transfers between devices with their start and end apart: 20, of which 8 were waited for; matrix products, arithmetic and copies ran while one was open for 8% of the time, Pallas kernels for 0%

commit v1 on v0

v1 whole, which is shorter than its diff:
```python
import jax
import jax.numpy as jnp
from jax import lax
from jax.experimental import pallas as pl
from jax.experimental.pallas import tpu as pltpu
from jax.sharding import PartitionSpec as P

SWEEPS = 3
BF = jnp.bfloat16
F32 = jnp.float32
I32 = jnp.int32
LIMIT = 48 << 20


def vmem(n):
    return [pl.BlockSpec(memory_space=pltpu.VMEM)] * n


def iota(shape, dim):
    return lax.broadcasted_iota(I32, shape, dim)


def nt(a, b):
    return lax.dot_general(a, b, (((1,), (1,)), ((), ())), preferred_element_type=F32)


def slot_rows(final, tmap, elem, point, count_ref, rows_ref):
    owners = rows_ref.shape[0]
    slots = elem.shape[1]
    cap = slots // owners
    traction = nt(tmap, final).astype(BF)
    hot = (iota((final.shape[0], slots), 0) == elem).astype(F32).astype(BF)
    pull = jnp.dot(traction, hot, preferred_element_type=F32)
    slot = iota((1, slots), 1)
    owner = slot // cap
    limit = jnp.zeros((1, slots), I32)
    for k in range(owners):
        limit = jnp.where(owner == k, count_ref[0, k], limit)
    live = (slot - owner * cap) < limit
    row = point // 128
    code = (128 + (point - row * 128)).astype(F32)
    for b in range(6):
        code = code * jnp.where((row >> b) & 1 == 1, F32(2.0 ** (2**b)), F32(1.0))
    code = jnp.where(live, code, 0.0)
    pull = jnp.where(live, pull, 0.0)
    for k in range(owners):
        for j in range(4):
            source = code if j == 3 else pull[j : j + 1]
            for h in range(2):
                start = k * cap + h * 128
                rows_ref[k, 2 * j + h : 2 * j + h + 1, :] = source[:, start : start + 128]


def pack_kernel(state_ref, tmap_ref, elem_ref, point_ref, count_ref, out_ref, rows_ref):
    width = state_ref.shape[2]
    final = state_ref[...].astype(BF).reshape(-1, width)
    slot_rows(final, tmap_ref[...], elem_ref[...], point_ref[...], count_ref, rows_ref)
    out_ref[...] = jnp.broadcast_to(rows_ref[...].astype(BF)[None], out_ref.shape)


def decode(code):
    row = jnp.zeros(code.shape, F32)
    for b in (5, 4, 3, 2, 1, 0):
        big = code >= F32(128.0 * 2.0 ** (2**b))
        row = row + jnp.where(big, F32(2**b), 0.0)
        code = code * jnp.where(big, F32(2.0 ** -(2**b)), 1.0)
    return row, code - 128.0


def owner_kernel(src_ref, got_ref, disp_ref, stiff_ref, kd_ref, new_ref, *rest):
    replies = rest[:4]
    row_ref, lane_ref, acc_ref = rest[4:]
    sources = got_ref.shape[0]
    rows = disp_ref.shape[1]
    for h in range(2):
        row, lane = decode(got_ref[:, 6 + h, :].astype(F32))
        row_ref[h] = row
        lane_ref[h] = lane
    row_ids = iota((rows, 128), 0).astype(F32)
    lane_ids = iota((128, 128), 0).astype(F32)
    acc_ref[...] = jnp.zeros_like(acc_ref)
    group = 8

    def body(i, carry):
        base = pl.multiple_of(i * group, group)
        row8 = [row_ref[h, pl.ds(base, group), :] for h in range(2)]
        lane8 = [lane_ref[h, pl.ds(base, group), :] for h in range(2)]
        total = jnp.zeros((3 * rows, 128), F32)
        for g in range(group):
            vals = got_ref[base + g].astype(F32)
            left = []
            right = []
            for h in range(2):
                mask = row_ids == row8[h][g : g + 1]
                left.append(
                    jnp.concatenate(
                        [
                            jnp.where(mask, vals[2 * c + h : 2 * c + h + 1], 0.0).astype(BF)
                            for c in range(3)
                        ],
                        axis=0,
                    )
                )
                right.append((lane_ids == lane8[h][g : g + 1]).astype(F32).astype(BF))
            total += nt(jnp.concatenate(left, axis=1), jnp.concatenate(right, axis=1))
        acc_ref[...] += total
        return carry

    lax.fori_loop(0, sources // group, body, 0)
    loads = acc_ref[...].reshape(3, rows, 128)
    new = disp_ref[...] + (loads - kd_ref[...]) / (36.0 * stiff_ref[...])[None]
    new_ref[...] = new
    flat = new.reshape(3 * rows, 128)
    high = flat.astype(BF)
    rest1 = flat - high.astype(F32)
    mid = rest1.astype(BF)
    low = (rest1 - mid.astype(F32)).astype(BF)
    for d in range(4):
        src = src_ref[d]
        for h in range(2):
            row = row_ref[h, pl.ds(src, 1), :]
            lane = lane_ref[h, pl.ds(src, 1), :]
            hot = (lane_ids == lane).astype(F32).astype(BF)
            picked = jnp.dot(high, hot, preferred_element_type=F32)
            picked += jnp.dot(mid, hot, preferred_element_type=F32)
            picked += jnp.dot(low, hot, preferred_element_type=F32)
            mask = row_ids == row
            for c in range(3):
                part = jnp.where(mask, picked[c * rows : (c + 1) * rows], 0.0)
                replies[d][c : c + 1, h * 128 : (h + 1) * 128] = part.sum(axis=0, keepdims=True)


def finish_kernel(src_ref, r0, r1, r2, r3, out_ref):
    cap = r0.shape[1]
    for d, reply in enumerate((r0, r1, r2, r3)):
        start = pl.multiple_of(src_ref[4 + d] * cap, cap)
        out_ref[:, pl.ds(start, cap)] = reply[0:3, :]


def shell_kernel(side_ref, disp_ref, stiff_ref, high_ref, low_ref, kd_ref, field_ref, bend_ref):
    rows = disp_ref.shape[1]
    top = side_ref[0] > 0
    bottom = side_ref[1] > 0
    halo = high_ref[...].astype(F32) + low_ref[...].astype(F32)
    field_ref[...] = jnp.zeros_like(field_ref)
    bend_ref[...] = jnp.zeros_like(bend_ref)
    field_ref[:, 8 : 8 + rows, :] = disp_ref[...]
    lane = iota((1, 1, 128), 2)

    def sides(x):
        left = jnp.where(lane == 0, 0.0, pltpu.roll(x, 1, 2))
        right = jnp.where(lane == 127, 0.0, pltpu.roll(x, 127, 2))
        return left + right

    for c in range(3):
        field_ref[c, 6:8, :] = jnp.where(top, halo[0, 2 * c : 2 * c + 2], 0.0)
        field_ref[c, 8 + rows : 10 + rows, :] = jnp.where(bottom, halo[1, 2 * c : 2 * c + 2], 0.0)
    mid = field_ref[:, 7 : 9 + rows, :]
    bend = 4.0 * mid - (
        field_ref[:, 6 : 8 + rows, :] + field_ref[:, 8 : 10 + rows, :] + sides(mid)
    )
    bend_ref[:, 7 : 9 + rows, :] = bend
    for c in range(3):
        bend_ref[c, 7:8, :] = jnp.where(top, bend_ref[c, 7:8, :], 0.0)
        bend_ref[c, 8 + rows : 9 + rows, :] = jnp.where(
            bottom, bend_ref[c, 8 + rows : 9 + rows, :], 0.0
        )
    mid = bend_ref[:, 8 : 8 + rows, :]
    again = 4.0 * mid - (
        bend_ref[:, 7 : 7 + rows, :] + bend_ref[:, 9 : 9 + rows, :] + sides(mid)
    )
    kd_ref[...] = stiff_ref[...][None] * (again + 4.0 * mid)


def smem():
    return pl.BlockSpec(memory_space=pltpu.SMEM)


def params():
    return pltpu.CompilerParams(vmem_limit_bytes=LIMIT)


def patch_pairs(d):
    return [(p, p ^ d) for p in range(4)]


def exchange_and_relax(message, displacement, stiffness, kd):
    slabs, owners = lax.axis_size("slab"), lax.axis_size("patch")
    rows = displacement.shape[1]
    sources = slabs * owners
    got = lax.all_to_all(
        message.reshape(sources, 8, 128), ("slab", "patch"), 0, 0, tiled=True
    )
    slab, patch = lax.axis_index("slab"), lax.axis_index("patch")
    peer = patch ^ jnp.arange(4, dtype=I32)
    where = jnp.concatenate([slab * owners + peer, peer])
    reply = jax.ShapeDtypeStruct((8, 256), F32)
    new, *replies = pl.pallas_call(
        owner_kernel,
        out_shape=(jax.ShapeDtypeStruct(displacement.shape, F32),) + (reply,) * 4,
        in_specs=[smem()] + vmem(4),
        out_specs=vmem(5),
        scratch_shapes=[
            pltpu.VMEM((2, sources, 128), F32),
            pltpu.VMEM((2, sources, 128), F32),
            pltpu.VMEM((3 * rows, 128), F32),
        ],
        compiler_params=params(),
        name="owner",
    )(where, got, displacement, stiffness, kd)
    back = [replies[0]] + [
        lax.ppermute(replies[d], "patch", patch_pairs(d)) for d in (1, 2, 3)
    ]
    wall = pl.pallas_call(
        finish_kernel,
        out_shape=jax.ShapeDtypeStruct((3, owners * 256), F32),
        in_specs=[smem()] + vmem(4),
        out_specs=pl.BlockSpec(memory_space=pltpu.VMEM),
        compiler_params=params(),
        name="finish",
    )(where, *back)
    return new, wall


def split(value):
    high = value.astype(BF)
    return high, (value - high.astype(F32)).astype(BF)


def shell_force(displacement, stiffness):
    patch = lax.axis_index("patch")
    rows = displacement.shape[1]
    last = lax.axis_size("patch") - 1
    even = patch % 2 == 0
    first_rows = displacement[:, :2].reshape(6, 128)
    last_rows = displacement[:, rows - 2 :].reshape(6, 128)
    to_one = jnp.concatenate(split(jnp.where(even, last_rows, first_rows)))
    to_three = jnp.concatenate(split(jnp.where(even, first_rows, last_rows)))
    from_one = lax.ppermute(to_one, "patch", patch_pairs(1))
    from_three = lax.ppermute(to_three, "patch", patch_pairs(3))
    above = jnp.where(even, from_three, from_one)
    below = jnp.where(even, from_one, from_three)
    halo = jnp.stack([above, below])
    side = jnp.stack([(patch > 0).astype(I32), (patch < last).astype(I32)])
    shape = displacement.shape
    return pl.pallas_call(
        shell_kernel,
        out_shape=jax.ShapeDtypeStruct(shape, F32),
        in_specs=[smem()] + vmem(4),
        out_specs=pl.BlockSpec(memory_space=pltpu.VMEM),
        scratch_shapes=[pltpu.VMEM((3, rows + 16, 128), F32)] * 2,
        compiler_params=params(),
        name="shell",
    )(side, displacement, stiffness, halo[:, :6], halo[:, 6:])


def extended(value, sides, width):
    edges = {}
    for axis, dim in sides:
        count, length = (lax.axis_size(axis), value.shape[dim])
        up = [(i, (i + 1) % count) for i in range(count - 1)]
        last = lax.slice_in_dim(value, length - width, length, axis=dim)
        leading = lax.slice_in_dim(value, 0, width, axis=dim)
        edges[dim] = (
            lax.ppermute(last, axis, up),
            lax.ppermute(leading, axis, [(b, a) for a, b in up]),
        )
    done = []
    for _, dim in sides:
        low, high = edges[dim]
        around = [(width, width) if d in done else (0, 0) for d in range(value.ndim)]
        value = jnp.concatenate([jnp.pad(low, around), value, jnp.pad(high, around)], axis=dim)
        done.append(dim)
    return value


def element_apply(rounded, scale, element_matrix, couple_x, couple_y):
    padded = extended(rounded, (("slab", 0), ("patch", 1)), 1)
    along_x = (padded[:-2, 1:-1].astype(F32) + padded[2:, 1:-1].astype(F32)).astype(BF)
    along_y = (padded[1:-1, :-2].astype(F32) + padded[1:-1, 2:].astype(F32)).astype(BF)
    width = rounded.shape[2]
    own = jnp.dot(rounded.reshape(-1, width), element_matrix, preferred_element_type=F32)
    side_x = jnp.dot(along_x.reshape(-1, width), couple_x, preferred_element_type=F32)
    side_y = jnp.dot(along_y.reshape(-1, width), couple_y, preferred_element_type=F32)
    return (
        scale[:, :, None] * own.reshape(rounded.shape)
        - side_x.reshape(rounded.shape)
        - side_y.reshape(rounded.shape)
    )


def shards(
    fluid_state,
    fluid_rhs,
    element_scale,
    element_matrix,
    couple_x,
    couple_y,
    block_inverse,
    traction_map,
    slot_elem,
    slot_point,
    slot_count,
    displacement,
    stiffness,
):
    width = fluid_state.shape[2]
    slots = slot_elem.shape[2]
    slabs, owners = lax.axis_size("slab"), lax.axis_size("patch")
    kd = shell_force(displacement, stiffness)
    state = fluid_state
    for sweep in range(SWEEPS):
        rounded = state.astype(BF)
        applied = element_apply(rounded, element_scale, element_matrix, couple_x, couple_y)
        residue = (fluid_rhs - applied).astype(BF)
        update = jnp.dot(
            residue.reshape(-1, width), block_inverse, preferred_element_type=F32
        ).reshape(state.shape)
        state = state + update / element_scale[:, :, None]
    tmap = jnp.pad(traction_map, ((0, 5), (0, 0)))
    message = pl.pallas_call(
        pack_kernel,
        out_shape=jax.ShapeDtypeStruct((slabs, owners, 8, 128), BF),
        in_specs=vmem(4) + [smem()],
        out_specs=pl.BlockSpec(memory_space=pltpu.VMEM),
        scratch_shapes=[pltpu.VMEM((owners, 8, 128), F32)],
        compiler_params=params(),
        name="pack",
    )(
        state,
        tmap,
        slot_elem.reshape(1, slots),
        slot_point.reshape(1, slots),
        slot_count.reshape(1, owners),
    )
    new, wall = exchange_and_relax(message, displacement, stiffness, kd)
    return state, new, wall.reshape(3, 1, 1, slots)


def solution(mesh):
    return jax.shard_map(
        shards,
        mesh=mesh,
        in_specs=(
            P("slab", "patch", None),
            P("slab", "patch", None),
            P("slab", "patch"),
            P(),
            P(),
            P(),
            P(),
            P(),
            P("slab", "patch", None),
            P("slab", "patch", None),
            P("slab", "patch", None),
            P(None, "patch", None),
            P("patch", None),
        ),
        out_specs=(
            P("slab", "patch", None),
            P(None, "patch", None),
            P(None, "slab", "patch", None),
        ),
        check_vma=False,
    )
```

time: 223 us -> 91.8 us (0.41)
  waiting for transfers between devices: 96.4 us -> 16.8 us
  local copies, waits for them, and re-layouts: 32.6 us -> 4.07 us
  other arithmetic: 15.3 us -> 1.16 us
  between operations: 14.6 us -> 1.12 us
  Pallas kernels: 0 us -> 11.7 us
  matrix products: 9.12 us -> 1.9 us
    all_gather x1 -> x0, waiting for transfers between devices: 77 us -> none  [gathered_total(): tiles = lax.all_gather(value, axis)]
    gather x2 -> x0, local copies, waits for them, and re-layouts: 12.5 us -> none  [the longest x1 8.57 us: shards(): picked = whole[:, (owner_ids * cells + points).reshape(-1)]]
    pallas_call x0 -> x4, Pallas kernels: none -> 11.7 us  [the longest x1 8.82 us: exchange_and_relax(): pl.pallas_call(owner_kernel, out_shape=(jax.ShapeDtypeStruct(displacement...]
    transpose x1 -> x0, local copies, waits for them, and re-layouts: 8.42 us -> none  [in_order(): return jnp.moveaxis(tiles, 0, dim).reshape(lengths)]
    scatter-add x1 -> x0, other arithmetic: 8.22 us -> none  [shards(): local.at[:, got_points.reshape(-1)]]
    all_to_all x3 -> x1, starting transfers between devices: 12.6 us -> 18.9 us  [exchange_and_relax(): lax.all_to_all(message.reshape(sources, 8, 128), ('slab', 'patch'), 0, 0,...]
    ppermute x4 -> x5, starting transfers between devices: 9.72 us -> 4.04 us  [the longest x3 2.14 us: exchange_and_relax(): lax.ppermute(replies[d], 'patch', patch_pairs(d))]
    ppermute x4 -> x5, waiting for transfers between devices: 5.37 us -> 1.72 us  [the longest x3 1.71 us: exchange_and_relax(): lax.ppermute(replies[d], 'patch', patch_pairs(d))]
  transfers between devices with their start and end apart: 20 -> 18, of which waited for: 8 -> 5; matrix products, arithmetic and copies ran while one was open for 8% -> 2% of each run, Pallas kernels for 0% -> 3%
where the time goes in v1:
time: 91.8 us; the launch traced here: 91.1 us
  starting transfers between devices  54.4 us (59%)
  waiting for transfers between devices  16.8 us (18%)
  Pallas kernels  11.7 us (13%)
  local copies, waits for them, and re-layouts  4.07 us (4%)
  matrix products  1.9 us (2%)
  other arithmetic  1.16 us (1%)
  between operations  1.12 us (1%)
    ppermute x6, starting transfers between devices, extended(): lax.ppermute(last, axis, up)  21.5 us
    all_to_all x1, starting transfers between devices, exchange_and_relax(): lax.all_to_all(message.reshape(sources, 8, 128), ('slab', 'patch'), 0, 0,...  18.9 us
    ppermute x6, starting transfers between devices, extended(): lax.ppermute(leading, axis, [(b, a) for a, b in up])  9.98 us
    all_to_all x1, waiting for transfers between devices, exchange_and_relax(): lax.all_to_all(message.reshape(sources, 8, 128), ('slab', 'patch'), 0, 0,...  9.81 us
    pallas_call x1, Pallas kernels, exchange_and_relax(): pl.pallas_call(owner_kernel, out_shape=(jax.ShapeDtypeStruct(displacement...  8.82 us
    ppermute x6, waiting for transfers between devices, extended(): lax.ppermute(leading, axis, [(b, a) for a, b in up])  5.24 us
    unnamed x29, local copies, waits for them, and re-layouts  4.01 us
    ppermute x3, starting transfers between devices, exchange_and_relax(): lax.ppermute(replies[d], 'patch', patch_pairs(d))  2.14 us
  transfers between devices with their start and end apart: 18, of which 5 were waited for; matrix products, arithmetic and copies ran while one was open for 2% of the time, Pallas kernels for 3%

profile of v1, /device:TPU:1, one launch (start us, length us, event | category | flops | bytes accessed | tf_op | source)
XLA Modules:
  0.0 91.1 jit_solution(16898728178132803141)
XLA Ops:
  0.6 0.9 %convert_element_type.101 = bf16[2,64,256]{2,1,0:T(8,128)(2,1)S(1)} convert(f32[2,64,256]{2,1,0:T(8,128)} %param.13) | non-fusion elementwise | flops 32768 | bytes 196608 | tf_op jit(solution)/shard_map/convert_element_type | solution.py:313
  1.6 4.5 %collective-permute-start = (bf16[1,64,256]{2,1,0:T(8,128)(2,1)S(1)}, bf16[1,64,256]{2,1,0:T(8,128)(2,1)S(1)}, u32[]{:S(2)}, u32[]{:S(2)}) collective-permute-start(bf16[1,64,256]{2,1,0:T(8,128)(2,1)S(1)} %get-tuple-element.35), channel_id=1, source_target_pairs={{0,4},{4,8},{8,12},{12,16},{16,20},{20,24},{24,28},{28,32},{32,36}... | collective-permute-start | bytes 98312 | tf_op jit(solution)/shard_map/ppermute | solution.py:265
  6.1 1.3 %collective-permute-start.1 = (bf16[1,64,256]{2,1,0:T(8,128)(2,1)S(1)}, bf16[1,64,256]{2,1,0:T(8,128)(2,1)S(1)}, u32[]{:S(2)}, u32[]{:S(2)}) collective-permute-start(bf16[1,64,256]{2,1,0:T(8,128)(2,1)S(1)} %get-tuple-element.36), channel_id=1, source_target_pairs={{4,0},{8,4},{12,8},{16,12},{20,16},{24,20},{28,24},{32,28},{36,32}... | collective-permute-start | bytes 98312 | tf_op jit(solution)/shard_map/ppermute | solution.py:266
  7.5 4.0 %collective-permute-start.2 = (bf16[2,1,256]{2,1,0:T(2,128)(2,1)S(1)}, bf16[2,1,256]{2,1,0:T(2,128)(2,1)S(1)}, u32[]{:S(2)}, u32[]{:S(2)}) collective-permute-start(bf16[2,1,256]{2,1,0:T(2,128)(2,1)S(1)} %get-tuple-element.33), channel_id=1, source_target_pairs={{0,1},{1,2},{2,3},{4,5},{5,6},{6,7},{8,9},{9,10},{10,11},{12,13},{... | collective-permute-start | bytes 3080 | tf_op jit(solution)/shard_map/ppermute | solution.py:265
  11.4 1.9 %collective-permute-start.3 = (bf16[2,1,256]{2,1,0:T(2,128)(2,1)S(1)}, bf16[2,1,256]{2,1,0:T(2,128)(2,1)S(1)}, u32[]{:S(2)}, u32[]{:S(2)}) collective-permute-start(bf16[2,1,256]{2,1,0:T(2,128)(2,1)S(1)} %get-tuple-element.34), channel_id=1, source_target_pairs={{1,0},{2,1},{3,2},{5,4},{6,5},{7,6},{9,8},{10,9},{11,10},{13,12},{... | collective-permute-start | bytes 3080 | tf_op jit(solution)/shard_map/ppermute | solution.py:266
  13.4 1.8 %collective-permute-start.12 = (bf16[12,128]{1,0:T(8,128)(2,1)S(1)}, bf16[12,128]{1,0:T(8,128)(2,1)S(1)}, u32[]{:S(2)}, u32[]{:S(2)}) collective-permute-start(bf16[12,128]{1,0:T(8,128)(2,1)S(1)} %pad_maximum_fusion.49), channel_id=1, source_target_pairs={{0,3},{1,2},{2,1},{3,0},{4,7},{5,6},{6,5},{7,4},{8,11},{9,10},{10,... | collective-permute-start | bytes 9224 | tf_op jit(solution)/shard_map/ppermute | solution.py:240
  15.3 0.7 copy-done.10
  15.9 0.2 convolution_multiply_fusion.2
  16.1 0.1 add_convert_fusion.15.side_ref
  16.2 0.1 pad_add_fusion.src_ref
  16.3 0.6 copy-done.11
  16.9 0.1 collective-permute-start.13
  17.0 0.2 convolution_subtract_fusion.5
  17.2 0.6 copy-done.9
  17.8 0.1 copy-done.12
  17.9 0.1 copy-done.13
  17.9 0.3 fusion.142
  18.3 0.2 convolution_multiply_fusion.1
  18.4 4.3 %collective-permute-start.4 = (bf16[1,64,256]{2,1,0:T(8,128)(2,1)S(1)}, bf16[1,64,256]{2,1,0:T(8,128)(2,1)S(1)}, u32[]{:S(2)}, u32[]{:S(2)}) collective-permute-start(bf16[1,64,256]{2,1,0:T(8,128)(2,1)S(1)} %get-tuple-element.31), channel_id=1, source_target_pairs={{0,4},{4,8},{8,12},{12,16},{16,20},{20,24},{24,28},{28,32},{32,36}... | collective-permute-start | bytes 98312 | tf_op jit(solution)/shard_map/ppermute | solution.py:265
  22.7 1.3 %collective-permute-start.5 = (bf16[1,64,256]{2,1,0:T(8,128)(2,1)S(1)}, bf16[1,64,256]{2,1,0:T(8,128)(2,1)S(1)}, u32[]{:S(2)}, u32[]{:S(2)}) collective-permute-start(bf16[1,64,256]{2,1,0:T(8,128)(2,1)S(1)} %get-tuple-element.32), channel_id=1, source_target_pairs={{4,0},{8,4},{12,8},{16,12},{20,16},{24,20},{28,24},{32,28},{36,32}... | collective-permute-start | bytes 98312 | tf_op jit(solution)/shard_map/ppermute | solution.py:266
  24.0 2.2 %collective-permute-start.6 = (bf16[2,1,256]{2,1,0:T(2,128)(2,1)S(1)}, bf16[2,1,256]{2,1,0:T(2,128)(2,1)S(1)}, u32[]{:S(2)}, u32[]{:S(2)}) collective-permute-start(bf16[2,1,256]{2,1,0:T(2,128)(2,1)S(1)} %get-tuple-element.29), channel_id=1, source_target_pairs={{0,1},{1,2},{2,3},{4,5},{5,6},{6,7},{8,9},{9,10},{10,11},{12,13},{... | collective-permute-start | bytes 3080 | tf_op jit(solution)/shard_map/ppermute | solution.py:265
  26.3 2.1 %collective-permute-start.7 = (bf16[2,1,256]{2,1,0:T(2,128)(2,1)S(1)}, bf16[2,1,256]{2,1,0:T(2,128)(2,1)S(1)}, u32[]{:S(2)}, u32[]{:S(2)}) collective-permute-start(bf16[2,1,256]{2,1,0:T(2,128)(2,1)S(1)} %get-tuple-element.30), channel_id=1, source_target_pairs={{1,0},{2,1},{3,2},{5,4},{6,5},{7,6},{9,8},{10,9},{11,10},{13,12},{... | collective-permute-start | bytes 3080 | tf_op jit(solution)/shard_map/ppermute | solution.py:266
  28.4 0.2 convolution_subtract_fusion.3
  28.6 2.6 %collective-permute-done.7 = bf16[2,1,256]{2,1,0:T(2,128)(2,1)S(1)} collective-permute-done((bf16[2,1,256]{2,1,0:T(2,128)(2,1)S(1)}, bf16[2,1,256]{2,1,0:T(2,128)(2,1)S(1)}, u32[]{:S(2)}, u32[]{:S(2)}) %collective-permute-start.7) | collective-permute-done | bytes 1056 | tf_op jit(solution)/shard_map/ppermute | solution.py:266
  31.2 0.3 fusion.145
  31.5 0.2 convolution_multiply_fusion
  31.7 4.3 %collective-permute-start.8 = (bf16[1,64,256]{2,1,0:T(8,128)(2,1)S(1)}, bf16[1,64,256]{2,1,0:T(8,128)(2,1)S(1)}, u32[]{:S(2)}, u32[]{:S(2)}) collective-permute-start(bf16[1,64,256]{2,1,0:T(8,128)(2,1)S(1)} %get-tuple-element.27), channel_id=1, source_target_pairs={{0,4},{4,8},{8,12},{12,16},{16,20},{20,24},{24,28},{28,32},{32,36}... | collective-permute-start | bytes 98312 | tf_op jit(solution)/shard_map/ppermute | solution.py:265
  35.9 1.3 %collective-permute-start.9 = (bf16[1,64,256]{2,1,0:T(8,128)(2,1)S(1)}, bf16[1,64,256]{2,1,0:T(8,128)(2,1)S(1)}, u32[]{:S(2)}, u32[]{:S(2)}) collective-permute-start(bf16[1,64,256]{2,1,0:T(8,128)(2,1)S(1)} %get-tuple-element.28), channel_id=1, source_target_pairs={{4,0},{8,4},{12,8},{16,12},{20,16},{24,20},{28,24},{32,28},{36,32}... | collective-permute-start | bytes 98312 | tf_op jit(solution)/shard_map/ppermute | solution.py:266
  37.2 2.2 %collective-permute-start.10 = (bf16[2,1,256]{2,1,0:T(2,128)(2,1)S(1)}, bf16[2,1,256]{2,1,0:T(2,128)(2,1)S(1)}, u32[]{:S(2)}, u32[]{:S(2)}) collective-permute-start(bf16[2,1,256]{2,1,0:T(2,128)(2,1)S(1)} %get-tuple-element.25), channel_id=1, source_target_pairs={{0,1},{1,2},{2,3},{4,5},{5,6},{6,7},{8,9},{9,10},{10,11},{12,13},{... | collective-permute-start | bytes 3080 | tf_op jit(solution)/shard_map/ppermute | solution.py:265
  39.5 2.1 %collective-permute-start.11 = (bf16[2,1,256]{2,1,0:T(2,128)(2,1)S(1)}, bf16[2,1,256]{2,1,0:T(2,128)(2,1)S(1)}, u32[]{:S(2)}, u32[]{:S(2)}) collective-permute-start(bf16[2,1,256]{2,1,0:T(2,128)(2,1)S(1)} %get-tuple-element.26), channel_id=1, source_target_pairs={{1,0},{2,1},{3,2},{5,4},{6,5},{7,6},{9,8},{10,9},{11,10},{13,12},{... | collective-permute-start | bytes 3080 | tf_op jit(solution)/shard_map/ppermute | solution.py:266
  41.6 0.2 convolution_subtract_fusion.1
  41.8 2.6 %collective-permute-done.11 = bf16[2,1,256]{2,1,0:T(2,128)(2,1)S(1)} collective-permute-done((bf16[2,1,256]{2,1,0:T(2,128)(2,1)S(1)}, bf16[2,1,256]{2,1,0:T(2,128)(2,1)S(1)}, u32[]{:S(2)}, u32[]{:S(2)}) %collective-permute-start.11) | collective-permute-done | bytes 1056 | tf_op jit(solution)/shard_map/ppermute | solution.py:266
  44.4 0.3 fusion.5.state_ref
  44.8 0.3 copy-done.5
  45.1 0.3 copy-done.4
  45.5 1.6 %pack.1 = bf16[32,4,8,128]{3,2,1,0:T(8,128)(2,1)} custom-call(f32[2,64,256]{2,1,0:T(8,128)S(1)} %fusion.5.state_ref, bf16[8,256]{1,0:T(8,128)(2,1)S(1)} %pad.29.tmap_ref, s32[1,1024]{1,0:T(1,128)S(1)} %bitcast.54, s32[1,1024]{1,0:T(1,128)S(1)} %bitcast.55, s32[1,4]{1,0:T(1,128)S(1)} %bitcast.56), custom_call_target="tpu_custom_call" | custom-call | tf_op jit(solution)/shard_map/pack/pallas_call | solution.py:321
  47.0 18.9 %all-to-all-start = ((bf16[128,8,128]{2,1,0:T(8,128)(2,1)}), bf16[128,8,128]{2,1,0:T(8,128)(2,1)S(1)}, u32[]{:S(2)}, u32[]{:S(2)}) async-start(bf16[128,8,128]{2,1,0:T(8,128)(2,1)} %bitcast.7), calls=%async_computation | async-start | bytes 524288 | tf_op jit(solution)/shard_map/all_to_all | solution.py:191
  66.0 0.7 copy-done.3
  66.7 0.8 shell.1.kd_ref
  67.5 9.8 %all-to-all-done.got_ref = bf16[128,8,128]{2,1,0:T(8,128)(2,1)S(1)} async-done(((bf16[128,8,128]{2,1,0:T(8,128)(2,1)}), bf16[128,8,128]{2,1,0:T(8,128)(2,1)S(1)}, u32[]{:S(2)}, u32[]{:S(2)}) %all-to-all-start) | async-done | bytes 262176 | tf_op jit(solution)/shard_map/all_to_all | solution.py:191
  77.3 8.8 %owner.1 = (f32[3,64,128]{2,1,0:T(8,128)}, f32[8,256]{1,0:T(8,128)S(1)}, f32[8,256]{1,0:T(8,128)S(1)}, f32[8,256]{1,0:T(8,128)S(1)}, f32[8,256]{1,0:T(8,128)S(1)}) custom-call(s32[8]{0:T(128)S(1)} %pad_add_fusion.src_ref, bf16[128,8,128]{2,1,0:T(8,128)(2,1)S(1)} %all-to-all-done.got_ref, f32[3,64,128]{2,1,0:T(8,128)S(1)} %copy-done.1, ...), custom_call_target="tpu_custom_call" | custom-call | tf_op jit(solution)/shard_map/owner/pallas_call | solution.py:198
  86.1 0.5 collective-permute-start.14
  86.6 0.3 collective-permute-start.15
  86.9 1.4 %collective-permute-start.16 = (f32[8,256]{1,0:T(8,128)S(1)}, f32[8,256]{1,0:T(8,128)S(1)}, u32[]{:S(2)}, u32[]{:S(2)}) collective-permute-start(f32[8,256]{1,0:T(8,128)S(1)} %get-tuple-element.12), channel_id=1, source_target_pairs={{0,3},{1,2},{2,1},{3,0},{4,7},{5,6},{6,5},{7,4},{8,11},{9,10},{10,... | collective-permute-start | bytes 24584 | tf_op jit(solution)/shard_map/ppermute | solution.py:212
  88.3 0.8 collective-permute-done.15.r2
  89.1 0.9 collective-permute-done.16.r3
  90.0 0.5 finish.1
  90.5 0.6 copy.17
  (50 shorter events, 0.2 us)
Async XLA Ops:
  0.6 16.6 %copy-start = (bf16[256,256]{1,0:T(8,128)(2,1)S(1)}, bf16[256,256]{1,0:T(8,128)(2,1)}, u32[]{:S(2)}) copy-start(bf16[256,256]{1,0:T(8,128)(2,1)} %param.19) | copy-start | bytes 393220
  1.6 11.8 %copy-start.1 = (f32[3,64,128]{2,1,0:T(8,128)S(1)}, f32[3,64,128]{2,1,0:T(8,128)}, u32[]{:S(2)}) copy-start(f32[3,64,128]{2,1,0:T(8,128)} %disp_ref.3) | copy-start | bytes 294916
  1.6 13.7 %copy-start.7 = (bf16[256,256]{1,0:T(8,128)(2,1)S(1)}, bf16[256,256]{1,0:T(8,128)(2,1)}, u32[]{:S(2)}) copy-start(bf16[256,256]{1,0:T(8,128)(2,1)} %param.16) | copy-start | bytes 393220
  1.6 15.3 %collective-permute-start = (bf16[1,64,256]{2,1,0:T(8,128)(2,1)S(1)}, bf16[1,64,256]{2,1,0:T(8,128)(2,1)S(1)}, u32[]{:S(2)}, u32[]{:S(2)}) collective-permute-start(bf16[1,64,256]{2,1,0:T(8,128)(2,1)S(1)} %get-tuple-element.35), channel_id=1, source_target_pairs={{0,4},{4,8},{8,12},{12,16},{16,20},{20,24},{24,28},{28,32},{32,36}... | collective-permute-start | bytes 98312 | tf_op jit(solution)/shard_map/ppermute | solution.py:265
  6.1 10.9 %collective-permute-start.1 = (bf16[1,64,256]{2,1,0:T(8,128)(2,1)S(1)}, bf16[1,64,256]{2,1,0:T(8,128)(2,1)S(1)}, u32[]{:S(2)}, u32[]{:S(2)}) collective-permute-start(bf16[1,64,256]{2,1,0:T(8,128)(2,1)S(1)} %get-tuple-element.36), channel_id=1, source_target_pairs={{4,0},{8,4},{12,8},{16,12},{20,16},{24,20},{28,24},{32,28},{36,32}... | collective-permute-start | bytes 98312 | tf_op jit(solution)/shard_map/ppermute | solution.py:266
  7.5 9.8 %collective-permute-start.2 = (bf16[2,1,256]{2,1,0:T(2,128)(2,1)S(1)}, bf16[2,1,256]{2,1,0:T(2,128)(2,1)S(1)}, u32[]{:S(2)}, u32[]{:S(2)}) collective-permute-start(bf16[2,1,256]{2,1,0:T(2,128)(2,1)S(1)} %get-tuple-element.33), channel_id=1, source_target_pairs={{0,1},{1,2},{2,3},{4,5},{5,6},{6,7},{8,9},{9,10},{10,11},{12,13},{... | collective-permute-start | bytes 3080 | tf_op jit(solution)/shard_map/ppermute | solution.py:265
  11.4 5.8 %collective-permute-start.3 = (bf16[2,1,256]{2,1,0:T(2,128)(2,1)S(1)}, bf16[2,1,256]{2,1,0:T(2,128)(2,1)S(1)}, u32[]{:S(2)}, u32[]{:S(2)}) collective-permute-start(bf16[2,1,256]{2,1,0:T(2,128)(2,1)S(1)} %get-tuple-element.34), channel_id=1, source_target_pairs={{1,0},{2,1},{3,2},{5,4},{6,5},{7,6},{9,8},{10,9},{11,10},{13,12},{... | collective-permute-start | bytes 3080 | tf_op jit(solution)/shard_map/ppermute | solution.py:266
  13.4 52.5 %collective-permute-start.12 = (bf16[12,128]{1,0:T(8,128)(2,1)S(1)}, bf16[12,128]{1,0:T(8,128)(2,1)S(1)}, u32[]{:S(2)}, u32[]{:S(2)}) collective-permute-start(bf16[12,128]{1,0:T(8,128)(2,1)S(1)} %pad_maximum_fusion.49), channel_id=1, source_target_pairs={{0,3},{1,2},{2,1},{3,0},{4,7},{5,6},{6,5},{7,4},{8,11},{9,10},{10,... | collective-permute-start | bytes 9224 | tf_op jit(solution)/shard_map/ppermute | solution.py:240
  15.3 0.7 copy-start.10
  15.9 1.1 %copy-start.8 = (bf16[256,256]{1,0:T(8,128)(2,1)S(1)}, bf16[256,256]{1,0:T(8,128)(2,1)}, u32[]{:S(2)}) copy-start(bf16[256,256]{1,0:T(8,128)(2,1)} %param.17) | copy-start | bytes 393220
  16.2 0.7 copy-start.11
  16.9 0.9 copy-start.9
  16.9 1.0 %copy-start.12 = (f32[2,64,256]{2,1,0:T(8,128)S(1)}, f32[2,64,256]{2,1,0:T(8,128)}, u32[]{:S(2)}) copy-start(f32[2,64,256]{2,1,0:T(8,128)} %param.14) | copy-start | bytes 393220
  16.9 1.0 %copy-start.13 = (bf16[256,256]{1,0:T(8,128)(2,1)S(1)}, bf16[256,256]{1,0:T(8,128)(2,1)}, u32[]{:S(2)}) copy-start(bf16[256,256]{1,0:T(8,128)(2,1)} %param.18) | copy-start | bytes 393220
  16.9 49.0 %collective-permute-start.13 = (bf16[12,128]{1,0:T(8,128)(2,1)S(1)}, bf16[12,128]{1,0:T(8,128)(2,1)S(1)}, u32[]{:S(2)}, u32[]{:S(2)}) collective-permute-start(bf16[12,128]{1,0:T(8,128)(2,1)S(1)} %pad_maximum_fusion.50), channel_id=1, source_target_pairs={{0,1},{1,0},{2,3},{3,2},{4,5},{5,4},{6,7},{7,6},{8,9},{9,8},{10,11... | collective-permute-start | bytes 9224 | tf_op jit(solution)/shard_map/ppermute | solution.py:239
  18.4 7.8 %collective-permute-start.4 = (bf16[1,64,256]{2,1,0:T(8,128)(2,1)S(1)}, bf16[1,64,256]{2,1,0:T(8,128)(2,1)S(1)}, u32[]{:S(2)}, u32[]{:S(2)}) collective-permute-start(bf16[1,64,256]{2,1,0:T(8,128)(2,1)S(1)} %get-tuple-element.31), channel_id=1, source_target_pairs={{0,4},{4,8},{8,12},{12,16},{16,20},{20,24},{24,28},{28,32},{32,36}... | collective-permute-start | bytes 98312 | tf_op jit(solution)/shard_map/ppermute | solution.py:265
  22.7 5.7 %collective-permute-start.5 = (bf16[1,64,256]{2,1,0:T(8,128)(2,1)S(1)}, bf16[1,64,256]{2,1,0:T(8,128)(2,1)S(1)}, u32[]{:S(2)}, u32[]{:S(2)}) collective-permute-start(bf16[1,64,256]{2,1,0:T(8,128)(2,1)S(1)} %get-tuple-element.32), channel_id=1, source_target_pairs={{4,0},{8,4},{12,8},{16,12},{20,16},{24,20},{28,24},{32,28},{36,32}... | collective-permute-start | bytes 98312 | tf_op jit(solution)/shard_map/ppermute | solution.py:266
  24.0 4.5 %collective-permute-start.6 = (bf16[2,1,256]{2,1,0:T(2,128)(2,1)S(1)}, bf16[2,1,256]{2,1,0:T(2,128)(2,1)S(1)}, u32[]{:S(2)}, u32[]{:S(2)}) collective-permute-start(bf16[2,1,256]{2,1,0:T(2,128)(2,1)S(1)} %get-tuple-element.29), channel_id=1, source_target_pairs={{0,1},{1,2},{2,3},{4,5},{5,6},{6,7},{8,9},{9,10},{10,11},{12,13},{... | collective-permute-start | bytes 3080 | tf_op jit(solution)/shard_map/ppermute | solution.py:265
  26.3 4.9 %collective-permute-start.7 = (bf16[2,1,256]{2,1,0:T(2,128)(2,1)S(1)}, bf16[2,1,256]{2,1,0:T(2,128)(2,1)S(1)}, u32[]{:S(2)}, u32[]{:S(2)}) collective-permute-start(bf16[2,1,256]{2,1,0:T(2,128)(2,1)S(1)} %get-tuple-element.30), channel_id=1, source_target_pairs={{1,0},{2,1},{3,2},{5,4},{6,5},{7,6},{9,8},{10,9},{11,10},{13,12},{... | collective-permute-start | bytes 3080 | tf_op jit(solution)/shard_map/ppermute | solution.py:266
  31.7 7.8 %collective-permute-start.8 = (bf16[1,64,256]{2,1,0:T(8,128)(2,1)S(1)}, bf16[1,64,256]{2,1,0:T(8,128)(2,1)S(1)}, u32[]{:S(2)}, u32[]{:S(2)}) collective-permute-start(bf16[1,64,256]{2,1,0:T(8,128)(2,1)S(1)} %get-tuple-element.27), channel_id=1, source_target_pairs={{0,4},{4,8},{8,12},{12,16},{16,20},{20,24},{24,28},{28,32},{32,36}... | collective-permute-start | bytes 98312 | tf_op jit(solution)/shard_map/ppermute | solution.py:265
  35.9 5.7 %collective-permute-start.9 = (bf16[1,64,256]{2,1,0:T(8,128)(2,1)S(1)}, bf16[1,64,256]{2,1,0:T(8,128)(2,1)S(1)}, u32[]{:S(2)}, u32[]{:S(2)}) collective-permute-start(bf16[1,64,256]{2,1,0:T(8,128)(2,1)S(1)} %get-tuple-element.28), channel_id=1, source_target_pairs={{4,0},{8,4},{12,8},{16,12},{20,16},{24,20},{28,24},{32,28},{36,32}... | collective-permute-start | bytes 98312 | tf_op jit(solution)/shard_map/ppermute | solution.py:266
  37.2 4.5 %collective-permute-start.10 = (bf16[2,1,256]{2,1,0:T(2,128)(2,1)S(1)}, bf16[2,1,256]{2,1,0:T(2,128)(2,1)S(1)}, u32[]{:S(2)}, u32[]{:S(2)}) collective-permute-start(bf16[2,1,256]{2,1,0:T(2,128)(2,1)S(1)} %get-tuple-element.25), channel_id=1, source_target_pairs={{0,1},{1,2},{2,3},{4,5},{5,6},{6,7},{8,9},{9,10},{10,11},{12,13},{... | collective-permute-start | bytes 3080 | tf_op jit(solution)/shard_map/ppermute | solution.py:265
  39.5 4.9 %collective-permute-start.11 = (bf16[2,1,256]{2,1,0:T(2,128)(2,1)S(1)}, bf16[2,1,256]{2,1,0:T(2,128)(2,1)S(1)}, u32[]{:S(2)}, u32[]{:S(2)}) collective-permute-start(bf16[2,1,256]{2,1,0:T(2,128)(2,1)S(1)} %get-tuple-element.26), channel_id=1, source_target_pairs={{1,0},{2,1},{3,2},{5,4},{6,5},{7,6},{9,8},{10,9},{11,10},{13,12},{... | collective-permute-start | bytes 3080 | tf_op jit(solution)/shard_map/ppermute | solution.py:266
  44.4 0.7 copy-start.5
  44.7 2.3 %copy-start.2 = (f32[2,64,256]{2,1,0:T(8,128)}, f32[2,64,256]{2,1,0:T(8,128)S(1)}, u32[]{:S(2)}) copy-start(f32[2,64,256]{2,1,0:T(8,128)S(1)} %fusion.5.state_ref) | copy-start | bytes 393220
  44.7 0.7 copy-start.4
  44.7 0.7 copy-start.6
  47.0 30.3 %all-to-all-start = ((bf16[128,8,128]{2,1,0:T(8,128)(2,1)}), bf16[128,8,128]{2,1,0:T(8,128)(2,1)S(1)}, u32[]{:S(2)}, u32[]{:S(2)}) async-start(bf16[128,8,128]{2,1,0:T(8,128)(2,1)} %bitcast.7), calls=%async_computation | async-start | bytes 524288 | tf_op jit(solution)/shard_map/all_to_all | solution.py:191
  65.9 0.8 copy-start.3
  86.1 2.1 %collective-permute-start.14 = (f32[8,256]{1,0:T(8,128)S(1)}, f32[8,256]{1,0:T(8,128)S(1)}, u32[]{:S(2)}, u32[]{:S(2)}) collective-permute-start(f32[8,256]{1,0:T(8,128)S(1)} %get-tuple-element.10), channel_id=1, source_target_pairs={{0,1},{1,0},{2,3},{3,2},{4,5},{5,4},{6,7},{7,6},{8,9},{9,8},{10,11... | collective-permute-start | bytes 24584 | tf_op jit(solution)/shard_map/ppermute | solution.py:212
  86.6 2.5 %collective-permute-start.15 = (f32[8,256]{1,0:T(8,128)S(1)}, f32[8,256]{1,0:T(8,128)S(1)}, u32[]{:S(2)}, u32[]{:S(2)}) collective-permute-start(f32[8,256]{1,0:T(8,128)S(1)} %get-tuple-element.11), channel_id=1, source_target_pairs={{0,2},{1,3},{2,0},{3,1},{4,6},{5,7},{6,4},{7,5},{8,10},{9,11},{10,... | collective-permute-start | bytes 24584 | tf_op jit(solution)/shard_map/ppermute | solution.py:212
  86.9 3.1 %collective-permute-start.16 = (f32[8,256]{1,0:T(8,128)S(1)}, f32[8,256]{1,0:T(8,128)S(1)}, u32[]{:S(2)}, u32[]{:S(2)}) collective-permute-start(f32[8,256]{1,0:T(8,128)S(1)} %get-tuple-element.12), channel_id=1, source_target_pairs={{0,3},{1,2},{2,1},{3,0},{4,7},{5,6},{6,5},{7,4},{8,11},{9,10},{10,... | collective-permute-start | bytes 24584 | tf_op jit(solution)/shard_map/ppermute | solution.py:212

commit v2 on v1

v2 whole, which is shorter than its diff:
```python
import jax
import jax.numpy as jnp
from jax import lax
from jax.experimental import pallas as pl
from jax.experimental.pallas import tpu as pltpu
from jax.sharding import PartitionSpec as P

SWEEPS = 3
BF = jnp.bfloat16
F32 = jnp.float32
I32 = jnp.int32
LIMIT = 48 << 20
STRIPS = 112


def vmem(n):
    return [pl.BlockSpec(memory_space=pltpu.VMEM)] * n


def iota(shape, dim):
    return lax.broadcasted_iota(I32, shape, dim)


def nt(a, b):
    return lax.dot_general(a, b, (((1,), (1,)), ((), ())), preferred_element_type=F32)


def slot_rows(final, tmap, elem, point, count_ref, rows_ref):
    owners = rows_ref.shape[0]
    slots = elem.shape[1]
    cap = slots // owners
    traction = nt(tmap, final).astype(BF)
    hot = (iota((final.shape[0], slots), 0) == elem).astype(F32).astype(BF)
    pull = jnp.dot(traction, hot, preferred_element_type=F32)
    slot = iota((1, slots), 1)
    owner = slot // cap
    limit = jnp.zeros((1, slots), I32)
    for k in range(owners):
        limit = jnp.where(owner == k, count_ref[0:1, k : k + 1], limit)
    live = (slot - owner * cap) < limit
    row = point // 128
    code = (128 + (point - row * 128)).astype(F32)
    for b in range(6):
        code = code * jnp.where((row >> b) & 1 == 1, F32(2.0 ** (2**b)), F32(1.0))
    code = jnp.where(live, code, 0.0)
    pull = jnp.where(live, pull, 0.0)
    for k in range(owners):
        for j in range(4):
            source = code if j == 3 else pull[j : j + 1]
            for h in range(2):
                start = k * cap + h * 128
                rows_ref[k, 2 * j + h : 2 * j + h + 1, :] = source[:, start : start + 128]


def decode(code):
    row = jnp.zeros(code.shape, F32)
    for b in (5, 4, 3, 2, 1, 0):
        big = code >= F32(128.0 * 2.0 ** (2**b))
        row = row + jnp.where(big, F32(2**b), 0.0)
        code = code * jnp.where(big, F32(2.0 ** -(2**b)), 1.0)
    return row, code - 128.0


def owner_kernel(got_ref, disp_ref, stiff_ref, kd_ref, new_ref, *rest):
    replies = rest[:4]
    row_ref, lane_ref, acc_ref = rest[4:]
    sources = got_ref.shape[0]
    rows = disp_ref.shape[1]
    patch = lax.axis_index("patch")
    first = lax.axis_index("slab") * 4
    for h in range(2):
        row, lane = decode(got_ref[:, 6 + h, :].astype(F32))
        row_ref[h] = row
        lane_ref[h] = lane
    row_ids = iota((rows, 128), 0).astype(F32)
    lane_ids = iota((128, 128), 0).astype(F32)
    acc_ref[...] = jnp.zeros_like(acc_ref)
    group = 8

    def body(i, carry):
        base = pl.multiple_of(i * group, group)
        row8 = [row_ref[h, pl.ds(base, group), :] for h in range(2)]
        lane8 = [lane_ref[h, pl.ds(base, group), :] for h in range(2)]
        total = jnp.zeros((3 * rows, 128), F32)
        for g in range(group):
            vals = got_ref[base + g].astype(F32)
            left = []
            right = []
            for h in range(2):
                mask = row_ids == row8[h][g : g + 1]
                left.append(
                    jnp.concatenate(
                        [
                            jnp.where(mask, vals[2 * c + h : 2 * c + h + 1], 0.0).astype(BF)
                            for c in range(3)
                        ],
                        axis=0,
                    )
                )
                right.append((lane_ids == lane8[h][g : g + 1]).astype(F32).astype(BF))
            total += nt(jnp.concatenate(left, axis=1), jnp.concatenate(right, axis=1))
        acc_ref[...] += total
        return carry

    lax.fori_loop(0, sources // group, body, 0)
    loads = acc_ref[...].reshape(3, rows, 128)
    new = disp_ref[...] + (loads - kd_ref[...]) / (36.0 * stiff_ref[...])[None]
    new_ref[...] = new
    flat = new.reshape(3 * rows, 128)
    high = flat.astype(BF)
    rest1 = flat - high.astype(F32)
    mid = rest1.astype(BF)
    low = (rest1 - mid.astype(F32)).astype(BF)
    for d in range(4):
        src = first + (patch ^ d)
        for h in range(2):
            row = row_ref[h, pl.ds(src, 1), :]
            lane = lane_ref[h, pl.ds(src, 1), :]
            hot = (lane_ids == lane).astype(F32).astype(BF)
            picked = jnp.dot(high, hot, preferred_element_type=F32)
            picked += jnp.dot(mid, hot, preferred_element_type=F32)
            picked += jnp.dot(low, hot, preferred_element_type=F32)
            mask = row_ids == row
            for c in range(3):
                part = jnp.where(mask, picked[c * rows : (c + 1) * rows], 0.0)
                replies[d][c : c + 1, h * 128 : (h + 1) * 128] = part.sum(axis=0, keepdims=True)


def finish_kernel(r0, r1, r2, r3, out_ref):
    cap = r0.shape[1]
    patch = lax.axis_index("patch")
    for d, reply in enumerate((r0, r1, r2, r3)):
        start = pl.multiple_of((patch ^ d) * cap, cap)
        for c in range(3):
            out_ref[c, 0, :, pl.ds(start, cap)] = reply[c : c + 1, :]


def shell_kernel(one_ref, three_ref, disp_ref, stiff_ref, kd_ref, field_ref, bend_ref):
    rows = disp_ref.shape[1]
    patch = lax.axis_index("patch")
    top = patch > 0
    bottom = patch < 3
    even = patch % 2 == 0
    one, three = (
        ref[STRIPS - 8 :, :128].astype(F32) + ref[STRIPS - 8 :, 128:].astype(F32)
        for ref in (one_ref, three_ref)
    )
    above = jnp.where(even, three, one)
    below = jnp.where(even, one, three)
    field_ref[...] = jnp.zeros_like(field_ref)
    bend_ref[...] = jnp.zeros_like(bend_ref)
    field_ref[:, 8 : 8 + rows, :] = disp_ref[...]
    lane = iota((1, 1, 128), 2)

    def sides(x):
        left = jnp.where(lane == 0, 0.0, pltpu.roll(x, 1, 2))
        right = jnp.where(lane == 127, 0.0, pltpu.roll(x, 127, 2))
        return left + right

    for c in range(3):
        field_ref[c, 6:8, :] = jnp.where(top, above[2 * c : 2 * c + 2], 0.0)
        field_ref[c, 8 + rows : 10 + rows, :] = jnp.where(bottom, below[2 * c : 2 * c + 2], 0.0)
    mid = field_ref[:, 7 : 9 + rows, :]
    bend = 4.0 * mid - (
        field_ref[:, 6 : 8 + rows, :] + field_ref[:, 8 : 10 + rows, :] + sides(mid)
    )
    bend_ref[:, 7 : 9 + rows, :] = bend
    for c in range(3):
        bend_ref[c, 7:8, :] = jnp.where(top, bend_ref[c, 7:8, :], 0.0)
        bend_ref[c, 8 + rows : 9 + rows, :] = jnp.where(
            bottom, bend_ref[c, 8 + rows : 9 + rows, :], 0.0
        )
    mid = bend_ref[:, 8 : 8 + rows, :]
    again = 4.0 * mid - (
        bend_ref[:, 7 : 7 + rows, :] + bend_ref[:, 9 : 9 + rows, :] + sides(mid)
    )
    kd_ref[...] = stiff_ref[...][None] * (again + 4.0 * mid)


def params():
    return pltpu.CompilerParams(vmem_limit_bytes=LIMIT)


def patch_pairs(d):
    return [(p, p ^ d) for p in range(4)]


def exchange_and_relax(message, displacement, stiffness, kd):
    slabs, owners = lax.axis_size("slab"), lax.axis_size("patch")
    rows = displacement.shape[1]
    sources = slabs * owners
    got = lax.all_to_all(
        message.reshape(sources, 8, 128), ("slab", "patch"), 0, 0, tiled=True
    )
    reply = jax.ShapeDtypeStruct((8, 256), F32)
    new, *replies = pl.pallas_call(
        owner_kernel,
        out_shape=(jax.ShapeDtypeStruct(displacement.shape, F32),) + (reply,) * 4,
        in_specs=vmem(4),
        out_specs=vmem(5),
        scratch_shapes=[
            pltpu.VMEM((2, sources, 128), F32),
            pltpu.VMEM((2, sources, 128), F32),
            pltpu.VMEM((3 * rows, 128), F32),
        ],
        compiler_params=params(),
        name="owner",
    )(got, displacement, stiffness, kd)
    back = [replies[0]] + [
        lax.ppermute(replies[d], "patch", patch_pairs(d)) for d in (1, 2, 3)
    ]
    wall = pl.pallas_call(
        finish_kernel,
        out_shape=jax.ShapeDtypeStruct((3, 1, 1, owners * 256), F32),
        in_specs=vmem(4),
        out_specs=pl.BlockSpec(memory_space=pltpu.VMEM),
        compiler_params=params(),
        name="finish",
    )(*back)
    return new, wall


def halves(value):
    high = value.astype(BF)
    low = (value - high.astype(F32)).astype(BF)
    return jnp.concatenate([high.astype(F32), low.astype(F32)], axis=1)


def near_kernel(state_ref, rhs_ref, scale_ref, out_ref):
    odd = lax.axis_index("slab") % 2
    cols = state_ref.shape[1]
    for i, row in enumerate((odd, 1 - odd)):
        out_ref[i * cols : (i + 1) * cols, :] = state_ref[row].astype(BF)
        out_ref[(i + 2) * cols : (i + 3) * cols, :] = rhs_ref[row].astype(BF)
    flip = odd == 1
    first = jnp.where(flip, scale_ref[1:2], scale_ref[0:1])
    second = jnp.where(flip, scale_ref[0:1], scale_ref[1:2])
    pair = jnp.concatenate([halves(first), halves(second), jnp.zeros((14, 256), F32)], axis=0)
    out_ref[4 * cols :, :] = pair.astype(BF)


def row_table(own, inner, outer):
    return (
        (outer, 1, 3, 1),
        (outer, 0, 2, 0),
        (own, 0, 2, 0),
        (own, 1, 3, 1),
        (inner, 1, 3, 1),
        (inner, 0, 2, 0),
    )


def strip_kernel(own_ref, inner_ref, outer_ref, disp_ref, one_ref, three_ref, relay_ref, build_ref):
    patch = lax.axis_index("patch")
    even = patch % 2 == 0
    cols = relay_ref.shape[0]
    relay_ref[...] = outer_ref[0:cols, :]
    table = row_table(own_ref, inner_ref, outer_ref)
    build_ref[:, 96:, :] = jnp.zeros((2, STRIPS - 96, 256), F32)
    for r, (ref, state, rhs, scale) in enumerate(table):
        for part, block in enumerate((state, rhs)):
            at = (part * 6 + r) * 8
            low = ref[block * cols : block * cols + 16, :].astype(F32)[0:8]
            high = ref[(block + 1) * cols - 16 : (block + 1) * cols, :].astype(F32)[8:16]
            build_ref[0, at : at + 8, :] = jnp.where(even, high, low)
            build_ref[1, at : at + 8, :] = jnp.where(even, low, high)
        line = ref[4 * cols : 4 * cols + 16, :].astype(F32)[scale : scale + 1]
        build_ref[0, 97 + r : 98 + r, :] = line
        build_ref[1, 97 + r : 98 + r, :] = line
    rows = disp_ref.shape[1]
    for c in range(3):
        top = halves(disp_ref[c, 0:2, :])
        bottom = halves(disp_ref[c, rows - 2 : rows, :])
        at = STRIPS - 8 + 2 * c
        build_ref[0, at : at + 2, :] = jnp.where(even, bottom, top)
        build_ref[1, at : at + 2, :] = jnp.where(even, top, bottom)
    one_ref[...] = build_ref[0].astype(BF)
    three_ref[...] = build_ref[1].astype(BF)


def sweep_kernel(
    state_ref,
    rhs_ref,
    scale_ref,
    inner_ref,
    outer_ref,
    one_ref,
    three_ref,
    relay_ref,
    matrix_ref,
    x_ref,
    y_ref,
    inverse_ref,
    tmap_ref,
    elem_ref,
    point_ref,
    count_ref,
    out_ref,
    message_ref,
    v_ref,
    r_ref,
    s_ref,
    i_ref,
    line_ref,
    side_ref,
    rows_ref,
):
    slab, patch = lax.axis_index("slab"), lax.axis_index("patch")
    last_slab, last_patch = lax.axis_size("slab") - 1, lax.axis_size("patch") - 1
    odd = slab % 2
    even = patch % 2 == 0
    cols, width = state_ref.shape[1], state_ref.shape[2]
    wide = cols + 16
    inside = (slab > 0) & (slab < last_slab)
    one = one_ref[...].astype(F32)
    three = three_ref[...].astype(F32)
    side_ref[0] = jnp.where(even, three, one)
    side_ref[1] = jnp.where(even, one, three)
    col = iota((wide, width), 0)
    valid = (col >= 8) & (col < 8 + cols)
    valid = valid | ((col < 8) & (patch > 0)) | ((col >= 8 + cols) & (patch < last_patch))
    edge = valid.astype(F32)
    keep = edge * inside.astype(F32)
    table = row_table(None, inner_ref, outer_ref)
    lane = iota((1, 128), 1)
    line_ref[...] = jnp.ones_like(line_ref)
    for r, (ref, state, rhs, scale) in enumerate(table):
        if ref is None:
            row = odd if r == 2 else 1 - odd
            v_ref[r + 1, 8 : 8 + cols, :] = state_ref[row]
            r_ref[r, 8 : 8 + cols, :] = rhs_ref[row]
            line = jnp.where(row == 1, scale_ref[1:2], scale_ref[0:1])
        else:
            v_ref[r + 1, 8 : 8 + cols, :] = ref[state * cols : (state + 1) * cols, :].astype(F32)
            r_ref[r, 8 : 8 + cols, :] = ref[rhs * cols : (rhs + 1) * cols, :].astype(F32)
            both = ref[4 * cols : 4 * cols + 16, :].astype(F32)[scale : scale + 1]
            line = both[:, :128] + both[:, 128:]
        for e, start in ((0, 0), (1, 8 + cols)):
            v_ref[r + 1, start : start + 8, :] = side_ref[e, 8 * r : 8 * r + 8, :]
            r_ref[r, start : start + 8, :] = side_ref[e, 48 + 8 * r : 56 + 8 * r, :]
            both = side_ref[e, 97 + r : 98 + r, :]
            far = pltpu.roll(both[:, :128] + both[:, 128:], 64, 1)
            here = (lane >= start) & (lane < start + 8)
            line = jnp.where(here, far, line)
        line_ref[r : r + 1, :] = jnp.where(line > 0.0, line, 1.0)
    v_ref[0] = jnp.zeros((wide, width), F32)
    v_ref[7] = jnp.zeros((wide, width), F32)
    v_ref[0, 8 : 8 + cols, :] = outer_ref[4 * cols + 16 : 5 * cols + 16, :].astype(F32)
    v_ref[7, 8 : 8 + cols, :] = relay_ref[...].astype(F32)
    for r in range(8):
        v_ref[r] = v_ref[r] * (keep if r < 3 else edge)
    lines = line_ref[...]
    columns = jnp.transpose(lines)
    inverses = jnp.transpose(1.0 / lines)
    for r in range(6):
        s_ref[r] = jnp.broadcast_to(columns[:wide, r : r + 1], (wide, width))
        i_ref[r] = jnp.broadcast_to(inverses[:wide, r : r + 1], (wide, width))
    for sweep in range(SWEEPS):
        a, b = 1 + sweep, 7 - sweep
        n = b - a
        near = v_ref[a - 1 : b + 1].astype(BF).astype(F32)
        mid = near[1 : n + 1]
        nx = (near[0:n] + near[2 : n + 2]).astype(BF)
        ny = (pltpu.roll(mid, 1, 1) + pltpu.roll(mid, wide - 1, 1)).astype(BF)
        flat = (n * wide, width)
        own = jnp.dot(mid.astype(BF).reshape(flat), matrix_ref[...], preferred_element_type=F32)
        side = jnp.dot(nx.reshape(flat), x_ref[...], preferred_element_type=F32)
        side += jnp.dot(ny.reshape(flat), y_ref[...], preferred_element_type=F32)
        scale = s_ref[a - 1 : b - 1].reshape(flat)
        rhs = r_ref[a - 1 : b - 1].reshape(flat)
        residue = (rhs - (scale * own - side)).astype(BF)
        update = jnp.dot(residue, inverse_ref[...], preferred_element_type=F32)
        update = update * i_ref[a - 1 : b - 1].reshape(flat)
        value = v_ref[a:b] + update.reshape(n, wide, width)
        for j in range(n):
            v_ref[a + j] = value[j] * (keep if a + j < 3 else edge)
    out_ref[odd] = v_ref[3, 8 : 8 + cols, :]
    out_ref[1 - odd] = v_ref[4, 8 : 8 + cols, :]
    final = out_ref[...].astype(BF).reshape(2 * cols, width)
    slot_rows(final, tmap_ref[...], elem_ref[...], point_ref[...], count_ref, rows_ref)
    message_ref[...] = jnp.broadcast_to(rows_ref[...].astype(BF)[None], message_ref.shape)


def call(kernel, name, out_shape, operands, scratch=()):
    return pl.pallas_call(
        kernel,
        out_shape=out_shape,
        in_specs=vmem(len(operands)),
        out_specs=jax.tree.map(lambda _: vmem(1)[0], out_shape),
        scratch_shapes=list(scratch),
        compiler_params=params(),
        name=name,
    )(*operands)


def shards(
    fluid_state,
    fluid_rhs,
    element_scale,
    element_matrix,
    couple_x,
    couple_y,
    block_inverse,
    traction_map,
    slot_elem,
    slot_point,
    slot_count,
    displacement,
    stiffness,
):
    cols, width = fluid_state.shape[1:]
    slots = slot_elem.shape[2]
    slabs, owners = lax.axis_size("slab"), lax.axis_size("patch")
    shape = jax.ShapeDtypeStruct
    inner_pairs = [(s, s ^ 1) for s in range(slabs)]
    outer_pairs = [(s, s + 1) for s in range(1, slabs - 1, 2)]
    outer_pairs = outer_pairs + [(b, a) for a, b in outer_pairs]
    scale = jnp.pad(element_scale, ((0, 0), (8, 120 - cols)))
    own = call(
        near_kernel, "near", shape((4 * cols + 16, width), BF), (fluid_state, fluid_rhs, scale)
    )
    inner = lax.ppermute(own, "slab", inner_pairs)
    outer = lax.ppermute(
        jnp.concatenate([own, inner[cols : 2 * cols]]), "slab", outer_pairs
    )
    strip = shape((STRIPS, width), BF)
    to_one, to_three, relay = call(
        strip_kernel,
        "strip",
        (strip, strip, shape((cols, width), BF)),
        (own, inner, outer, displacement),
        [pltpu.VMEM((2, STRIPS, width), F32)],
    )
    relayed = lax.ppermute(relay, "slab", inner_pairs)
    from_one = lax.ppermute(to_one, "patch", patch_pairs(1))
    from_three = lax.ppermute(to_three, "patch", [(1, 2), (2, 1)])
    wide = cols + 16
    state, message = call(
        sweep_kernel,
        "sweep",
        (shape(fluid_state.shape, F32), shape((slabs, owners, 8, 128), BF)),
        (
            fluid_state,
            fluid_rhs,
            scale,
            inner,
            outer,
            from_one,
            from_three,
            relayed,
            element_matrix,
            couple_x,
            couple_y,
            block_inverse,
            traction_map,
            slot_elem.reshape(1, slots),
            slot_point.reshape(1, slots),
            slot_count.reshape(1, owners),
        ),
        [
            pltpu.VMEM((8, wide, width), F32),
            pltpu.VMEM((6, wide, width), F32),
            pltpu.VMEM((6, wide, width), F32),
            pltpu.VMEM((6, wide, width), F32),
            pltpu.VMEM((8, 128), F32),
            pltpu.VMEM((2, STRIPS, width), F32),
            pltpu.VMEM((owners, 8, 128), F32),
        ],
    )
    kd = call(
        shell_kernel,
        "shell",
        shape(displacement.shape, F32),
        (from_one, from_three, displacement, stiffness),
        [pltpu.VMEM((3, displacement.shape[1] + 16, 128), F32)] * 2,
    )
    new, wall = exchange_and_relax(message, displacement, stiffness, kd)
    return state, new, wall


def solution(mesh):
    return jax.shard_map(
        shards,
        mesh=mesh,
        in_specs=(
            P("slab", "patch", None),
            P("slab", "patch", None),
            P("slab", "patch"),
            P(),
            P(),
            P(),
            P(),
            P(),
            P("slab", "patch", None),
            P("slab", "patch", None),
            P("slab", "patch", None),
            P(None, "patch", None),
            P("patch", None),
        ),
        out_specs=(
            P("slab", "patch", None),
            P(None, "patch", None),
            P(None, "slab", "patch", None),
        ),
        check_vma=False,
    )
```

time: 91.8 us -> 66.4 us (0.72)
  starting transfers between devices: 54.4 us -> 33.1 us
  matrix products: 1.9 us -> 0 us
  other arithmetic: 1.16 us -> 0.01 us
    ppermute x14 -> x5, starting transfers between devices: 33.3 us -> 15.9 us  [the longest x1 8.15 us: shards(): relayed = lax.ppermute(relay, 'slab', inner_pairs)]
    all_to_all x1, starting transfers between devices: 18.9 us -> 15.1 us  [exchange_and_relax(): lax.all_to_all(message.reshape(sources, 8, 128), ('slab', 'patch'), 0, 0,...]
    dot_general x9 -> x0, matrix products: 1.9 us -> none  [the longest x3 0.91 us: shards(): jnp.dot(residue.reshape(-1, width), block_inverse, preferred_element_type...]
    unnamed x29 -> x24, local copies, waits for them, and re-layouts: 4.01 us -> 2.44 us
    all_to_all x1, waiting for transfers between devices: 9.81 us -> 11.1 us  [exchange_and_relax(): lax.all_to_all(message.reshape(sources, 8, 128), ('slab', 'patch'), 0, 0,...]
    convert_element_type x3 -> x0, other arithmetic: 0.96 us -> none  [the longest x1 0.95 us: shards(): rounded = state.astype(BF)]
    ppermute x14 -> x5, waiting for transfers between devices: 5.26 us -> 4.69 us  [the longest x1 3.38 us: shards(): inner = lax.ppermute(own, 'slab', inner_pairs)]
    pallas_call x3 -> x5, Pallas kernels: 2.92 us -> 3.19 us  [the longest x4 2.59 us: call(): pl.pallas_call(kernel, out_shape=out_shape, in_specs=vmem(len(operands)),...]
  transfers between devices with their start and end apart: 18 -> 9, of which waited for: 5 -> 5; matrix products, arithmetic and copies ran while one was open for 2% -> 0% of each run, Pallas kernels for 3% -> 0%
where the time goes in v2:
time: 66.4 us; the launch traced here: 66.1 us
  starting transfers between devices  33.1 us (50%)
  waiting for transfers between devices  17.4 us (26%)
  Pallas kernels  11.6 us (17%)
  local copies, waits for them, and re-layouts  3.2 us (5%)
  between operations  0.81 us (1%)
    all_to_all x1, starting transfers between devices, exchange_and_relax(): lax.all_to_all(message.reshape(sources, 8, 128), ('slab', 'patch'), 0, 0,...  15.1 us
    all_to_all x1, waiting for transfers between devices, exchange_and_relax(): lax.all_to_all(message.reshape(sources, 8, 128), ('slab', 'patch'), 0, 0,...  11.1 us
    pallas_call x1, Pallas kernels, exchange_and_relax(): pl.pallas_call(owner_kernel, out_shape=(jax.ShapeDtypeStruct(displacement...  8.36 us
    ppermute x1, starting transfers between devices, shards(): relayed = lax.ppermute(relay, 'slab', inner_pairs)  8.15 us
    ppermute x1, waiting for transfers between devices, shards(): inner = lax.ppermute(own, 'slab', inner_pairs)  3.38 us
    ppermute x1, starting transfers between devices, shards(): from_three = lax.ppermute(to_three, 'patch', [(1, 2), (2, 1)])  3.04 us
    pallas_call x4, Pallas kernels, call(): pl.pallas_call(kernel, out_shape=out_shape, in_specs=vmem(len(operands)),...  2.59 us
    ppermute x1, starting transfers between devices, shards(): inner = lax.ppermute(own, 'slab', inner_pairs)  2.55 us
  transfers between devices with their start and end apart: 9, of which 5 were waited for; matrix products, arithmetic and copies ran while one was open for 0% of the time, Pallas kernels for 0%

profile of v2, /device:TPU:1, one launch (start us, length us, event | category | flops | bytes accessed | tf_op | source)
XLA Modules:
  0.0 66.1 jit_solution(14492547085267622108)
XLA Ops:
  0.6 0.8 %pad.4.scale_ref = f32[2,128]{1,0:T(2,128)S(1)} pad(f32[2,64]{1,0:T(2,128)} %param.15, f32[]{:T(128)} %constant.2.clone.1), padding=0_0x8_56 | pad | bytes 1540 | tf_op jit(solution)/shard_map/jit(_pad)/pad | solution.py:418
  1.4 0.0 copy-start.1
  1.4 0.9 %copy-done.1 = f32[2,64,256]{2,1,0:T(8,128)S(1)} copy-done((f32[2,64,256]{2,1,0:T(8,128)S(1)}, f32[2,64,256]{2,1,0:T(8,128)}, u32[]{:S(2)}) %copy-start.1) | copy-done | bytes 131096
  2.3 0.0 copy-start.2
  2.3 0.9 %copy-done.2 = f32[2,64,256]{2,1,0:T(8,128)S(1)} copy-done((f32[2,64,256]{2,1,0:T(8,128)S(1)}, f32[2,64,256]{2,1,0:T(8,128)}, u32[]{:S(2)}) %copy-start.2) | copy-done | bytes 131096
  3.2 2.5 %collective-permute-start = (bf16[272,256]{1,0:T(8,128)(2,1)S(1)}, bf16[272,256]{1,0:T(8,128)(2,1)S(1)}, u32[]{:S(2)}, u32[]{:S(2)}) collective-permute-start(bf16[272,256]{1,0:T(8,128)(2,1)S(1)} %near.1.own_ref), channel_id=1, source_target_pairs={{0,4},{4,0},{8,12},{12,8},{16,20},{20,16},{24,28},{28,24},{32,36},... | collective-permute-start | bytes 417800 | tf_op jit(solution)/shard_map/ppermute | solution.py:422
  5.8 3.4 %collective-permute-done.inner_ref = bf16[272,256]{1,0:T(8,128)(2,1)S(1)} collective-permute-done((bf16[272,256]{1,0:T(8,128)(2,1)S(1)}, bf16[272,256]{1,0:T(8,128)(2,1)S(1)}, u32[]{:S(2)}, u32[]{:S(2)}) %collective-permute-start) | collective-permute-done | bytes 139296 | tf_op jit(solution)/shard_map/ppermute | solution.py:422
  9.1 0.0 copy-start
  9.2 0.0 copy-start.3
  9.2 0.0 copy-start.4
  9.2 0.0 copy-start.5
  9.2 0.0 copy-start.6
  9.2 0.8 %collective-permute-start.1 = (bf16[336,256]{1,0:T(8,128)(2,1)S(1)}, bf16[336,256]{1,0:T(8,128)(2,1)S(1)}, u32[]{:S(2)}, u32[]{:S(2)}) collective-permute-start(bf16[336,256]{1,0:T(8,128)(2,1)S(1)} %pad_maximum_fusion), channel_id=1, source_target_pairs={{4,8},{12,16},{20,24},{28,32},{36,40},{44,48},{52,56},{60,64},{68,... | collective-permute-start | bytes 516104 | tf_op jit(solution)/shard_map/ppermute | solution.py:423
  10.0 0.0 collective-permute-done.1.outer_ref
  10.0 0.0 copy-done
  10.0 0.0 copy-start.10
  10.1 1.3 %collective-permute-start.2 = (bf16[112,256]{1,0:T(8,128)(2,1)S(1)}, bf16[112,256]{1,0:T(8,128)(2,1)S(1)}, u32[]{:S(2)}, u32[]{:S(2)}) collective-permute-start(bf16[112,256]{1,0:T(8,128)(2,1)S(1)} %get-tuple-element.13), channel_id=1, source_target_pairs={{0,1},{1,0},{2,3},{3,2},{4,5},{5,4},{6,7},{7,6},{8,9},{9,8},{10,11... | collective-permute-start | bytes 172040 | tf_op jit(solution)/shard_map/ppermute | solution.py:435
  11.4 0.0 copy-start.9
  11.4 0.0 copy-start.8
  11.4 3.0 %collective-permute-start.3 = (bf16[112,256]{1,0:T(8,128)(2,1)S(1)}, bf16[112,256]{1,0:T(8,128)(2,1)S(1)}, u32[]{:S(2)}, u32[]{:S(2)}) collective-permute-start(bf16[112,256]{1,0:T(8,128)(2,1)S(1)} %get-tuple-element.14), channel_id=1, source_target_pairs={{1,2},{2,1},{5,6},{6,5},{9,10},{10,9},{13,14},{14,13},{17,18},{18,... | collective-permute-start | bytes 172040 | tf_op jit(solution)/shard_map/ppermute | solution.py:436
  14.5 8.1 %collective-permute-start.4 = (bf16[64,256]{1,0:T(8,128)(2,1)S(1)}, bf16[64,256]{1,0:T(8,128)(2,1)S(1)}, u32[]{:S(2)}, u32[]{:S(2)}) collective-permute-start(bf16[64,256]{1,0:T(8,128)(2,1)S(1)} %get-tuple-element.15), channel_id=1, source_target_pairs={{0,4},{4,0},{8,12},{12,8},{16,20},{20,16},{24,28},{28,24},{32,36},... | collective-permute-start | bytes 98312 | tf_op jit(solution)/shard_map/ppermute | solution.py:434
  22.6 1.3 %collective-permute-done.4.relay_ref = bf16[64,256]{1,0:T(8,128)(2,1)S(1)} collective-permute-done((bf16[64,256]{1,0:T(8,128)(2,1)S(1)}, bf16[64,256]{1,0:T(8,128)(2,1)S(1)}, u32[]{:S(2)}, u32[]{:S(2)}) %collective-permute-start.4) | collective-permute-done | bytes 32800 | tf_op jit(solution)/shard_map/ppermute | solution.py:434
  23.9 0.0 collective-permute-done.2.one_ref
  23.9 0.0 collective-permute-done.3.three_ref
  23.9 0.0 copy-start.11
  23.9 0.0 copy-done.3
  24.0 0.0 copy-done.4
  24.0 0.0 copy-done.5
  24.0 0.0 copy-done.6
  24.0 0.0 copy-done.10
  24.0 0.0 copy-done.9
  24.0 0.0 copy-done.8
  24.0 0.6 copy-done.11
  24.6 2.3 %sweep.1 = (f32[2,64,256]{2,1,0:T(8,128)}, bf16[32,4,8,128]{3,2,1,0:T(8,128)(2,1)}) custom-call(f32[2,64,256]{2,1,0:T(8,128)S(1)} %copy-done.1, f32[2,64,256]{2,1,0:T(8,128)S(1)} %copy-done.2, f32[2,128]{1,0:T(2,128)S(1)} %pad.4.scale_ref, bf16[272,256]{1,0:T(8,128)(2,1)S(1)} %collective-permute-done.inner_ref, ...), custom_call_target="tpu_custom_call" | custom-call | tf_op jit(solution)/shard_map/sweep/pallas_call | solution.py:385
  26.9 0.0 copy-start.7
  26.9 15.1 %all-to-all-start = ((bf16[128,8,128]{2,1,0:T(8,128)(2,1)}), bf16[128,8,128]{2,1,0:T(8,128)(2,1)S(1)}, u32[]{:S(2)}, u32[]{:S(2)}) async-start(bf16[128,8,128]{2,1,0:T(8,128)(2,1)} %bitcast.3), calls=%async_computation | async-start | bytes 524288 | tf_op jit(solution)/shard_map/all_to_all | solution.py:192
  42.0 0.0 copy-done.7
  42.0 0.3 shell.1.kd_ref
  42.3 11.1 %all-to-all-done.got_ref = bf16[128,8,128]{2,1,0:T(8,128)(2,1)S(1)} async-done(((bf16[128,8,128]{2,1,0:T(8,128)(2,1)}), bf16[128,8,128]{2,1,0:T(8,128)(2,1)S(1)}, u32[]{:S(2)}, u32[]{:S(2)}) %all-to-all-start) | async-done | bytes 262176 | tf_op jit(solution)/shard_map/all_to_all | solution.py:192
  53.4 8.4 %owner.1 = (f32[3,64,128]{2,1,0:T(8,128)}, f32[8,256]{1,0:T(8,128)S(1)}, f32[8,256]{1,0:T(8,128)S(1)}, f32[8,256]{1,0:T(8,128)S(1)}, f32[8,256]{1,0:T(8,128)S(1)}) custom-call(bf16[128,8,128]{2,1,0:T(8,128)(2,1)S(1)} %all-to-all-done.got_ref, f32[3,64,128]{2,1,0:T(8,128)S(1)} %copy-done, f32[64,128]{1,0:T(8,128)S(1)} %copy-done.7, f32[3,64,128]{2,1,0:T(8,128)S(1)} %shell.1.kd_ref), custom_call_target="tpu_custom_call" | custom-call | tf_op jit(solution)/shard_map/owner/pallas_call | solution.py:196
  61.7 0.4 collective-permute-start.5
  62.1 0.3 collective-permute-start.6
  62.4 1.5 %collective-permute-start.7 = (f32[8,256]{1,0:T(8,128)S(1)}, f32[8,256]{1,0:T(8,128)S(1)}, u32[]{:S(2)}, u32[]{:S(2)}) collective-permute-start(f32[8,256]{1,0:T(8,128)S(1)} %get-tuple-element.22), channel_id=1, source_target_pairs={{0,3},{1,2},{2,1},{3,0},{4,7},{5,6},{6,5},{7,4},{8,11},{9,10},{10,... | collective-permute-start | bytes 24584 | tf_op jit(solution)/shard_map/ppermute | solution.py:210
  63.9 0.0 collective-permute-done.5.r1
  63.9 0.7 %collective-permute-done.6.r2 = f32[8,256]{1,0:T(8,128)S(1)} collective-permute-done((f32[8,256]{1,0:T(8,128)S(1)}, f32[8,256]{1,0:T(8,128)S(1)}, u32[]{:S(2)}, u32[]{:S(2)}) %collective-permute-start.6) | collective-permute-done | bytes 8224 | tf_op jit(solution)/shard_map/ppermute | solution.py:210
  64.6 0.9 %collective-permute-done.7.r3 = f32[8,256]{1,0:T(8,128)S(1)} collective-permute-done((f32[8,256]{1,0:T(8,128)S(1)}, f32[8,256]{1,0:T(8,128)S(1)}, u32[]{:S(2)}, u32[]{:S(2)}) %collective-permute-start.7) | collective-permute-done | bytes 8224 | tf_op jit(solution)/shard_map/ppermute | solution.py:210
  65.5 0.6 finish.1
  (4 shorter events, 0.1 us)
Async XLA Ops:
  1.4 0.9 %copy-start.1 = (f32[2,64,256]{2,1,0:T(8,128)S(1)}, f32[2,64,256]{2,1,0:T(8,128)}, u32[]{:S(2)}) copy-start(f32[2,64,256]{2,1,0:T(8,128)} %state_ref.3) | copy-start | bytes 393220
  2.3 0.9 %copy-start.2 = (f32[2,64,256]{2,1,0:T(8,128)S(1)}, f32[2,64,256]{2,1,0:T(8,128)}, u32[]{:S(2)}) copy-start(f32[2,64,256]{2,1,0:T(8,128)} %rhs_ref.3) | copy-start | bytes 393220
  3.2 5.9 %collective-permute-start = (bf16[272,256]{1,0:T(8,128)(2,1)S(1)}, bf16[272,256]{1,0:T(8,128)(2,1)S(1)}, u32[]{:S(2)}, u32[]{:S(2)}) collective-permute-start(bf16[272,256]{1,0:T(8,128)(2,1)S(1)} %near.1.own_ref), channel_id=1, source_target_pairs={{0,4},{4,0},{8,12},{12,8},{16,20},{20,16},{24,28},{28,24},{32,36},... | collective-permute-start | bytes 417800 | tf_op jit(solution)/shard_map/ppermute | solution.py:422
  9.1 0.9 %copy-start = (f32[3,64,128]{2,1,0:T(8,128)S(1)}, f32[3,64,128]{2,1,0:T(8,128)}, u32[]{:S(2)}) copy-start(f32[3,64,128]{2,1,0:T(8,128)} %disp_ref.5) | copy-start | bytes 294916
  9.2 14.8 %copy-start.3 = (bf16[256,256]{1,0:T(8,128)(2,1)S(1)}, bf16[256,256]{1,0:T(8,128)(2,1)}, u32[]{:S(2)}) copy-start(bf16[256,256]{1,0:T(8,128)(2,1)} %matrix_ref.1) | copy-start | bytes 393220
  9.2 14.8 %copy-start.4 = (bf16[256,256]{1,0:T(8,128)(2,1)S(1)}, bf16[256,256]{1,0:T(8,128)(2,1)}, u32[]{:S(2)}) copy-start(bf16[256,256]{1,0:T(8,128)(2,1)} %x_ref.1) | copy-start | bytes 393220
  9.2 14.8 %copy-start.5 = (bf16[256,256]{1,0:T(8,128)(2,1)S(1)}, bf16[256,256]{1,0:T(8,128)(2,1)}, u32[]{:S(2)}) copy-start(bf16[256,256]{1,0:T(8,128)(2,1)} %y_ref.1) | copy-start | bytes 393220
  9.2 14.8 %copy-start.6 = (bf16[256,256]{1,0:T(8,128)(2,1)S(1)}, bf16[256,256]{1,0:T(8,128)(2,1)}, u32[]{:S(2)}) copy-start(bf16[256,256]{1,0:T(8,128)(2,1)} %inverse_ref.1) | copy-start | bytes 393220
  9.2 0.8 %collective-permute-start.1 = (bf16[336,256]{1,0:T(8,128)(2,1)S(1)}, bf16[336,256]{1,0:T(8,128)(2,1)S(1)}, u32[]{:S(2)}, u32[]{:S(2)}) collective-permute-start(bf16[336,256]{1,0:T(8,128)(2,1)S(1)} %pad_maximum_fusion), channel_id=1, source_target_pairs={{4,8},{12,16},{20,24},{28,32},{36,40},{44,48},{52,56},{60,64},{68,... | collective-permute-start | bytes 516104 | tf_op jit(solution)/shard_map/ppermute | solution.py:423
  10.0 14.0 %copy-start.10 = (bf16[3,256]{1,0:T(4,128)(2,1)S(1)}, bf16[3,256]{1,0:T(4,128)(2,1)}, u32[]{:S(2)}) copy-start(bf16[3,256]{1,0:T(4,128)(2,1)} %tmap_ref.1) | copy-start | bytes 4612
  10.1 13.8 %collective-permute-start.2 = (bf16[112,256]{1,0:T(8,128)(2,1)S(1)}, bf16[112,256]{1,0:T(8,128)(2,1)S(1)}, u32[]{:S(2)}, u32[]{:S(2)}) collective-permute-start(bf16[112,256]{1,0:T(8,128)(2,1)S(1)} %get-tuple-element.13), channel_id=1, source_target_pairs={{0,1},{1,0},{2,3},{3,2},{4,5},{5,4},{6,7},{7,6},{8,9},{9,8},{10,11... | collective-permute-start | bytes 172040 | tf_op jit(solution)/shard_map/ppermute | solution.py:435
  11.4 12.6 %copy-start.9 = (s32[1,1,1024]{2,1,0:T(1,128)S(1)}, s32[1,1,1024]{2,1,0:T(1,128)}, u32[]{:S(2)}) copy-start(s32[1,1,1024]{2,1,0:T(1,128)} %param.22) | copy-start | bytes 12292
  11.4 12.6 %copy-start.8 = (s32[1,1,1024]{2,1,0:T(1,128)S(1)}, s32[1,1,1024]{2,1,0:T(1,128)}, u32[]{:S(2)}) copy-start(s32[1,1,1024]{2,1,0:T(1,128)} %param.21) | copy-start | bytes 12292
  11.4 12.5 %collective-permute-start.3 = (bf16[112,256]{1,0:T(8,128)(2,1)S(1)}, bf16[112,256]{1,0:T(8,128)(2,1)S(1)}, u32[]{:S(2)}, u32[]{:S(2)}) collective-permute-start(bf16[112,256]{1,0:T(8,128)(2,1)S(1)} %get-tuple-element.14), channel_id=1, source_target_pairs={{1,2},{2,1},{5,6},{6,5},{9,10},{10,9},{13,14},{14,13},{17,18},{18,... | collective-permute-start | bytes 172040 | tf_op jit(solution)/shard_map/ppermute | solution.py:436
  14.5 9.5 %collective-permute-start.4 = (bf16[64,256]{1,0:T(8,128)(2,1)S(1)}, bf16[64,256]{1,0:T(8,128)(2,1)S(1)}, u32[]{:S(2)}, u32[]{:S(2)}) collective-permute-start(bf16[64,256]{1,0:T(8,128)(2,1)S(1)} %get-tuple-element.15), channel_id=1, source_target_pairs={{0,4},{4,0},{8,12},{12,8},{16,20},{20,16},{24,28},{28,24},{32,36},... | collective-permute-start | bytes 98312 | tf_op jit(solution)/shard_map/ppermute | solution.py:434
  23.9 0.7 copy-start.11
  26.9 15.1 %copy-start.7 = (f32[64,128]{1,0:T(8,128)S(1)}, f32[64,128]{1,0:T(8,128)}, u32[]{:S(2)}) copy-start(f32[64,128]{1,0:T(8,128)} %stiff_ref.3) | copy-start | bytes 98308
  26.9 26.5 %all-to-all-start = ((bf16[128,8,128]{2,1,0:T(8,128)(2,1)}), bf16[128,8,128]{2,1,0:T(8,128)(2,1)S(1)}, u32[]{:S(2)}, u32[]{:S(2)}) async-start(bf16[128,8,128]{2,1,0:T(8,128)(2,1)} %bitcast.3), calls=%async_computation | async-start | bytes 524288 | tf_op jit(solution)/shard_map/all_to_all | solution.py:192
  61.7 2.1 %collective-permute-start.5 = (f32[8,256]{1,0:T(8,128)S(1)}, f32[8,256]{1,0:T(8,128)S(1)}, u32[]{:S(2)}, u32[]{:S(2)}) collective-permute-start(f32[8,256]{1,0:T(8,128)S(1)} %get-tuple-element.20), channel_id=1, source_target_pairs={{0,1},{1,0},{2,3},{3,2},{4,5},{5,4},{6,7},{7,6},{8,9},{9,8},{10,11... | collective-permute-start | bytes 24584 | tf_op jit(solution)/shard_map/ppermute | solution.py:210
  62.1 2.5 %collective-permute-start.6 = (f32[8,256]{1,0:T(8,128)S(1)}, f32[8,256]{1,0:T(8,128)S(1)}, u32[]{:S(2)}, u32[]{:S(2)}) collective-permute-start(f32[8,256]{1,0:T(8,128)S(1)} %get-tuple-element.21), channel_id=1, source_target_pairs={{0,2},{1,3},{2,0},{3,1},{4,6},{5,7},{6,4},{7,5},{8,10},{9,11},{10,... | collective-permute-start | bytes 24584 | tf_op jit(solution)/shard_map/ppermute | solution.py:210
  62.4 3.1 %collective-permute-start.7 = (f32[8,256]{1,0:T(8,128)S(1)}, f32[8,256]{1,0:T(8,128)S(1)}, u32[]{:S(2)}, u32[]{:S(2)}) collective-permute-start(f32[8,256]{1,0:T(8,128)S(1)} %get-tuple-element.22), channel_id=1, source_target_pairs={{0,3},{1,2},{2,1},{3,0},{4,7},{5,6},{6,5},{7,4},{8,11},{9,10},{10,... | collective-permute-start | bytes 24584 | tf_op jit(solution)/shard_map/ppermute | solution.py:210

commit v3 on v2

--- a/solution.py
+++ b/solution.py
@@ -10,11 +10,15 @@
 F32 = jnp.float32
 I32 = jnp.int32
 LIMIT = 48 << 20
-STRIPS = 112
+EDGE = 40
 
 
 def vmem(n):
     return [pl.BlockSpec(memory_space=pltpu.VMEM)] * n
+
+
+def hbm(n):
+    return [pl.BlockSpec(memory_space=pltpu.HBM)] * n
 
 
 def iota(shape, dim):
@@ -61,9 +65,10 @@
     return row, code - 128.0
 
 
-def owner_kernel(got_ref, disp_ref, stiff_ref, kd_ref, new_ref, *rest):
-    replies = rest[:4]
-    row_ref, lane_ref, acc_ref = rest[4:]
+def owner_kernel(
+    got_ref, disp_ref, stiff_ref, kd_ref, new_ref, r0, r1, r2, r3, row_ref, lane_ref, hold_ref, sem
+):
+    replies = (r0, r1, r2, r3)
     sources = got_ref.shape[0]
     rows = disp_ref.shape[1]
     patch = lax.axis_index("patch")
@@ -72,51 +77,45 @@
         row, lane = decode(got_ref[:, 6 + h, :].astype(F32))
         row_ref[h] = row
         lane_ref[h] = lane
-    row_ids = iota((rows, 128), 0).astype(F32)
-    lane_ids = iota((128, 128), 0).astype(F32)
-    acc_ref[...] = jnp.zeros_like(acc_ref)
+    row_ids = iota((rows, 128), 0).astype(F32).astype(BF)
+    lane_ids = iota((128, 128), 0).astype(F32).astype(BF)
+    none = jnp.zeros((rows, 128), BF)
+    ones, zeros = jnp.ones((128, 128), BF), jnp.zeros((128, 128), BF)
+    total = jnp.zeros((3 * rows, 128), F32)
     group = 8
-
-    def body(i, carry):
-        base = pl.multiple_of(i * group, group)
-        row8 = [row_ref[h, pl.ds(base, group), :] for h in range(2)]
-        lane8 = [lane_ref[h, pl.ds(base, group), :] for h in range(2)]
-        total = jnp.zeros((3 * rows, 128), F32)
+    for base in range(0, sources, group):
+        row8 = [row_ref[h, base : base + group, :].astype(BF) for h in range(2)]
+        lane8 = [lane_ref[h, base : base + group, :].astype(BF) for h in range(2)]
         for g in range(group):
-            vals = got_ref[base + g].astype(F32)
-            left = []
-            right = []
+            vals = got_ref[base + g]
+            left, right = [], []
             for h in range(2):
                 mask = row_ids == row8[h][g : g + 1]
                 left.append(
                     jnp.concatenate(
-                        [
-                            jnp.where(mask, vals[2 * c + h : 2 * c + h + 1], 0.0).astype(BF)
-                            for c in range(3)
-                        ],
+                        [jnp.where(mask, vals[2 * c + h : 2 * c + h + 1], none) for c in range(3)],
                         axis=0,
                     )
                 )
-                right.append((lane_ids == lane8[h][g : g + 1]).astype(F32).astype(BF))
+                right.append(jnp.where(lane_ids == lane8[h][g : g + 1], ones, zeros))
             total += nt(jnp.concatenate(left, axis=1), jnp.concatenate(right, axis=1))
-        acc_ref[...] += total
-        return carry
-
-    lax.fori_loop(0, sources // group, body, 0)
-    loads = acc_ref[...].reshape(3, rows, 128)
+    loads = total.reshape(3, rows, 128)
     new = disp_ref[...] + (loads - kd_ref[...]) / (36.0 * stiff_ref[...])[None]
-    new_ref[...] = new
+    hold_ref[...] = new
+    out = pltpu.make_async_copy(hold_ref, new_ref, sem)
+    out.start()
     flat = new.reshape(3 * rows, 128)
     high = flat.astype(BF)
     rest1 = flat - high.astype(F32)
     mid = rest1.astype(BF)
     low = (rest1 - mid.astype(F32)).astype(BF)
+    row_ids = iota((rows, 128), 0).astype(F32)
     for d in range(4):
         src = first + (patch ^ d)
         for h in range(2):
             row = row_ref[h, pl.ds(src, 1), :]
             lane = lane_ref[h, pl.ds(src, 1), :]
-            hot = (lane_ids == lane).astype(F32).astype(BF)
+            hot = jnp.where(lane_ids == lane.astype(BF), ones, zeros)
             picked = jnp.dot(high, hot, preferred_element_type=F32)
             picked += jnp.dot(mid, hot, preferred_element_type=F32)
             picked += jnp.dot(low, hot, preferred_element_type=F32)
@@ -124,6 +123,7 @@
             for c in range(3):
                 part = jnp.where(mask, picked[c * rows : (c + 1) * rows], 0.0)
                 replies[d][c : c + 1, h * 128 : (h + 1) * 128] = part.sum(axis=0, keepdims=True)
+    out.wait()
 
 
 def finish_kernel(r0, r1, r2, r3, out_ref):
@@ -142,7 +142,7 @@
     bottom = patch < 3
     even = patch % 2 == 0
     one, three = (
-        ref[STRIPS - 8 :, :128].astype(F32) + ref[STRIPS - 8 :, 128:].astype(F32)
+        ref[EDGE:, :128].astype(F32) + ref[EDGE:, 128:].astype(F32)
         for ref in (one_ref, three_ref)
     )
     above = jnp.where(even, three, one)
@@ -197,11 +197,12 @@
         owner_kernel,
         out_shape=(jax.ShapeDtypeStruct(displacement.shape, F32),) + (reply,) * 4,
         in_specs=vmem(4),
-        out_specs=vmem(5),
+        out_specs=hbm(1) + vmem(4),
         scratch_shapes=[
             pltpu.VMEM((2, sources, 128), F32),
             pltpu.VMEM((2, sources, 128), F32),
-            pltpu.VMEM((3 * rows, 128), F32),
+            pltpu.VMEM((3, rows, 128), F32),
+            pltpu.SemaphoreType.DMA,
         ],
         compiler_params=params(),
         name="owner",
@@ -226,52 +227,57 @@
     return jnp.concatenate([high.astype(F32), low.astype(F32)], axis=1)
 
 
-def near_kernel(state_ref, rhs_ref, scale_ref, out_ref):
+def lines_of(scale_ref, pad_ref):
+    pad_ref[...] = jnp.zeros_like(pad_ref)
+    pad_ref[0:2, 0 : scale_ref.shape[1]] = scale_ref[...]
+    return pltpu.roll(pad_ref[...], 8, 1)
+
+
+def near_kernel(
+    state_hbm, rhs_hbm, scale_hbm, disp_hbm, own_ref, one_ref, three_ref,
+    state_ref, rhs_ref, scale_ref, disp_ref, pad_ref, build_ref, sems,
+):
+    copies = [
+        pltpu.make_async_copy(a, b, sems.at[i])
+        for i, (a, b) in enumerate(
+            (
+                (scale_hbm, scale_ref),
+                (state_hbm, state_ref),
+                (rhs_hbm, rhs_ref),
+                (disp_hbm, disp_ref),
+            )
+        )
+    ]
+    for copy in copies:
+        copy.start()
     odd = lax.axis_index("slab") % 2
+    even = lax.axis_index("patch") % 2 == 0
     cols = state_ref.shape[1]
+    for copy in copies:
+        copy.wait()
     for i, row in enumerate((odd, 1 - odd)):
-        out_ref[i * cols : (i + 1) * cols, :] = state_ref[row].astype(BF)
-        out_ref[(i + 2) * cols : (i + 3) * cols, :] = rhs_ref[row].astype(BF)
+        for part, ref in ((0, state_ref), (2, rhs_ref)):
+            value = ref[row]
+            at = part + i
+            own_ref[at * cols : (at + 1) * cols, :] = value.astype(BF)
+            low, high = value[0:8], value[cols - 8 : cols]
+            build_ref[0, 8 * at : 8 * at + 8, :] = jnp.where(even, high, low)
+            build_ref[1, 8 * at : 8 * at + 8, :] = jnp.where(even, low, high)
+    lines = lines_of(scale_ref, pad_ref)
     flip = odd == 1
-    first = jnp.where(flip, scale_ref[1:2], scale_ref[0:1])
-    second = jnp.where(flip, scale_ref[0:1], scale_ref[1:2])
-    pair = jnp.concatenate([halves(first), halves(second), jnp.zeros((14, 256), F32)], axis=0)
-    out_ref[4 * cols :, :] = pair.astype(BF)
-
-
-def row_table(own, inner, outer):
-    return (
-        (outer, 1, 3, 1),
-        (outer, 0, 2, 0),
-        (own, 0, 2, 0),
-        (own, 1, 3, 1),
-        (inner, 1, 3, 1),
-        (inner, 0, 2, 0),
-    )
-
-
-def strip_kernel(own_ref, inner_ref, outer_ref, disp_ref, one_ref, three_ref, relay_ref, build_ref):
-    patch = lax.axis_index("patch")
-    even = patch % 2 == 0
-    cols = relay_ref.shape[0]
-    relay_ref[...] = outer_ref[0:cols, :]
-    table = row_table(own_ref, inner_ref, outer_ref)
-    build_ref[:, 96:, :] = jnp.zeros((2, STRIPS - 96, 256), F32)
-    for r, (ref, state, rhs, scale) in enumerate(table):
-        for part, block in enumerate((state, rhs)):
-            at = (part * 6 + r) * 8
-            low = ref[block * cols : block * cols + 16, :].astype(F32)[0:8]
-            high = ref[(block + 1) * cols - 16 : (block + 1) * cols, :].astype(F32)[8:16]
-            build_ref[0, at : at + 8, :] = jnp.where(even, high, low)
-            build_ref[1, at : at + 8, :] = jnp.where(even, low, high)
-        line = ref[4 * cols : 4 * cols + 16, :].astype(F32)[scale : scale + 1]
-        build_ref[0, 97 + r : 98 + r, :] = line
-        build_ref[1, 97 + r : 98 + r, :] = line
+    first = jnp.where(flip, lines[1:2], lines[0:1])
+    second = jnp.where(flip, lines[0:1], lines[1:2])
+    pair = jnp.concatenate([halves(first), halves(second), jnp.zeros((6, 256), F32)], axis=0)
+    own_ref[4 * cols : 4 * cols + 8, :] = pair.astype(BF)
+    own_ref[4 * cols + 8 :, :] = jnp.zeros((8, 256), BF)
+    for e in range(2):
+        build_ref[e, 32:40, :] = pair
+        build_ref[e, EDGE:, :] = jnp.zeros((8, 256), F32)
     rows = disp_ref.shape[1]
     for c in range(3):
         top = halves(disp_ref[c, 0:2, :])
         bottom = halves(disp_ref[c, rows - 2 : rows, :])
-        at = STRIPS - 8 + 2 * c
+        at = EDGE + 2 * c
         build_ref[0, at : at + 2, :] = jnp.where(even, bottom, top)
         build_ref[1, at : at + 2, :] = jnp.where(even, top, bottom)
     one_ref[...] = build_ref[0].astype(BF)
@@ -292,19 +298,31 @@
     y_ref,
     inverse_ref,
     tmap_ref,
-    elem_ref,
-    point_ref,
-    count_ref,
-    out_ref,
+    elem_hbm,
+    point_hbm,
+    count_hbm,
+    out_hbm,
     message_ref,
     v_ref,
     r_ref,
     s_ref,
     i_ref,
     line_ref,
-    side_ref,
     rows_ref,
+    elem_ref,
+    point_ref,
+    count_ref,
+    out_ref,
+    sems,
 ):
+    copies = [
+        pltpu.make_async_copy(a, b, sems.at[i])
+        for i, (a, b) in enumerate(
+            ((elem_hbm, elem_ref), (point_hbm, point_ref), (count_hbm, count_ref))
+        )
+    ]
+    for copy in copies:
+        copy.start()
     slab, patch = lax.axis_index("slab"), lax.axis_index("patch")
     last_slab, last_patch = lax.axis_size("slab") - 1, lax.axis_size("patch") - 1
     odd = slab % 2
@@ -312,41 +330,51 @@
     cols, width = state_ref.shape[1], state_ref.shape[2]
     wide = cols + 16
     inside = (slab > 0) & (slab < last_slab)
-    one = one_ref[...].astype(F32)
-    three = three_ref[...].astype(F32)
-    side_ref[0] = jnp.where(even, three, one)
-    side_ref[1] = jnp.where(even, one, three)
     col = iota((wide, width), 0)
     valid = (col >= 8) & (col < 8 + cols)
     valid = valid | ((col < 8) & (patch > 0)) | ((col >= 8 + cols) & (patch < last_patch))
     edge = valid.astype(F32)
     keep = edge * inside.astype(F32)
-    table = row_table(None, inner_ref, outer_ref)
+    head = 5 * cols + 16
+    strips = {
+        0: (one_ref[0:EDGE], three_ref[0:EDGE]),
+        1: (relay_ref[cols : cols + EDGE], relay_ref[cols + EDGE : cols + 2 * EDGE]),
+        2: (outer_ref[head : head + EDGE], outer_ref[head + EDGE : head + 2 * EDGE]),
+    }
+    sides = {}
+    for kind, pair in strips.items():
+        one, three = (x.astype(F32) for x in pair)
+        sides[kind] = (jnp.where(even, three, one), jnp.where(even, one, three))
     lane = iota((1, 128), 1)
-    line_ref[...] = jnp.ones_like(line_ref)
-    for r, (ref, state, rhs, scale) in enumerate(table):
-        if ref is None:
-            row = odd if r == 2 else 1 - odd
+    line_ref[...] = jnp.zeros_like(line_ref)
+    line_ref[0:2, 0:cols] = scale_ref[...]
+    exact = pltpu.roll(line_ref[...], 8, 1)
+    table = ((2, 1), (2, 0), (0, 0), (0, 1), (1, 1), (1, 0))
+    for r, (kind, i) in enumerate(table):
+        if kind == 0:
+            row = odd if i == 0 else 1 - odd
             v_ref[r + 1, 8 : 8 + cols, :] = state_ref[row]
             r_ref[r, 8 : 8 + cols, :] = rhs_ref[row]
-            line = jnp.where(row == 1, scale_ref[1:2], scale_ref[0:1])
+            line = jnp.where(row == 1, exact[1:2], exact[0:1])
         else:
-            v_ref[r + 1, 8 : 8 + cols, :] = ref[state * cols : (state + 1) * cols, :].astype(F32)
-            r_ref[r, 8 : 8 + cols, :] = ref[rhs * cols : (rhs + 1) * cols, :].astype(F32)
-            both = ref[4 * cols : 4 * cols + 16, :].astype(F32)[scale : scale + 1]
+            ref = inner_ref if kind == 1 else outer_ref
+            v_ref[r + 1, 8 : 8 + cols, :] = ref[i * cols : (i + 1) * cols, :].astype(F32)
+            r_ref[r, 8 : 8 + cols, :] = ref[(i + 2) * cols : (i + 3) * cols, :].astype(F32)
+            both = ref[4 * cols : 4 * cols + 16, :].astype(F32)[i : i + 1]
             line = both[:, :128] + both[:, 128:]
-        for e, start in ((0, 0), (1, 8 + cols)):
-            v_ref[r + 1, start : start + 8, :] = side_ref[e, 8 * r : 8 * r + 8, :]
-            r_ref[r, start : start + 8, :] = side_ref[e, 48 + 8 * r : 56 + 8 * r, :]
-            both = side_ref[e, 97 + r : 98 + r, :]
+        for side, start in zip(sides[kind], (0, 8 + cols)):
+            v_ref[r + 1, start : start + 8, :] = side[8 * i : 8 * i + 8]
+            r_ref[r, start : start + 8, :] = side[16 + 8 * i : 24 + 8 * i]
+            both = side[32 + i : 33 + i]
             far = pltpu.roll(both[:, :128] + both[:, 128:], 64, 1)
             here = (lane >= start) & (lane < start + 8)
             line = jnp.where(here, far, line)
         line_ref[r : r + 1, :] = jnp.where(line > 0.0, line, 1.0)
+    line_ref[6:8, :] = jnp.ones((2, 128), F32)
     v_ref[0] = jnp.zeros((wide, width), F32)
     v_ref[7] = jnp.zeros((wide, width), F32)
-    v_ref[0, 8 : 8 + cols, :] = outer_ref[4 * cols + 16 : 5 * cols + 16, :].astype(F32)
-    v_ref[7, 8 : 8 + cols, :] = relay_ref[...].astype(F32)
+    v_ref[0, 8 : 8 + cols, :] = outer_ref[4 * cols + 16 : head, :].astype(F32)
+    v_ref[7, 8 : 8 + cols, :] = relay_ref[0:cols, :].astype(F32)
     for r in range(8):
         v_ref[r] = v_ref[r] * (keep if r < 3 else edge)
     lines = line_ref[...]
@@ -376,17 +404,22 @@
             v_ref[a + j] = value[j] * (keep if a + j < 3 else edge)
     out_ref[odd] = v_ref[3, 8 : 8 + cols, :]
     out_ref[1 - odd] = v_ref[4, 8 : 8 + cols, :]
+    out = pltpu.make_async_copy(out_ref, out_hbm, sems.at[3])
+    out.start()
     final = out_ref[...].astype(BF).reshape(2 * cols, width)
-    slot_rows(final, tmap_ref[...], elem_ref[...], point_ref[...], count_ref, rows_ref)
+    for copy in copies:
+        copy.wait()
+    slot_rows(final, tmap_ref[...], elem_ref[0], point_ref[0], count_ref.at[0], rows_ref)
     message_ref[...] = jnp.broadcast_to(rows_ref[...].astype(BF)[None], message_ref.shape)
-
-
-def call(kernel, name, out_shape, operands, scratch=()):
+    out.wait()
+
+
+def call(kernel, name, out_shape, operands, scratch=(), in_specs=None, out_specs=None):
     return pl.pallas_call(
         kernel,
         out_shape=out_shape,
-        in_specs=vmem(len(operands)),
-        out_specs=jax.tree.map(lambda _: vmem(1)[0], out_shape),
+        in_specs=in_specs or vmem(len(operands)),
+        out_specs=out_specs or jax.tree.map(lambda _: vmem(1)[0], out_shape),
         scratch_shapes=list(scratch),
         compiler_params=params(),
         name=name,
@@ -415,25 +448,31 @@
     inner_pairs = [(s, s ^ 1) for s in range(slabs)]
     outer_pairs = [(s, s + 1) for s in range(1, slabs - 1, 2)]
     outer_pairs = outer_pairs + [(b, a) for a, b in outer_pairs]
-    scale = jnp.pad(element_scale, ((0, 0), (8, 120 - cols)))
-    own = call(
-        near_kernel, "near", shape((4 * cols + 16, width), BF), (fluid_state, fluid_rhs, scale)
+    strip = shape((EDGE + 8, width), BF)
+    own, to_one, to_three = call(
+        near_kernel,
+        "near",
+        (shape((4 * cols + 16, width), BF), strip, strip),
+        (fluid_state, fluid_rhs, element_scale, displacement),
+        [
+            pltpu.VMEM(fluid_state.shape, F32),
+            pltpu.VMEM(fluid_rhs.shape, F32),
+            pltpu.VMEM(element_scale.shape, F32),
+            pltpu.VMEM(displacement.shape, F32),
+            pltpu.VMEM((8, 128), F32),
+            pltpu.VMEM((2, EDGE + 8, width), F32),
+            pltpu.SemaphoreType.DMA((4,)),
+        ],
+        in_specs=hbm(4),
     )
     inner = lax.ppermute(own, "slab", inner_pairs)
+    from_three = lax.ppermute(to_three, "patch", [(1, 2), (2, 1)])
+    from_one = lax.ppermute(to_one, "patch", patch_pairs(1))
+    strips = [from_one[:EDGE], from_three[:EDGE]]
     outer = lax.ppermute(
-        jnp.concatenate([own, inner[cols : 2 * cols]]), "slab", outer_pairs
-    )
-    strip = shape((STRIPS, width), BF)
-    to_one, to_three, relay = call(
-        strip_kernel,
-        "strip",
-        (strip, strip, shape((cols, width), BF)),
-        (own, inner, outer, displacement),
-        [pltpu.VMEM((2, STRIPS, width), F32)],
-    )
-    relayed = lax.ppermute(relay, "slab", inner_pairs)
-    from_one = lax.ppermute(to_one, "patch", patch_pairs(1))
-    from_three = lax.ppermute(to_three, "patch", [(1, 2), (2, 1)])
+        jnp.concatenate([own, inner[cols : 2 * cols]] + strips), "slab", outer_pairs
+    )
+    relay = lax.ppermute(jnp.concatenate([outer[:cols]] + strips), "slab", inner_pairs)
     wide = cols + 16
     state, message = call(
         sweep_kernel,
@@ -442,20 +481,20 @@
         (
             fluid_state,
             fluid_rhs,
-            scale,
+            element_scale,
             inner,
             outer,
             from_one,
             from_three,
-            relayed,
+            relay,
             element_matrix,
             couple_x,
             couple_y,
             block_inverse,
             traction_map,
-            slot_elem.reshape(1, slots),
-            slot_point.reshape(1, slots),
-            slot_count.reshape(1, owners),
+            slot_elem,
+            slot_point,
+            slot_count,
         ),
         [
             pltpu.VMEM((8, wide, width), F32),
@@ -463,9 +502,15 @@
             pltpu.VMEM((6, wide, width), F32),
             pltpu.VMEM((6, wide, width), F32),
             pltpu.VMEM((8, 128), F32),
-            pltpu.VMEM((2, STRIPS, width), F32),
             pltpu.VMEM((owners, 8, 128), F32),
+            pltpu.VMEM((1, 1, slots), I32),
+            pltpu.VMEM((1, 1, slots), I32),
+            pltpu.VMEM((1, 1, owners), I32),
+            pltpu.VMEM(fluid_state.shape, F32),
+            pltpu.SemaphoreType.DMA((4,)),
         ],
+        in_specs=vmem(13) + hbm(3),
+        out_specs=tuple(hbm(1) + vmem(1)),
     )
     kd = call(
         shell_kernel,

time: 66.4 us -> 64.6 us (0.973)
  Pallas kernels: 11.6 us -> 9.23 us
    ppermute x1, waiting for transfers between devices: 3.38 us -> 0.01 us  [shards(): inner = lax.ppermute(own, 'slab', inner_pairs)]
    pallas_call x1, Pallas kernels: 8.36 us -> 5.12 us  [exchange_and_relax(): pl.pallas_call(owner_kernel, out_shape=(jax.ShapeDtypeStruct(displacement...]
    ppermute x1, waiting for transfers between devices: 0.01 us -> 2.11 us  [shards(): from_three = lax.ppermute(to_three, 'patch', [(1, 2), (2, 1)])]
    ppermute x2, waiting for transfers between devices: 1.31 us -> 2.35 us  [the longest x1 2.35 us: shards(): lax.ppermute(jnp.concatenate([outer[:cols]] + strips), 'slab', inner_pairs)]
    unnamed x24 -> x28, local copies, waits for them, and re-layouts: 2.44 us -> 3.44 us
    pallas_call x4 -> x3, Pallas kernels: 2.59 us -> 3.51 us  [call(): pl.pallas_call(kernel, out_shape=out_shape, in_specs=in_specs or vmem(len...]
    pad x1 -> x0, local copies, waits for them, and re-layouts: 0.75 us -> none  [shards(): scale = jnp.pad(element_scale, ((0, 0), (8, 120 - cols)))]
where the time goes in v3:
time: 64.6 us; the launch traced here: 64.3 us
  starting transfers between devices  33.4 us (52%)
  waiting for transfers between devices  17.3 us (27%)
  Pallas kernels  9.23 us (14%)
  local copies, waits for them, and re-layouts  3.45 us (5%)
  between operations  0.89 us (1%)
    all_to_all x1, starting transfers between devices, exchange_and_relax(): lax.all_to_all(message.reshape(sources, 8, 128), ('slab', 'patch'), 0, 0,...  15.3 us
    all_to_all x1, waiting for transfers between devices, exchange_and_relax(): lax.all_to_all(message.reshape(sources, 8, 128), ('slab', 'patch'), 0, 0,...  11.1 us
    ppermute x1, starting transfers between devices, shards(): lax.ppermute(jnp.concatenate([outer[:cols]] + strips), 'slab', inner_pairs)  8.66 us
    pallas_call x1, Pallas kernels, exchange_and_relax(): pl.pallas_call(owner_kernel, out_shape=(jax.ShapeDtypeStruct(displacement...  5.12 us
    pallas_call x3, Pallas kernels, call(): pl.pallas_call(kernel, out_shape=out_shape, in_specs=in_specs or vmem(len...  3.51 us
    unnamed x28, local copies, waits for them, and re-layouts  3.44 us
    ppermute x1, starting transfers between devices, shards(): from_three = lax.ppermute(to_three, 'patch', [(1, 2), (2, 1)])  3 us
    ppermute x1, starting transfers between devices, shards(): inner = lax.ppermute(own, 'slab', inner_pairs)  2.55 us
  transfers between devices with their start and end apart: 9, of which 5 were waited for; matrix products, arithmetic and copies ran while one was open for 0% of the time, Pallas kernels for 0%

profile of v3, /device:TPU:1, one launch (start us, length us, event | category | flops | bytes accessed | tf_op | source)
XLA Modules:
  0.0 64.3 jit_solution(9513784699156427750)
XLA Ops:
  0.6 0.0 copy-start
  0.6 0.9 %copy-done = f32[3,64,128]{2,1,0:T(8,128)S(1)} copy-done((f32[3,64,128]{2,1,0:T(8,128)S(1)}, f32[3,64,128]{2,1,0:T(8,128)}, u32[]{:S(2)}) %copy-start) | copy-done | bytes 98328
  1.5 0.9 %copy-done.2 = f32[2,64,256]{2,1,0:T(8,128)S(1)} copy-done((f32[2,64,256]{2,1,0:T(8,128)S(1)}, f32[2,64,256]{2,1,0:T(8,128)}, u32[]{:S(2)}) %copy-start.2) | copy-done | bytes 131096
  2.4 0.9 %copy-done.3 = f32[2,64,256]{2,1,0:T(8,128)S(1)} copy-done((f32[2,64,256]{2,1,0:T(8,128)S(1)}, f32[2,64,256]{2,1,0:T(8,128)}, u32[]{:S(2)}) %copy-start.3) | copy-done | bytes 131096
  3.3 0.7 %copy-done.11 = f32[2,64]{1,0:T(2,128)S(1)} copy-done((f32[2,64]{1,0:T(2,128)S(1)}, f32[2,64]{1,0:T(2,128)}, u32[]{:S(2)}) %copy-start.11) | copy-done | bytes 536
  4.0 0.6 near.1
  4.6 2.5 %collective-permute-start = (bf16[272,256]{1,0:T(8,128)(2,1)S(1)}, bf16[272,256]{1,0:T(8,128)(2,1)S(1)}, u32[]{:S(2)}, u32[]{:S(2)}) collective-permute-start(bf16[272,256]{1,0:T(8,128)(2,1)S(1)} %get-tuple-element.13), channel_id=1, source_target_pairs={{0,4},{4,0},{8,12},{12,8},{16,20},{20,16},{24,28},{28,24},{32,36},... | collective-permute-start | bytes 417800 | tf_op jit(solution)/shard_map/ppermute | solution.py:468
  7.2 1.0 %collective-permute-start.1 = (bf16[48,256]{1,0:T(8,128)(2,1)S(1)}, bf16[48,256]{1,0:T(8,128)(2,1)S(1)}, u32[]{:S(2)}, u32[]{:S(2)}) collective-permute-start(bf16[48,256]{1,0:T(8,128)(2,1)S(1)} %get-tuple-element.14), channel_id=1, source_target_pairs={{0,1},{1,0},{2,3},{3,2},{4,5},{5,4},{6,7},{7,6},{8,9},{9,8},{10,11... | collective-permute-start | bytes 73736 | tf_op jit(solution)/shard_map/ppermute | solution.py:470
  8.1 3.0 %collective-permute-start.2 = (bf16[48,256]{1,0:T(8,128)(2,1)S(1)}, bf16[48,256]{1,0:T(8,128)(2,1)S(1)}, u32[]{:S(2)}, u32[]{:S(2)}) collective-permute-start(bf16[48,256]{1,0:T(8,128)(2,1)S(1)} %get-tuple-element.15), channel_id=1, source_target_pairs={{1,2},{2,1},{5,6},{6,5},{9,10},{10,9},{13,14},{14,13},{17,18},{18,... | collective-permute-start | bytes 73736 | tf_op jit(solution)/shard_map/ppermute | solution.py:469
  11.1 0.0 collective-permute-done.1.one_ref
  11.1 2.1 %collective-permute-done.2.three_ref = bf16[48,256]{1,0:T(8,128)(2,1)S(1)} collective-permute-done((bf16[48,256]{1,0:T(8,128)(2,1)S(1)}, bf16[48,256]{1,0:T(8,128)(2,1)S(1)}, u32[]{:S(2)}, u32[]{:S(2)}) %collective-permute-start.2) | collective-permute-done | bytes 24608 | tf_op jit(solution)/shard_map/ppermute | solution.py:469
  13.3 0.0 collective-permute-done.inner_ref
  13.3 0.0 copy-start.5
  13.3 0.0 copy-start.6
  13.3 0.0 copy-start.7
  13.3 0.0 copy-start.4
  13.3 0.8 %collective-permute-start.3 = (bf16[416,256]{1,0:T(8,128)(2,1)S(1)}, bf16[416,256]{1,0:T(8,128)(2,1)S(1)}, u32[]{:S(2)}, u32[]{:S(2)}) collective-permute-start(bf16[416,256]{1,0:T(8,128)(2,1)S(1)} %pad_maximum_fusion), channel_id=1, source_target_pairs={{4,8},{12,16},{20,24},{28,32},{36,40},{44,48},{52,56},{60,64},{68,... | collective-permute-start | bytes 638984 | tf_op jit(solution)/shard_map/ppermute | solution.py:472
  14.2 0.0 collective-permute-done.3.outer_ref
  14.2 0.0 copy-start.9
  14.2 0.0 copy-start.10
  14.2 0.0 copy-start.12
  14.2 0.0 copy-start.13
  14.2 8.7 %collective-permute-start.4 = (bf16[144,256]{1,0:T(8,128)(2,1)S(1)}, bf16[144,256]{1,0:T(8,128)(2,1)S(1)}, u32[]{:S(2)}, u32[]{:S(2)}) collective-permute-start(bf16[144,256]{1,0:T(8,128)(2,1)S(1)} %pad_maximum_fusion.1), channel_id=1, source_target_pairs={{0,4},{4,0},{8,12},{12,8},{16,20},{20,16},{24,28},{28,24},{32,36},... | collective-permute-start | bytes 221192 | tf_op jit(solution)/shard_map/ppermute | solution.py:475
  22.9 2.3 %collective-permute-done.4.relay_ref = bf16[144,256]{1,0:T(8,128)(2,1)S(1)} collective-permute-done((bf16[144,256]{1,0:T(8,128)(2,1)S(1)}, bf16[144,256]{1,0:T(8,128)(2,1)S(1)}, u32[]{:S(2)}, u32[]{:S(2)}) %collective-permute-start.4) | collective-permute-done | bytes 73760 | tf_op jit(solution)/shard_map/ppermute | solution.py:475
  25.3 0.0 copy-done.5
  25.3 0.0 copy-done.6
  25.3 0.0 copy-done.7
  25.3 0.0 copy-done.4
  25.3 0.0 copy-done.9
  25.3 0.0 copy-done.10
  25.3 0.0 copy-done.12
  25.3 0.0 copy-done.13
  25.3 2.7 %sweep.1 = (f32[2,64,256]{2,1,0:T(8,128)}, bf16[32,4,8,128]{3,2,1,0:T(8,128)(2,1)}) custom-call(f32[2,64,256]{2,1,0:T(8,128)S(1)} %copy-done.2, f32[2,64,256]{2,1,0:T(8,128)S(1)} %copy-done.3, f32[2,64]{1,0:T(2,128)S(1)} %copy-done.11, bf16[272,256]{1,0:T(8,128)(2,1)S(1)} %collective-permute-done.inner_ref, ...), custom_call_target="tpu_custom_call" | custom-call | tf_op jit(solution)/shard_map/sweep/pallas_call | solution.py:418
  28.0 0.0 copy-start.1
  28.0 0.0 copy-start.8
  28.0 15.3 %all-to-all-start = ((bf16[128,8,128]{2,1,0:T(8,128)(2,1)}), bf16[128,8,128]{2,1,0:T(8,128)(2,1)S(1)}, u32[]{:S(2)}, u32[]{:S(2)}) async-start(bf16[128,8,128]{2,1,0:T(8,128)(2,1)} %bitcast), calls=%async_computation | async-start | bytes 524288 | tf_op jit(solution)/shard_map/all_to_all | solution.py:192
  43.3 0.0 copy-done.1
  43.3 0.0 copy-done.8
  43.3 0.3 shell.1.kd_ref
  43.6 11.1 %all-to-all-done.got_ref = bf16[128,8,128]{2,1,0:T(8,128)(2,1)S(1)} async-done(((bf16[128,8,128]{2,1,0:T(8,128)(2,1)}), bf16[128,8,128]{2,1,0:T(8,128)(2,1)S(1)}, u32[]{:S(2)}, u32[]{:S(2)}) %all-to-all-start) | async-done | bytes 262176 | tf_op jit(solution)/shard_map/all_to_all | solution.py:192
  54.6 5.1 %owner.1 = (f32[3,64,128]{2,1,0:T(8,128)}, f32[8,256]{1,0:T(8,128)S(1)}, f32[8,256]{1,0:T(8,128)S(1)}, f32[8,256]{1,0:T(8,128)S(1)}, f32[8,256]{1,0:T(8,128)S(1)}) custom-call(bf16[128,8,128]{2,1,0:T(8,128)(2,1)S(1)} %all-to-all-done.got_ref, f32[3,64,128]{2,1,0:T(8,128)S(1)} %copy-done.1, f32[64,128]{1,0:T(8,128)S(1)} %copy-done.8, ...), custom_call_target="tpu_custom_call" | custom-call | tf_op jit(solution)/shard_map/owner/pallas_call | solution.py:196
  59.8 0.5 collective-permute-start.5
  60.3 0.3 collective-permute-start.6
  60.6 1.4 %collective-permute-start.7 = (f32[8,256]{1,0:T(8,128)S(1)}, f32[8,256]{1,0:T(8,128)S(1)}, u32[]{:S(2)}, u32[]{:S(2)}) collective-permute-start(f32[8,256]{1,0:T(8,128)S(1)} %get-tuple-element.22), channel_id=1, source_target_pairs={{0,3},{1,2},{2,1},{3,0},{4,7},{5,6},{6,5},{7,4},{8,11},{9,10},{10,... | collective-permute-start | bytes 24584 | tf_op jit(solution)/shard_map/ppermute | solution.py:211
  62.0 0.0 collective-permute-done.5.r1
  62.0 0.8 %collective-permute-done.6.r2 = f32[8,256]{1,0:T(8,128)S(1)} collective-permute-done((f32[8,256]{1,0:T(8,128)S(1)}, f32[8,256]{1,0:T(8,128)S(1)}, u32[]{:S(2)}, u32[]{:S(2)}) %collective-permute-start.6) | collective-permute-done | bytes 8224 | tf_op jit(solution)/shard_map/ppermute | solution.py:211
  62.8 0.9 %collective-permute-done.7.r3 = f32[8,256]{1,0:T(8,128)S(1)} collective-permute-done((f32[8,256]{1,0:T(8,128)S(1)}, f32[8,256]{1,0:T(8,128)S(1)}, u32[]{:S(2)}, u32[]{:S(2)}) %collective-permute-start.7) | collective-permute-done | bytes 8224 | tf_op jit(solution)/shard_map/ppermute | solution.py:211
  63.7 0.6 finish.1
  (9 shorter events, 0.0 us)
Async XLA Ops:
  0.6 0.9 %copy-start = (f32[3,64,128]{2,1,0:T(8,128)S(1)}, f32[3,64,128]{2,1,0:T(8,128)}, u32[]{:S(2)}) copy-start(f32[3,64,128]{2,1,0:T(8,128)} %disp_ref.3) | copy-start | bytes 294916
  1.5 0.9 %copy-start.2 = (f32[2,64,256]{2,1,0:T(8,128)S(1)}, f32[2,64,256]{2,1,0:T(8,128)}, u32[]{:S(2)}) copy-start(f32[2,64,256]{2,1,0:T(8,128)} %state_ref.1) | copy-start | bytes 393220
  2.4 0.9 %copy-start.3 = (f32[2,64,256]{2,1,0:T(8,128)S(1)}, f32[2,64,256]{2,1,0:T(8,128)}, u32[]{:S(2)}) copy-start(f32[2,64,256]{2,1,0:T(8,128)} %rhs_ref.1) | copy-start | bytes 393220
  3.3 0.7 %copy-start.11 = (f32[2,64]{1,0:T(2,128)S(1)}, f32[2,64]{1,0:T(2,128)}, u32[]{:S(2)}) copy-start(f32[2,64]{1,0:T(2,128)} %scale_ref.1) | copy-start | bytes 1540
  4.6 8.6 %collective-permute-start = (bf16[272,256]{1,0:T(8,128)(2,1)S(1)}, bf16[272,256]{1,0:T(8,128)(2,1)S(1)}, u32[]{:S(2)}, u32[]{:S(2)}) collective-permute-start(bf16[272,256]{1,0:T(8,128)(2,1)S(1)} %get-tuple-element.13), channel_id=1, source_target_pairs={{0,4},{4,0},{8,12},{12,8},{16,20},{20,16},{24,28},{28,24},{32,36},... | collective-permute-start | bytes 417800 | tf_op jit(solution)/shard_map/ppermute | solution.py:468
  7.2 4.0 %collective-permute-start.1 = (bf16[48,256]{1,0:T(8,128)(2,1)S(1)}, bf16[48,256]{1,0:T(8,128)(2,1)S(1)}, u32[]{:S(2)}, u32[]{:S(2)}) collective-permute-start(bf16[48,256]{1,0:T(8,128)(2,1)S(1)} %get-tuple-element.14), channel_id=1, source_target_pairs={{0,1},{1,0},{2,3},{3,2},{4,5},{5,4},{6,7},{7,6},{8,9},{9,8},{10,11... | collective-permute-start | bytes 73736 | tf_op jit(solution)/shard_map/ppermute | solution.py:470
  8.1 5.1 %collective-permute-start.2 = (bf16[48,256]{1,0:T(8,128)(2,1)S(1)}, bf16[48,256]{1,0:T(8,128)(2,1)S(1)}, u32[]{:S(2)}, u32[]{:S(2)}) collective-permute-start(bf16[48,256]{1,0:T(8,128)(2,1)S(1)} %get-tuple-element.15), channel_id=1, source_target_pairs={{1,2},{2,1},{5,6},{6,5},{9,10},{10,9},{13,14},{14,13},{17,18},{18,... | collective-permute-start | bytes 73736 | tf_op jit(solution)/shard_map/ppermute | solution.py:469
  13.3 12.0 %copy-start.5 = (bf16[256,256]{1,0:T(8,128)(2,1)S(1)}, bf16[256,256]{1,0:T(8,128)(2,1)}, u32[]{:S(2)}) copy-start(bf16[256,256]{1,0:T(8,128)(2,1)} %x_ref.1) | copy-start | bytes 393220
  13.3 12.0 %copy-start.6 = (bf16[256,256]{1,0:T(8,128)(2,1)S(1)}, bf16[256,256]{1,0:T(8,128)(2,1)}, u32[]{:S(2)}) copy-start(bf16[256,256]{1,0:T(8,128)(2,1)} %y_ref.1) | copy-start | bytes 393220
  13.3 12.0 %copy-start.7 = (bf16[256,256]{1,0:T(8,128)(2,1)S(1)}, bf16[256,256]{1,0:T(8,128)(2,1)}, u32[]{:S(2)}) copy-start(bf16[256,256]{1,0:T(8,128)(2,1)} %inverse_ref.1) | copy-start | bytes 393220
  13.3 11.9 %copy-start.4 = (bf16[256,256]{1,0:T(8,128)(2,1)S(1)}, bf16[256,256]{1,0:T(8,128)(2,1)}, u32[]{:S(2)}) copy-start(bf16[256,256]{1,0:T(8,128)(2,1)} %matrix_ref.1) | copy-start | bytes 393220
  13.3 0.8 %collective-permute-start.3 = (bf16[416,256]{1,0:T(8,128)(2,1)S(1)}, bf16[416,256]{1,0:T(8,128)(2,1)S(1)}, u32[]{:S(2)}, u32[]{:S(2)}) collective-permute-start(bf16[416,256]{1,0:T(8,128)(2,1)S(1)} %pad_maximum_fusion), channel_id=1, source_target_pairs={{4,8},{12,16},{20,24},{28,32},{36,40},{44,48},{52,56},{60,64},{68,... | collective-permute-start | bytes 638984 | tf_op jit(solution)/shard_map/ppermute | solution.py:472
  14.2 11.1 %copy-start.9 = (s32[1,1,1024]{2,1,0:T(1,128)S(1)}, s32[1,1,1024]{2,1,0:T(1,128)}, u32[]{:S(2)}) copy-start(s32[1,1,1024]{2,1,0:T(1,128)} %elem_hbm.1) | copy-start | bytes 12292
  14.2 11.1 %copy-start.10 = (s32[1,1,1024]{2,1,0:T(1,128)S(1)}, s32[1,1,1024]{2,1,0:T(1,128)}, u32[]{:S(2)}) copy-start(s32[1,1,1024]{2,1,0:T(1,128)} %point_hbm.1) | copy-start | bytes 12292
  14.2 11.1 %copy-start.12 = (bf16[3,256]{1,0:T(4,128)(2,1)S(1)}, bf16[3,256]{1,0:T(4,128)(2,1)}, u32[]{:S(2)}) copy-start(bf16[3,256]{1,0:T(4,128)(2,1)} %tmap_ref.1) | copy-start | bytes 4612
  14.2 11.1 %copy-start.13 = (s32[1,1,4]{2,1,0:T(1,128)S(1)}, s32[1,1,4]{2,1,0:T(1,128)}, u32[]{:S(2)}) copy-start(s32[1,1,4]{2,1,0:T(1,128)} %count_hbm.1) | copy-start | bytes 52
  14.2 11.0 %collective-permute-start.4 = (bf16[144,256]{1,0:T(8,128)(2,1)S(1)}, bf16[144,256]{1,0:T(8,128)(2,1)S(1)}, u32[]{:S(2)}, u32[]{:S(2)}) collective-permute-start(bf16[144,256]{1,0:T(8,128)(2,1)S(1)} %pad_maximum_fusion.1), channel_id=1, source_target_pairs={{0,4},{4,0},{8,12},{12,8},{16,20},{20,16},{24,28},{28,24},{32,36},... | collective-permute-start | bytes 221192 | tf_op jit(solution)/shard_map/ppermute | solution.py:475
  28.0 15.3 %copy-start.1 = (f32[3,64,128]{2,1,0:T(8,128)S(1)}, f32[3,64,128]{2,1,0:T(8,128)}, u32[]{:S(2)}) copy-start(f32[3,64,128]{2,1,0:T(8,128)} %disp_ref.3) | copy-start | bytes 294916
  28.0 15.3 %copy-start.8 = (f32[64,128]{1,0:T(8,128)S(1)}, f32[64,128]{1,0:T(8,128)}, u32[]{:S(2)}) copy-start(f32[64,128]{1,0:T(8,128)} %stiff_ref.3) | copy-start | bytes 98308
  28.0 26.6 %all-to-all-start = ((bf16[128,8,128]{2,1,0:T(8,128)(2,1)}), bf16[128,8,128]{2,1,0:T(8,128)(2,1)S(1)}, u32[]{:S(2)}, u32[]{:S(2)}) async-start(bf16[128,8,128]{2,1,0:T(8,128)(2,1)} %bitcast), calls=%async_computation | async-start | bytes 524288 | tf_op jit(solution)/shard_map/all_to_all | solution.py:192
  59.8 2.2 %collective-permute-start.5 = (f32[8,256]{1,0:T(8,128)S(1)}, f32[8,256]{1,0:T(8,128)S(1)}, u32[]{:S(2)}, u32[]{:S(2)}) collective-permute-start(f32[8,256]{1,0:T(8,128)S(1)} %get-tuple-element.20), channel_id=1, source_target_pairs={{0,1},{1,0},{2,3},{3,2},{4,5},{5,4},{6,7},{7,6},{8,9},{9,8},{10,11... | collective-permute-start | bytes 24584 | tf_op jit(solution)/shard_map/ppermute | solution.py:211
  60.3 2.5 %collective-permute-start.6 = (f32[8,256]{1,0:T(8,128)S(1)}, f32[8,256]{1,0:T(8,128)S(1)}, u32[]{:S(2)}, u32[]{:S(2)}) collective-permute-start(f32[8,256]{1,0:T(8,128)S(1)} %get-tuple-element.21), channel_id=1, source_target_pairs={{0,2},{1,3},{2,0},{3,1},{4,6},{5,7},{6,4},{7,5},{8,10},{9,11},{10,... | collective-permute-start | bytes 24584 | tf_op jit(solution)/shard_map/ppermute | solution.py:211
  60.6 3.1 %collective-permute-start.7 = (f32[8,256]{1,0:T(8,128)S(1)}, f32[8,256]{1,0:T(8,128)S(1)}, u32[]{:S(2)}, u32[]{:S(2)}) collective-permute-start(f32[8,256]{1,0:T(8,128)S(1)} %get-tuple-element.22), channel_id=1, source_target_pairs={{0,3},{1,2},{2,1},{3,0},{4,7},{5,6},{6,5},{7,4},{8,11},{9,10},{10,... | collective-permute-start | bytes 24584 | tf_op jit(solution)/shard_map/ppermute | solution.py:211

commit v4 on v3

--- a/solution.py
+++ b/solution.py
@@ -10,7 +10,7 @@
 F32 = jnp.float32
 I32 = jnp.int32
 LIMIT = 48 << 20
-EDGE = 40
+EDGE = 24
 
 
 def vmem(n):
@@ -106,9 +106,7 @@
     out.start()
     flat = new.reshape(3 * rows, 128)
     high = flat.astype(BF)
-    rest1 = flat - high.astype(F32)
-    mid = rest1.astype(BF)
-    low = (rest1 - mid.astype(F32)).astype(BF)
+    low = (flat - high.astype(F32)).astype(BF)
     row_ids = iota((rows, 128), 0).astype(F32)
     for d in range(4):
         src = first + (patch ^ d)
@@ -117,7 +115,6 @@
             lane = lane_ref[h, pl.ds(src, 1), :]
             hot = jnp.where(lane_ids == lane.astype(BF), ones, zeros)
             picked = jnp.dot(high, hot, preferred_element_type=F32)
-            picked += jnp.dot(mid, hot, preferred_element_type=F32)
             picked += jnp.dot(low, hot, preferred_element_type=F32)
             mask = row_ids == row
             for c in range(3):
@@ -234,7 +231,7 @@
 
 
 def near_kernel(
-    state_hbm, rhs_hbm, scale_hbm, disp_hbm, own_ref, one_ref, three_ref,
+    state_hbm, rhs_hbm, scale_hbm, disp_hbm, near_ref, own_ref, one_ref, three_ref,
     state_ref, rhs_ref, scale_ref, disp_ref, pad_ref, build_ref, sems,
 ):
     copies = [
@@ -260,18 +257,18 @@
             value = ref[row]
             at = part + i
             own_ref[at * cols : (at + 1) * cols, :] = value.astype(BF)
-            low, high = value[0:8], value[cols - 8 : cols]
-            build_ref[0, 8 * at : 8 * at + 8, :] = jnp.where(even, high, low)
-            build_ref[1, 8 * at : 8 * at + 8, :] = jnp.where(even, low, high)
+            low, high = value[0:4], value[cols - 4 : cols]
+            build_ref[0, 4 * at : 4 * at + 4, :] = jnp.where(even, high, low)
+            build_ref[1, 4 * at : 4 * at + 4, :] = jnp.where(even, low, high)
+    near_ref[...] = state_ref[1 - odd].astype(BF)
     lines = lines_of(scale_ref, pad_ref)
     flip = odd == 1
     first = jnp.where(flip, lines[1:2], lines[0:1])
     second = jnp.where(flip, lines[0:1], lines[1:2])
     pair = jnp.concatenate([halves(first), halves(second), jnp.zeros((6, 256), F32)], axis=0)
-    own_ref[4 * cols : 4 * cols + 8, :] = pair.astype(BF)
-    own_ref[4 * cols + 8 :, :] = jnp.zeros((8, 256), BF)
+    own_ref[4 * cols :, :] = pair.astype(BF)
     for e in range(2):
-        build_ref[e, 32:40, :] = pair
+        build_ref[e, 16:24, :] = pair
         build_ref[e, EDGE:, :] = jnp.zeros((8, 256), F32)
     rows = disp_ref.shape[1]
     for c in range(3):
@@ -288,6 +285,7 @@
     state_ref,
     rhs_ref,
     scale_ref,
+    near_ref,
     inner_ref,
     outer_ref,
     one_ref,
@@ -335,10 +333,15 @@
     valid = valid | ((col < 8) & (patch > 0)) | ((col >= 8 + cols) & (patch < last_patch))
     edge = valid.astype(F32)
     keep = edge * inside.astype(F32)
-    head = 5 * cols + 16
+    v_ref[:, 0:8, :] = jnp.zeros((8, 8, width), F32)
+    v_ref[:, 8 + cols :, :] = jnp.zeros((8, 8, width), F32)
+    r_ref[:, 0:8, :] = jnp.zeros((6, 8, width), F32)
+    r_ref[:, 8 + cols :, :] = jnp.zeros((6, 8, width), F32)
+    head = 5 * cols + 8
+    tail = 3 * cols + 8
     strips = {
         0: (one_ref[0:EDGE], three_ref[0:EDGE]),
-        1: (relay_ref[cols : cols + EDGE], relay_ref[cols + EDGE : cols + 2 * EDGE]),
+        1: (inner_ref[tail : tail + EDGE], inner_ref[tail + EDGE : tail + 2 * EDGE]),
         2: (outer_ref[head : head + EDGE], outer_ref[head + EDGE : head + 2 * EDGE]),
     }
     sides = {}
@@ -357,24 +360,28 @@
             r_ref[r, 8 : 8 + cols, :] = rhs_ref[row]
             line = jnp.where(row == 1, exact[1:2], exact[0:1])
         else:
-            ref = inner_ref if kind == 1 else outer_ref
-            v_ref[r + 1, 8 : 8 + cols, :] = ref[i * cols : (i + 1) * cols, :].astype(F32)
-            r_ref[r, 8 : 8 + cols, :] = ref[(i + 2) * cols : (i + 3) * cols, :].astype(F32)
-            both = ref[4 * cols : 4 * cols + 16, :].astype(F32)[i : i + 1]
+            if kind == 1:
+                value = near_ref[...] if i == 1 else inner_ref[0:cols]
+                ref, at = inner_ref, (i + 1) * cols
+            else:
+                value = outer_ref[i * cols : (i + 1) * cols]
+                ref, at = outer_ref, (i + 2) * cols
+            v_ref[r + 1, 8 : 8 + cols, :] = value.astype(F32)
+            r_ref[r, 8 : 8 + cols, :] = ref[at : at + cols, :].astype(F32)
+            below = (3 if kind == 1 else 4) * cols
+            both = ref[below : below + 8, :].astype(F32)[i : i + 1]
             line = both[:, :128] + both[:, 128:]
-        for side, start in zip(sides[kind], (0, 8 + cols)):
-            v_ref[r + 1, start : start + 8, :] = side[8 * i : 8 * i + 8]
-            r_ref[r, start : start + 8, :] = side[16 + 8 * i : 24 + 8 * i]
-            both = side[32 + i : 33 + i]
+        for side, start in zip(sides[kind], (4, 8 + cols)):
+            v_ref[r + 1, start : start + 4, :] = side[4 * i : 4 * i + 4]
+            r_ref[r, start : start + 4, :] = side[8 + 4 * i : 12 + 4 * i]
+            both = side[16 + i : 17 + i]
             far = pltpu.roll(both[:, :128] + both[:, 128:], 64, 1)
-            here = (lane >= start) & (lane < start + 8)
+            here = (lane >= start) & (lane < start + 4)
             line = jnp.where(here, far, line)
         line_ref[r : r + 1, :] = jnp.where(line > 0.0, line, 1.0)
     line_ref[6:8, :] = jnp.ones((2, 128), F32)
-    v_ref[0] = jnp.zeros((wide, width), F32)
-    v_ref[7] = jnp.zeros((wide, width), F32)
-    v_ref[0, 8 : 8 + cols, :] = outer_ref[4 * cols + 16 : head, :].astype(F32)
-    v_ref[7, 8 : 8 + cols, :] = relay_ref[0:cols, :].astype(F32)
+    v_ref[0, 8 : 8 + cols, :] = outer_ref[4 * cols + 8 : head, :].astype(F32)
+    v_ref[7, 8 : 8 + cols, :] = relay_ref[...].astype(F32)
     for r in range(8):
         v_ref[r] = v_ref[r] * (keep if r < 3 else edge)
     lines = line_ref[...]
@@ -449,11 +456,14 @@
     outer_pairs = [(s, s + 1) for s in range(1, slabs - 1, 2)]
     outer_pairs = outer_pairs + [(b, a) for a, b in outer_pairs]
     strip = shape((EDGE + 8, width), BF)
-    own, to_one, to_three = call(
+    near, own, to_one, to_three = call(
         near_kernel,
         "near",
-        (shape((4 * cols + 16, width), BF), strip, strip),
-        (fluid_state, fluid_rhs, element_scale, displacement),
+        (shape((cols, width), BF), shape((4 * cols + 8, width), BF), strip, strip),
+        tuple(
+            pltpu.with_memory_space_constraint(x, pltpu.HBM)
+            for x in (fluid_state, fluid_rhs, element_scale, displacement)
+        ),
         [
             pltpu.VMEM(fluid_state.shape, F32),
             pltpu.VMEM(fluid_rhs.shape, F32),
@@ -465,14 +475,15 @@
         ],
         in_specs=hbm(4),
     )
-    inner = lax.ppermute(own, "slab", inner_pairs)
+    inner_near = lax.ppermute(near, "slab", inner_pairs)
     from_three = lax.ppermute(to_three, "patch", [(1, 2), (2, 1)])
     from_one = lax.ppermute(to_one, "patch", patch_pairs(1))
     strips = [from_one[:EDGE], from_three[:EDGE]]
-    outer = lax.ppermute(
-        jnp.concatenate([own, inner[cols : 2 * cols]] + strips), "slab", outer_pairs
-    )
-    relay = lax.ppermute(jnp.concatenate([outer[:cols]] + strips), "slab", inner_pairs)
+    outer = lax.ppermute(jnp.concatenate([own, inner_near] + strips), "slab", outer_pairs)
+    inner = lax.ppermute(
+        jnp.concatenate([own[:cols], own[2 * cols :]] + strips), "slab", inner_pairs
+    )
+    relay = lax.ppermute(outer[:cols], "slab", inner_pairs)
     wide = cols + 16
     state, message = call(
         sweep_kernel,
@@ -482,6 +493,7 @@
             fluid_state,
             fluid_rhs,
             element_scale,
+            inner_near,
             inner,
             outer,
             from_one,
@@ -509,7 +521,7 @@
             pltpu.VMEM(fluid_state.shape, F32),
             pltpu.SemaphoreType.DMA((4,)),
         ],
-        in_specs=vmem(13) + hbm(3),
+        in_specs=vmem(14) + hbm(3),
         out_specs=tuple(hbm(1) + vmem(1)),
     )
     kd = call(

time: 64.6 us -> 58.5 us (0.906)
  local copies, waits for them, and re-layouts: 3.45 us -> 0.1 us
  starting transfers between devices: 33.4 us -> 31.6 us
  waiting for transfers between devices: 17.3 us -> 16.1 us
    unnamed x28 -> x26, local copies, waits for them, and re-layouts: 3.44 us -> 0.08 us
    ppermute x3 -> x4, starting transfers between devices: 12 us -> 10.5 us  [the longest x1 4.3 us: shards(): lax.ppermute(jnp.concatenate([own[:cols], own[2 * cols:]] + strips), 'sla...]
    ppermute x3 -> x4, waiting for transfers between devices: 2.35 us -> 1.31 us  [the longest x1 1.3 us: shards(): relay = lax.ppermute(outer[:cols], 'slab', inner_pairs)]
  transfers between devices with their start and end apart: 9 -> 10, of which waited for: 5 -> 5; matrix products, arithmetic and copies ran while one was open for 0% -> 0% of each run, Pallas kernels for 0% -> 0%
where the time goes in v4:
time: 58.5 us; the launch traced here: 58.3 us
  starting transfers between devices  31.6 us (54%)
  waiting for transfers between devices  16.1 us (28%)
  Pallas kernels  9.56 us (16%)
  between operations  0.92 us (2%)
    all_to_all x1, starting transfers between devices, exchange_and_relax(): lax.all_to_all(message.reshape(sources, 8, 128), ('slab', 'patch'), 0, 0,...  15 us
    all_to_all x1, waiting for transfers between devices, exchange_and_relax(): lax.all_to_all(message.reshape(sources, 8, 128), ('slab', 'patch'), 0, 0,...  11.1 us
    pallas_call x1, Pallas kernels, exchange_and_relax(): pl.pallas_call(owner_kernel, out_shape=(jax.ShapeDtypeStruct(displacement...  4.83 us
    ppermute x1, starting transfers between devices, shards(): lax.ppermute(jnp.concatenate([own[:cols], own[2 * cols:]] + strips), 'sla...  4.3 us
    pallas_call x3, Pallas kernels, call(): pl.pallas_call(kernel, out_shape=out_shape, in_specs=in_specs or vmem(len...  4.12 us
    ppermute x1, starting transfers between devices, shards(): from_three = lax.ppermute(to_three, 'patch', [(1, 2), (2, 1)])  3 us
    ppermute x1, starting transfers between devices, shards(): relay = lax.ppermute(outer[:cols], 'slab', inner_pairs)  2.84 us
    ppermute x1, starting transfers between devices, shards(): inner_near = lax.ppermute(near, 'slab', inner_pairs)  2.55 us
  transfers between devices with their start and end apart: 10, of which 5 were waited for; matrix products, arithmetic and copies ran while one was open for 0% of the time, Pallas kernels for 0%

profile of v4, /device:TPU:1, one launch (start us, length us, event | category | flops | bytes accessed | tf_op | source)
XLA Modules:
  0.0 58.3 jit_solution(13579954371078998589)
XLA Ops:
  0.6 1.2 %near.1 = (bf16[64,256]{1,0:T(8,128)(2,1)S(1)}, bf16[264,256]{1,0:T(8,128)(2,1)S(1)}, bf16[32,256]{1,0:T(8,128)(2,1)S(1)}, bf16[32,256]{1,0:T(8,128)(2,1)S(1)}) custom-call(f32[2,64,256]{2,1,0:T(8,128)} %state_ref.1, f32[2,64,256]{2,1,0:T(8,128)} %rhs_ref.1, f32[2,64]{1,0:T(2,128)} %scale_ref.1, f32[3,64,128]{2,1,0:T(8,128)} %disp_ref.3), custom_call_target="tpu_custom_call" | custom-call | tf_op jit(solution)/shard_map/near/pallas_call | solution.py:425
  1.8 2.5 %collective-permute-start = (bf16[64,256]{1,0:T(8,128)(2,1)S(1)}, bf16[64,256]{1,0:T(8,128)(2,1)S(1)}, u32[]{:S(2)}, u32[]{:S(2)}) collective-permute-start(bf16[64,256]{1,0:T(8,128)(2,1)S(1)} %get-tuple-element.14), channel_id=1, source_target_pairs={{0,4},{4,0},{8,12},{12,8},{16,20},{20,16},{24,28},{28,24},{32,36},... | collective-permute-start | bytes 98312 | tf_op jit(solution)/shard_map/ppermute | solution.py:478
  4.4 1.0 %collective-permute-start.1 = (bf16[32,256]{1,0:T(8,128)(2,1)S(1)}, bf16[32,256]{1,0:T(8,128)(2,1)S(1)}, u32[]{:S(2)}, u32[]{:S(2)}) collective-permute-start(bf16[32,256]{1,0:T(8,128)(2,1)S(1)} %get-tuple-element.16), channel_id=1, source_target_pairs={{0,1},{1,0},{2,3},{3,2},{4,5},{5,4},{6,7},{7,6},{8,9},{9,8},{10,11... | collective-permute-start | bytes 49160 | tf_op jit(solution)/shard_map/ppermute | solution.py:480
  5.3 3.0 %collective-permute-start.2 = (bf16[32,256]{1,0:T(8,128)(2,1)S(1)}, bf16[32,256]{1,0:T(8,128)(2,1)S(1)}, u32[]{:S(2)}, u32[]{:S(2)}) collective-permute-start(bf16[32,256]{1,0:T(8,128)(2,1)S(1)} %get-tuple-element.17), channel_id=1, source_target_pairs={{1,2},{2,1},{5,6},{6,5},{9,10},{10,9},{13,14},{14,13},{17,18},{18,... | collective-permute-start | bytes 49160 | tf_op jit(solution)/shard_map/ppermute | solution.py:479
  8.3 0.0 copy-start.6
  8.4 0.0 collective-permute-done.1.one_ref
  8.4 2.0 %collective-permute-done.2.three_ref = bf16[32,256]{1,0:T(8,128)(2,1)S(1)} collective-permute-done((bf16[32,256]{1,0:T(8,128)(2,1)S(1)}, bf16[32,256]{1,0:T(8,128)(2,1)S(1)}, u32[]{:S(2)}, u32[]{:S(2)}) %collective-permute-start.2) | collective-permute-done | bytes 16416 | tf_op jit(solution)/shard_map/ppermute | solution.py:479
  10.4 0.0 collective-permute-done.near_ref
  10.4 0.0 copy-start.4
  10.4 0.0 copy-start.5
  10.4 0.0 copy-start.1
  10.4 0.0 copy-start.2
  10.4 0.8 %collective-permute-start.4 = (bf16[376,256]{1,0:T(8,128)(2,1)S(1)}, bf16[376,256]{1,0:T(8,128)(2,1)S(1)}, u32[]{:S(2)}, u32[]{:S(2)}) collective-permute-start(bf16[376,256]{1,0:T(8,128)(2,1)S(1)} %pad_maximum_fusion), channel_id=1, source_target_pairs={{4,8},{12,16},{20,24},{28,32},{36,40},{44,48},{52,56},{60,64},{68,... | collective-permute-start | bytes 577544 | tf_op jit(solution)/shard_map/ppermute | solution.py:482
  11.3 0.0 copy-start.8
  11.3 0.0 copy-start.9
  11.3 0.0 copy-start.10
  11.3 0.0 copy-start.11
  11.3 0.0 copy-start.12
  11.3 4.3 %collective-permute-start.3 = (bf16[248,256]{1,0:T(8,128)(2,1)S(1)}, bf16[248,256]{1,0:T(8,128)(2,1)S(1)}, u32[]{:S(2)}, u32[]{:S(2)}) collective-permute-start(bf16[248,256]{1,0:T(8,128)(2,1)S(1)} %pad_maximum_fusion.1), channel_id=1, source_target_pairs={{0,4},{4,0},{8,12},{12,8},{16,20},{20,16},{24,28},{28,24},{32,36},... | collective-permute-start | bytes 380936 | tf_op jit(solution)/shard_map/ppermute | solution.py:483
  15.6 0.0 collective-permute-done.4.outer_ref
  15.6 2.8 %collective-permute-start.5 = (bf16[64,256]{1,0:T(8,128)(2,1)S(1)}, bf16[64,256]{1,0:T(8,128)(2,1)S(1)}, u32[]{:S(2)}, u32[]{:S(2)}) collective-permute-start(bf16[64,256]{1,0:T(8,128)(2,1)S(1)} %slice.22), channel_id=1, source_target_pairs={{0,4},{4,0},{8,12},{12,8},{16,20},{20,16},{24,28},{28,24},{32,36},... | collective-permute-start | bytes 98312 | tf_op jit(solution)/shard_map/ppermute | solution.py:486
  18.5 0.0 collective-permute-done.3.inner_ref
  18.5 1.3 %collective-permute-done.5.relay_ref = bf16[64,256]{1,0:T(8,128)(2,1)S(1)} collective-permute-done((bf16[64,256]{1,0:T(8,128)(2,1)S(1)}, bf16[64,256]{1,0:T(8,128)(2,1)S(1)}, u32[]{:S(2)}, u32[]{:S(2)}) %collective-permute-start.5) | collective-permute-done | bytes 32800 | tf_op jit(solution)/shard_map/ppermute | solution.py:486
  19.8 0.0 copy-done.6
  19.8 0.0 copy-done.3
  19.8 0.0 copy-done.4
  19.8 0.0 copy-done.5
  19.8 0.0 copy-done.1
  19.8 0.0 copy-done.2
  19.8 0.0 copy-done.8
  19.8 0.0 copy-done.9
  19.8 0.0 copy-done.10
  19.9 0.0 copy-done.11
  19.9 0.0 copy-done.12
  19.9 2.7 %sweep.1 = (f32[2,64,256]{2,1,0:T(8,128)}, bf16[32,4,8,128]{3,2,1,0:T(8,128)(2,1)}) custom-call(f32[2,64,256]{2,1,0:T(8,128)S(1)} %copy-done.1, f32[2,64,256]{2,1,0:T(8,128)S(1)} %copy-done.2, f32[2,64]{1,0:T(2,128)S(1)} %copy-done.10, bf16[64,256]{1,0:T(8,128)(2,1)S(1)} %collective-permute-done.near_ref, ...), custom_call_target="tpu_custom_call" | custom-call | tf_op jit(solution)/shard_map/sweep/pallas_call | solution.py:425
  22.6 0.0 copy-start
  22.6 0.0 copy-start.7
  22.6 15.0 %all-to-all-start = ((bf16[128,8,128]{2,1,0:T(8,128)(2,1)}), bf16[128,8,128]{2,1,0:T(8,128)(2,1)S(1)}, u32[]{:S(2)}, u32[]{:S(2)}) async-start(bf16[128,8,128]{2,1,0:T(8,128)(2,1)} %bitcast), calls=%async_computation | async-start | bytes 524288 | tf_op jit(solution)/shard_map/all_to_all | solution.py:189
  37.6 0.3 shell.1.kd_ref
  37.9 11.1 %all-to-all-done.got_ref = bf16[128,8,128]{2,1,0:T(8,128)(2,1)S(1)} async-done(((bf16[128,8,128]{2,1,0:T(8,128)(2,1)}), bf16[128,8,128]{2,1,0:T(8,128)(2,1)S(1)}, u32[]{:S(2)}, u32[]{:S(2)}) %all-to-all-start) | async-done | bytes 262176 | tf_op jit(solution)/shard_map/all_to_all | solution.py:189
  48.9 4.8 %owner.1 = (f32[3,64,128]{2,1,0:T(8,128)}, f32[8,256]{1,0:T(8,128)S(1)}, f32[8,256]{1,0:T(8,128)S(1)}, f32[8,256]{1,0:T(8,128)S(1)}, f32[8,256]{1,0:T(8,128)S(1)}) custom-call(bf16[128,8,128]{2,1,0:T(8,128)(2,1)S(1)} %all-to-all-done.got_ref, f32[3,64,128]{2,1,0:T(8,128)S(1)} %copy-done, f32[64,128]{1,0:T(8,128)S(1)} %copy-done.7, f32[3,64,128]{2,1,0:T(8,128)S(1)} %shell.1.kd_ref), custom_call_target="tpu_custom_call" | custom-call | tf_op jit(solution)/shard_map/owner/pallas_call | solution.py:193
  53.8 0.5 collective-permute-start.6
  54.3 0.3 collective-permute-start.7
  54.6 1.4 %collective-permute-start.8 = (f32[8,256]{1,0:T(8,128)S(1)}, f32[8,256]{1,0:T(8,128)S(1)}, u32[]{:S(2)}, u32[]{:S(2)}) collective-permute-start(f32[8,256]{1,0:T(8,128)S(1)} %get-tuple-element.24), channel_id=1, source_target_pairs={{0,3},{1,2},{2,1},{3,0},{4,7},{5,6},{6,5},{7,4},{8,11},{9,10},{10,... | collective-permute-start | bytes 24584 | tf_op jit(solution)/shard_map/ppermute | solution.py:208
  56.0 0.0 collective-permute-done.6.r1
  56.0 0.8 %collective-permute-done.7.r2 = f32[8,256]{1,0:T(8,128)S(1)} collective-permute-done((f32[8,256]{1,0:T(8,128)S(1)}, f32[8,256]{1,0:T(8,128)S(1)}, u32[]{:S(2)}, u32[]{:S(2)}) %collective-permute-start.7) | collective-permute-done | bytes 8224 | tf_op jit(solution)/shard_map/ppermute | solution.py:208
  56.8 0.9 %collective-permute-done.8.r3 = f32[8,256]{1,0:T(8,128)S(1)} collective-permute-done((f32[8,256]{1,0:T(8,128)S(1)}, f32[8,256]{1,0:T(8,128)S(1)}, u32[]{:S(2)}, u32[]{:S(2)}) %collective-permute-start.8) | collective-permute-done | bytes 8224 | tf_op jit(solution)/shard_map/ppermute | solution.py:208
  57.7 0.6 %finish.1 = f32[3,1,1,1024]{3,2,1,0:T(1,128)} custom-call(f32[8,256]{1,0:T(8,128)S(1)} %get-tuple-element.21.r0, f32[8,256]{1,0:T(8,128)S(1)} %collective-permute-done.6.r1, f32[8,256]{1,0:T(8,128)S(1)} %collective-permute-done.7.r2, f32[8,256]{1,0:T(8,128)S(1)} %collective-permute-done.8.r3), custom_call_target="tpu_custom_call" | custom-call | tf_op jit(solution)/shard_map/finish/pallas_call | solution.py:210
  (10 shorter events, 0.1 us)
Async XLA Ops:
  1.8 8.6 %collective-permute-start = (bf16[64,256]{1,0:T(8,128)(2,1)S(1)}, bf16[64,256]{1,0:T(8,128)(2,1)S(1)}, u32[]{:S(2)}, u32[]{:S(2)}) collective-permute-start(bf16[64,256]{1,0:T(8,128)(2,1)S(1)} %get-tuple-element.14), channel_id=1, source_target_pairs={{0,4},{4,0},{8,12},{12,8},{16,20},{20,16},{24,28},{28,24},{32,36},... | collective-permute-start | bytes 98312 | tf_op jit(solution)/shard_map/ppermute | solution.py:478
  4.4 4.0 %collective-permute-start.1 = (bf16[32,256]{1,0:T(8,128)(2,1)S(1)}, bf16[32,256]{1,0:T(8,128)(2,1)S(1)}, u32[]{:S(2)}, u32[]{:S(2)}) collective-permute-start(bf16[32,256]{1,0:T(8,128)(2,1)S(1)} %get-tuple-element.16), channel_id=1, source_target_pairs={{0,1},{1,0},{2,3},{3,2},{4,5},{5,4},{6,7},{7,6},{8,9},{9,8},{10,11... | collective-permute-start | bytes 49160 | tf_op jit(solution)/shard_map/ppermute | solution.py:480
  5.3 5.0 %collective-permute-start.2 = (bf16[32,256]{1,0:T(8,128)(2,1)S(1)}, bf16[32,256]{1,0:T(8,128)(2,1)S(1)}, u32[]{:S(2)}, u32[]{:S(2)}) collective-permute-start(bf16[32,256]{1,0:T(8,128)(2,1)S(1)} %get-tuple-element.17), channel_id=1, source_target_pairs={{1,2},{2,1},{5,6},{6,5},{9,10},{10,9},{13,14},{14,13},{17,18},{18,... | collective-permute-start | bytes 49160 | tf_op jit(solution)/shard_map/ppermute | solution.py:479
  8.3 11.4 %copy-start.6 = (bf16[256,256]{1,0:T(8,128)(2,1)S(1)}, bf16[256,256]{1,0:T(8,128)(2,1)}, u32[]{:S(2)}) copy-start(bf16[256,256]{1,0:T(8,128)(2,1)} %inverse_ref.1) | copy-start | bytes 393220
  10.4 9.4 %copy-start.3 = (bf16[256,256]{1,0:T(8,128)(2,1)S(1)}, bf16[256,256]{1,0:T(8,128)(2,1)}, u32[]{:S(2)}) copy-start(bf16[256,256]{1,0:T(8,128)(2,1)} %matrix_ref.1) | copy-start | bytes 393220
  10.4 9.4 %copy-start.4 = (bf16[256,256]{1,0:T(8,128)(2,1)S(1)}, bf16[256,256]{1,0:T(8,128)(2,1)}, u32[]{:S(2)}) copy-start(bf16[256,256]{1,0:T(8,128)(2,1)} %x_ref.1) | copy-start | bytes 393220
  10.4 9.4 %copy-start.5 = (bf16[256,256]{1,0:T(8,128)(2,1)S(1)}, bf16[256,256]{1,0:T(8,128)(2,1)}, u32[]{:S(2)}) copy-start(bf16[256,256]{1,0:T(8,128)(2,1)} %y_ref.1) | copy-start | bytes 393220
  10.4 9.4 %copy-start.1 = (f32[2,64,256]{2,1,0:T(8,128)S(1)}, f32[2,64,256]{2,1,0:T(8,128)}, u32[]{:S(2)}) copy-start(f32[2,64,256]{2,1,0:T(8,128)} %state_ref.1) | copy-start | bytes 393220
  10.4 9.4 %copy-start.2 = (f32[2,64,256]{2,1,0:T(8,128)S(1)}, f32[2,64,256]{2,1,0:T(8,128)}, u32[]{:S(2)}) copy-start(f32[2,64,256]{2,1,0:T(8,128)} %rhs_ref.1) | copy-start | bytes 393220
  10.4 5.2 %collective-permute-start.4 = (bf16[376,256]{1,0:T(8,128)(2,1)S(1)}, bf16[376,256]{1,0:T(8,128)(2,1)S(1)}, u32[]{:S(2)}, u32[]{:S(2)}) collective-permute-start(bf16[376,256]{1,0:T(8,128)(2,1)S(1)} %pad_maximum_fusion), channel_id=1, source_target_pairs={{4,8},{12,16},{20,24},{28,32},{36,40},{44,48},{52,56},{60,64},{68,... | collective-permute-start | bytes 577544 | tf_op jit(solution)/shard_map/ppermute | solution.py:482
  11.3 8.5 %copy-start.8 = (s32[1,1,1024]{2,1,0:T(1,128)S(1)}, s32[1,1,1024]{2,1,0:T(1,128)}, u32[]{:S(2)}) copy-start(s32[1,1,1024]{2,1,0:T(1,128)} %elem_hbm.1) | copy-start | bytes 12292
  11.3 8.5 %copy-start.9 = (s32[1,1,1024]{2,1,0:T(1,128)S(1)}, s32[1,1,1024]{2,1,0:T(1,128)}, u32[]{:S(2)}) copy-start(s32[1,1,1024]{2,1,0:T(1,128)} %point_hbm.1) | copy-start | bytes 12292
  11.3 8.5 %copy-start.10 = (f32[2,64]{1,0:T(2,128)S(1)}, f32[2,64]{1,0:T(2,128)}, u32[]{:S(2)}) copy-start(f32[2,64]{1,0:T(2,128)} %scale_ref.1) | copy-start | bytes 1540
  11.3 8.5 %copy-start.11 = (bf16[3,256]{1,0:T(4,128)(2,1)S(1)}, bf16[3,256]{1,0:T(4,128)(2,1)}, u32[]{:S(2)}) copy-start(bf16[3,256]{1,0:T(4,128)(2,1)} %tmap_ref.1) | copy-start | bytes 4612
  11.3 8.5 %copy-start.12 = (s32[1,1,4]{2,1,0:T(1,128)S(1)}, s32[1,1,4]{2,1,0:T(1,128)}, u32[]{:S(2)}) copy-start(s32[1,1,4]{2,1,0:T(1,128)} %count_hbm.1) | copy-start | bytes 52
  11.3 7.1 %collective-permute-start.3 = (bf16[248,256]{1,0:T(8,128)(2,1)S(1)}, bf16[248,256]{1,0:T(8,128)(2,1)S(1)}, u32[]{:S(2)}, u32[]{:S(2)}) collective-permute-start(bf16[248,256]{1,0:T(8,128)(2,1)S(1)} %pad_maximum_fusion.1), channel_id=1, source_target_pairs={{0,4},{4,0},{8,12},{12,8},{16,20},{20,16},{24,28},{28,24},{32,36},... | collective-permute-start | bytes 380936 | tf_op jit(solution)/shard_map/ppermute | solution.py:483
  15.6 4.1 %collective-permute-start.5 = (bf16[64,256]{1,0:T(8,128)(2,1)S(1)}, bf16[64,256]{1,0:T(8,128)(2,1)S(1)}, u32[]{:S(2)}, u32[]{:S(2)}) collective-permute-start(bf16[64,256]{1,0:T(8,128)(2,1)S(1)} %slice.22), channel_id=1, source_target_pairs={{0,4},{4,0},{8,12},{12,8},{16,20},{20,16},{24,28},{28,24},{32,36},... | collective-permute-start | bytes 98312 | tf_op jit(solution)/shard_map/ppermute | solution.py:486
  22.6 15.0 %copy-start = (f32[3,64,128]{2,1,0:T(8,128)S(1)}, f32[3,64,128]{2,1,0:T(8,128)}, u32[]{:S(2)}) copy-start(f32[3,64,128]{2,1,0:T(8,128)} %disp_ref.3) | copy-start | bytes 294916
  22.6 15.0 %copy-start.7 = (f32[64,128]{1,0:T(8,128)S(1)}, f32[64,128]{1,0:T(8,128)}, u32[]{:S(2)}) copy-start(f32[64,128]{1,0:T(8,128)} %stiff_ref.3) | copy-start | bytes 98308
  22.6 26.4 %all-to-all-start = ((bf16[128,8,128]{2,1,0:T(8,128)(2,1)}), bf16[128,8,128]{2,1,0:T(8,128)(2,1)S(1)}, u32[]{:S(2)}, u32[]{:S(2)}) async-start(bf16[128,8,128]{2,1,0:T(8,128)(2,1)} %bitcast), calls=%async_computation | async-start | bytes 524288 | tf_op jit(solution)/shard_map/all_to_all | solution.py:189
  53.8 2.2 %collective-permute-start.6 = (f32[8,256]{1,0:T(8,128)S(1)}, f32[8,256]{1,0:T(8,128)S(1)}, u32[]{:S(2)}, u32[]{:S(2)}) collective-permute-start(f32[8,256]{1,0:T(8,128)S(1)} %get-tuple-element.22), channel_id=1, source_target_pairs={{0,1},{1,0},{2,3},{3,2},{4,5},{5,4},{6,7},{7,6},{8,9},{9,8},{10,11... | collective-permute-start | bytes 24584 | tf_op jit(solution)/shard_map/ppermute | solution.py:208
  54.3 2.5 %collective-permute-start.7 = (f32[8,256]{1,0:T(8,128)S(1)}, f32[8,256]{1,0:T(8,128)S(1)}, u32[]{:S(2)}, u32[]{:S(2)}) collective-permute-start(f32[8,256]{1,0:T(8,128)S(1)} %get-tuple-element.23), channel_id=1, source_target_pairs={{0,2},{1,3},{2,0},{3,1},{4,6},{5,7},{6,4},{7,5},{8,10},{9,11},{10,... | collective-permute-start | bytes 24584 | tf_op jit(solution)/shard_map/ppermute | solution.py:208
  54.6 3.1 %collective-permute-start.8 = (f32[8,256]{1,0:T(8,128)S(1)}, f32[8,256]{1,0:T(8,128)S(1)}, u32[]{:S(2)}, u32[]{:S(2)}) collective-permute-start(f32[8,256]{1,0:T(8,128)S(1)} %get-tuple-element.24), channel_id=1, source_target_pairs={{0,3},{1,2},{2,1},{3,0},{4,7},{5,6},{6,5},{7,4},{8,11},{9,10},{10,... | collective-permute-start | bytes 24584 | tf_op jit(solution)/shard_map/ppermute | solution.py:208

commit v5 on v4

--- a/solution.py
+++ b/solution.py
@@ -381,7 +381,8 @@
         line_ref[r : r + 1, :] = jnp.where(line > 0.0, line, 1.0)
     line_ref[6:8, :] = jnp.ones((2, 128), F32)
     v_ref[0, 8 : 8 + cols, :] = outer_ref[4 * cols + 8 : head, :].astype(F32)
-    v_ref[7, 8 : 8 + cols, :] = relay_ref[...].astype(F32)
+    beyond = (slab != 1) & (slab != last_slab - 1)
+    v_ref[7, 8 : 8 + cols, :] = relay_ref[...].astype(F32) * beyond.astype(F32)
     for r in range(8):
         v_ref[r] = v_ref[r] * (keep if r < 3 else edge)
     lines = line_ref[...]
@@ -453,7 +454,7 @@
     slabs, owners = lax.axis_size("slab"), lax.axis_size("patch")
     shape = jax.ShapeDtypeStruct
     inner_pairs = [(s, s ^ 1) for s in range(slabs)]
-    outer_pairs = [(s, s + 1) for s in range(1, slabs - 1, 2)]
+    outer_pairs = [(s, (s + 1) % slabs) for s in range(1, slabs, 2)]
     outer_pairs = outer_pairs + [(b, a) for a, b in outer_pairs]
     strip = shape((EDGE + 8, width), BF)
     near, own, to_one, to_three = call(
@@ -476,7 +477,7 @@
         in_specs=hbm(4),
     )
     inner_near = lax.ppermute(near, "slab", inner_pairs)
-    from_three = lax.ppermute(to_three, "patch", [(1, 2), (2, 1)])
+    from_three = lax.ppermute(to_three, "patch", patch_pairs(3))
     from_one = lax.ppermute(to_one, "patch", patch_pairs(1))
     strips = [from_one[:EDGE], from_three[:EDGE]]
     outer = lax.ppermute(jnp.concatenate([own, inner_near] + strips), "slab", outer_pairs)

time: 58.5 us -> 57.6 us (0.985)
  starting transfers between devices: 31.6 us -> 24.4 us
  waiting for transfers between devices: 16.1 us -> 22.4 us
    ppermute x1, starting transfers between devices: 0.8 us -> 7.23 us  [shards(): lax.ppermute(jnp.concatenate([own, inner_near] + strips), 'slab', outer_p...]
    ppermute x1, waiting for transfers between devices: 0.01 us -> 4.85 us  [shards(): lax.ppermute(jnp.concatenate([own, inner_near] + strips), 'slab', outer_p...]
    all_to_all x1, starting transfers between devices: 15 us -> 10.2 us  [exchange_and_relax(): lax.all_to_all(message.reshape(sources, 8, 128), ('slab', 'patch'), 0, 0,...]
    ppermute x1, starting transfers between devices: 4.3 us -> 0.09 us  [shards(): lax.ppermute(jnp.concatenate([own[:cols], own[2 * cols:]] + strips), 'sla...]
    ppermute x1, starting transfers between devices: 2.84 us -> 0.01 us  [shards(): relay = lax.ppermute(outer[:cols], 'slab', inner_pairs)]
    ppermute x1, starting transfers between devices: 3 us -> 1.1 us  [shards(): from_three = lax.ppermute(to_three, 'patch', patch_pairs(3))]
    ppermute x1, waiting for transfers between devices: 1.3 us -> 2.76 us  [shards(): relay = lax.ppermute(outer[:cols], 'slab', inner_pairs)]
  transfers between devices with their start and end apart: 10 -> 10, of which waited for: 5 -> 6; matrix products, arithmetic and copies ran while one was open for 0% -> 0% of each run, Pallas kernels for 0% -> 0%
where the time goes in v5:
time: 57.6 us; the launch traced here: 57.4 us
  starting transfers between devices  24.4 us (42%)
  waiting for transfers between devices  22.4 us (39%)
  Pallas kernels  9.55 us (17%)
  between operations  0.9 us (2%)
    all_to_all x1, waiting for transfers between devices, exchange_and_relax(): lax.all_to_all(message.reshape(sources, 8, 128), ('slab', 'patch'), 0, 0,...  11.1 us
    all_to_all x1, starting transfers between devices, exchange_and_relax(): lax.all_to_all(message.reshape(sources, 8, 128), ('slab', 'patch'), 0, 0,...  10.2 us
    ppermute x1, starting transfers between devices, shards(): lax.ppermute(jnp.concatenate([own, inner_near] + strips), 'slab', outer_p...  7.23 us
    ppermute x1, waiting for transfers between devices, shards(): lax.ppermute(jnp.concatenate([own, inner_near] + strips), 'slab', outer_p...  4.85 us
    pallas_call x1, Pallas kernels, exchange_and_relax(): pl.pallas_call(owner_kernel, out_shape=(jax.ShapeDtypeStruct(displacement...  4.83 us
    pallas_call x3, Pallas kernels, call(): pl.pallas_call(kernel, out_shape=out_shape, in_specs=in_specs or vmem(len...  4.11 us
    ppermute x1, waiting for transfers between devices, shards(): relay = lax.ppermute(outer[:cols], 'slab', inner_pairs)  2.76 us
    ppermute x1, starting transfers between devices, shards(): inner_near = lax.ppermute(near, 'slab', inner_pairs)  2.55 us
  transfers between devices with their start and end apart: 10, of which 6 were waited for; matrix products, arithmetic and copies ran while one was open for 0% of the time, Pallas kernels for 0%

profile of v5, /device:TPU:1, one launch (start us, length us, event | category | flops | bytes accessed | tf_op | source)
XLA Modules:
  0.0 57.4 jit_solution(13649076747929855281)
XLA Ops:
  0.6 1.2 %near.1 = (bf16[64,256]{1,0:T(8,128)(2,1)S(1)}, bf16[264,256]{1,0:T(8,128)(2,1)S(1)}, bf16[32,256]{1,0:T(8,128)(2,1)S(1)}, bf16[32,256]{1,0:T(8,128)(2,1)S(1)}) custom-call(f32[2,64,256]{2,1,0:T(8,128)} %state_ref.1, f32[2,64,256]{2,1,0:T(8,128)} %rhs_ref.1, f32[2,64]{1,0:T(2,128)} %scale_ref.1, f32[3,64,128]{2,1,0:T(8,128)} %disp_ref.3), custom_call_target="tpu_custom_call" | custom-call | tf_op jit(solution)/shard_map/near/pallas_call | solution.py:426
  1.8 2.5 %collective-permute-start = (bf16[64,256]{1,0:T(8,128)(2,1)S(1)}, bf16[64,256]{1,0:T(8,128)(2,1)S(1)}, u32[]{:S(2)}, u32[]{:S(2)}) collective-permute-start(bf16[64,256]{1,0:T(8,128)(2,1)S(1)} %get-tuple-element.14), channel_id=1, source_target_pairs={{0,4},{4,0},{8,12},{12,8},{16,20},{20,16},{24,28},{28,24},{32,36},... | collective-permute-start | bytes 98312 | tf_op jit(solution)/shard_map/ppermute | solution.py:479
  4.4 1.0 %collective-permute-start.1 = (bf16[32,256]{1,0:T(8,128)(2,1)S(1)}, bf16[32,256]{1,0:T(8,128)(2,1)S(1)}, u32[]{:S(2)}, u32[]{:S(2)}) collective-permute-start(bf16[32,256]{1,0:T(8,128)(2,1)S(1)} %get-tuple-element.16), channel_id=1, source_target_pairs={{0,1},{1,0},{2,3},{3,2},{4,5},{5,4},{6,7},{7,6},{8,9},{9,8},{10,11... | collective-permute-start | bytes 49160 | tf_op jit(solution)/shard_map/ppermute | solution.py:481
  5.3 1.1 %collective-permute-start.2 = (bf16[32,256]{1,0:T(8,128)(2,1)S(1)}, bf16[32,256]{1,0:T(8,128)(2,1)S(1)}, u32[]{:S(2)}, u32[]{:S(2)}) collective-permute-start(bf16[32,256]{1,0:T(8,128)(2,1)S(1)} %get-tuple-element.17), channel_id=1, source_target_pairs={{0,3},{1,2},{2,1},{3,0},{4,7},{5,6},{6,5},{7,4},{8,11},{9,10},{10,... | collective-permute-start | bytes 49160 | tf_op jit(solution)/shard_map/ppermute | solution.py:480
  6.4 0.0 collective-permute-done.1.one_ref
  6.5 2.0 %collective-permute-done.2.three_ref = bf16[32,256]{1,0:T(8,128)(2,1)S(1)} collective-permute-done((bf16[32,256]{1,0:T(8,128)(2,1)S(1)}, bf16[32,256]{1,0:T(8,128)(2,1)S(1)}, u32[]{:S(2)}, u32[]{:S(2)}) %collective-permute-start.2) | collective-permute-done | bytes 16416 | tf_op jit(solution)/shard_map/ppermute | solution.py:480
  8.5 0.0 collective-permute-done.near_ref
  8.5 0.0 copy-start.4
  8.5 0.0 copy-start.5
  8.5 0.0 copy-start.1
  8.6 0.0 copy-start.2
  8.6 7.2 %collective-permute-start.4 = (bf16[376,256]{1,0:T(8,128)(2,1)S(1)}, bf16[376,256]{1,0:T(8,128)(2,1)S(1)}, u32[]{:S(2)}, u32[]{:S(2)}) collective-permute-start(bf16[376,256]{1,0:T(8,128)(2,1)S(1)} %pad_maximum_fusion), channel_id=1, source_target_pairs={{4,8},{12,16},{20,24},{28,32},{36,40},{44,48},{52,56},{60,64},{68,... | collective-permute-start | bytes 577544 | tf_op jit(solution)/shard_map/ppermute | solution.py:483
  15.8 0.0 copy-start.8
  15.8 0.0 copy-start.9
  15.8 0.0 copy-start.10
  15.8 0.0 copy-start.11
  15.9 0.0 copy-start.12
  15.9 0.1 collective-permute-start.3
  16.0 4.8 %collective-permute-done.4.outer_ref = bf16[376,256]{1,0:T(8,128)(2,1)S(1)} collective-permute-done((bf16[376,256]{1,0:T(8,128)(2,1)S(1)}, bf16[376,256]{1,0:T(8,128)(2,1)S(1)}, u32[]{:S(2)}, u32[]{:S(2)}) %collective-permute-start.4) | collective-permute-done | bytes 192544 | tf_op jit(solution)/shard_map/ppermute | solution.py:483
  20.8 0.0 collective-permute-start.5
  20.8 0.0 collective-permute-done.3.inner_ref
  20.8 2.8 %collective-permute-done.5.relay_ref = bf16[64,256]{1,0:T(8,128)(2,1)S(1)} collective-permute-done((bf16[64,256]{1,0:T(8,128)(2,1)S(1)}, bf16[64,256]{1,0:T(8,128)(2,1)S(1)}, u32[]{:S(2)}, u32[]{:S(2)}) %collective-permute-start.5) | collective-permute-done | bytes 32800 | tf_op jit(solution)/shard_map/ppermute | solution.py:487
  23.6 0.0 copy-done.6
  23.6 0.0 copy-done.3
  23.6 0.0 copy-done.4
  23.6 0.0 copy-done.5
  23.6 0.0 copy-done.1
  23.6 0.0 copy-done.2
  23.6 0.0 copy-done.8
  23.6 0.0 copy-done.9
  23.6 0.0 copy-done.10
  23.7 0.0 copy-done.11
  23.7 0.0 copy-done.12
  23.7 2.7 %sweep.1 = (f32[2,64,256]{2,1,0:T(8,128)}, bf16[32,4,8,128]{3,2,1,0:T(8,128)(2,1)}) custom-call(f32[2,64,256]{2,1,0:T(8,128)S(1)} %copy-done.1, f32[2,64,256]{2,1,0:T(8,128)S(1)} %copy-done.2, f32[2,64]{1,0:T(2,128)S(1)} %copy-done.10, bf16[64,256]{1,0:T(8,128)(2,1)S(1)} %collective-permute-done.near_ref, ...), custom_call_target="tpu_custom_call" | custom-call | tf_op jit(solution)/shard_map/sweep/pallas_call | solution.py:426
  26.4 0.0 copy-start
  26.4 0.0 copy-start.7
  26.4 10.2 %all-to-all-start = ((bf16[128,8,128]{2,1,0:T(8,128)(2,1)}), bf16[128,8,128]{2,1,0:T(8,128)(2,1)S(1)}, u32[]{:S(2)}, u32[]{:S(2)}) async-start(bf16[128,8,128]{2,1,0:T(8,128)(2,1)} %bitcast), calls=%async_computation | async-start | bytes 524288 | tf_op jit(solution)/shard_map/all_to_all | solution.py:189
  36.6 0.0 copy-done
  36.6 0.3 shell.1.kd_ref
  36.9 11.1 %all-to-all-done.got_ref = bf16[128,8,128]{2,1,0:T(8,128)(2,1)S(1)} async-done(((bf16[128,8,128]{2,1,0:T(8,128)(2,1)}), bf16[128,8,128]{2,1,0:T(8,128)(2,1)S(1)}, u32[]{:S(2)}, u32[]{:S(2)}) %all-to-all-start) | async-done | bytes 262176 | tf_op jit(solution)/shard_map/all_to_all | solution.py:189
  48.0 4.8 %owner.1 = (f32[3,64,128]{2,1,0:T(8,128)}, f32[8,256]{1,0:T(8,128)S(1)}, f32[8,256]{1,0:T(8,128)S(1)}, f32[8,256]{1,0:T(8,128)S(1)}, f32[8,256]{1,0:T(8,128)S(1)}) custom-call(bf16[128,8,128]{2,1,0:T(8,128)(2,1)S(1)} %all-to-all-done.got_ref, f32[3,64,128]{2,1,0:T(8,128)S(1)} %copy-done, f32[64,128]{1,0:T(8,128)S(1)} %copy-done.7, f32[3,64,128]{2,1,0:T(8,128)S(1)} %shell.1.kd_ref), custom_call_target="tpu_custom_call" | custom-call | tf_op jit(solution)/shard_map/owner/pallas_call | solution.py:193
  52.8 0.5 collective-permute-start.6
  53.3 0.3 collective-permute-start.7
  53.6 1.4 %collective-permute-start.8 = (f32[8,256]{1,0:T(8,128)S(1)}, f32[8,256]{1,0:T(8,128)S(1)}, u32[]{:S(2)}, u32[]{:S(2)}) collective-permute-start(f32[8,256]{1,0:T(8,128)S(1)} %get-tuple-element.24), channel_id=1, source_target_pairs={{0,3},{1,2},{2,1},{3,0},{4,7},{5,6},{6,5},{7,4},{8,11},{9,10},{10,... | collective-permute-start | bytes 24584 | tf_op jit(solution)/shard_map/ppermute | solution.py:208
  55.1 0.0 collective-permute-done.6.r1
  55.1 0.8 %collective-permute-done.7.r2 = f32[8,256]{1,0:T(8,128)S(1)} collective-permute-done((f32[8,256]{1,0:T(8,128)S(1)}, f32[8,256]{1,0:T(8,128)S(1)}, u32[]{:S(2)}, u32[]{:S(2)}) %collective-permute-start.7) | collective-permute-done | bytes 8224 | tf_op jit(solution)/shard_map/ppermute | solution.py:208
  55.9 0.9 %collective-permute-done.8.r3 = f32[8,256]{1,0:T(8,128)S(1)} collective-permute-done((f32[8,256]{1,0:T(8,128)S(1)}, f32[8,256]{1,0:T(8,128)S(1)}, u32[]{:S(2)}, u32[]{:S(2)}) %collective-permute-start.8) | collective-permute-done | bytes 8224 | tf_op jit(solution)/shard_map/ppermute | solution.py:208
  56.8 0.6 %finish.1 = f32[3,1,1,1024]{3,2,1,0:T(1,128)} custom-call(f32[8,256]{1,0:T(8,128)S(1)} %get-tuple-element.21.r0, f32[8,256]{1,0:T(8,128)S(1)} %collective-permute-done.6.r1, f32[8,256]{1,0:T(8,128)S(1)} %collective-permute-done.7.r2, f32[8,256]{1,0:T(8,128)S(1)} %collective-permute-done.8.r3), custom_call_target="tpu_custom_call" | custom-call | tf_op jit(solution)/shard_map/finish/pallas_call | solution.py:210
  (10 shorter events, 0.0 us)
Async XLA Ops:
  1.8 6.7 %collective-permute-start = (bf16[64,256]{1,0:T(8,128)(2,1)S(1)}, bf16[64,256]{1,0:T(8,128)(2,1)S(1)}, u32[]{:S(2)}, u32[]{:S(2)}) collective-permute-start(bf16[64,256]{1,0:T(8,128)(2,1)S(1)} %get-tuple-element.14), channel_id=1, source_target_pairs={{0,4},{4,0},{8,12},{12,8},{16,20},{20,16},{24,28},{28,24},{32,36},... | collective-permute-start | bytes 98312 | tf_op jit(solution)/shard_map/ppermute | solution.py:479
  4.4 2.1 %collective-permute-start.1 = (bf16[32,256]{1,0:T(8,128)(2,1)S(1)}, bf16[32,256]{1,0:T(8,128)(2,1)S(1)}, u32[]{:S(2)}, u32[]{:S(2)}) collective-permute-start(bf16[32,256]{1,0:T(8,128)(2,1)S(1)} %get-tuple-element.16), channel_id=1, source_target_pairs={{0,1},{1,0},{2,3},{3,2},{4,5},{5,4},{6,7},{7,6},{8,9},{9,8},{10,11... | collective-permute-start | bytes 49160 | tf_op jit(solution)/shard_map/ppermute | solution.py:481
  5.3 3.2 %collective-permute-start.2 = (bf16[32,256]{1,0:T(8,128)(2,1)S(1)}, bf16[32,256]{1,0:T(8,128)(2,1)S(1)}, u32[]{:S(2)}, u32[]{:S(2)}) collective-permute-start(bf16[32,256]{1,0:T(8,128)(2,1)S(1)} %get-tuple-element.17), channel_id=1, source_target_pairs={{0,3},{1,2},{2,1},{3,0},{4,7},{5,6},{6,5},{7,4},{8,11},{9,10},{10,... | collective-permute-start | bytes 49160 | tf_op jit(solution)/shard_map/ppermute | solution.py:480
  6.4 17.2 %copy-start.6 = (bf16[256,256]{1,0:T(8,128)(2,1)S(1)}, bf16[256,256]{1,0:T(8,128)(2,1)}, u32[]{:S(2)}) copy-start(bf16[256,256]{1,0:T(8,128)(2,1)} %inverse_ref.1) | copy-start | bytes 393220
  8.5 15.1 %copy-start.3 = (bf16[256,256]{1,0:T(8,128)(2,1)S(1)}, bf16[256,256]{1,0:T(8,128)(2,1)}, u32[]{:S(2)}) copy-start(bf16[256,256]{1,0:T(8,128)(2,1)} %matrix_ref.1) | copy-start | bytes 393220
  8.5 15.1 %copy-start.4 = (bf16[256,256]{1,0:T(8,128)(2,1)S(1)}, bf16[256,256]{1,0:T(8,128)(2,1)}, u32[]{:S(2)}) copy-start(bf16[256,256]{1,0:T(8,128)(2,1)} %x_ref.1) | copy-start | bytes 393220
  8.5 15.1 %copy-start.5 = (bf16[256,256]{1,0:T(8,128)(2,1)S(1)}, bf16[256,256]{1,0:T(8,128)(2,1)}, u32[]{:S(2)}) copy-start(bf16[256,256]{1,0:T(8,128)(2,1)} %y_ref.1) | copy-start | bytes 393220
  8.5 15.1 %copy-start.1 = (f32[2,64,256]{2,1,0:T(8,128)S(1)}, f32[2,64,256]{2,1,0:T(8,128)}, u32[]{:S(2)}) copy-start(f32[2,64,256]{2,1,0:T(8,128)} %state_ref.1) | copy-start | bytes 393220
  8.6 15.1 %copy-start.2 = (f32[2,64,256]{2,1,0:T(8,128)S(1)}, f32[2,64,256]{2,1,0:T(8,128)}, u32[]{:S(2)}) copy-start(f32[2,64,256]{2,1,0:T(8,128)} %rhs_ref.1) | copy-start | bytes 393220
  8.6 12.2 %collective-permute-start.4 = (bf16[376,256]{1,0:T(8,128)(2,1)S(1)}, bf16[376,256]{1,0:T(8,128)(2,1)S(1)}, u32[]{:S(2)}, u32[]{:S(2)}) collective-permute-start(bf16[376,256]{1,0:T(8,128)(2,1)S(1)} %pad_maximum_fusion), channel_id=1, source_target_pairs={{4,8},{12,16},{20,24},{28,32},{36,40},{44,48},{52,56},{60,64},{68,... | collective-permute-start | bytes 577544 | tf_op jit(solution)/shard_map/ppermute | solution.py:483
  15.8 7.8 %copy-start.8 = (s32[1,1,1024]{2,1,0:T(1,128)S(1)}, s32[1,1,1024]{2,1,0:T(1,128)}, u32[]{:S(2)}) copy-start(s32[1,1,1024]{2,1,0:T(1,128)} %elem_hbm.1) | copy-start | bytes 12292
  15.8 7.8 %copy-start.9 = (s32[1,1,1024]{2,1,0:T(1,128)S(1)}, s32[1,1,1024]{2,1,0:T(1,128)}, u32[]{:S(2)}) copy-start(s32[1,1,1024]{2,1,0:T(1,128)} %point_hbm.1) | copy-start | bytes 12292
  15.8 7.8 %copy-start.10 = (f32[2,64]{1,0:T(2,128)S(1)}, f32[2,64]{1,0:T(2,128)}, u32[]{:S(2)}) copy-start(f32[2,64]{1,0:T(2,128)} %scale_ref.1) | copy-start | bytes 1540
  15.8 7.8 %copy-start.11 = (bf16[3,256]{1,0:T(4,128)(2,1)S(1)}, bf16[3,256]{1,0:T(4,128)(2,1)}, u32[]{:S(2)}) copy-start(bf16[3,256]{1,0:T(4,128)(2,1)} %tmap_ref.1) | copy-start | bytes 4612
  15.9 7.8 %copy-start.12 = (s32[1,1,4]{2,1,0:T(1,128)S(1)}, s32[1,1,4]{2,1,0:T(1,128)}, u32[]{:S(2)}) copy-start(s32[1,1,4]{2,1,0:T(1,128)} %count_hbm.1) | copy-start | bytes 52
  15.9 5.0 %collective-permute-start.3 = (bf16[248,256]{1,0:T(8,128)(2,1)S(1)}, bf16[248,256]{1,0:T(8,128)(2,1)S(1)}, u32[]{:S(2)}, u32[]{:S(2)}) collective-permute-start(bf16[248,256]{1,0:T(8,128)(2,1)S(1)} %pad_maximum_fusion.1), channel_id=1, source_target_pairs={{0,4},{4,0},{8,12},{12,8},{16,20},{20,16},{24,28},{28,24},{32,36},... | collective-permute-start | bytes 380936 | tf_op jit(solution)/shard_map/ppermute | solution.py:484
  20.8 2.8 %collective-permute-start.5 = (bf16[64,256]{1,0:T(8,128)(2,1)S(1)}, bf16[64,256]{1,0:T(8,128)(2,1)S(1)}, u32[]{:S(2)}, u32[]{:S(2)}) collective-permute-start(bf16[64,256]{1,0:T(8,128)(2,1)S(1)} %slice.22), channel_id=1, source_target_pairs={{0,4},{4,0},{8,12},{12,8},{16,20},{20,16},{24,28},{28,24},{32,36},... | collective-permute-start | bytes 98312 | tf_op jit(solution)/shard_map/ppermute | solution.py:487
  26.4 10.3 %copy-start = (f32[3,64,128]{2,1,0:T(8,128)S(1)}, f32[3,64,128]{2,1,0:T(8,128)}, u32[]{:S(2)}) copy-start(f32[3,64,128]{2,1,0:T(8,128)} %disp_ref.3) | copy-start | bytes 294916
  26.4 10.3 %copy-start.7 = (f32[64,128]{1,0:T(8,128)S(1)}, f32[64,128]{1,0:T(8,128)}, u32[]{:S(2)}) copy-start(f32[64,128]{1,0:T(8,128)} %stiff_ref.3) | copy-start | bytes 98308
  26.4 21.6 %all-to-all-start = ((bf16[128,8,128]{2,1,0:T(8,128)(2,1)}), bf16[128,8,128]{2,1,0:T(8,128)(2,1)S(1)}, u32[]{:S(2)}, u32[]{:S(2)}) async-start(bf16[128,8,128]{2,1,0:T(8,128)(2,1)} %bitcast), calls=%async_computation | async-start | bytes 524288 | tf_op jit(solution)/shard_map/all_to_all | solution.py:189
  52.8 2.2 %collective-permute-start.6 = (f32[8,256]{1,0:T(8,128)S(1)}, f32[8,256]{1,0:T(8,128)S(1)}, u32[]{:S(2)}, u32[]{:S(2)}) collective-permute-start(f32[8,256]{1,0:T(8,128)S(1)} %get-tuple-element.22), channel_id=1, source_target_pairs={{0,1},{1,0},{2,3},{3,2},{4,5},{5,4},{6,7},{7,6},{8,9},{9,8},{10,11... | collective-permute-start | bytes 24584 | tf_op jit(solution)/shard_map/ppermute | solution.py:208
  53.3 2.5 %collective-permute-start.7 = (f32[8,256]{1,0:T(8,128)S(1)}, f32[8,256]{1,0:T(8,128)S(1)}, u32[]{:S(2)}, u32[]{:S(2)}) collective-permute-start(f32[8,256]{1,0:T(8,128)S(1)} %get-tuple-element.23), channel_id=1, source_target_pairs={{0,2},{1,3},{2,0},{3,1},{4,6},{5,7},{6,4},{7,5},{8,10},{9,11},{10,... | collective-permute-start | bytes 24584 | tf_op jit(solution)/shard_map/ppermute | solution.py:208
  53.6 3.1 %collective-permute-start.8 = (f32[8,256]{1,0:T(8,128)S(1)}, f32[8,256]{1,0:T(8,128)S(1)}, u32[]{:S(2)}, u32[]{:S(2)}) collective-permute-start(f32[8,256]{1,0:T(8,128)S(1)} %get-tuple-element.24), channel_id=1, source_target_pairs={{0,3},{1,2},{2,1},{3,0},{4,7},{5,6},{6,5},{7,4},{8,11},{9,10},{10,... | collective-permute-start | bytes 24584 | tf_op jit(solution)/shard_map/ppermute | solution.py:208

commit v6 on v5

--- a/solution.py
+++ b/solution.py
@@ -66,7 +66,7 @@
 
 
 def owner_kernel(
-    got_ref, disp_ref, stiff_ref, kd_ref, new_ref, r0, r1, r2, r3, row_ref, lane_ref, hold_ref, sem
+    got_ref, disp_ref, stiff_ref, kd_ref, new_ref, r0, r1, r2, r3, row_ref, lane_ref
 ):
     replies = (r0, r1, r2, r3)
     sources = got_ref.shape[0]
@@ -101,9 +101,7 @@
             total += nt(jnp.concatenate(left, axis=1), jnp.concatenate(right, axis=1))
     loads = total.reshape(3, rows, 128)
     new = disp_ref[...] + (loads - kd_ref[...]) / (36.0 * stiff_ref[...])[None]
-    hold_ref[...] = new
-    out = pltpu.make_async_copy(hold_ref, new_ref, sem)
-    out.start()
+    new_ref[...] = new
     flat = new.reshape(3 * rows, 128)
     high = flat.astype(BF)
     low = (flat - high.astype(F32)).astype(BF)
@@ -120,7 +118,24 @@
             for c in range(3):
                 part = jnp.where(mask, picked[c * rows : (c + 1) * rows], 0.0)
                 replies[d][c : c + 1, h * 128 : (h + 1) * 128] = part.sum(axis=0, keepdims=True)
-    out.wait()
+
+
+def store_kernel(value_ref, out_ref, sem):
+    copy = pltpu.make_async_copy(value_ref, out_ref, sem)
+    copy.start()
+    copy.wait()
+
+
+def store(value, name):
+    return pl.pallas_call(
+        store_kernel,
+        out_shape=jax.ShapeDtypeStruct(value.shape, value.dtype),
+        in_specs=vmem(1),
+        out_specs=hbm(1)[0],
+        scratch_shapes=[pltpu.SemaphoreType.DMA],
+        compiler_params=params(),
+        name=name,
+    )(value)
 
 
 def finish_kernel(r0, r1, r2, r3, out_ref):
@@ -132,7 +147,11 @@
             out_ref[c, 0, :, pl.ds(start, cap)] = reply[c : c + 1, :]
 
 
-def shell_kernel(one_ref, three_ref, disp_ref, stiff_ref, kd_ref, field_ref, bend_ref):
+def shell_kernel(
+    one_ref, three_ref, disp_ref, stiff_ref, state_ref, kd_ref, out_ref, field_ref, bend_ref, sem
+):
+    copy = pltpu.make_async_copy(state_ref, out_ref, sem)
+    copy.start()
     rows = disp_ref.shape[1]
     patch = lax.axis_index("patch")
     top = patch > 0
@@ -172,6 +191,7 @@
         bend_ref[:, 7 : 7 + rows, :] + bend_ref[:, 9 : 9 + rows, :] + sides(mid)
     )
     kd_ref[...] = stiff_ref[...][None] * (again + 4.0 * mid)
+    copy.wait()
 
 
 def params():
@@ -194,12 +214,10 @@
         owner_kernel,
         out_shape=(jax.ShapeDtypeStruct(displacement.shape, F32),) + (reply,) * 4,
         in_specs=vmem(4),
-        out_specs=hbm(1) + vmem(4),
+        out_specs=vmem(5),
         scratch_shapes=[
             pltpu.VMEM((2, sources, 128), F32),
             pltpu.VMEM((2, sources, 128), F32),
-            pltpu.VMEM((3, rows, 128), F32),
-            pltpu.SemaphoreType.DMA,
         ],
         compiler_params=params(),
         name="owner",
@@ -215,7 +233,7 @@
         compiler_params=params(),
         name="finish",
     )(*back)
-    return new, wall
+    return store(new, "store_shell"), wall
 
 
 def halves(value):
@@ -299,8 +317,8 @@
     elem_hbm,
     point_hbm,
     count_hbm,
-    out_hbm,
-    message_ref,
+    out_ref,
+    message_hbm,
     v_ref,
     r_ref,
     s_ref,
@@ -310,7 +328,7 @@
     elem_ref,
     point_ref,
     count_ref,
-    out_ref,
+    message_ref,
     sems,
 ):
     copies = [
@@ -412,14 +430,20 @@
             v_ref[a + j] = value[j] * (keep if a + j < 3 else edge)
     out_ref[odd] = v_ref[3, 8 : 8 + cols, :]
     out_ref[1 - odd] = v_ref[4, 8 : 8 + cols, :]
-    out = pltpu.make_async_copy(out_ref, out_hbm, sems.at[3])
-    out.start()
     final = out_ref[...].astype(BF).reshape(2 * cols, width)
     for copy in copies:
         copy.wait()
     slot_rows(final, tmap_ref[...], elem_ref[0], point_ref[0], count_ref.at[0], rows_ref)
     message_ref[...] = jnp.broadcast_to(rows_ref[...].astype(BF)[None], message_ref.shape)
-    out.wait()
+    part = message_ref.shape[0]
+    copies = [
+        pltpu.make_async_copy(message_ref, message_hbm.at[i * part : (i + 1) * part], sems.at[3 + i])
+        for i in range(message_hbm.shape[0] // part)
+    ]
+    for copy in copies:
+        copy.start()
+    for copy in copies:
+        copy.wait()
 
 
 def call(kernel, name, out_shape, operands, scratch=(), in_specs=None, out_specs=None):
@@ -519,21 +543,22 @@
             pltpu.VMEM((1, 1, slots), I32),
             pltpu.VMEM((1, 1, slots), I32),
             pltpu.VMEM((1, 1, owners), I32),
-            pltpu.VMEM(fluid_state.shape, F32),
-            pltpu.SemaphoreType.DMA((4,)),
+            pltpu.VMEM((slabs // 4, owners, 8, 128), BF),
+            pltpu.SemaphoreType.DMA((7,)),
         ],
         in_specs=vmem(14) + hbm(3),
-        out_specs=tuple(hbm(1) + vmem(1)),
-    )
-    kd = call(
+        out_specs=tuple(vmem(1) + hbm(1)),
+    )
+    kd, final = call(
         shell_kernel,
         "shell",
-        shape(displacement.shape, F32),
-        (from_one, from_three, displacement, stiffness),
-        [pltpu.VMEM((3, displacement.shape[1] + 16, 128), F32)] * 2,
+        (shape(displacement.shape, F32), shape(state.shape, F32)),
+        (from_one, from_three, displacement, stiffness, state),
+        [pltpu.VMEM((3, displacement.shape[1] + 16, 128), F32)] * 2 + [pltpu.SemaphoreType.DMA],
+        out_specs=tuple(vmem(1) + hbm(1)),
     )
     new, wall = exchange_and_relax(message, displacement, stiffness, kd)
-    return state, new, wall
+    return final, new, wall
 
 
 def solution(mesh):

time: 57.6 us -> 56.8 us (0.986)
  waiting for transfers between devices: 22.4 us -> 21.4 us
    ppermute x3, waiting for transfers between devices: 1.71 us -> 1.04 us  [exchange_and_relax(): lax.ppermute(replies[d], 'patch', patch_pairs(d))]
    pallas_call x0 -> x1, Pallas kernels: none -> 0.65 us  [store(): pl.pallas_call(store_kernel, out_shape=jax.ShapeDtypeStruct(value.shape,...]
  transfers between devices with their start and end apart: 10 -> 10, of which waited for: 6 -> 6; matrix products, arithmetic and copies ran while one was open for 0% -> 0% of each run, Pallas kernels for 0% -> 2%
where the time goes in v6:
time: 56.8 us; the launch traced here: 56.6 us
  starting transfers between devices  24.4 us (43%)
  waiting for transfers between devices  21.4 us (38%)
  Pallas kernels  9.84 us (17%)
  between operations  0.9 us (2%)
    all_to_all x1, waiting for transfers between devices, exchange_and_relax(): lax.all_to_all(message.reshape(sources, 8, 128), ('slab', 'patch'), 0, 0,...  10.7 us
    all_to_all x1, starting transfers between devices, exchange_and_relax(): lax.all_to_all(message.reshape(sources, 8, 128), ('slab', 'patch'), 0, 0,...  10.2 us
    ppermute x1, starting transfers between devices, shards(): lax.ppermute(jnp.concatenate([own, inner_near] + strips), 'slab', outer_p...  7.23 us
    ppermute x1, waiting for transfers between devices, shards(): lax.ppermute(jnp.concatenate([own, inner_near] + strips), 'slab', outer_p...  4.85 us
    pallas_call x1, Pallas kernels, exchange_and_relax(): pl.pallas_call(owner_kernel, out_shape=(jax.ShapeDtypeStruct(displacement...  4.4 us
    pallas_call x3, Pallas kernels, call(): pl.pallas_call(kernel, out_shape=out_shape, in_specs=in_specs or vmem(len...  4.18 us
    ppermute x1, waiting for transfers between devices, shards(): relay = lax.ppermute(outer[:cols], 'slab', inner_pairs)  2.76 us
    ppermute x1, starting transfers between devices, shards(): inner_near = lax.ppermute(near, 'slab', inner_pairs)  2.55 us
  transfers between devices with their start and end apart: 10, of which 6 were waited for; matrix products, arithmetic and copies ran while one was open for 0% of the time, Pallas kernels for 2%

profile of v6, /device:TPU:1, one launch (start us, length us, event | category | flops | bytes accessed | tf_op | source)
XLA Modules:
  0.0 56.6 jit_solution(6592796294849033257)
XLA Ops:
  0.6 1.2 %near.1 = (bf16[64,256]{1,0:T(8,128)(2,1)S(1)}, bf16[264,256]{1,0:T(8,128)(2,1)S(1)}, bf16[32,256]{1,0:T(8,128)(2,1)S(1)}, bf16[32,256]{1,0:T(8,128)(2,1)S(1)}) custom-call(f32[2,64,256]{2,1,0:T(8,128)} %state_ref.1, f32[2,64,256]{2,1,0:T(8,128)} %rhs_ref.1, f32[2,64]{1,0:T(2,128)} %scale_ref.1, f32[3,64,128]{2,1,0:T(8,128)} %disp_ref.3), custom_call_target="tpu_custom_call" | custom-call | tf_op jit(solution)/shard_map/near/pallas_call | solution.py:450
  1.8 2.5 %collective-permute-start.2 = (bf16[64,256]{1,0:T(8,128)(2,1)S(1)}, bf16[64,256]{1,0:T(8,128)(2,1)S(1)}, u32[]{:S(2)}, u32[]{:S(2)}) collective-permute-start(bf16[64,256]{1,0:T(8,128)(2,1)S(1)} %get-tuple-element.18), channel_id=1, source_target_pairs={{0,4},{4,0},{8,12},{12,8},{16,20},{20,16},{24,28},{28,24},{32,36},... | collective-permute-start | bytes 98312 | tf_op jit(solution)/shard_map/ppermute | solution.py:503
  4.4 1.0 %collective-permute-start = (bf16[32,256]{1,0:T(8,128)(2,1)S(1)}, bf16[32,256]{1,0:T(8,128)(2,1)S(1)}, u32[]{:S(2)}, u32[]{:S(2)}) collective-permute-start(bf16[32,256]{1,0:T(8,128)(2,1)S(1)} %get-tuple-element.16), channel_id=1, source_target_pairs={{0,1},{1,0},{2,3},{3,2},{4,5},{5,4},{6,7},{7,6},{8,9},{9,8},{10,11... | collective-permute-start | bytes 49160 | tf_op jit(solution)/shard_map/ppermute | solution.py:505
  5.3 1.1 %collective-permute-start.1 = (bf16[32,256]{1,0:T(8,128)(2,1)S(1)}, bf16[32,256]{1,0:T(8,128)(2,1)S(1)}, u32[]{:S(2)}, u32[]{:S(2)}) collective-permute-start(bf16[32,256]{1,0:T(8,128)(2,1)S(1)} %get-tuple-element.17), channel_id=1, source_target_pairs={{0,3},{1,2},{2,1},{3,0},{4,7},{5,6},{6,5},{7,4},{8,11},{9,10},{10,... | collective-permute-start | bytes 49160 | tf_op jit(solution)/shard_map/ppermute | solution.py:504
  6.4 0.0 collective-permute-done.one_ref
  6.5 2.0 %collective-permute-done.1.three_ref = bf16[32,256]{1,0:T(8,128)(2,1)S(1)} collective-permute-done((bf16[32,256]{1,0:T(8,128)(2,1)S(1)}, bf16[32,256]{1,0:T(8,128)(2,1)S(1)}, u32[]{:S(2)}, u32[]{:S(2)}) %collective-permute-start.1) | collective-permute-done | bytes 16416 | tf_op jit(solution)/shard_map/ppermute | solution.py:504
  8.5 0.0 collective-permute-done.2.near_ref
  8.5 0.0 copy-start.4
  8.5 0.0 copy-start.5
  8.5 0.0 copy-start.1
  8.6 0.0 copy-start.2
  8.6 7.2 %collective-permute-start.4 = (bf16[376,256]{1,0:T(8,128)(2,1)S(1)}, bf16[376,256]{1,0:T(8,128)(2,1)S(1)}, u32[]{:S(2)}, u32[]{:S(2)}) collective-permute-start(bf16[376,256]{1,0:T(8,128)(2,1)S(1)} %pad_maximum_fusion), channel_id=1, source_target_pairs={{4,8},{12,16},{20,24},{28,32},{36,40},{44,48},{52,56},{60,64},{68,... | collective-permute-start | bytes 577544 | tf_op jit(solution)/shard_map/ppermute | solution.py:507
  15.8 0.0 copy-start.8
  15.8 0.0 copy-start.9
  15.8 0.0 copy-start.10
  15.8 0.0 copy-start.11
  15.9 0.0 copy-start.12
  15.9 0.1 collective-permute-start.3
  16.0 4.8 %collective-permute-done.4.outer_ref = bf16[376,256]{1,0:T(8,128)(2,1)S(1)} collective-permute-done((bf16[376,256]{1,0:T(8,128)(2,1)S(1)}, bf16[376,256]{1,0:T(8,128)(2,1)S(1)}, u32[]{:S(2)}, u32[]{:S(2)}) %collective-permute-start.4) | collective-permute-done | bytes 192544 | tf_op jit(solution)/shard_map/ppermute | solution.py:507
  20.8 0.0 collective-permute-start.5
  20.8 0.0 collective-permute-done.3.inner_ref
  20.8 2.8 %collective-permute-done.5.relay_ref = bf16[64,256]{1,0:T(8,128)(2,1)S(1)} collective-permute-done((bf16[64,256]{1,0:T(8,128)(2,1)S(1)}, bf16[64,256]{1,0:T(8,128)(2,1)S(1)}, u32[]{:S(2)}, u32[]{:S(2)}) %collective-permute-start.5) | collective-permute-done | bytes 32800 | tf_op jit(solution)/shard_map/ppermute | solution.py:511
  23.6 0.0 copy-done.6
  23.6 0.0 copy-done.5
  23.6 0.0 copy-done.1
  23.6 0.0 copy-done.2
  23.6 0.0 copy-done.8
  23.6 0.0 copy-done.9
  23.6 0.0 copy-done.10
  23.7 0.0 copy-done.11
  23.7 0.0 copy-done.12
  23.7 2.3 %sweep.1 = (f32[2,64,256]{2,1,0:T(8,128)S(1)}, bf16[32,4,8,128]{3,2,1,0:T(8,128)(2,1)}) custom-call(f32[2,64,256]{2,1,0:T(8,128)S(1)} %copy-done.1, f32[2,64,256]{2,1,0:T(8,128)S(1)} %copy-done.2, f32[2,64]{1,0:T(2,128)S(1)} %copy-done.10, bf16[64,256]{1,0:T(8,128)(2,1)S(1)} %collective-permute-done.2.near_ref, ...), custom_call_target="tpu_custom_call" | custom-call | tf_op jit(solution)/shard_map/sweep/pallas_call | solution.py:450
  26.0 0.0 copy-start
  26.0 0.0 copy-start.7
  26.0 10.2 %all-to-all-start = ((bf16[128,8,128]{2,1,0:T(8,128)(2,1)}), bf16[128,8,128]{2,1,0:T(8,128)(2,1)S(1)}, u32[]{:S(2)}, u32[]{:S(2)}) async-start(bf16[128,8,128]{2,1,0:T(8,128)(2,1)} %bitcast), calls=%async_computation | async-start | bytes 524288 | tf_op jit(solution)/shard_map/all_to_all | solution.py:209
  36.3 0.0 copy-done
  36.3 0.0 copy-done.7
  36.3 0.7 %shell.1 = (f32[3,64,128]{2,1,0:T(8,128)S(1)}, f32[2,64,256]{2,1,0:T(8,128)}) custom-call(bf16[32,256]{1,0:T(8,128)(2,1)S(1)} %collective-permute-done.one_ref, bf16[32,256]{1,0:T(8,128)(2,1)S(1)} %collective-permute-done.1.three_ref, f32[3,64,128]{2,1,0:T(8,128)S(1)} %copy-done, f32[64,128]{1,0:T(8,128)S(1)} %copy-done.7, ...), custom_call_target="tpu_custom_call" | custom-call | tf_op jit(solution)/shard_map/shell/pallas_call | solution.py:450
  37.0 10.7 %all-to-all-done.got_ref = bf16[128,8,128]{2,1,0:T(8,128)(2,1)S(1)} async-done(((bf16[128,8,128]{2,1,0:T(8,128)(2,1)}), bf16[128,8,128]{2,1,0:T(8,128)(2,1)S(1)}, u32[]{:S(2)}, u32[]{:S(2)}) %all-to-all-start) | async-done | bytes 262176 | tf_op jit(solution)/shard_map/all_to_all | solution.py:209
  47.7 4.4 %owner.1 = (f32[3,64,128]{2,1,0:T(8,128)S(1)}, f32[8,256]{1,0:T(8,128)S(1)}, f32[8,256]{1,0:T(8,128)S(1)}, f32[8,256]{1,0:T(8,128)S(1)}, f32[8,256]{1,0:T(8,128)S(1)}) custom-call(bf16[128,8,128]{2,1,0:T(8,128)(2,1)S(1)} %all-to-all-done.got_ref, f32[3,64,128]{2,1,0:T(8,128)S(1)} %copy-done, f32[64,128]{1,0:T(8,128)S(1)} %copy-done.7, ...), custom_call_target="tpu_custom_call" | custom-call | tf_op jit(solution)/shard_map/owner/pallas_call | solution.py:213
  52.1 0.5 collective-permute-start.6
  52.6 0.3 collective-permute-start.7
  52.9 1.4 %collective-permute-start.8 = (f32[8,256]{1,0:T(8,128)S(1)}, f32[8,256]{1,0:T(8,128)S(1)}, u32[]{:S(2)}, u32[]{:S(2)}) collective-permute-start(f32[8,256]{1,0:T(8,128)S(1)} %get-tuple-element.28), channel_id=1, source_target_pairs={{0,3},{1,2},{2,1},{3,0},{4,7},{5,6},{6,5},{7,4},{8,11},{9,10},{10,... | collective-permute-start | bytes 24584 | tf_op jit(solution)/shard_map/ppermute | solution.py:226
  54.3 0.6 %store_shell.1 = f32[3,64,128]{2,1,0:T(8,128)} custom-call(f32[3,64,128]{2,1,0:T(8,128)S(1)} %get-tuple-element.24.value_ref), custom_call_target="tpu_custom_call" | custom-call | tf_op jit(solution)/shard_map/store_shell/pallas_call | solution.py:130
  55.0 0.0 collective-permute-done.6.r1
  55.0 0.1 collective-permute-done.7.r2
  55.1 0.9 %collective-permute-done.8.r3 = f32[8,256]{1,0:T(8,128)S(1)} collective-permute-done((f32[8,256]{1,0:T(8,128)S(1)}, f32[8,256]{1,0:T(8,128)S(1)}, u32[]{:S(2)}, u32[]{:S(2)}) %collective-permute-start.8) | collective-permute-done | bytes 8224 | tf_op jit(solution)/shard_map/ppermute | solution.py:226
  56.0 0.6 %finish.1 = f32[3,1,1,1024]{3,2,1,0:T(1,128)} custom-call(f32[8,256]{1,0:T(8,128)S(1)} %get-tuple-element.25.r0, f32[8,256]{1,0:T(8,128)S(1)} %collective-permute-done.6.r1, f32[8,256]{1,0:T(8,128)S(1)} %collective-permute-done.7.r2, f32[8,256]{1,0:T(8,128)S(1)} %collective-permute-done.8.r3), custom_call_target="tpu_custom_call" | custom-call | tf_op jit(solution)/shard_map/finish/pallas_call | solution.py:228
  (11 shorter events, 0.0 us)
Async XLA Ops:
  1.8 6.7 %collective-permute-start.2 = (bf16[64,256]{1,0:T(8,128)(2,1)S(1)}, bf16[64,256]{1,0:T(8,128)(2,1)S(1)}, u32[]{:S(2)}, u32[]{:S(2)}) collective-permute-start(bf16[64,256]{1,0:T(8,128)(2,1)S(1)} %get-tuple-element.18), channel_id=1, source_target_pairs={{0,4},{4,0},{8,12},{12,8},{16,20},{20,16},{24,28},{28,24},{32,36},... | collective-permute-start | bytes 98312 | tf_op jit(solution)/shard_map/ppermute | solution.py:503
  4.4 2.1 %collective-permute-start = (bf16[32,256]{1,0:T(8,128)(2,1)S(1)}, bf16[32,256]{1,0:T(8,128)(2,1)S(1)}, u32[]{:S(2)}, u32[]{:S(2)}) collective-permute-start(bf16[32,256]{1,0:T(8,128)(2,1)S(1)} %get-tuple-element.16), channel_id=1, source_target_pairs={{0,1},{1,0},{2,3},{3,2},{4,5},{5,4},{6,7},{7,6},{8,9},{9,8},{10,11... | collective-permute-start | bytes 49160 | tf_op jit(solution)/shard_map/ppermute | solution.py:505
  5.3 3.2 %collective-permute-start.1 = (bf16[32,256]{1,0:T(8,128)(2,1)S(1)}, bf16[32,256]{1,0:T(8,128)(2,1)S(1)}, u32[]{:S(2)}, u32[]{:S(2)}) collective-permute-start(bf16[32,256]{1,0:T(8,128)(2,1)S(1)} %get-tuple-element.17), channel_id=1, source_target_pairs={{0,3},{1,2},{2,1},{3,0},{4,7},{5,6},{6,5},{7,4},{8,11},{9,10},{10,... | collective-permute-start | bytes 49160 | tf_op jit(solution)/shard_map/ppermute | solution.py:504
  6.4 17.2 %copy-start.6 = (bf16[256,256]{1,0:T(8,128)(2,1)S(1)}, bf16[256,256]{1,0:T(8,128)(2,1)}, u32[]{:S(2)}) copy-start(bf16[256,256]{1,0:T(8,128)(2,1)} %inverse_ref.1) | copy-start | bytes 393220
  8.5 15.1 %copy-start.3 = (bf16[256,256]{1,0:T(8,128)(2,1)S(1)}, bf16[256,256]{1,0:T(8,128)(2,1)}, u32[]{:S(2)}) copy-start(bf16[256,256]{1,0:T(8,128)(2,1)} %matrix_ref.1) | copy-start | bytes 393220
  8.5 15.1 %copy-start.4 = (bf16[256,256]{1,0:T(8,128)(2,1)S(1)}, bf16[256,256]{1,0:T(8,128)(2,1)}, u32[]{:S(2)}) copy-start(bf16[256,256]{1,0:T(8,128)(2,1)} %x_ref.1) | copy-start | bytes 393220
  8.5 15.1 %copy-start.5 = (bf16[256,256]{1,0:T(8,128)(2,1)S(1)}, bf16[256,256]{1,0:T(8,128)(2,1)}, u32[]{:S(2)}) copy-start(bf16[256,256]{1,0:T(8,128)(2,1)} %y_ref.1) | copy-start | bytes 393220
  8.5 15.1 %copy-start.1 = (f32[2,64,256]{2,1,0:T(8,128)S(1)}, f32[2,64,256]{2,1,0:T(8,128)}, u32[]{:S(2)}) copy-start(f32[2,64,256]{2,1,0:T(8,128)} %state_ref.1) | copy-start | bytes 393220
  8.6 15.1 %copy-start.2 = (f32[2,64,256]{2,1,0:T(8,128)S(1)}, f32[2,64,256]{2,1,0:T(8,128)}, u32[]{:S(2)}) copy-start(f32[2,64,256]{2,1,0:T(8,128)} %rhs_ref.1) | copy-start | bytes 393220
  8.6 12.2 %collective-permute-start.4 = (bf16[376,256]{1,0:T(8,128)(2,1)S(1)}, bf16[376,256]{1,0:T(8,128)(2,1)S(1)}, u32[]{:S(2)}, u32[]{:S(2)}) collective-permute-start(bf16[376,256]{1,0:T(8,128)(2,1)S(1)} %pad_maximum_fusion), channel_id=1, source_target_pairs={{4,8},{12,16},{20,24},{28,32},{36,40},{44,48},{52,56},{60,64},{68,... | collective-permute-start | bytes 577544 | tf_op jit(solution)/shard_map/ppermute | solution.py:507
  15.8 7.8 %copy-start.8 = (s32[1,1,1024]{2,1,0:T(1,128)S(1)}, s32[1,1,1024]{2,1,0:T(1,128)}, u32[]{:S(2)}) copy-start(s32[1,1,1024]{2,1,0:T(1,128)} %elem_hbm.1) | copy-start | bytes 12292
  15.8 7.8 %copy-start.9 = (s32[1,1,1024]{2,1,0:T(1,128)S(1)}, s32[1,1,1024]{2,1,0:T(1,128)}, u32[]{:S(2)}) copy-start(s32[1,1,1024]{2,1,0:T(1,128)} %point_hbm.1) | copy-start | bytes 12292
  15.8 7.8 %copy-start.10 = (f32[2,64]{1,0:T(2,128)S(1)}, f32[2,64]{1,0:T(2,128)}, u32[]{:S(2)}) copy-start(f32[2,64]{1,0:T(2,128)} %scale_ref.1) | copy-start | bytes 1540
  15.8 7.8 %copy-start.11 = (bf16[3,256]{1,0:T(4,128)(2,1)S(1)}, bf16[3,256]{1,0:T(4,128)(2,1)}, u32[]{:S(2)}) copy-start(bf16[3,256]{1,0:T(4,128)(2,1)} %tmap_ref.1) | copy-start | bytes 4612
  15.9 7.8 %copy-start.12 = (s32[1,1,4]{2,1,0:T(1,128)S(1)}, s32[1,1,4]{2,1,0:T(1,128)}, u32[]{:S(2)}) copy-start(s32[1,1,4]{2,1,0:T(1,128)} %count_hbm.1) | copy-start | bytes 52
  15.9 5.0 %collective-permute-start.3 = (bf16[248,256]{1,0:T(8,128)(2,1)S(1)}, bf16[248,256]{1,0:T(8,128)(2,1)S(1)}, u32[]{:S(2)}, u32[]{:S(2)}) collective-permute-start(bf16[248,256]{1,0:T(8,128)(2,1)S(1)} %pad_maximum_fusion.1), channel_id=1, source_target_pairs={{0,4},{4,0},{8,12},{12,8},{16,20},{20,16},{24,28},{28,24},{32,36},... | collective-permute-start | bytes 380936 | tf_op jit(solution)/shard_map/ppermute | solution.py:508
  20.8 2.8 %collective-permute-start.5 = (bf16[64,256]{1,0:T(8,128)(2,1)S(1)}, bf16[64,256]{1,0:T(8,128)(2,1)S(1)}, u32[]{:S(2)}, u32[]{:S(2)}) collective-permute-start(bf16[64,256]{1,0:T(8,128)(2,1)S(1)} %slice.22), channel_id=1, source_target_pairs={{0,4},{4,0},{8,12},{12,8},{16,20},{20,16},{24,28},{28,24},{32,36},... | collective-permute-start | bytes 98312 | tf_op jit(solution)/shard_map/ppermute | solution.py:511
  26.0 10.3 %copy-start = (f32[3,64,128]{2,1,0:T(8,128)S(1)}, f32[3,64,128]{2,1,0:T(8,128)}, u32[]{:S(2)}) copy-start(f32[3,64,128]{2,1,0:T(8,128)} %disp_ref.3) | copy-start | bytes 294916
  26.0 10.3 %copy-start.7 = (f32[64,128]{1,0:T(8,128)S(1)}, f32[64,128]{1,0:T(8,128)}, u32[]{:S(2)}) copy-start(f32[64,128]{1,0:T(8,128)} %stiff_ref.3) | copy-start | bytes 98308
  26.0 21.6 %all-to-all-start = ((bf16[128,8,128]{2,1,0:T(8,128)(2,1)}), bf16[128,8,128]{2,1,0:T(8,128)(2,1)S(1)}, u32[]{:S(2)}, u32[]{:S(2)}) async-start(bf16[128,8,128]{2,1,0:T(8,128)(2,1)} %bitcast), calls=%async_computation | async-start | bytes 524288 | tf_op jit(solution)/shard_map/all_to_all | solution.py:209
  52.1 2.9 %collective-permute-start.6 = (f32[8,256]{1,0:T(8,128)S(1)}, f32[8,256]{1,0:T(8,128)S(1)}, u32[]{:S(2)}, u32[]{:S(2)}) collective-permute-start(f32[8,256]{1,0:T(8,128)S(1)} %get-tuple-element.26), channel_id=1, source_target_pairs={{0,1},{1,0},{2,3},{3,2},{4,5},{5,4},{6,7},{7,6},{8,9},{9,8},{10,11... | collective-permute-start | bytes 24584 | tf_op jit(solution)/shard_map/ppermute | solution.py:226
  52.6 2.5 %collective-permute-start.7 = (f32[8,256]{1,0:T(8,128)S(1)}, f32[8,256]{1,0:T(8,128)S(1)}, u32[]{:S(2)}, u32[]{:S(2)}) collective-permute-start(f32[8,256]{1,0:T(8,128)S(1)} %get-tuple-element.27), channel_id=1, source_target_pairs={{0,2},{1,3},{2,0},{3,1},{4,6},{5,7},{6,4},{7,5},{8,10},{9,11},{10,... | collective-permute-start | bytes 24584 | tf_op jit(solution)/shard_map/ppermute | solution.py:226
  52.9 3.1 %collective-permute-start.8 = (f32[8,256]{1,0:T(8,128)S(1)}, f32[8,256]{1,0:T(8,128)S(1)}, u32[]{:S(2)}, u32[]{:S(2)}) collective-permute-start(f32[8,256]{1,0:T(8,128)S(1)} %get-tuple-element.28), channel_id=1, source_target_pairs={{0,3},{1,2},{2,1},{3,0},{4,7},{5,6},{6,5},{7,4},{8,11},{9,10},{10,... | collective-permute-start | bytes 24584 | tf_op jit(solution)/shard_map/ppermute | solution.py:226

commit v7 on v6

--- a/solution.py
+++ b/solution.py
@@ -10,7 +10,8 @@
 F32 = jnp.float32
 I32 = jnp.int32
 LIMIT = 48 << 20
-EDGE = 24
+EDGE = 16
+THIN = 8
 
 
 def vmem(n):
@@ -29,13 +30,9 @@
     return lax.dot_general(a, b, (((1,), (1,)), ((), ())), preferred_element_type=F32)
 
 
-def slot_rows(final, tmap, elem, point, count_ref, rows_ref):
-    owners = rows_ref.shape[0]
-    slots = elem.shape[1]
+def slot_codes(point, count_ref, owners):
+    slots = point.shape[1]
     cap = slots // owners
-    traction = nt(tmap, final).astype(BF)
-    hot = (iota((final.shape[0], slots), 0) == elem).astype(F32).astype(BF)
-    pull = jnp.dot(traction, hot, preferred_element_type=F32)
     slot = iota((1, slots), 1)
     owner = slot // cap
     limit = jnp.zeros((1, slots), I32)
@@ -46,14 +43,7 @@
     code = (128 + (point - row * 128)).astype(F32)
     for b in range(6):
         code = code * jnp.where((row >> b) & 1 == 1, F32(2.0 ** (2**b)), F32(1.0))
-    code = jnp.where(live, code, 0.0)
-    pull = jnp.where(live, pull, 0.0)
-    for k in range(owners):
-        for j in range(4):
-            source = code if j == 3 else pull[j : j + 1]
-            for h in range(2):
-                start = k * cap + h * 128
-                rows_ref[k, 2 * j + h : 2 * j + h + 1, :] = source[:, start : start + 128]
+    return live, jnp.where(live, code, 0.0)
 
 
 def decode(code):
@@ -270,14 +260,23 @@
     cols = state_ref.shape[1]
     for copy in copies:
         copy.wait()
+    for e in range(2):
+        build_ref[e] = jnp.zeros((EDGE + 8, 256), F32)
     for i, row in enumerate((odd, 1 - odd)):
-        for part, ref in ((0, state_ref), (2, rhs_ref)):
+        for part, ref, at, third in (
+            (0, state_ref, 2 * i, 8 + i),
+            (2, rhs_ref, (4, 10)[i], None),
+        ):
             value = ref[row]
-            at = part + i
-            own_ref[at * cols : (at + 1) * cols, :] = value.astype(BF)
-            low, high = value[0:4], value[cols - 4 : cols]
-            build_ref[0, 4 * at : 4 * at + 4, :] = jnp.where(even, high, low)
-            build_ref[1, 4 * at : 4 * at + 4, :] = jnp.where(even, low, high)
+            block = part + i
+            own_ref[block * cols : (block + 1) * cols, :] = value.astype(BF)
+            low, high = value[0:2], value[cols - 2 : cols]
+            build_ref[0, at : at + 2, :] = jnp.where(even, high, low)
+            build_ref[1, at : at + 2, :] = jnp.where(even, low, high)
+            if third is not None:
+                low, high = value[2:3], value[cols - 3 : cols - 2]
+                build_ref[0, third : third + 1, :] = jnp.where(even, high, low)
+                build_ref[1, third : third + 1, :] = jnp.where(even, low, high)
     near_ref[...] = state_ref[1 - odd].astype(BF)
     lines = lines_of(scale_ref, pad_ref)
     flip = odd == 1
@@ -286,8 +285,7 @@
     pair = jnp.concatenate([halves(first), halves(second), jnp.zeros((6, 256), F32)], axis=0)
     own_ref[4 * cols :, :] = pair.astype(BF)
     for e in range(2):
-        build_ref[e, 16:24, :] = pair
-        build_ref[e, EDGE:, :] = jnp.zeros((8, 256), F32)
+        build_ref[e, 6:8, :] = pair[0:2]
     rows = disp_ref.shape[1]
     for c in range(3):
         top = halves(disp_ref[c, 0:2, :])
@@ -299,7 +297,7 @@
     three_ref[...] = build_ref[1].astype(BF)
 
 
-def sweep_kernel(
+def first_kernel(
     state_ref,
     rhs_ref,
     scale_ref,
@@ -308,7 +306,6 @@
     outer_ref,
     one_ref,
     three_ref,
-    relay_ref,
     matrix_ref,
     x_ref,
     y_ref,
@@ -317,18 +314,18 @@
     elem_hbm,
     point_hbm,
     count_hbm,
-    out_ref,
-    message_hbm,
+    keep_ref,
+    rest_ref,
+    hot_ref,
+    part_ref,
     v_ref,
     r_ref,
     s_ref,
     i_ref,
     line_ref,
-    rows_ref,
     elem_ref,
     point_ref,
     count_ref,
-    message_ref,
     sems,
 ):
     copies = [
@@ -351,8 +348,8 @@
     valid = valid | ((col < 8) & (patch > 0)) | ((col >= 8 + cols) & (patch < last_patch))
     edge = valid.astype(F32)
     keep = edge * inside.astype(F32)
-    v_ref[:, 0:8, :] = jnp.zeros((8, 8, width), F32)
-    v_ref[:, 8 + cols :, :] = jnp.zeros((8, 8, width), F32)
+    v_ref[:, 0:8, :] = jnp.zeros((7, 8, width), F32)
+    v_ref[:, 8 + cols :, :] = jnp.zeros((7, 8, width), F32)
     r_ref[:, 0:8, :] = jnp.zeros((6, 8, width), F32)
     r_ref[:, 8 + cols :, :] = jnp.zeros((6, 8, width), F32)
     head = 5 * cols + 8
@@ -360,7 +357,7 @@
     strips = {
         0: (one_ref[0:EDGE], three_ref[0:EDGE]),
         1: (inner_ref[tail : tail + EDGE], inner_ref[tail + EDGE : tail + 2 * EDGE]),
-        2: (outer_ref[head : head + EDGE], outer_ref[head + EDGE : head + 2 * EDGE]),
+        2: (outer_ref[head : head + THIN], outer_ref[head + THIN : head + 2 * THIN]),
     }
     sides = {}
     for kind, pair in strips.items():
@@ -389,19 +386,22 @@
             below = (3 if kind == 1 else 4) * cols
             both = ref[below : below + 8, :].astype(F32)[i : i + 1]
             line = both[:, :128] + both[:, 128:]
-        for side, start in zip(sides[kind], (4, 8 + cols)):
-            v_ref[r + 1, start : start + 4, :] = side[4 * i : 4 * i + 4]
-            r_ref[r, start : start + 4, :] = side[8 + 4 * i : 12 + 4 * i]
-            both = side[16 + i : 17 + i]
+        for side, start, far in zip(sides[kind], (6, 8 + cols), (5, 10 + cols)):
+            v_ref[r + 1, start : start + 2, :] = side[2 * i : 2 * i + 2]
+            if i == 0:
+                r_ref[r, start : start + 2, :] = side[4:6]
+            elif kind < 2:
+                r_ref[r, start : start + 2, :] = side[10:12]
+            if kind == 0:
+                v_ref[r + 1, far : far + 1, :] = side[8 + i : 9 + i]
+            both = side[6 + i : 7 + i]
             far = pltpu.roll(both[:, :128] + both[:, 128:], 64, 1)
-            here = (lane >= start) & (lane < start + 4)
+            here = (lane >= start) & (lane < start + 2)
             line = jnp.where(here, far, line)
         line_ref[r : r + 1, :] = jnp.where(line > 0.0, line, 1.0)
     line_ref[6:8, :] = jnp.ones((2, 128), F32)
     v_ref[0, 8 : 8 + cols, :] = outer_ref[4 * cols + 8 : head, :].astype(F32)
-    beyond = (slab != 1) & (slab != last_slab - 1)
-    v_ref[7, 8 : 8 + cols, :] = relay_ref[...].astype(F32) * beyond.astype(F32)
-    for r in range(8):
+    for r in range(7):
         v_ref[r] = v_ref[r] * (keep if r < 3 else edge)
     lines = line_ref[...]
     columns = jnp.transpose(lines)
@@ -410,34 +410,106 @@
         s_ref[r] = jnp.broadcast_to(columns[:wide, r : r + 1], (wide, width))
         i_ref[r] = jnp.broadcast_to(inverses[:wide, r : r + 1], (wide, width))
     for sweep in range(SWEEPS):
-        a, b = 1 + sweep, 7 - sweep
+        a, b = 1 + sweep, 6 - sweep
         n = b - a
-        near = v_ref[a - 1 : b + 1].astype(BF).astype(F32)
-        mid = near[1 : n + 1]
-        nx = (near[0:n] + near[2 : n + 2]).astype(BF)
-        ny = (pltpu.roll(mid, 1, 1) + pltpu.roll(mid, wide - 1, 1)).astype(BF)
-        flat = (n * wide, width)
-        own = jnp.dot(mid.astype(BF).reshape(flat), matrix_ref[...], preferred_element_type=F32)
-        side = jnp.dot(nx.reshape(flat), x_ref[...], preferred_element_type=F32)
-        side += jnp.dot(ny.reshape(flat), y_ref[...], preferred_element_type=F32)
-        scale = s_ref[a - 1 : b - 1].reshape(flat)
-        rhs = r_ref[a - 1 : b - 1].reshape(flat)
-        residue = (rhs - (scale * own - side)).astype(BF)
-        update = jnp.dot(residue, inverse_ref[...], preferred_element_type=F32)
-        update = update * i_ref[a - 1 : b - 1].reshape(flat)
-        value = v_ref[a:b] + update.reshape(n, wide, width)
+        if sweep == 0:
+            keep_ref[0:2] = v_ref[5:7]
+        elif sweep == 1:
+            keep_ref[2:4] = v_ref[4:6]
+        else:
+            keep_ref[4:6] = v_ref[3:5]
+        value = relaxed(
+            v_ref[a:b],
+            v_ref[a - 1 : b - 1],
+            v_ref[a + 1 : b + 1],
+            r_ref[a - 1 : b - 1],
+            s_ref[a - 1 : b - 1],
+            i_ref[a - 1 : b - 1],
+            (matrix_ref, x_ref, y_ref, inverse_ref),
+        )
         for j in range(n):
             v_ref[a + j] = value[j] * (keep if a + j < 3 else edge)
-    out_ref[odd] = v_ref[3, 8 : 8 + cols, :]
-    out_ref[1 - odd] = v_ref[4, 8 : 8 + cols, :]
-    final = out_ref[...].astype(BF).reshape(2 * cols, width)
+    keep_ref[6] = v_ref[3]
+    for i, ref in enumerate((r_ref, s_ref, i_ref)):
+        rest_ref[3 * i : 3 * i + 3] = ref[3:6]
     for copy in copies:
         copy.wait()
-    slot_rows(final, tmap_ref[...], elem_ref[0], point_ref[0], count_ref.at[0], rows_ref)
-    message_ref[...] = jnp.broadcast_to(rows_ref[...].astype(BF)[None], message_ref.shape)
+    elem = elem_ref[0]
+    live, code = slot_codes(point_ref[0], count_ref.at[0], part_ref.shape[0])
+    place = iota((cols, elem.shape[1]), 0)
+    hot = ((place + odd * cols == elem) & live).astype(F32).astype(BF)
+    hot_ref[...] = ((place + (1 - odd) * cols == elem) & live).astype(F32).astype(BF)
+    final = v_ref[3, 8 : 8 + cols, :].astype(BF)
+    pull = jnp.dot(nt(tmap_ref[...], final).astype(BF), hot, preferred_element_type=F32)
+    message_rows(pull, part_ref)
+    for k in range(part_ref.shape[0]):
+        for h in range(2):
+            start = k * 256 + h * 128
+            part_ref[k, 6 + h : 7 + h, :] = code[:, start : start + 128]
+
+
+def message_rows(pull, rows_ref):
+    for k in range(rows_ref.shape[0]):
+        for j in range(3):
+            for h in range(2):
+                start = k * 256 + h * 128
+                rows_ref[k, 2 * j + h : 2 * j + h + 1, :] = pull[j : j + 1, start : start + 128]
+
+
+def relaxed(center, up, down, rhs, scale, inverse_scale, matrices):
+    matrix_ref, x_ref, y_ref, inverse_ref = matrices
+    n, wide, width = center.shape
+    flat = (n * wide, width)
+    up, mid, down = (x.astype(BF).astype(F32) for x in (up, center, down))
+    nx = (up + down).astype(BF)
+    ny = (pltpu.roll(mid, 1, 1) + pltpu.roll(mid, wide - 1, 1)).astype(BF)
+    own = jnp.dot(mid.astype(BF).reshape(flat), matrix_ref[...], preferred_element_type=F32)
+    side = jnp.dot(nx.reshape(flat), x_ref[...], preferred_element_type=F32)
+    side += jnp.dot(ny.reshape(flat), y_ref[...], preferred_element_type=F32)
+    residue = (rhs.reshape(flat) - (scale.reshape(flat) * own - side)).astype(BF)
+    update = jnp.dot(residue, inverse_ref[...], preferred_element_type=F32)
+    update = update * inverse_scale.reshape(flat)
+    return center + update.reshape(center.shape)
+
+
+def last_kernel(
+    keep_ref, rest_ref, hot_ref, part_ref, relay_ref, matrix_ref, x_ref, y_ref, inverse_ref,
+    tmap_ref, out_ref, message_hbm, far_ref, rows_ref, message_ref, sems,
+):
+    slab = lax.axis_index("slab")
+    last_slab = lax.axis_size("slab") - 1
+    odd = slab % 2
+    cols = relay_ref.shape[0]
+    matrices = (matrix_ref, x_ref, y_ref, inverse_ref)
+    beyond = (slab != 1) & (slab != last_slab - 1)
+    far_ref[...] = jnp.zeros_like(far_ref)
+    far_ref[0, 8 : 8 + cols, :] = relay_ref[...].astype(F32) * beyond.astype(F32)
+
+    def step(center, up, down, r):
+        return relaxed(
+            center, up, down, rest_ref[r : r + 1], rest_ref[3 + r : 4 + r],
+            rest_ref[6 + r : 7 + r], matrices,
+        )
+
+    far = step(keep_ref[1:2], keep_ref[0:1], far_ref[...], 2)
+    near = step(keep_ref[3:4], keep_ref[2:3], far, 1)
+    own = step(keep_ref[5:6], keep_ref[4:5], near, 0)
+    far_ref[...] = own
+    inner = far_ref[0, 8 : 8 + cols, :]
+    out_ref[odd] = keep_ref[6, 8 : 8 + cols, :]
+    out_ref[1 - odd] = inner
+    pull = jnp.dot(
+        nt(tmap_ref[...], inner.astype(BF)).astype(BF), hot_ref[...], preferred_element_type=F32
+    )
+    message_rows(pull, rows_ref)
+    owners = rows_ref.shape[0]
+    for k in range(owners):
+        rows_ref[k, 6:8, :] = jnp.zeros((2, 128), F32)
+    rows = (rows_ref[...] + part_ref[...]).astype(BF)
+    message_ref[...] = jnp.broadcast_to(rows[None], message_ref.shape)
     part = message_ref.shape[0]
     copies = [
-        pltpu.make_async_copy(message_ref, message_hbm.at[i * part : (i + 1) * part], sems.at[3 + i])
+        pltpu.make_async_copy(message_ref, message_hbm.at[i * part : (i + 1) * part], sems.at[i])
         for i in range(message_hbm.shape[0] // part)
     ]
     for copy in copies:
@@ -504,16 +576,24 @@
     from_three = lax.ppermute(to_three, "patch", patch_pairs(3))
     from_one = lax.ppermute(to_one, "patch", patch_pairs(1))
     strips = [from_one[:EDGE], from_three[:EDGE]]
-    outer = lax.ppermute(jnp.concatenate([own, inner_near] + strips), "slab", outer_pairs)
+    thin = [from_one[:THIN], from_three[:THIN]]
+    outer = lax.ppermute(jnp.concatenate([own, inner_near] + thin), "slab", outer_pairs)
     inner = lax.ppermute(
         jnp.concatenate([own[:cols], own[2 * cols :]] + strips), "slab", inner_pairs
     )
     relay = lax.ppermute(outer[:cols], "slab", inner_pairs)
     wide = cols + 16
-    state, message = call(
-        sweep_kernel,
-        "sweep",
-        (shape(fluid_state.shape, F32), shape((slabs, owners, 8, 128), BF)),
+    rows = shape((owners, 8, 128), F32)
+    matrices = (element_matrix, couple_x, couple_y, block_inverse)
+    left = call(
+        first_kernel,
+        "first",
+        (
+            shape((7, wide, width), F32),
+            shape((9, wide, width), F32),
+            shape((cols, slots), BF),
+            rows,
+        ),
         (
             fluid_state,
             fluid_rhs,
@@ -523,30 +603,36 @@
             outer,
             from_one,
             from_three,
-            relay,
-            element_matrix,
-            couple_x,
-            couple_y,
-            block_inverse,
+            *matrices,
             traction_map,
             slot_elem,
             slot_point,
             slot_count,
         ),
         [
-            pltpu.VMEM((8, wide, width), F32),
+            pltpu.VMEM((7, wide, width), F32),
             pltpu.VMEM((6, wide, width), F32),
             pltpu.VMEM((6, wide, width), F32),
             pltpu.VMEM((6, wide, width), F32),
             pltpu.VMEM((8, 128), F32),
-            pltpu.VMEM((owners, 8, 128), F32),
             pltpu.VMEM((1, 1, slots), I32),
             pltpu.VMEM((1, 1, slots), I32),
             pltpu.VMEM((1, 1, owners), I32),
+            pltpu.SemaphoreType.DMA((3,)),
+        ],
+        in_specs=vmem(13) + hbm(3),
+    )
+    state, message = call(
+        last_kernel,
+        "last",
+        (shape(fluid_state.shape, F32), shape((slabs, owners, 8, 128), BF)),
+        (*left, relay, *matrices, traction_map),
+        [
+            pltpu.VMEM((1, wide, width), F32),
+            pltpu.VMEM((owners, 8, 128), F32),
             pltpu.VMEM((slabs // 4, owners, 8, 128), BF),
-            pltpu.SemaphoreType.DMA((7,)),
+            pltpu.SemaphoreType.DMA((4,)),
         ],
-        in_specs=vmem(14) + hbm(3),
         out_specs=tuple(vmem(1) + hbm(1)),
     )
     kd, final = call(

time: 56.8 us -> 55.8 us (0.982)
  waiting for transfers between devices: 21.4 us -> 18.8 us
  Pallas kernels: 9.84 us -> 10.8 us
  local copies, waits for them, and re-layouts: 0.09 us -> 0.66 us
    ppermute x1, waiting for transfers between devices: 2.76 us -> 1.12 us  [shards(): relay = lax.ppermute(outer[:cols], 'slab', inner_pairs)]
    pallas_call x3 -> x4, Pallas kernels: 4.18 us -> 5.15 us  [call(): pl.pallas_call(kernel, out_shape=out_shape, in_specs=in_specs or vmem(len...]
    ppermute x1, waiting for transfers between devices: 2.03 us -> 1.39 us  [shards(): from_three = lax.ppermute(to_three, 'patch', patch_pairs(3))]
  transfers between devices with their start and end apart: 10 -> 10, of which waited for: 6 -> 6; matrix products, arithmetic and copies ran while one was open for 0% -> 0% of each run, Pallas kernels for 2% -> 5%
where the time goes in v7:
time: 55.8 us; the launch traced here: 55.7 us
  starting transfers between devices  24.4 us (44%)
  waiting for transfers between devices  18.8 us (34%)
  Pallas kernels  10.8 us (19%)
  between operations  0.97 us (2%)
  local copies, waits for them, and re-layouts  0.66 us (1%)
    all_to_all x1, waiting for transfers between devices, exchange_and_relax(): lax.all_to_all(message.reshape(sources, 8, 128), ('slab', 'patch'), 0, 0,...  10.7 us
    all_to_all x1, starting transfers between devices, exchange_and_relax(): lax.all_to_all(message.reshape(sources, 8, 128), ('slab', 'patch'), 0, 0,...  10.2 us
    ppermute x1, starting transfers between devices, shards(): lax.ppermute(jnp.concatenate([own, inner_near] + thin), 'slab', outer_pairs)  7.23 us
    pallas_call x4, Pallas kernels, call(): pl.pallas_call(kernel, out_shape=out_shape, in_specs=in_specs or vmem(len...  5.15 us
    ppermute x1, waiting for transfers between devices, shards(): lax.ppermute(jnp.concatenate([own, inner_near] + thin), 'slab', outer_pairs)  4.56 us
    pallas_call x1, Pallas kernels, exchange_and_relax(): pl.pallas_call(owner_kernel, out_shape=(jax.ShapeDtypeStruct(displacement...  4.4 us
    ppermute x1, starting transfers between devices, shards(): inner_near = lax.ppermute(near, 'slab', inner_pairs)  2.55 us
    ppermute x3, starting transfers between devices, exchange_and_relax(): lax.ppermute(replies[d], 'patch', patch_pairs(d))  2.22 us
  transfers between devices with their start and end apart: 10, of which 6 were waited for; matrix products, arithmetic and copies ran while one was open for 0% of the time, Pallas kernels for 5%

profile of v7, /device:TPU:1, one launch (start us, length us, event | category | flops | bytes accessed | tf_op | source)
XLA Modules:
  0.0 55.7 jit_solution(5359195415718360955)
XLA Ops:
  0.6 1.2 %near.1 = (bf16[64,256]{1,0:T(8,128)(2,1)S(1)}, bf16[264,256]{1,0:T(8,128)(2,1)S(1)}, bf16[24,256]{1,0:T(8,128)(2,1)S(1)}, bf16[24,256]{1,0:T(8,128)(2,1)S(1)}) custom-call(f32[2,64,256]{2,1,0:T(8,128)} %state_ref.1, f32[2,64,256]{2,1,0:T(8,128)} %rhs_ref.1, f32[2,64]{1,0:T(2,128)} %scale_ref.1, f32[3,64,128]{2,1,0:T(8,128)} %disp_ref.3), custom_call_target="tpu_custom_call" | custom-call | tf_op jit(solution)/shard_map/near/pallas_call | solution.py:522
  1.8 2.5 %collective-permute-start.2 = (bf16[64,256]{1,0:T(8,128)(2,1)S(1)}, bf16[64,256]{1,0:T(8,128)(2,1)S(1)}, u32[]{:S(2)}, u32[]{:S(2)}) collective-permute-start(bf16[64,256]{1,0:T(8,128)(2,1)S(1)} %get-tuple-element.22), channel_id=1, source_target_pairs={{0,4},{4,0},{8,12},{12,8},{16,20},{20,16},{24,28},{28,24},{32,36},... | collective-permute-start | bytes 98312 | tf_op jit(solution)/shard_map/ppermute | solution.py:575
  4.4 1.0 %collective-permute-start = (bf16[24,256]{1,0:T(8,128)(2,1)S(1)}, bf16[24,256]{1,0:T(8,128)(2,1)S(1)}, u32[]{:S(2)}, u32[]{:S(2)}) collective-permute-start(bf16[24,256]{1,0:T(8,128)(2,1)S(1)} %get-tuple-element.20), channel_id=1, source_target_pairs={{0,1},{1,0},{2,3},{3,2},{4,5},{5,4},{6,7},{7,6},{8,9},{9,8},{10,11... | collective-permute-start | bytes 36872 | tf_op jit(solution)/shard_map/ppermute | solution.py:577
  5.3 1.1 %collective-permute-start.1 = (bf16[24,256]{1,0:T(8,128)(2,1)S(1)}, bf16[24,256]{1,0:T(8,128)(2,1)S(1)}, u32[]{:S(2)}, u32[]{:S(2)}) collective-permute-start(bf16[24,256]{1,0:T(8,128)(2,1)S(1)} %get-tuple-element.21), channel_id=1, source_target_pairs={{0,3},{1,2},{2,1},{3,0},{4,7},{5,6},{6,5},{7,4},{8,11},{9,10},{10,... | collective-permute-start | bytes 36872 | tf_op jit(solution)/shard_map/ppermute | solution.py:576
  6.4 0.0 collective-permute-done.one_ref
  6.4 0.0 copy-start.8
  6.5 0.0 copy-start.11
  6.5 0.0 copy-start.12
  6.5 0.6 copy-done.8
  7.0 1.4 %collective-permute-done.1.three_ref = bf16[24,256]{1,0:T(8,128)(2,1)S(1)} collective-permute-done((bf16[24,256]{1,0:T(8,128)(2,1)S(1)}, bf16[24,256]{1,0:T(8,128)(2,1)S(1)}, u32[]{:S(2)}, u32[]{:S(2)}) %collective-permute-start.1) | collective-permute-done | bytes 12320 | tf_op jit(solution)/shard_map/ppermute | solution.py:576
  8.5 0.0 copy-start.13
  8.5 0.0 copy-start.14
  8.5 0.0 collective-permute-done.2.near_ref
  8.5 0.0 copy-start.3
  8.5 0.0 copy-start.4
  8.5 0.0 copy-start.5
  8.6 0.0 copy-start.1
  8.6 0.0 copy-start.2
  8.6 7.2 %collective-permute-start.4 = (bf16[344,256]{1,0:T(8,128)(2,1)S(1)}, bf16[344,256]{1,0:T(8,128)(2,1)S(1)}, u32[]{:S(2)}, u32[]{:S(2)}) collective-permute-start(bf16[344,256]{1,0:T(8,128)(2,1)S(1)} %pad_maximum_fusion), channel_id=1, source_target_pairs={{4,8},{12,16},{20,24},{28,32},{36,40},{44,48},{52,56},{60,64},{68,... | collective-permute-start | bytes 528392 | tf_op jit(solution)/shard_map/ppermute | solution.py:580
  15.8 0.0 slice-done
  15.8 0.1 collective-permute-start.3
  15.9 4.6 %collective-permute-done.4.outer_ref = bf16[344,256]{1,0:T(8,128)(2,1)S(1)} collective-permute-done((bf16[344,256]{1,0:T(8,128)(2,1)S(1)}, bf16[344,256]{1,0:T(8,128)(2,1)S(1)}, u32[]{:S(2)}, u32[]{:S(2)}) %collective-permute-start.4) | collective-permute-done | bytes 176160 | tf_op jit(solution)/shard_map/ppermute | solution.py:580
  20.5 0.0 collective-permute-start.5
  20.5 0.0 collective-permute-done.3.inner_ref
  20.5 0.0 copy-done.6
  20.5 0.0 copy-done.11
  20.5 0.0 copy-done.12
  20.5 0.0 copy-done.9
  20.5 0.0 copy-done.10
  20.6 1.5 %first.1 = (f32[7,80,256]{2,1,0:T(8,128)S(1)}, f32[9,80,256]{2,1,0:T(8,128)S(1)}, bf16[64,1024]{1,0:T(8,128)(2,1)S(1)}, f32[4,8,128]{2,1,0:T(8,128)S(1)}) custom-call(f32[2,64,256]{2,1,0:T(8,128)S(1)} %copy-done.5, f32[2,64,256]{2,1,0:T(8,128)S(1)} %copy-done.6, f32[2,64]{1,0:T(2,128)S(1)} %copy-done.13, ...), custom_call_target="tpu_custom_call" | custom-call | tf_op jit(solution)/shard_map/first/pallas_call | solution.py:522
  22.1 1.1 %collective-permute-done.5.relay_ref = bf16[64,256]{1,0:T(8,128)(2,1)S(1)} collective-permute-done((bf16[64,256]{1,0:T(8,128)(2,1)S(1)}, bf16[64,256]{1,0:T(8,128)(2,1)S(1)}, u32[]{:S(2)}, u32[]{:S(2)}) %collective-permute-start.5) | collective-permute-done | bytes 32800 | tf_op jit(solution)/shard_map/ppermute | solution.py:584
  23.2 1.8 %last.1 = (f32[2,64,256]{2,1,0:T(8,128)S(1)}, bf16[32,4,8,128]{3,2,1,0:T(8,128)(2,1)}) custom-call(f32[7,80,256]{2,1,0:T(8,128)S(1)} %get-tuple-element.24.keep_ref, f32[9,80,256]{2,1,0:T(8,128)S(1)} %get-tuple-element.25.rest_ref, bf16[64,1024]{1,0:T(8,128)(2,1)S(1)} %get-tuple-element.26.hot_ref, f32[4,8,128]{2,1,0:T(8,128)S(1)} %get-tuple-element.27.part_ref, ...), custom_call_target="tpu_custom_call" | custom-call | tf_op jit(solution)/shard_map/last/pallas_call | solution.py:522
  25.1 0.0 copy-start
  25.1 0.0 copy-start.7
  25.1 10.2 %all-to-all-start = ((bf16[128,8,128]{2,1,0:T(8,128)(2,1)}), bf16[128,8,128]{2,1,0:T(8,128)(2,1)S(1)}, u32[]{:S(2)}, u32[]{:S(2)}) async-start(bf16[128,8,128]{2,1,0:T(8,128)(2,1)} %bitcast), calls=%async_computation | async-start | bytes 524288 | tf_op jit(solution)/shard_map/all_to_all | solution.py:199
  35.3 0.0 copy-done
  35.3 0.0 copy-done.7
  35.3 0.7 %shell.1 = (f32[3,64,128]{2,1,0:T(8,128)S(1)}, f32[2,64,256]{2,1,0:T(8,128)}) custom-call(bf16[24,256]{1,0:T(8,128)(2,1)S(1)} %copy-done.9, bf16[24,256]{1,0:T(8,128)(2,1)S(1)} %collective-permute-done.1.three_ref, f32[3,64,128]{2,1,0:T(8,128)S(1)} %copy-done, f32[64,128]{1,0:T(8,128)S(1)} %copy-done.7, f32[2,64,256]{2,1,0:T(8,128)S(1)} %get-tuple-element.28.state_ref), custom_call_target="tpu_custom_call" | custom-call | tf_op jit(solution)/shard_map/shell/pallas_call | solution.py:522
  36.0 10.7 %all-to-all-done.got_ref = bf16[128,8,128]{2,1,0:T(8,128)(2,1)S(1)} async-done(((bf16[128,8,128]{2,1,0:T(8,128)(2,1)}), bf16[128,8,128]{2,1,0:T(8,128)(2,1)S(1)}, u32[]{:S(2)}, u32[]{:S(2)}) %all-to-all-start) | async-done | bytes 262176 | tf_op jit(solution)/shard_map/all_to_all | solution.py:199
  46.7 4.4 %owner.1 = (f32[3,64,128]{2,1,0:T(8,128)S(1)}, f32[8,256]{1,0:T(8,128)S(1)}, f32[8,256]{1,0:T(8,128)S(1)}, f32[8,256]{1,0:T(8,128)S(1)}, f32[8,256]{1,0:T(8,128)S(1)}) custom-call(bf16[128,8,128]{2,1,0:T(8,128)(2,1)S(1)} %all-to-all-done.got_ref, f32[3,64,128]{2,1,0:T(8,128)S(1)} %copy-done, f32[64,128]{1,0:T(8,128)S(1)} %copy-done.7, ...), custom_call_target="tpu_custom_call" | custom-call | tf_op jit(solution)/shard_map/owner/pallas_call | solution.py:203
  51.1 0.5 collective-permute-start.6
  51.6 0.3 collective-permute-start.7
  51.9 1.4 %collective-permute-start.8 = (f32[8,256]{1,0:T(8,128)S(1)}, f32[8,256]{1,0:T(8,128)S(1)}, u32[]{:S(2)}, u32[]{:S(2)}) collective-permute-start(f32[8,256]{1,0:T(8,128)S(1)} %get-tuple-element.36), channel_id=1, source_target_pairs={{0,3},{1,2},{2,1},{3,0},{4,7},{5,6},{6,5},{7,4},{8,11},{9,10},{10,... | collective-permute-start | bytes 24584 | tf_op jit(solution)/shard_map/ppermute | solution.py:216
  53.3 0.6 %store_shell.1 = f32[3,64,128]{2,1,0:T(8,128)} custom-call(f32[3,64,128]{2,1,0:T(8,128)S(1)} %get-tuple-element.32.value_ref), custom_call_target="tpu_custom_call" | custom-call | tf_op jit(solution)/shard_map/store_shell/pallas_call | solution.py:120
  54.0 0.0 collective-permute-done.6.r1
  54.0 0.1 collective-permute-done.7.r2
  54.1 0.9 %collective-permute-done.8.r3 = f32[8,256]{1,0:T(8,128)S(1)} collective-permute-done((f32[8,256]{1,0:T(8,128)S(1)}, f32[8,256]{1,0:T(8,128)S(1)}, u32[]{:S(2)}, u32[]{:S(2)}) %collective-permute-start.8) | collective-permute-done | bytes 8224 | tf_op jit(solution)/shard_map/ppermute | solution.py:216
  55.0 0.6 %finish.1 = f32[3,1,1,1024]{3,2,1,0:T(1,128)} custom-call(f32[8,256]{1,0:T(8,128)S(1)} %get-tuple-element.33.r0, f32[8,256]{1,0:T(8,128)S(1)} %collective-permute-done.6.r1, f32[8,256]{1,0:T(8,128)S(1)} %collective-permute-done.7.r2, f32[8,256]{1,0:T(8,128)S(1)} %collective-permute-done.8.r3), custom_call_target="tpu_custom_call" | custom-call | tf_op jit(solution)/shard_map/finish/pallas_call | solution.py:218
  (19 shorter events, 0.1 us)
Async XLA Ops:
  1.8 6.7 %collective-permute-start.2 = (bf16[64,256]{1,0:T(8,128)(2,1)S(1)}, bf16[64,256]{1,0:T(8,128)(2,1)S(1)}, u32[]{:S(2)}, u32[]{:S(2)}) collective-permute-start(bf16[64,256]{1,0:T(8,128)(2,1)S(1)} %get-tuple-element.22), channel_id=1, source_target_pairs={{0,4},{4,0},{8,12},{12,8},{16,20},{20,16},{24,28},{28,24},{32,36},... | collective-permute-start | bytes 98312 | tf_op jit(solution)/shard_map/ppermute | solution.py:575
  4.4 2.1 %collective-permute-start = (bf16[24,256]{1,0:T(8,128)(2,1)S(1)}, bf16[24,256]{1,0:T(8,128)(2,1)S(1)}, u32[]{:S(2)}, u32[]{:S(2)}) collective-permute-start(bf16[24,256]{1,0:T(8,128)(2,1)S(1)} %get-tuple-element.20), channel_id=1, source_target_pairs={{0,1},{1,0},{2,3},{3,2},{4,5},{5,4},{6,7},{7,6},{8,9},{9,8},{10,11... | collective-permute-start | bytes 36872 | tf_op jit(solution)/shard_map/ppermute | solution.py:577
  5.3 3.1 %collective-permute-start.1 = (bf16[24,256]{1,0:T(8,128)(2,1)S(1)}, bf16[24,256]{1,0:T(8,128)(2,1)S(1)}, u32[]{:S(2)}, u32[]{:S(2)}) collective-permute-start(bf16[24,256]{1,0:T(8,128)(2,1)S(1)} %get-tuple-element.21), channel_id=1, source_target_pairs={{0,3},{1,2},{2,1},{3,0},{4,7},{5,6},{6,5},{7,4},{8,11},{9,10},{10,... | collective-permute-start | bytes 36872 | tf_op jit(solution)/shard_map/ppermute | solution.py:576
  6.4 14.1 %copy-start.6 = (f32[2,64,256]{2,1,0:T(8,128)S(1)}, f32[2,64,256]{2,1,0:T(8,128)}, u32[]{:S(2)}) copy-start(f32[2,64,256]{2,1,0:T(8,128)} %rhs_ref.1) | copy-start | bytes 393220
  6.4 0.6 %copy-start.8 = (bf16[24,256]{1,0:T(8,128)(2,1)}, bf16[24,256]{1,0:T(8,128)(2,1)S(1)}, u32[]{:S(2)}) copy-start(bf16[24,256]{1,0:T(8,128)(2,1)S(1)} %collective-permute-done.one_ref) | copy-start | bytes 36868
  6.5 14.0 %copy-start.11 = (s32[1,1,1024]{2,1,0:T(1,128)S(1)}, s32[1,1,1024]{2,1,0:T(1,128)}, u32[]{:S(2)}) copy-start(s32[1,1,1024]{2,1,0:T(1,128)} %elem_hbm.1) | copy-start | bytes 12292
  6.5 14.0 %copy-start.12 = (s32[1,1,1024]{2,1,0:T(1,128)S(1)}, s32[1,1,1024]{2,1,0:T(1,128)}, u32[]{:S(2)}) copy-start(s32[1,1,1024]{2,1,0:T(1,128)} %point_hbm.1) | copy-start | bytes 12292
  8.4 12.1 %copy-start.9 = (bf16[24,256]{1,0:T(8,128)(2,1)S(1)}, bf16[24,256]{1,0:T(8,128)(2,1)}, u32[]{:S(2)}) copy-start(bf16[24,256]{1,0:T(8,128)(2,1)} %copy-done.8) | copy-start | bytes 36868
  8.4 7.4 %slice-start = ((bf16[24,256]{1,0:T(8,128)(2,1)}), bf16[16,256]{1,0:T(8,128)(2,1)S(1)}, s32[]{:S(2)}) async-start(bf16[24,256]{1,0:T(8,128)(2,1)} %copy-done.8), calls=%async_computation.1 | async-start | bytes 16384 | tf_op jit(solution)/shard_map/slice | solution.py:578
  8.4 12.1 %copy-start.10 = (bf16[3,256]{1,0:T(4,128)(2,1)S(1)}, bf16[3,256]{1,0:T(4,128)(2,1)}, u32[]{:S(2)}) copy-start(bf16[3,256]{1,0:T(4,128)(2,1)} %tmap_ref.3) | copy-start | bytes 4612
  8.5 12.1 %copy-start.13 = (f32[2,64]{1,0:T(2,128)S(1)}, f32[2,64]{1,0:T(2,128)}, u32[]{:S(2)}) copy-start(f32[2,64]{1,0:T(2,128)} %scale_ref.1) | copy-start | bytes 1540
  8.5 12.1 %copy-start.14 = (s32[1,1,4]{2,1,0:T(1,128)S(1)}, s32[1,1,4]{2,1,0:T(1,128)}, u32[]{:S(2)}) copy-start(s32[1,1,4]{2,1,0:T(1,128)} %count_hbm.1) | copy-start | bytes 52
  8.5 12.1 %copy-start.3 = (bf16[256,256]{1,0:T(8,128)(2,1)S(1)}, bf16[256,256]{1,0:T(8,128)(2,1)}, u32[]{:S(2)}) copy-start(bf16[256,256]{1,0:T(8,128)(2,1)} %y_ref.3) | copy-start | bytes 393220
  8.5 12.1 %copy-start.4 = (bf16[256,256]{1,0:T(8,128)(2,1)S(1)}, bf16[256,256]{1,0:T(8,128)(2,1)}, u32[]{:S(2)}) copy-start(bf16[256,256]{1,0:T(8,128)(2,1)} %inverse_ref.3) | copy-start | bytes 393220
  8.5 12.1 %copy-start.5 = (f32[2,64,256]{2,1,0:T(8,128)S(1)}, f32[2,64,256]{2,1,0:T(8,128)}, u32[]{:S(2)}) copy-start(f32[2,64,256]{2,1,0:T(8,128)} %state_ref.1) | copy-start | bytes 393220
  8.6 12.0 %copy-start.1 = (bf16[256,256]{1,0:T(8,128)(2,1)S(1)}, bf16[256,256]{1,0:T(8,128)(2,1)}, u32[]{:S(2)}) copy-start(bf16[256,256]{1,0:T(8,128)(2,1)} %matrix_ref.3) | copy-start | bytes 393220
  8.6 12.0 %copy-start.2 = (bf16[256,256]{1,0:T(8,128)(2,1)S(1)}, bf16[256,256]{1,0:T(8,128)(2,1)}, u32[]{:S(2)}) copy-start(bf16[256,256]{1,0:T(8,128)(2,1)} %x_ref.3) | copy-start | bytes 393220
  8.6 11.9 %collective-permute-start.4 = (bf16[344,256]{1,0:T(8,128)(2,1)S(1)}, bf16[344,256]{1,0:T(8,128)(2,1)S(1)}, u32[]{:S(2)}, u32[]{:S(2)}) collective-permute-start(bf16[344,256]{1,0:T(8,128)(2,1)S(1)} %pad_maximum_fusion), channel_id=1, source_target_pairs={{4,8},{12,16},{20,24},{28,32},{36,40},{44,48},{52,56},{60,64},{68,... | collective-permute-start | bytes 528392 | tf_op jit(solution)/shard_map/ppermute | solution.py:580
  15.8 4.7 %collective-permute-start.3 = (bf16[232,256]{1,0:T(8,128)(2,1)S(1)}, bf16[232,256]{1,0:T(8,128)(2,1)S(1)}, u32[]{:S(2)}, u32[]{:S(2)}) collective-permute-start(bf16[232,256]{1,0:T(8,128)(2,1)S(1)} %pad_maximum_fusion.1), channel_id=1, source_target_pairs={{0,4},{4,0},{8,12},{12,8},{16,20},{20,16},{24,28},{28,24},{32,36},... | collective-permute-start | bytes 356360 | tf_op jit(solution)/shard_map/ppermute | solution.py:581
  20.5 2.8 %collective-permute-start.5 = (bf16[64,256]{1,0:T(8,128)(2,1)S(1)}, bf16[64,256]{1,0:T(8,128)(2,1)S(1)}, u32[]{:S(2)}, u32[]{:S(2)}) collective-permute-start(bf16[64,256]{1,0:T(8,128)(2,1)S(1)} %slice.32), channel_id=1, source_target_pairs={{0,4},{4,0},{8,12},{12,8},{16,20},{20,16},{24,28},{28,24},{32,36},... | collective-permute-start | bytes 98312 | tf_op jit(solution)/shard_map/ppermute | solution.py:584
  25.1 10.3 %copy-start = (f32[3,64,128]{2,1,0:T(8,128)S(1)}, f32[3,64,128]{2,1,0:T(8,128)}, u32[]{:S(2)}) copy-start(f32[3,64,128]{2,1,0:T(8,128)} %disp_ref.3) | copy-start | bytes 294916
  25.1 10.3 %copy-start.7 = (f32[64,128]{1,0:T(8,128)S(1)}, f32[64,128]{1,0:T(8,128)}, u32[]{:S(2)}) copy-start(f32[64,128]{1,0:T(8,128)} %stiff_ref.3) | copy-start | bytes 98308
  25.1 21.6 %all-to-all-start = ((bf16[128,8,128]{2,1,0:T(8,128)(2,1)}), bf16[128,8,128]{2,1,0:T(8,128)(2,1)S(1)}, u32[]{:S(2)}, u32[]{:S(2)}) async-start(bf16[128,8,128]{2,1,0:T(8,128)(2,1)} %bitcast), calls=%async_computation | async-start | bytes 524288 | tf_op jit(solution)/shard_map/all_to_all | solution.py:199
  51.1 2.9 %collective-permute-start.6 = (f32[8,256]{1,0:T(8,128)S(1)}, f32[8,256]{1,0:T(8,128)S(1)}, u32[]{:S(2)}, u32[]{:S(2)}) collective-permute-start(f32[8,256]{1,0:T(8,128)S(1)} %get-tuple-element.34), channel_id=1, source_target_pairs={{0,1},{1,0},{2,3},{3,2},{4,5},{5,4},{6,7},{7,6},{8,9},{9,8},{10,11... | collective-permute-start | bytes 24584 | tf_op jit(solution)/shard_map/ppermute | solution.py:216
  51.6 2.5 %collective-permute-start.7 = (f32[8,256]{1,0:T(8,128)S(1)}, f32[8,256]{1,0:T(8,128)S(1)}, u32[]{:S(2)}, u32[]{:S(2)}) collective-permute-start(f32[8,256]{1,0:T(8,128)S(1)} %get-tuple-element.35), channel_id=1, source_target_pairs={{0,2},{1,3},{2,0},{3,1},{4,6},{5,7},{6,4},{7,5},{8,10},{9,11},{10,... | collective-permute-start | bytes 24584 | tf_op jit(solution)/shard_map/ppermute | solution.py:216
  51.9 3.1 %collective-permute-start.8 = (f32[8,256]{1,0:T(8,128)S(1)}, f32[8,256]{1,0:T(8,128)S(1)}, u32[]{:S(2)}, u32[]{:S(2)}) collective-permute-start(f32[8,256]{1,0:T(8,128)S(1)} %get-tuple-element.36), channel_id=1, source_target_pairs={{0,3},{1,2},{2,1},{3,0},{4,7},{5,6},{6,5},{7,4},{8,11},{9,10},{10,... | collective-permute-start | bytes 24584 | tf_op jit(solution)/shard_map/ppermute | solution.py:216

commit v8 on v6

--- a/solution.py
+++ b/solution.py
@@ -10,7 +10,8 @@
 F32 = jnp.float32
 I32 = jnp.int32
 LIMIT = 48 << 20
-EDGE = 24
+EDGE = 16
+THIN = 8
 
 
 def vmem(n):
@@ -29,13 +30,9 @@
     return lax.dot_general(a, b, (((1,), (1,)), ((), ())), preferred_element_type=F32)
 
 
-def slot_rows(final, tmap, elem, point, count_ref, rows_ref):
-    owners = rows_ref.shape[0]
-    slots = elem.shape[1]
+def slot_codes(point, count_ref, owners):
+    slots = point.shape[1]
     cap = slots // owners
-    traction = nt(tmap, final).astype(BF)
-    hot = (iota((final.shape[0], slots), 0) == elem).astype(F32).astype(BF)
-    pull = jnp.dot(traction, hot, preferred_element_type=F32)
     slot = iota((1, slots), 1)
     owner = slot // cap
     limit = jnp.zeros((1, slots), I32)
@@ -46,14 +43,7 @@
     code = (128 + (point - row * 128)).astype(F32)
     for b in range(6):
         code = code * jnp.where((row >> b) & 1 == 1, F32(2.0 ** (2**b)), F32(1.0))
-    code = jnp.where(live, code, 0.0)
-    pull = jnp.where(live, pull, 0.0)
-    for k in range(owners):
-        for j in range(4):
-            source = code if j == 3 else pull[j : j + 1]
-            for h in range(2):
-                start = k * cap + h * 128
-                rows_ref[k, 2 * j + h : 2 * j + h + 1, :] = source[:, start : start + 128]
+    return live, jnp.where(live, code, 0.0)
 
 
 def decode(code):
@@ -158,7 +148,7 @@
     bottom = patch < 3
     even = patch % 2 == 0
     one, three = (
-        ref[EDGE:, :128].astype(F32) + ref[EDGE:, 128:].astype(F32)
+        ref[:, :128].astype(F32) + ref[:, 128:].astype(F32)
         for ref in (one_ref, three_ref)
     )
     above = jnp.where(even, three, one)
@@ -270,14 +260,23 @@
     cols = state_ref.shape[1]
     for copy in copies:
         copy.wait()
+    for e in range(2):
+        build_ref[e] = jnp.zeros((EDGE + 8, 256), F32)
     for i, row in enumerate((odd, 1 - odd)):
-        for part, ref in ((0, state_ref), (2, rhs_ref)):
+        for part, ref, at, third in (
+            (0, state_ref, 2 * i, 8 + i),
+            (2, rhs_ref, (4, 10)[i], None),
+        ):
             value = ref[row]
-            at = part + i
-            own_ref[at * cols : (at + 1) * cols, :] = value.astype(BF)
-            low, high = value[0:4], value[cols - 4 : cols]
-            build_ref[0, 4 * at : 4 * at + 4, :] = jnp.where(even, high, low)
-            build_ref[1, 4 * at : 4 * at + 4, :] = jnp.where(even, low, high)
+            block = part + i
+            own_ref[block * cols : (block + 1) * cols, :] = value.astype(BF)
+            low, high = value[0:2], value[cols - 2 : cols]
+            build_ref[0, at : at + 2, :] = jnp.where(even, high, low)
+            build_ref[1, at : at + 2, :] = jnp.where(even, low, high)
+            if third is not None:
+                low, high = value[2:3], value[cols - 3 : cols - 2]
+                build_ref[0, third : third + 1, :] = jnp.where(even, high, low)
+                build_ref[1, third : third + 1, :] = jnp.where(even, low, high)
     near_ref[...] = state_ref[1 - odd].astype(BF)
     lines = lines_of(scale_ref, pad_ref)
     flip = odd == 1
@@ -286,8 +285,7 @@
     pair = jnp.concatenate([halves(first), halves(second), jnp.zeros((6, 256), F32)], axis=0)
     own_ref[4 * cols :, :] = pair.astype(BF)
     for e in range(2):
-        build_ref[e, 16:24, :] = pair
-        build_ref[e, EDGE:, :] = jnp.zeros((8, 256), F32)
+        build_ref[e, 6:8, :] = pair[0:2]
     rows = disp_ref.shape[1]
     for c in range(3):
         top = halves(disp_ref[c, 0:2, :])
@@ -306,6 +304,7 @@
     near_ref,
     inner_ref,
     outer_ref,
+    rest_ref,
     one_ref,
     three_ref,
     relay_ref,
@@ -324,10 +323,10 @@
     s_ref,
     i_ref,
     line_ref,
-    rows_ref,
     elem_ref,
     point_ref,
     count_ref,
+    rows_ref,
     message_ref,
     sems,
 ):
@@ -355,12 +354,11 @@
     v_ref[:, 8 + cols :, :] = jnp.zeros((8, 8, width), F32)
     r_ref[:, 0:8, :] = jnp.zeros((6, 8, width), F32)
     r_ref[:, 8 + cols :, :] = jnp.zeros((6, 8, width), F32)
-    head = 5 * cols + 8
     tail = 3 * cols + 8
     strips = {
         0: (one_ref[0:EDGE], three_ref[0:EDGE]),
         1: (inner_ref[tail : tail + EDGE], inner_ref[tail + EDGE : tail + 2 * EDGE]),
-        2: (outer_ref[head : head + EDGE], outer_ref[head + EDGE : head + 2 * EDGE]),
+        2: (rest_ref[cols : cols + THIN], rest_ref[cols + THIN : cols + 2 * THIN]),
     }
     sides = {}
     for kind, pair in strips.items():
@@ -389,16 +387,21 @@
             below = (3 if kind == 1 else 4) * cols
             both = ref[below : below + 8, :].astype(F32)[i : i + 1]
             line = both[:, :128] + both[:, 128:]
-        for side, start in zip(sides[kind], (4, 8 + cols)):
-            v_ref[r + 1, start : start + 4, :] = side[4 * i : 4 * i + 4]
-            r_ref[r, start : start + 4, :] = side[8 + 4 * i : 12 + 4 * i]
-            both = side[16 + i : 17 + i]
+        for side, start, far in zip(sides[kind], (6, 8 + cols), (5, 10 + cols)):
+            v_ref[r + 1, start : start + 2, :] = side[2 * i : 2 * i + 2]
+            if i == 0:
+                r_ref[r, start : start + 2, :] = side[4:6]
+            elif kind < 2:
+                r_ref[r, start : start + 2, :] = side[10:12]
+            if kind == 0:
+                v_ref[r + 1, far : far + 1, :] = side[8 + i : 9 + i]
+            both = side[6 + i : 7 + i]
             far = pltpu.roll(both[:, :128] + both[:, 128:], 64, 1)
-            here = (lane >= start) & (lane < start + 4)
+            here = (lane >= start) & (lane < start + 2)
             line = jnp.where(here, far, line)
         line_ref[r : r + 1, :] = jnp.where(line > 0.0, line, 1.0)
     line_ref[6:8, :] = jnp.ones((2, 128), F32)
-    v_ref[0, 8 : 8 + cols, :] = outer_ref[4 * cols + 8 : head, :].astype(F32)
+    v_ref[0, 8 : 8 + cols, :] = rest_ref[0:cols, :].astype(F32)
     beyond = (slab != 1) & (slab != last_slab - 1)
     v_ref[7, 8 : 8 + cols, :] = relay_ref[...].astype(F32) * beyond.astype(F32)
     for r in range(8):
@@ -411,29 +414,33 @@
         i_ref[r] = jnp.broadcast_to(inverses[:wide, r : r + 1], (wide, width))
     for sweep in range(SWEEPS):
         a, b = 1 + sweep, 7 - sweep
-        n = b - a
-        near = v_ref[a - 1 : b + 1].astype(BF).astype(F32)
-        mid = near[1 : n + 1]
-        nx = (near[0:n] + near[2 : n + 2]).astype(BF)
-        ny = (pltpu.roll(mid, 1, 1) + pltpu.roll(mid, wide - 1, 1)).astype(BF)
-        flat = (n * wide, width)
-        own = jnp.dot(mid.astype(BF).reshape(flat), matrix_ref[...], preferred_element_type=F32)
-        side = jnp.dot(nx.reshape(flat), x_ref[...], preferred_element_type=F32)
-        side += jnp.dot(ny.reshape(flat), y_ref[...], preferred_element_type=F32)
-        scale = s_ref[a - 1 : b - 1].reshape(flat)
-        rhs = r_ref[a - 1 : b - 1].reshape(flat)
-        residue = (rhs - (scale * own - side)).astype(BF)
-        update = jnp.dot(residue, inverse_ref[...], preferred_element_type=F32)
-        update = update * i_ref[a - 1 : b - 1].reshape(flat)
-        value = v_ref[a:b] + update.reshape(n, wide, width)
-        for j in range(n):
+        value = relaxed(
+            v_ref[a:b],
+            v_ref[a - 1 : b - 1],
+            v_ref[a + 1 : b + 1],
+            r_ref[a - 1 : b - 1],
+            s_ref[a - 1 : b - 1],
+            i_ref[a - 1 : b - 1],
+            (matrix_ref, x_ref, y_ref, inverse_ref),
+        )
+        for j in range(b - a):
             v_ref[a + j] = value[j] * (keep if a + j < 3 else edge)
     out_ref[odd] = v_ref[3, 8 : 8 + cols, :]
     out_ref[1 - odd] = v_ref[4, 8 : 8 + cols, :]
     final = out_ref[...].astype(BF).reshape(2 * cols, width)
     for copy in copies:
         copy.wait()
-    slot_rows(final, tmap_ref[...], elem_ref[0], point_ref[0], count_ref.at[0], rows_ref)
+    elem = elem_ref[0]
+    owners = rows_ref.shape[0]
+    live, code = slot_codes(point_ref[0], count_ref.at[0], owners)
+    hot = ((iota((2 * cols, elem.shape[1]), 0) == elem) & live).astype(F32).astype(BF)
+    pull = jnp.dot(nt(tmap_ref[...], final).astype(BF), hot, preferred_element_type=F32)
+    for k in range(owners):
+        for j in range(4):
+            source = code if j == 3 else pull[j : j + 1]
+            for h in range(2):
+                start = k * 256 + h * 128
+                rows_ref[k, 2 * j + h : 2 * j + h + 1, :] = source[:, start : start + 128]
     message_ref[...] = jnp.broadcast_to(rows_ref[...].astype(BF)[None], message_ref.shape)
     part = message_ref.shape[0]
     copies = [
@@ -444,6 +451,22 @@
         copy.start()
     for copy in copies:
         copy.wait()
+
+
+def relaxed(center, up, down, rhs, scale, inverse_scale, matrices):
+    matrix_ref, x_ref, y_ref, inverse_ref = matrices
+    n, wide, width = center.shape
+    flat = (n * wide, width)
+    up, mid, down = (x.astype(BF).astype(F32) for x in (up, center, down))
+    nx = (up + down).astype(BF)
+    ny = (pltpu.roll(mid, 1, 1) + pltpu.roll(mid, wide - 1, 1)).astype(BF)
+    own = jnp.dot(mid.astype(BF).reshape(flat), matrix_ref[...], preferred_element_type=F32)
+    side = jnp.dot(nx.reshape(flat), x_ref[...], preferred_element_type=F32)
+    side += jnp.dot(ny.reshape(flat), y_ref[...], preferred_element_type=F32)
+    residue = (rhs.reshape(flat) - (scale.reshape(flat) * own - side)).astype(BF)
+    update = jnp.dot(residue, inverse_ref[...], preferred_element_type=F32)
+    update = update * inverse_scale.reshape(flat)
+    return center + update.reshape(center.shape)
 
 
 def call(kernel, name, out_shape, operands, scratch=(), in_specs=None, out_specs=None):
@@ -500,14 +523,16 @@
         ],
         in_specs=hbm(4),
     )
+    outer = lax.ppermute(own, "slab", outer_pairs)
     inner_near = lax.ppermute(near, "slab", inner_pairs)
     from_three = lax.ppermute(to_three, "patch", patch_pairs(3))
     from_one = lax.ppermute(to_one, "patch", patch_pairs(1))
     strips = [from_one[:EDGE], from_three[:EDGE]]
-    outer = lax.ppermute(jnp.concatenate([own, inner_near] + strips), "slab", outer_pairs)
-    inner = lax.ppermute(
-        jnp.concatenate([own[:cols], own[2 * cols :]] + strips), "slab", inner_pairs
-    )
+    thin = [from_one[:THIN], from_three[:THIN]]
+    rest = lax.ppermute(jnp.concatenate([inner_near] + thin), "slab", outer_pairs)
+    others = jnp.concatenate([own[:cols], own[2 * cols :]] + strips)
+    others, _ = lax.optimization_barrier((others, inner_near))
+    inner = lax.ppermute(others, "slab", inner_pairs)
     relay = lax.ppermute(outer[:cols], "slab", inner_pairs)
     wide = cols + 16
     state, message = call(
@@ -521,6 +546,7 @@
             inner_near,
             inner,
             outer,
+            rest,
             from_one,
             from_three,
             relay,
@@ -539,21 +565,21 @@
             pltpu.VMEM((6, wide, width), F32),
             pltpu.VMEM((6, wide, width), F32),
             pltpu.VMEM((8, 128), F32),
-            pltpu.VMEM((owners, 8, 128), F32),
             pltpu.VMEM((1, 1, slots), I32),
             pltpu.VMEM((1, 1, slots), I32),
             pltpu.VMEM((1, 1, owners), I32),
+            pltpu.VMEM((owners, 8, 128), F32),
             pltpu.VMEM((slabs // 4, owners, 8, 128), BF),
             pltpu.SemaphoreType.DMA((7,)),
         ],
-        in_specs=vmem(14) + hbm(3),
+        in_specs=vmem(15) + hbm(3),
         out_specs=tuple(vmem(1) + hbm(1)),
     )
     kd, final = call(
         shell_kernel,
         "shell",
         (shape(displacement.shape, F32), shape(state.shape, F32)),
-        (from_one, from_three, displacement, stiffness, state),
+        (from_one[EDGE:], from_three[EDGE:], displacement, stiffness, state),
         [pltpu.VMEM((3, displacement.shape[1] + 16, 128), F32)] * 2 + [pltpu.SemaphoreType.DMA],
         out_specs=tuple(vmem(1) + hbm(1)),
     )

time: 56.8 us -> 53 us (0.933)
  waiting for transfers between devices: 21.4 us -> 17.8 us
    ppermute x1, waiting for transfers between devices: 2.76 us -> 0.01 us  [shards(): relay = lax.ppermute(outer[:cols], 'slab', inner_pairs)]
    all_to_all x1, starting transfers between devices: 10.2 us -> 7.83 us  [exchange_and_relax(): lax.all_to_all(message.reshape(sources, 8, 128), ('slab', 'patch'), 0, 0,...]
    ppermute x2 -> x3, starting transfers between devices: 7.32 us -> 9.52 us  [the longest x1 6.86 us: shards(): outer = lax.ppermute(own, 'slab', outer_pairs)]
    ppermute x1, waiting for transfers between devices: 2.03 us -> 0.01 us  [shards(): from_three = lax.ppermute(to_three, 'patch', patch_pairs(3))]
    ppermute x2 -> x3, waiting for transfers between devices: 4.85 us -> 6.07 us  [the longest x1 5.4 us: shards(): lax.ppermute(jnp.concatenate([inner_near] + thin), 'slab', outer_pairs)]
    ppermute x1, starting transfers between devices: 2.55 us -> 1.64 us  [shards(): inner_near = lax.ppermute(near, 'slab', inner_pairs)]
  transfers between devices with their start and end apart: 10 -> 11, of which waited for: 6 -> 5; matrix products, arithmetic and copies ran while one was open for 0% -> 0% of each run, Pallas kernels for 2% -> 2%
where the time goes in v8:
time: 53 us; the launch traced here: 52.8 us
  starting transfers between devices  24 us (45%)
  waiting for transfers between devices  17.8 us (34%)
  Pallas kernels  9.93 us (19%)
  between operations  0.96 us (2%)
    all_to_all x1, waiting for transfers between devices, exchange_and_relax(): lax.all_to_all(message.reshape(sources, 8, 128), ('slab', 'patch'), 0, 0,...  10.7 us
    all_to_all x1, starting transfers between devices, exchange_and_relax(): lax.all_to_all(message.reshape(sources, 8, 128), ('slab', 'patch'), 0, 0,...  7.83 us
    ppermute x1, starting transfers between devices, shards(): outer = lax.ppermute(own, 'slab', outer_pairs)  6.86 us
    ppermute x1, waiting for transfers between devices, shards(): lax.ppermute(jnp.concatenate([inner_near] + thin), 'slab', outer_pairs)  5.4 us
    pallas_call x1, Pallas kernels, exchange_and_relax(): pl.pallas_call(owner_kernel, out_shape=(jax.ShapeDtypeStruct(displacement...  4.4 us
    pallas_call x3, Pallas kernels, call(): pl.pallas_call(kernel, out_shape=out_shape, in_specs=in_specs or vmem(len...  4.28 us
    ppermute x1, starting transfers between devices, shards(): lax.ppermute(jnp.concatenate([inner_near] + thin), 'slab', outer_pairs)  2.58 us
    ppermute x3, starting transfers between devices, exchange_and_relax(): lax.ppermute(replies[d], 'patch', patch_pairs(d))  2.22 us
  transfers between devices with their start and end apart: 11, of which 5 were waited for; matrix products, arithmetic and copies ran while one was open for 0% of the time, Pallas kernels for 2%

profile of v8, /device:TPU:1, one launch (start us, length us, event | category | flops | bytes accessed | tf_op | source)
XLA Modules:
  0.0 52.8 jit_solution(6743146381308803393)
XLA Ops:
  0.6 0.0 copy-start.6
  0.6 0.0 copy-start.8
  0.7 0.0 copy-start.9
  0.7 1.2 %near.1 = (bf16[64,256]{1,0:T(8,128)(2,1)S(1)}, bf16[264,256]{1,0:T(8,128)(2,1)S(1)}, bf16[24,256]{1,0:T(8,128)(2,1)S(1)}, bf16[24,256]{1,0:T(8,128)(2,1)S(1)}) custom-call(f32[2,64,256]{2,1,0:T(8,128)} %state_ref.1, f32[2,64,256]{2,1,0:T(8,128)} %rhs_ref.1, f32[2,64]{1,0:T(2,128)} %scale_ref.1, f32[3,64,128]{2,1,0:T(8,128)} %disp_ref.3), custom_call_target="tpu_custom_call" | custom-call | tf_op jit(solution)/shard_map/near/pallas_call | solution.py:473
  1.9 1.5 %collective-permute-start = (bf16[24,256]{1,0:T(8,128)(2,1)S(1)}, bf16[24,256]{1,0:T(8,128)(2,1)S(1)}, u32[]{:S(2)}, u32[]{:S(2)}) collective-permute-start(bf16[24,256]{1,0:T(8,128)(2,1)S(1)} %get-tuple-element.17), channel_id=1, source_target_pairs={{0,1},{1,0},{2,3},{3,2},{4,5},{5,4},{6,7},{7,6},{8,9},{9,8},{10,11... | collective-permute-start | bytes 36872 | tf_op jit(solution)/shard_map/ppermute | solution.py:529
  3.4 1.3 %collective-permute-start.1 = (bf16[24,256]{1,0:T(8,128)(2,1)S(1)}, bf16[24,256]{1,0:T(8,128)(2,1)S(1)}, u32[]{:S(2)}, u32[]{:S(2)}) collective-permute-start(bf16[24,256]{1,0:T(8,128)(2,1)S(1)} %get-tuple-element.18), channel_id=1, source_target_pairs={{0,3},{1,2},{2,1},{3,0},{4,7},{5,6},{6,5},{7,4},{8,11},{9,10},{10,... | collective-permute-start | bytes 36872 | tf_op jit(solution)/shard_map/ppermute | solution.py:528
  4.7 1.6 %collective-permute-start.2 = (bf16[64,256]{1,0:T(8,128)(2,1)S(1)}, bf16[64,256]{1,0:T(8,128)(2,1)S(1)}, u32[]{:S(2)}, u32[]{:S(2)}) collective-permute-start(bf16[64,256]{1,0:T(8,128)(2,1)S(1)} %get-tuple-element.19), channel_id=1, source_target_pairs={{0,4},{4,0},{8,12},{12,8},{16,20},{20,16},{24,28},{28,24},{32,36},... | collective-permute-start | bytes 98312 | tf_op jit(solution)/shard_map/ppermute | solution.py:527
  6.3 6.9 %collective-permute-start.4 = (bf16[264,256]{1,0:T(8,128)(2,1)S(1)}, bf16[264,256]{1,0:T(8,128)(2,1)S(1)}, u32[]{:S(2)}, u32[]{:S(2)}) collective-permute-start(bf16[264,256]{1,0:T(8,128)(2,1)S(1)} %get-tuple-element.20), channel_id=1, source_target_pairs={{4,8},{12,16},{20,24},{28,32},{36,40},{44,48},{52,56},{60,64},{68,... | collective-permute-start | bytes 405512 | tf_op jit(solution)/shard_map/ppermute | solution.py:526
  13.2 0.0 collective-permute-done.one_ref
  13.2 0.0 collective-permute-done.1.three_ref
  13.3 0.0 copy-start.3
  13.3 0.0 copy-start.2
  13.3 0.0 copy-start.1
  13.3 0.0 collective-permute-done.2.near_ref
  13.3 0.1 collective-permute-start.3
  13.4 0.0 copy-start.10
  13.5 0.0 copy-start.11
  13.5 0.0 copy-start.12
  13.5 2.6 %collective-permute-start.5 = (bf16[80,256]{1,0:T(8,128)(2,1)S(1)}, bf16[80,256]{1,0:T(8,128)(2,1)S(1)}, u32[]{:S(2)}, u32[]{:S(2)}) collective-permute-start(bf16[80,256]{1,0:T(8,128)(2,1)S(1)} %pad_maximum_fusion.1), channel_id=1, source_target_pairs={{4,8},{12,16},{20,24},{28,32},{36,40},{44,48},{52,56},{60,64},{68,... | collective-permute-start | bytes 122888 | tf_op jit(solution)/shard_map/ppermute | solution.py:532
  16.1 0.7 %collective-permute-done.4.outer_ref = bf16[264,256]{1,0:T(8,128)(2,1)S(1)} collective-permute-done((bf16[264,256]{1,0:T(8,128)(2,1)S(1)}, bf16[264,256]{1,0:T(8,128)(2,1)S(1)}, u32[]{:S(2)}, u32[]{:S(2)}) %collective-permute-start.4) | collective-permute-done | bytes 135200 | tf_op jit(solution)/shard_map/ppermute | solution.py:526
  16.7 0.0 collective-permute-start.6
  16.7 5.4 %collective-permute-done.5.rest_ref = bf16[80,256]{1,0:T(8,128)(2,1)S(1)} collective-permute-done((bf16[80,256]{1,0:T(8,128)(2,1)S(1)}, bf16[80,256]{1,0:T(8,128)(2,1)S(1)}, u32[]{:S(2)}, u32[]{:S(2)}) %collective-permute-start.5) | collective-permute-done | bytes 40992 | tf_op jit(solution)/shard_map/ppermute | solution.py:532
  22.1 0.0 collective-permute-done.3.inner_ref
  22.1 0.0 collective-permute-done.6.relay_ref
  22.1 0.0 copy-done.6
  22.1 0.0 copy-done.8
  22.2 0.0 copy-done.9
  22.2 0.0 copy-done.5
  22.2 0.0 copy-done.4
  22.2 0.0 copy-done.3
  22.2 0.0 copy-done.2
  22.2 0.0 copy-done.1
  22.2 0.0 copy-done.10
  22.2 2.4 %sweep.1 = (f32[2,64,256]{2,1,0:T(8,128)S(1)}, bf16[32,4,8,128]{3,2,1,0:T(8,128)(2,1)}) custom-call(f32[2,64,256]{2,1,0:T(8,128)S(1)} %copy-done.1, f32[2,64,256]{2,1,0:T(8,128)S(1)} %copy-done.2, f32[2,64]{1,0:T(2,128)S(1)} %copy-done.10, bf16[64,256]{1,0:T(8,128)(2,1)S(1)} %collective-permute-done.2.near_ref, ...), custom_call_target="tpu_custom_call" | custom-call | tf_op jit(solution)/shard_map/sweep/pallas_call | solution.py:473
  24.6 0.0 copy-start
  24.6 0.0 copy-start.7
  24.6 7.8 %all-to-all-start = ((bf16[128,8,128]{2,1,0:T(8,128)(2,1)}), bf16[128,8,128]{2,1,0:T(8,128)(2,1)S(1)}, u32[]{:S(2)}, u32[]{:S(2)}) async-start(bf16[128,8,128]{2,1,0:T(8,128)(2,1)} %bitcast), calls=%async_computation | async-start | bytes 524288 | tf_op jit(solution)/shard_map/all_to_all | solution.py:199
  32.5 0.7 %shell.1 = (f32[3,64,128]{2,1,0:T(8,128)S(1)}, f32[2,64,256]{2,1,0:T(8,128)}) custom-call(bf16[8,256]{1,0:T(8,128)(2,1)S(1)} %get-tuple-element.32.one_ref, bf16[8,256]{1,0:T(8,128)(2,1)S(1)} %get-tuple-element.34.three_ref, f32[3,64,128]{2,1,0:T(8,128)S(1)} %copy-done, f32[64,128]{1,0:T(8,128)S(1)} %copy-done.7, f32[2,64,256]{2,1,0:T(8,128)S(1)} %get-tuple-element.22.state_ref), custom_call_target="tpu_custom_call" | custom-call | tf_op jit(solution)/shard_map/shell/pallas_call | solution.py:473
  33.2 10.7 %all-to-all-done.got_ref = bf16[128,8,128]{2,1,0:T(8,128)(2,1)S(1)} async-done(((bf16[128,8,128]{2,1,0:T(8,128)(2,1)}), bf16[128,8,128]{2,1,0:T(8,128)(2,1)S(1)}, u32[]{:S(2)}, u32[]{:S(2)}) %all-to-all-start) | async-done | bytes 262176 | tf_op jit(solution)/shard_map/all_to_all | solution.py:199
  43.9 4.4 %owner.1 = (f32[3,64,128]{2,1,0:T(8,128)S(1)}, f32[8,256]{1,0:T(8,128)S(1)}, f32[8,256]{1,0:T(8,128)S(1)}, f32[8,256]{1,0:T(8,128)S(1)}, f32[8,256]{1,0:T(8,128)S(1)}) custom-call(bf16[128,8,128]{2,1,0:T(8,128)(2,1)S(1)} %all-to-all-done.got_ref, f32[3,64,128]{2,1,0:T(8,128)S(1)} %copy-done, f32[64,128]{1,0:T(8,128)S(1)} %copy-done.7, ...), custom_call_target="tpu_custom_call" | custom-call | tf_op jit(solution)/shard_map/owner/pallas_call | solution.py:203
  48.3 0.5 collective-permute-start.7
  48.8 0.3 collective-permute-start.8
  49.1 1.4 %collective-permute-start.9 = (f32[8,256]{1,0:T(8,128)S(1)}, f32[8,256]{1,0:T(8,128)S(1)}, u32[]{:S(2)}, u32[]{:S(2)}) collective-permute-start(f32[8,256]{1,0:T(8,128)S(1)} %get-tuple-element.30), channel_id=1, source_target_pairs={{0,3},{1,2},{2,1},{3,0},{4,7},{5,6},{6,5},{7,4},{8,11},{9,10},{10,... | collective-permute-start | bytes 24584 | tf_op jit(solution)/shard_map/ppermute | solution.py:216
  50.5 0.6 %store_shell.1 = f32[3,64,128]{2,1,0:T(8,128)} custom-call(f32[3,64,128]{2,1,0:T(8,128)S(1)} %get-tuple-element.26.value_ref), custom_call_target="tpu_custom_call" | custom-call | tf_op jit(solution)/shard_map/store_shell/pallas_call | solution.py:120
  51.1 0.0 collective-permute-done.7.r1
  51.2 0.1 collective-permute-done.8.r2
  51.3 0.9 %collective-permute-done.9.r3 = f32[8,256]{1,0:T(8,128)S(1)} collective-permute-done((f32[8,256]{1,0:T(8,128)S(1)}, f32[8,256]{1,0:T(8,128)S(1)}, u32[]{:S(2)}, u32[]{:S(2)}) %collective-permute-start.9) | collective-permute-done | bytes 8224 | tf_op jit(solution)/shard_map/ppermute | solution.py:216
  52.2 0.6 %finish.1 = f32[3,1,1,1024]{3,2,1,0:T(1,128)} custom-call(f32[8,256]{1,0:T(8,128)S(1)} %get-tuple-element.27.r0, f32[8,256]{1,0:T(8,128)S(1)} %collective-permute-done.7.r1, f32[8,256]{1,0:T(8,128)S(1)} %collective-permute-done.8.r2, f32[8,256]{1,0:T(8,128)S(1)} %collective-permute-done.9.r3), custom_call_target="tpu_custom_call" | custom-call | tf_op jit(solution)/shard_map/finish/pallas_call | solution.py:218
  (15 shorter events, 0.1 us)
Async XLA Ops:
  0.6 21.5 %copy-start.6 = (bf16[256,256]{1,0:T(8,128)(2,1)S(1)}, bf16[256,256]{1,0:T(8,128)(2,1)}, u32[]{:S(2)}) copy-start(bf16[256,256]{1,0:T(8,128)(2,1)} %inverse_ref.1) | copy-start | bytes 393220
  0.6 21.5 %copy-start.8 = (s32[1,1,1024]{2,1,0:T(1,128)S(1)}, s32[1,1,1024]{2,1,0:T(1,128)}, u32[]{:S(2)}) copy-start(s32[1,1,1024]{2,1,0:T(1,128)} %elem_hbm.1) | copy-start | bytes 12292
  0.7 21.5 %copy-start.9 = (s32[1,1,1024]{2,1,0:T(1,128)S(1)}, s32[1,1,1024]{2,1,0:T(1,128)}, u32[]{:S(2)}) copy-start(s32[1,1,1024]{2,1,0:T(1,128)} %point_hbm.1) | copy-start | bytes 12292
  1.9 11.3 %collective-permute-start = (bf16[24,256]{1,0:T(8,128)(2,1)S(1)}, bf16[24,256]{1,0:T(8,128)(2,1)S(1)}, u32[]{:S(2)}, u32[]{:S(2)}) collective-permute-start(bf16[24,256]{1,0:T(8,128)(2,1)S(1)} %get-tuple-element.17), channel_id=1, source_target_pairs={{0,1},{1,0},{2,3},{3,2},{4,5},{5,4},{6,7},{7,6},{8,9},{9,8},{10,11... | collective-permute-start | bytes 36872 | tf_op jit(solution)/shard_map/ppermute | solution.py:529
  3.4 9.8 %collective-permute-start.1 = (bf16[24,256]{1,0:T(8,128)(2,1)S(1)}, bf16[24,256]{1,0:T(8,128)(2,1)S(1)}, u32[]{:S(2)}, u32[]{:S(2)}) collective-permute-start(bf16[24,256]{1,0:T(8,128)(2,1)S(1)} %get-tuple-element.18), channel_id=1, source_target_pairs={{0,3},{1,2},{2,1},{3,0},{4,7},{5,6},{6,5},{7,4},{8,11},{9,10},{10,... | collective-permute-start | bytes 36872 | tf_op jit(solution)/shard_map/ppermute | solution.py:528
  4.7 8.6 %collective-permute-start.2 = (bf16[64,256]{1,0:T(8,128)(2,1)S(1)}, bf16[64,256]{1,0:T(8,128)(2,1)S(1)}, u32[]{:S(2)}, u32[]{:S(2)}) collective-permute-start(bf16[64,256]{1,0:T(8,128)(2,1)S(1)} %get-tuple-element.19), channel_id=1, source_target_pairs={{0,4},{4,0},{8,12},{12,8},{16,20},{20,16},{24,28},{28,24},{32,36},... | collective-permute-start | bytes 98312 | tf_op jit(solution)/shard_map/ppermute | solution.py:527
  6.3 10.4 %collective-permute-start.4 = (bf16[264,256]{1,0:T(8,128)(2,1)S(1)}, bf16[264,256]{1,0:T(8,128)(2,1)S(1)}, u32[]{:S(2)}, u32[]{:S(2)}) collective-permute-start(bf16[264,256]{1,0:T(8,128)(2,1)S(1)} %get-tuple-element.20), channel_id=1, source_target_pairs={{4,8},{12,16},{20,24},{28,32},{36,40},{44,48},{52,56},{60,64},{68,... | collective-permute-start | bytes 405512 | tf_op jit(solution)/shard_map/ppermute | solution.py:526
  13.2 9.0 %copy-start.5 = (bf16[256,256]{1,0:T(8,128)(2,1)S(1)}, bf16[256,256]{1,0:T(8,128)(2,1)}, u32[]{:S(2)}) copy-start(bf16[256,256]{1,0:T(8,128)(2,1)} %y_ref.1) | copy-start | bytes 393220
  13.2 9.0 %copy-start.4 = (bf16[256,256]{1,0:T(8,128)(2,1)S(1)}, bf16[256,256]{1,0:T(8,128)(2,1)}, u32[]{:S(2)}) copy-start(bf16[256,256]{1,0:T(8,128)(2,1)} %x_ref.1) | copy-start | bytes 393220
  13.3 8.9 %copy-start.3 = (bf16[256,256]{1,0:T(8,128)(2,1)S(1)}, bf16[256,256]{1,0:T(8,128)(2,1)}, u32[]{:S(2)}) copy-start(bf16[256,256]{1,0:T(8,128)(2,1)} %matrix_ref.1) | copy-start | bytes 393220
  13.3 8.9 %copy-start.2 = (f32[2,64,256]{2,1,0:T(8,128)S(1)}, f32[2,64,256]{2,1,0:T(8,128)}, u32[]{:S(2)}) copy-start(f32[2,64,256]{2,1,0:T(8,128)} %rhs_ref.1) | copy-start | bytes 393220
  13.3 8.9 %copy-start.1 = (f32[2,64,256]{2,1,0:T(8,128)S(1)}, f32[2,64,256]{2,1,0:T(8,128)}, u32[]{:S(2)}) copy-start(f32[2,64,256]{2,1,0:T(8,128)} %state_ref.1) | copy-start | bytes 393220
  13.3 8.8 %collective-permute-start.3 = (bf16[232,256]{1,0:T(8,128)(2,1)S(1)}, bf16[232,256]{1,0:T(8,128)(2,1)S(1)}, u32[]{:S(2)}, u32[]{:S(2)}) collective-permute-start(bf16[232,256]{1,0:T(8,128)(2,1)S(1)} %pad_maximum_fusion), channel_id=1, source_target_pairs={{0,4},{4,0},{8,12},{12,8},{16,20},{20,16},{24,28},{28,24},{32,36},... | collective-permute-start | bytes 356360 | tf_op jit(solution)/shard_map/ppermute | solution.py:535
  13.4 8.8 %copy-start.10 = (f32[2,64]{1,0:T(2,128)S(1)}, f32[2,64]{1,0:T(2,128)}, u32[]{:S(2)}) copy-start(f32[2,64]{1,0:T(2,128)} %scale_ref.1) | copy-start | bytes 1540
  13.5 8.8 %copy-start.11 = (bf16[3,256]{1,0:T(4,128)(2,1)S(1)}, bf16[3,256]{1,0:T(4,128)(2,1)}, u32[]{:S(2)}) copy-start(bf16[3,256]{1,0:T(4,128)(2,1)} %tmap_ref.1) | copy-start | bytes 4612
  13.5 8.8 %copy-start.12 = (s32[1,1,4]{2,1,0:T(1,128)S(1)}, s32[1,1,4]{2,1,0:T(1,128)}, u32[]{:S(2)}) copy-start(s32[1,1,4]{2,1,0:T(1,128)} %count_hbm.1) | copy-start | bytes 52
  13.5 8.7 %collective-permute-start.5 = (bf16[80,256]{1,0:T(8,128)(2,1)S(1)}, bf16[80,256]{1,0:T(8,128)(2,1)S(1)}, u32[]{:S(2)}, u32[]{:S(2)}) collective-permute-start(bf16[80,256]{1,0:T(8,128)(2,1)S(1)} %pad_maximum_fusion.1), channel_id=1, source_target_pairs={{4,8},{12,16},{20,24},{28,32},{36,40},{44,48},{52,56},{60,64},{68,... | collective-permute-start | bytes 122888 | tf_op jit(solution)/shard_map/ppermute | solution.py:532
  16.7 5.4 %collective-permute-start.6 = (bf16[64,256]{1,0:T(8,128)(2,1)S(1)}, bf16[64,256]{1,0:T(8,128)(2,1)S(1)}, u32[]{:S(2)}, u32[]{:S(2)}) collective-permute-start(bf16[64,256]{1,0:T(8,128)(2,1)S(1)} %slice.42), channel_id=1, source_target_pairs={{0,4},{4,0},{8,12},{12,8},{16,20},{20,16},{24,28},{28,24},{32,36},... | collective-permute-start | bytes 98312 | tf_op jit(solution)/shard_map/ppermute | solution.py:536
  24.6 7.9 %copy-start = (f32[3,64,128]{2,1,0:T(8,128)S(1)}, f32[3,64,128]{2,1,0:T(8,128)}, u32[]{:S(2)}) copy-start(f32[3,64,128]{2,1,0:T(8,128)} %disp_ref.3) | copy-start | bytes 294916
  24.6 7.9 %copy-start.7 = (f32[64,128]{1,0:T(8,128)S(1)}, f32[64,128]{1,0:T(8,128)}, u32[]{:S(2)}) copy-start(f32[64,128]{1,0:T(8,128)} %stiff_ref.3) | copy-start | bytes 98308
  24.6 19.2 %all-to-all-start = ((bf16[128,8,128]{2,1,0:T(8,128)(2,1)}), bf16[128,8,128]{2,1,0:T(8,128)(2,1)S(1)}, u32[]{:S(2)}, u32[]{:S(2)}) async-start(bf16[128,8,128]{2,1,0:T(8,128)(2,1)} %bitcast), calls=%async_computation | async-start | bytes 524288 | tf_op jit(solution)/shard_map/all_to_all | solution.py:199
  48.3 2.9 %collective-permute-start.7 = (f32[8,256]{1,0:T(8,128)S(1)}, f32[8,256]{1,0:T(8,128)S(1)}, u32[]{:S(2)}, u32[]{:S(2)}) collective-permute-start(f32[8,256]{1,0:T(8,128)S(1)} %get-tuple-element.28), channel_id=1, source_target_pairs={{0,1},{1,0},{2,3},{3,2},{4,5},{5,4},{6,7},{7,6},{8,9},{9,8},{10,11... | collective-permute-start | bytes 24584 | tf_op jit(solution)/shard_map/ppermute | solution.py:216
  48.8 2.5 %collective-permute-start.8 = (f32[8,256]{1,0:T(8,128)S(1)}, f32[8,256]{1,0:T(8,128)S(1)}, u32[]{:S(2)}, u32[]{:S(2)}) collective-permute-start(f32[8,256]{1,0:T(8,128)S(1)} %get-tuple-element.29), channel_id=1, source_target_pairs={{0,2},{1,3},{2,0},{3,1},{4,6},{5,7},{6,4},{7,5},{8,10},{9,11},{10,... | collective-permute-start | bytes 24584 | tf_op jit(solution)/shard_map/ppermute | solution.py:216
  49.1 3.1 %collective-permute-start.9 = (f32[8,256]{1,0:T(8,128)S(1)}, f32[8,256]{1,0:T(8,128)S(1)}, u32[]{:S(2)}, u32[]{:S(2)}) collective-permute-start(f32[8,256]{1,0:T(8,128)S(1)} %get-tuple-element.30), channel_id=1, source_target_pairs={{0,3},{1,2},{2,1},{3,0},{4,7},{5,6},{6,5},{7,4},{8,11},{9,10},{10,... | collective-permute-start | bytes 24584 | tf_op jit(solution)/shard_map/ppermute | solution.py:216

commit v9 on v8

--- a/solution.py
+++ b/solution.py
@@ -239,7 +239,7 @@
 
 
 def near_kernel(
-    state_hbm, rhs_hbm, scale_hbm, disp_hbm, near_ref, own_ref, one_ref, three_ref,
+    state_hbm, rhs_hbm, scale_hbm, disp_hbm, near_ref, own_ref, far_ref, one_ref, three_ref,
     state_ref, rhs_ref, scale_ref, disp_ref, pad_ref, build_ref, sems,
 ):
     copies = [
@@ -269,7 +269,10 @@
         ):
             value = ref[row]
             block = part + i
-            own_ref[block * cols : (block + 1) * cols, :] = value.astype(BF)
+            if block == 3:
+                far_ref[...] = value.astype(BF)
+            else:
+                own_ref[block * cols : (block + 1) * cols, :] = value.astype(BF)
             low, high = value[0:2], value[cols - 2 : cols]
             build_ref[0, at : at + 2, :] = jnp.where(even, high, low)
             build_ref[1, at : at + 2, :] = jnp.where(even, low, high)
@@ -283,7 +286,7 @@
     first = jnp.where(flip, lines[1:2], lines[0:1])
     second = jnp.where(flip, lines[0:1], lines[1:2])
     pair = jnp.concatenate([halves(first), halves(second), jnp.zeros((6, 256), F32)], axis=0)
-    own_ref[4 * cols :, :] = pair.astype(BF)
+    own_ref[3 * cols :, :] = pair.astype(BF)
     for e in range(2):
         build_ref[e, 6:8, :] = pair[0:2]
     rows = disp_ref.shape[1]
@@ -378,13 +381,14 @@
         else:
             if kind == 1:
                 value = near_ref[...] if i == 1 else inner_ref[0:cols]
-                ref, at = inner_ref, (i + 1) * cols
+                rhs = inner_ref[2 * cols + 8 : 3 * cols + 8] if i == 1 else inner_ref[cols : 2 * cols]
+                ref, below = inner_ref, 2 * cols
             else:
                 value = outer_ref[i * cols : (i + 1) * cols]
-                ref, at = outer_ref, (i + 2) * cols
+                rhs = rest_ref[cols + 2 * THIN :] if i == 1 else outer_ref[2 * cols : 3 * cols]
+                ref, below = outer_ref, 3 * cols
             v_ref[r + 1, 8 : 8 + cols, :] = value.astype(F32)
-            r_ref[r, 8 : 8 + cols, :] = ref[at : at + cols, :].astype(F32)
-            below = (3 if kind == 1 else 4) * cols
+            r_ref[r, 8 : 8 + cols, :] = rhs.astype(F32)
             both = ref[below : below + 8, :].astype(F32)[i : i + 1]
             line = both[:, :128] + both[:, 128:]
         for side, start, far in zip(sides[kind], (6, 8 + cols), (5, 10 + cols)):
@@ -504,10 +508,11 @@
     outer_pairs = [(s, (s + 1) % slabs) for s in range(1, slabs, 2)]
     outer_pairs = outer_pairs + [(b, a) for a, b in outer_pairs]
     strip = shape((EDGE + 8, width), BF)
-    near, own, to_one, to_three = call(
+    row = shape((cols, width), BF)
+    near, own, far, to_one, to_three = call(
         near_kernel,
         "near",
-        (shape((cols, width), BF), shape((4 * cols + 8, width), BF), strip, strip),
+        (row, shape((3 * cols + 8, width), BF), row, strip, strip),
         tuple(
             pltpu.with_memory_space_constraint(x, pltpu.HBM)
             for x in (fluid_state, fluid_rhs, element_scale, displacement)
@@ -529,8 +534,8 @@
     from_one = lax.ppermute(to_one, "patch", patch_pairs(1))
     strips = [from_one[:EDGE], from_three[:EDGE]]
     thin = [from_one[:THIN], from_three[:THIN]]
-    rest = lax.ppermute(jnp.concatenate([inner_near] + thin), "slab", outer_pairs)
-    others = jnp.concatenate([own[:cols], own[2 * cols :]] + strips)
+    rest = lax.ppermute(jnp.concatenate([inner_near] + thin + [far]), "slab", outer_pairs)
+    others = jnp.concatenate([own[:cols], own[2 * cols :], far] + strips)
     others, _ = lax.optimization_barrier((others, inner_near))
     inner = lax.ppermute(others, "slab", inner_pairs)
     relay = lax.ppermute(outer[:cols], "slab", inner_pairs)

time: 53 us -> 52.4 us (0.989)
  starting transfers between devices: 24 us -> 23 us
    ppermute x1, waiting for transfers between devices: 5.4 us -> 6.41 us  [shards(): lax.ppermute(jnp.concatenate([inner_near] + thin + [far]), 'slab', outer_...]
    all_to_all x1, starting transfers between devices: 7.83 us -> 6.85 us  [exchange_and_relax(): lax.all_to_all(message.reshape(sources, 8, 128), ('slab', 'patch'), 0, 0,...]
    ppermute x1, waiting for transfers between devices: 0.67 us -> 0.01 us  [shards(): outer = lax.ppermute(own, 'slab', outer_pairs)]
  transfers between devices with their start and end apart: 11 -> 11, of which waited for: 5 -> 4; matrix products, arithmetic and copies ran while one was open for 0% -> 0% of each run, Pallas kernels for 2% -> 3%
where the time goes in v9:
time: 52.4 us; the launch traced here: 52.2 us
  starting transfers between devices  23 us (44%)
  waiting for transfers between devices  18.2 us (35%)
  Pallas kernels  9.92 us (19%)
  between operations  0.97 us (2%)
    all_to_all x1, waiting for transfers between devices, exchange_and_relax(): lax.all_to_all(message.reshape(sources, 8, 128), ('slab', 'patch'), 0, 0,...  10.7 us
    ppermute x1, starting transfers between devices, shards(): outer = lax.ppermute(own, 'slab', outer_pairs)  6.86 us
    all_to_all x1, starting transfers between devices, exchange_and_relax(): lax.all_to_all(message.reshape(sources, 8, 128), ('slab', 'patch'), 0, 0,...  6.85 us
    ppermute x1, waiting for transfers between devices, shards(): lax.ppermute(jnp.concatenate([inner_near] + thin + [far]), 'slab', outer_...  6.41 us
    pallas_call x1, Pallas kernels, exchange_and_relax(): pl.pallas_call(owner_kernel, out_shape=(jax.ShapeDtypeStruct(displacement...  4.4 us
    pallas_call x3, Pallas kernels, call(): pl.pallas_call(kernel, out_shape=out_shape, in_specs=in_specs or vmem(len...  4.27 us
    ppermute x1, starting transfers between devices, shards(): lax.ppermute(jnp.concatenate([inner_near] + thin + [far]), 'slab', outer_...  2.58 us
    ppermute x3, starting transfers between devices, exchange_and_relax(): lax.ppermute(replies[d], 'patch', patch_pairs(d))  2.22 us
  transfers between devices with their start and end apart: 11, of which 4 were waited for; matrix products, arithmetic and copies ran while one was open for 0% of the time, Pallas kernels for 3%

profile of v9, /device:TPU:1, one launch (start us, length us, event | category | flops | bytes accessed | tf_op | source)
XLA Modules:
  0.0 52.2 jit_solution(15956815327989163421)
XLA Ops:
  0.6 0.0 copy-start.4
  0.6 0.0 copy-start.5
  0.7 0.0 copy-start.6
  0.7 1.2 %near.1 = (bf16[64,256]{1,0:T(8,128)(2,1)S(1)}, bf16[200,256]{1,0:T(8,128)(2,1)S(1)}, bf16[64,256]{1,0:T(8,128)(2,1)S(1)}, bf16[24,256]{1,0:T(8,128)(2,1)S(1)}, bf16[24,256]{1,0:T(8,128)(2,1)S(1)}) custom-call(f32[2,64,256]{2,1,0:T(8,128)} %state_ref.1, f32[2,64,256]{2,1,0:T(8,128)} %rhs_ref.1, f32[2,64]{1,0:T(2,128)} %scale_ref.1, f32[3,64,128]{2,1,0:T(8,128)} %disp_ref.3), custom_call_target="tpu_custom_call" | custom-call | tf_op jit(solution)/shard_map/near/pallas_call | solution.py:477
  1.9 1.5 %collective-permute-start = (bf16[24,256]{1,0:T(8,128)(2,1)S(1)}, bf16[24,256]{1,0:T(8,128)(2,1)S(1)}, u32[]{:S(2)}, u32[]{:S(2)}) collective-permute-start(bf16[24,256]{1,0:T(8,128)(2,1)S(1)} %get-tuple-element.18), channel_id=1, source_target_pairs={{0,1},{1,0},{2,3},{3,2},{4,5},{5,4},{6,7},{7,6},{8,9},{9,8},{10,11... | collective-permute-start | bytes 36872 | tf_op jit(solution)/shard_map/ppermute | solution.py:534
  3.4 1.3 %collective-permute-start.1 = (bf16[24,256]{1,0:T(8,128)(2,1)S(1)}, bf16[24,256]{1,0:T(8,128)(2,1)S(1)}, u32[]{:S(2)}, u32[]{:S(2)}) collective-permute-start(bf16[24,256]{1,0:T(8,128)(2,1)S(1)} %get-tuple-element.19), channel_id=1, source_target_pairs={{0,3},{1,2},{2,1},{3,0},{4,7},{5,6},{6,5},{7,4},{8,11},{9,10},{10,... | collective-permute-start | bytes 36872 | tf_op jit(solution)/shard_map/ppermute | solution.py:533
  4.7 1.6 %collective-permute-start.2 = (bf16[64,256]{1,0:T(8,128)(2,1)S(1)}, bf16[64,256]{1,0:T(8,128)(2,1)S(1)}, u32[]{:S(2)}, u32[]{:S(2)}) collective-permute-start(bf16[64,256]{1,0:T(8,128)(2,1)S(1)} %get-tuple-element.20), channel_id=1, source_target_pairs={{0,4},{4,0},{8,12},{12,8},{16,20},{20,16},{24,28},{28,24},{32,36},... | collective-permute-start | bytes 98312 | tf_op jit(solution)/shard_map/ppermute | solution.py:532
  6.3 6.9 %collective-permute-start.4 = (bf16[200,256]{1,0:T(8,128)(2,1)S(1)}, bf16[200,256]{1,0:T(8,128)(2,1)S(1)}, u32[]{:S(2)}, u32[]{:S(2)}) collective-permute-start(bf16[200,256]{1,0:T(8,128)(2,1)S(1)} %get-tuple-element.21), channel_id=1, source_target_pairs={{4,8},{12,16},{20,24},{28,32},{36,40},{44,48},{52,56},{60,64},{68,... | collective-permute-start | bytes 307208 | tf_op jit(solution)/shard_map/ppermute | solution.py:531
  13.2 0.0 collective-permute-done.one_ref
  13.2 0.0 copy-start.8
  13.2 0.0 copy-start.9
  13.2 0.0 copy-start.1
  13.3 0.0 copy-start.2
  13.3 0.0 collective-permute-done.1.three_ref
  13.3 0.0 collective-permute-done.2.near_ref
  13.3 0.1 collective-permute-start.3
  13.4 0.0 copy-start.10
  13.4 0.0 copy-start.11
  13.5 0.0 copy-start.12
  13.5 2.6 %collective-permute-start.5 = (bf16[144,256]{1,0:T(8,128)(2,1)S(1)}, bf16[144,256]{1,0:T(8,128)(2,1)S(1)}, u32[]{:S(2)}, u32[]{:S(2)}) collective-permute-start(bf16[144,256]{1,0:T(8,128)(2,1)S(1)} %pad_maximum_fusion), channel_id=1, source_target_pairs={{4,8},{12,16},{20,24},{28,32},{36,40},{44,48},{52,56},{60,64},{68,... | collective-permute-start | bytes 221192 | tf_op jit(solution)/shard_map/ppermute | solution.py:537
  16.1 0.0 collective-permute-done.4.outer_ref
  16.1 0.0 collective-permute-start.6
  16.1 6.4 %collective-permute-done.5.rest_ref = bf16[144,256]{1,0:T(8,128)(2,1)S(1)} collective-permute-done((bf16[144,256]{1,0:T(8,128)(2,1)S(1)}, bf16[144,256]{1,0:T(8,128)(2,1)S(1)}, u32[]{:S(2)}, u32[]{:S(2)}) %collective-permute-start.5) | collective-permute-done | bytes 73760 | tf_op jit(solution)/shard_map/ppermute | solution.py:537
  22.5 0.0 collective-permute-done.6.relay_ref
  22.5 0.0 collective-permute-done.3.inner_ref
  22.5 0.0 copy-done.4
  22.5 0.0 copy-done.5
  22.5 0.0 copy-done.6
  22.5 0.0 copy-done.3
  22.5 0.0 copy-done.8
  22.5 0.0 copy-done.9
  22.6 2.4 %sweep.1 = (f32[2,64,256]{2,1,0:T(8,128)S(1)}, bf16[32,4,8,128]{3,2,1,0:T(8,128)(2,1)}) custom-call(f32[2,64,256]{2,1,0:T(8,128)S(1)} %copy-done.1, f32[2,64,256]{2,1,0:T(8,128)S(1)} %copy-done.2, f32[2,64]{1,0:T(2,128)S(1)} %copy-done.10, bf16[64,256]{1,0:T(8,128)(2,1)S(1)} %collective-permute-done.2.near_ref, ...), custom_call_target="tpu_custom_call" | custom-call | tf_op jit(solution)/shard_map/sweep/pallas_call | solution.py:477
  25.0 0.0 copy-start
  25.0 0.0 copy-start.7
  25.0 6.9 %all-to-all-start = ((bf16[128,8,128]{2,1,0:T(8,128)(2,1)}), bf16[128,8,128]{2,1,0:T(8,128)(2,1)S(1)}, u32[]{:S(2)}, u32[]{:S(2)}) async-start(bf16[128,8,128]{2,1,0:T(8,128)(2,1)} %bitcast), calls=%async_computation | async-start | bytes 524288 | tf_op jit(solution)/shard_map/all_to_all | solution.py:199
  31.8 0.0 copy-done
  31.9 0.0 copy-done.7
  31.9 0.7 %shell.1 = (f32[3,64,128]{2,1,0:T(8,128)S(1)}, f32[2,64,256]{2,1,0:T(8,128)}) custom-call(bf16[8,256]{1,0:T(8,128)(2,1)S(1)} %get-tuple-element.34.one_ref, bf16[8,256]{1,0:T(8,128)(2,1)S(1)} %get-tuple-element.36.three_ref, f32[3,64,128]{2,1,0:T(8,128)S(1)} %copy-done, f32[64,128]{1,0:T(8,128)S(1)} %copy-done.7, f32[2,64,256]{2,1,0:T(8,128)S(1)} %get-tuple-element.24.state_ref), custom_call_target="tpu_custom_call" | custom-call | tf_op jit(solution)/shard_map/shell/pallas_call | solution.py:477
  32.5 10.7 %all-to-all-done.got_ref = bf16[128,8,128]{2,1,0:T(8,128)(2,1)S(1)} async-done(((bf16[128,8,128]{2,1,0:T(8,128)(2,1)}), bf16[128,8,128]{2,1,0:T(8,128)(2,1)S(1)}, u32[]{:S(2)}, u32[]{:S(2)}) %all-to-all-start) | async-done | bytes 262176 | tf_op jit(solution)/shard_map/all_to_all | solution.py:199
  43.2 4.4 %owner.1 = (f32[3,64,128]{2,1,0:T(8,128)S(1)}, f32[8,256]{1,0:T(8,128)S(1)}, f32[8,256]{1,0:T(8,128)S(1)}, f32[8,256]{1,0:T(8,128)S(1)}, f32[8,256]{1,0:T(8,128)S(1)}) custom-call(bf16[128,8,128]{2,1,0:T(8,128)(2,1)S(1)} %all-to-all-done.got_ref, f32[3,64,128]{2,1,0:T(8,128)S(1)} %copy-done, f32[64,128]{1,0:T(8,128)S(1)} %copy-done.7, ...), custom_call_target="tpu_custom_call" | custom-call | tf_op jit(solution)/shard_map/owner/pallas_call | solution.py:203
  47.6 0.5 collective-permute-start.7
  48.1 0.3 collective-permute-start.8
  48.4 1.4 %collective-permute-start.9 = (f32[8,256]{1,0:T(8,128)S(1)}, f32[8,256]{1,0:T(8,128)S(1)}, u32[]{:S(2)}, u32[]{:S(2)}) collective-permute-start(f32[8,256]{1,0:T(8,128)S(1)} %get-tuple-element.32), channel_id=1, source_target_pairs={{0,3},{1,2},{2,1},{3,0},{4,7},{5,6},{6,5},{7,4},{8,11},{9,10},{10,... | collective-permute-start | bytes 24584 | tf_op jit(solution)/shard_map/ppermute | solution.py:216
  49.9 0.6 %store_shell.1 = f32[3,64,128]{2,1,0:T(8,128)} custom-call(f32[3,64,128]{2,1,0:T(8,128)S(1)} %get-tuple-element.28.value_ref), custom_call_target="tpu_custom_call" | custom-call | tf_op jit(solution)/shard_map/store_shell/pallas_call | solution.py:120
  50.5 0.0 collective-permute-done.7.r1
  50.5 0.1 collective-permute-done.8.r2
  50.7 0.9 %collective-permute-done.9.r3 = f32[8,256]{1,0:T(8,128)S(1)} collective-permute-done((f32[8,256]{1,0:T(8,128)S(1)}, f32[8,256]{1,0:T(8,128)S(1)}, u32[]{:S(2)}, u32[]{:S(2)}) %collective-permute-start.9) | collective-permute-done | bytes 8224 | tf_op jit(solution)/shard_map/ppermute | solution.py:216
  51.6 0.6 %finish.1 = f32[3,1,1,1024]{3,2,1,0:T(1,128)} custom-call(f32[8,256]{1,0:T(8,128)S(1)} %get-tuple-element.29.r0, f32[8,256]{1,0:T(8,128)S(1)} %collective-permute-done.7.r1, f32[8,256]{1,0:T(8,128)S(1)} %collective-permute-done.8.r2, f32[8,256]{1,0:T(8,128)S(1)} %collective-permute-done.9.r3), custom_call_target="tpu_custom_call" | custom-call | tf_op jit(solution)/shard_map/finish/pallas_call | solution.py:218
  (15 shorter events, 0.0 us)
Async XLA Ops:
  0.6 21.9 %copy-start.4 = (bf16[256,256]{1,0:T(8,128)(2,1)S(1)}, bf16[256,256]{1,0:T(8,128)(2,1)}, u32[]{:S(2)}) copy-start(bf16[256,256]{1,0:T(8,128)(2,1)} %x_ref.1) | copy-start | bytes 393220
  0.6 21.8 %copy-start.5 = (bf16[256,256]{1,0:T(8,128)(2,1)S(1)}, bf16[256,256]{1,0:T(8,128)(2,1)}, u32[]{:S(2)}) copy-start(bf16[256,256]{1,0:T(8,128)(2,1)} %y_ref.1) | copy-start | bytes 393220
  0.7 21.8 %copy-start.6 = (bf16[256,256]{1,0:T(8,128)(2,1)S(1)}, bf16[256,256]{1,0:T(8,128)(2,1)}, u32[]{:S(2)}) copy-start(bf16[256,256]{1,0:T(8,128)(2,1)} %inverse_ref.1) | copy-start | bytes 393220
  1.9 11.3 %collective-permute-start = (bf16[24,256]{1,0:T(8,128)(2,1)S(1)}, bf16[24,256]{1,0:T(8,128)(2,1)S(1)}, u32[]{:S(2)}, u32[]{:S(2)}) collective-permute-start(bf16[24,256]{1,0:T(8,128)(2,1)S(1)} %get-tuple-element.18), channel_id=1, source_target_pairs={{0,1},{1,0},{2,3},{3,2},{4,5},{5,4},{6,7},{7,6},{8,9},{9,8},{10,11... | collective-permute-start | bytes 36872 | tf_op jit(solution)/shard_map/ppermute | solution.py:534
  3.4 9.9 %collective-permute-start.1 = (bf16[24,256]{1,0:T(8,128)(2,1)S(1)}, bf16[24,256]{1,0:T(8,128)(2,1)S(1)}, u32[]{:S(2)}, u32[]{:S(2)}) collective-permute-start(bf16[24,256]{1,0:T(8,128)(2,1)S(1)} %get-tuple-element.19), channel_id=1, source_target_pairs={{0,3},{1,2},{2,1},{3,0},{4,7},{5,6},{6,5},{7,4},{8,11},{9,10},{10,... | collective-permute-start | bytes 36872 | tf_op jit(solution)/shard_map/ppermute | solution.py:533
  4.7 8.6 %collective-permute-start.2 = (bf16[64,256]{1,0:T(8,128)(2,1)S(1)}, bf16[64,256]{1,0:T(8,128)(2,1)S(1)}, u32[]{:S(2)}, u32[]{:S(2)}) collective-permute-start(bf16[64,256]{1,0:T(8,128)(2,1)S(1)} %get-tuple-element.20), channel_id=1, source_target_pairs={{0,4},{4,0},{8,12},{12,8},{16,20},{20,16},{24,28},{28,24},{32,36},... | collective-permute-start | bytes 98312 | tf_op jit(solution)/shard_map/ppermute | solution.py:532
  6.3 9.7 %collective-permute-start.4 = (bf16[200,256]{1,0:T(8,128)(2,1)S(1)}, bf16[200,256]{1,0:T(8,128)(2,1)S(1)}, u32[]{:S(2)}, u32[]{:S(2)}) collective-permute-start(bf16[200,256]{1,0:T(8,128)(2,1)S(1)} %get-tuple-element.21), channel_id=1, source_target_pairs={{4,8},{12,16},{20,24},{28,32},{36,40},{44,48},{52,56},{60,64},{68,... | collective-permute-start | bytes 307208 | tf_op jit(solution)/shard_map/ppermute | solution.py:531
  13.2 9.3 %copy-start.3 = (bf16[256,256]{1,0:T(8,128)(2,1)S(1)}, bf16[256,256]{1,0:T(8,128)(2,1)}, u32[]{:S(2)}) copy-start(bf16[256,256]{1,0:T(8,128)(2,1)} %matrix_ref.1) | copy-start | bytes 393220
  13.2 9.3 %copy-start.8 = (s32[1,1,1024]{2,1,0:T(1,128)S(1)}, s32[1,1,1024]{2,1,0:T(1,128)}, u32[]{:S(2)}) copy-start(s32[1,1,1024]{2,1,0:T(1,128)} %elem_hbm.1) | copy-start | bytes 12292
  13.2 9.3 %copy-start.9 = (s32[1,1,1024]{2,1,0:T(1,128)S(1)}, s32[1,1,1024]{2,1,0:T(1,128)}, u32[]{:S(2)}) copy-start(s32[1,1,1024]{2,1,0:T(1,128)} %point_hbm.1) | copy-start | bytes 12292
  13.2 9.3 %copy-start.1 = (f32[2,64,256]{2,1,0:T(8,128)S(1)}, f32[2,64,256]{2,1,0:T(8,128)}, u32[]{:S(2)}) copy-start(f32[2,64,256]{2,1,0:T(8,128)} %state_ref.1) | copy-start | bytes 393220
  13.3 9.3 %copy-start.2 = (f32[2,64,256]{2,1,0:T(8,128)S(1)}, f32[2,64,256]{2,1,0:T(8,128)}, u32[]{:S(2)}) copy-start(f32[2,64,256]{2,1,0:T(8,128)} %rhs_ref.1) | copy-start | bytes 393220
  13.3 9.2 %collective-permute-start.3 = (bf16[232,256]{1,0:T(8,128)(2,1)S(1)}, bf16[232,256]{1,0:T(8,128)(2,1)S(1)}, u32[]{:S(2)}, u32[]{:S(2)}) collective-permute-start(bf16[232,256]{1,0:T(8,128)(2,1)S(1)} %constant_dynamic-update-slice_fusion), channel_id=1, source_target_pairs={{0,4},{4,0},{8,12},{12,8},{16,20},{20,16},{24,28},{28,24},{32,36},... | collective-permute-start | bytes 356360 | tf_op jit(solution)/shard_map/ppermute | solution.py:540
  13.4 9.1 %copy-start.10 = (f32[2,64]{1,0:T(2,128)S(1)}, f32[2,64]{1,0:T(2,128)}, u32[]{:S(2)}) copy-start(f32[2,64]{1,0:T(2,128)} %scale_ref.1) | copy-start | bytes 1540
  13.4 9.1 %copy-start.11 = (bf16[3,256]{1,0:T(4,128)(2,1)S(1)}, bf16[3,256]{1,0:T(4,128)(2,1)}, u32[]{:S(2)}) copy-start(bf16[3,256]{1,0:T(4,128)(2,1)} %tmap_ref.1) | copy-start | bytes 4612
  13.5 9.1 %copy-start.12 = (s32[1,1,4]{2,1,0:T(1,128)S(1)}, s32[1,1,4]{2,1,0:T(1,128)}, u32[]{:S(2)}) copy-start(s32[1,1,4]{2,1,0:T(1,128)} %count_hbm.1) | copy-start | bytes 52
  13.5 9.0 %collective-permute-start.5 = (bf16[144,256]{1,0:T(8,128)(2,1)S(1)}, bf16[144,256]{1,0:T(8,128)(2,1)S(1)}, u32[]{:S(2)}, u32[]{:S(2)}) collective-permute-start(bf16[144,256]{1,0:T(8,128)(2,1)S(1)} %pad_maximum_fusion), channel_id=1, source_target_pairs={{4,8},{12,16},{20,24},{28,32},{36,40},{44,48},{52,56},{60,64},{68,... | collective-permute-start | bytes 221192 | tf_op jit(solution)/shard_map/ppermute | solution.py:537
  16.1 6.4 %collective-permute-start.6 = (bf16[64,256]{1,0:T(8,128)(2,1)S(1)}, bf16[64,256]{1,0:T(8,128)(2,1)S(1)}, u32[]{:S(2)}, u32[]{:S(2)}) collective-permute-start(bf16[64,256]{1,0:T(8,128)(2,1)S(1)} %slice.42), channel_id=1, source_target_pairs={{0,4},{4,0},{8,12},{12,8},{16,20},{20,16},{24,28},{28,24},{32,36},... | collective-permute-start | bytes 98312 | tf_op jit(solution)/shard_map/ppermute | solution.py:541
  25.0 6.9 %copy-start = (f32[3,64,128]{2,1,0:T(8,128)S(1)}, f32[3,64,128]{2,1,0:T(8,128)}, u32[]{:S(2)}) copy-start(f32[3,64,128]{2,1,0:T(8,128)} %disp_ref.3) | copy-start | bytes 294916
  25.0 6.9 %copy-start.7 = (f32[64,128]{1,0:T(8,128)S(1)}, f32[64,128]{1,0:T(8,128)}, u32[]{:S(2)}) copy-start(f32[64,128]{1,0:T(8,128)} %stiff_ref.3) | copy-start | bytes 98308
  25.0 18.2 %all-to-all-start = ((bf16[128,8,128]{2,1,0:T(8,128)(2,1)}), bf16[128,8,128]{2,1,0:T(8,128)(2,1)S(1)}, u32[]{:S(2)}, u32[]{:S(2)}) async-start(bf16[128,8,128]{2,1,0:T(8,128)(2,1)} %bitcast), calls=%async_computation | async-start | bytes 524288 | tf_op jit(solution)/shard_map/all_to_all | solution.py:199
  47.6 2.9 %collective-permute-start.7 = (f32[8,256]{1,0:T(8,128)S(1)}, f32[8,256]{1,0:T(8,128)S(1)}, u32[]{:S(2)}, u32[]{:S(2)}) collective-permute-start(f32[8,256]{1,0:T(8,128)S(1)} %get-tuple-element.30), channel_id=1, source_target_pairs={{0,1},{1,0},{2,3},{3,2},{4,5},{5,4},{6,7},{7,6},{8,9},{9,8},{10,11... | collective-permute-start | bytes 24584 | tf_op jit(solution)/shard_map/ppermute | solution.py:216
  48.1 2.5 %collective-permute-start.8 = (f32[8,256]{1,0:T(8,128)S(1)}, f32[8,256]{1,0:T(8,128)S(1)}, u32[]{:S(2)}, u32[]{:S(2)}) collective-permute-start(f32[8,256]{1,0:T(8,128)S(1)} %get-tuple-element.31), channel_id=1, source_target_pairs={{0,2},{1,3},{2,0},{3,1},{4,6},{5,7},{6,4},{7,5},{8,10},{9,11},{10,... | collective-permute-start | bytes 24584 | tf_op jit(solution)/shard_map/ppermute | solution.py:216
  48.4 3.1 %collective-permute-start.9 = (f32[8,256]{1,0:T(8,128)S(1)}, f32[8,256]{1,0:T(8,128)S(1)}, u32[]{:S(2)}, u32[]{:S(2)}) collective-permute-start(f32[8,256]{1,0:T(8,128)S(1)} %get-tuple-element.32), channel_id=1, source_target_pairs={{0,3},{1,2},{2,1},{3,0},{4,7},{5,6},{6,5},{7,4},{8,11},{9,10},{10,... | collective-permute-start | bytes 24584 | tf_op jit(solution)/shard_map/ppermute | solution.py:216

commit v10 on v9

--- a/solution.py
+++ b/solution.py
@@ -55,18 +55,11 @@
     return row, code - 128.0
 
 
-def owner_kernel(
-    got_ref, disp_ref, stiff_ref, kd_ref, new_ref, r0, r1, r2, r3, row_ref, lane_ref
-):
-    replies = (r0, r1, r2, r3)
+def owner_kernel(got_ref, disp_ref, stiff_ref, kd_ref, new_ref, r0, r1, r2, r3, pick_ref):
     sources = got_ref.shape[0]
     rows = disp_ref.shape[1]
     patch = lax.axis_index("patch")
     first = lax.axis_index("slab") * 4
-    for h in range(2):
-        row, lane = decode(got_ref[:, 6 + h, :].astype(F32))
-        row_ref[h] = row
-        lane_ref[h] = lane
     row_ids = iota((rows, 128), 0).astype(F32).astype(BF)
     lane_ids = iota((128, 128), 0).astype(F32).astype(BF)
     none = jnp.zeros((rows, 128), BF)
@@ -74,8 +67,9 @@
     total = jnp.zeros((3 * rows, 128), F32)
     group = 8
     for base in range(0, sources, group):
-        row8 = [row_ref[h, base : base + group, :].astype(BF) for h in range(2)]
-        lane8 = [lane_ref[h, base : base + group, :].astype(BF) for h in range(2)]
+        codes = [decode(got_ref[base : base + group, 6 + h, :].astype(F32)) for h in range(2)]
+        row8 = [row.astype(BF) for row, _ in codes]
+        lane8 = [lane.astype(BF) for _, lane in codes]
         for g in range(group):
             vals = got_ref[base + g]
             left, right = [], []
@@ -95,19 +89,27 @@
     flat = new.reshape(3 * rows, 128)
     high = flat.astype(BF)
     low = (flat - high.astype(F32)).astype(BF)
-    row_ids = iota((rows, 128), 0).astype(F32)
+    both = jnp.concatenate([high, low], axis=0)
     for d in range(4):
-        src = first + (patch ^ d)
         for h in range(2):
-            row = row_ref[h, pl.ds(src, 1), :]
-            lane = lane_ref[h, pl.ds(src, 1), :]
-            hot = jnp.where(lane_ids == lane.astype(BF), ones, zeros)
-            picked = jnp.dot(high, hot, preferred_element_type=F32)
-            picked += jnp.dot(low, hot, preferred_element_type=F32)
-            mask = row_ids == row
-            for c in range(3):
-                part = jnp.where(mask, picked[c * rows : (c + 1) * rows], 0.0)
-                replies[d][c : c + 1, h * 128 : (h + 1) * 128] = part.sum(axis=0, keepdims=True)
+            code = got_ref[pl.ds(first + (patch ^ d), 1), 6 + h, :]
+            pick_ref[2 * d + h : 2 * d + h + 1, :] = code.astype(F32)
+    row, lane = decode(pick_ref[...])
+    wide_ids = iota((rows, 256), 0).astype(F32)
+    for d, reply in enumerate((r0, r1, r2, r3)):
+        at = 2 * d
+        hot = jnp.concatenate(
+            [
+                jnp.where(lane_ids == lane[at + h : at + h + 1].astype(BF), ones, zeros)
+                for h in range(2)
+            ],
+            axis=1,
+        )
+        picked = jnp.dot(both, hot, preferred_element_type=F32)
+        mask = wide_ids == jnp.concatenate([row[at : at + 1], row[at + 1 : at + 2]], axis=1)
+        for c in range(3):
+            part = picked[c * rows : (c + 1) * rows] + picked[(c + 3) * rows : (c + 4) * rows]
+            reply[c : c + 1, :] = jnp.where(mask, part, 0.0).sum(axis=0, keepdims=True)
 
 
 def store_kernel(value_ref, out_ref, sem):
@@ -205,10 +207,7 @@
         out_shape=(jax.ShapeDtypeStruct(displacement.shape, F32),) + (reply,) * 4,
         in_specs=vmem(4),
         out_specs=vmem(5),
-        scratch_shapes=[
-            pltpu.VMEM((2, sources, 128), F32),
-            pltpu.VMEM((2, sources, 128), F32),
-        ],
+        scratch_shapes=[pltpu.VMEM((8, 128), F32)],
         compiler_params=params(),
         name="owner",
     )(got, displacement, stiffness, kd)

time: 52.4 us -> 52.1 us (level)
  no operation moved by 1% of the time
where the time goes in v10:
time: 52.1 us; the launch traced here: 51.9 us
  starting transfers between devices  23 us (44%)
  waiting for transfers between devices  18.1 us (35%)
  Pallas kernels  9.66 us (19%)
  between operations  0.98 us (2%)
    all_to_all x1, waiting for transfers between devices, exchange_and_relax(): lax.all_to_all(message.reshape(sources, 8, 128), ('slab', 'patch'), 0, 0,...  10.7 us
    ppermute x1, starting transfers between devices, shards(): outer = lax.ppermute(own, 'slab', outer_pairs)  6.86 us
    all_to_all x1, starting transfers between devices, exchange_and_relax(): lax.all_to_all(message.reshape(sources, 8, 128), ('slab', 'patch'), 0, 0,...  6.85 us
    ppermute x1, waiting for transfers between devices, shards(): lax.ppermute(jnp.concatenate([inner_near] + thin + [far]), 'slab', outer_...  6.41 us
    pallas_call x3, Pallas kernels, call(): pl.pallas_call(kernel, out_shape=out_shape, in_specs=in_specs or vmem(len...  4.27 us
    pallas_call x1, Pallas kernels, exchange_and_relax(): pl.pallas_call(owner_kernel, out_shape=(jax.ShapeDtypeStruct(displacement...  4.13 us
    ppermute x1, starting transfers between devices, shards(): lax.ppermute(jnp.concatenate([inner_near] + thin + [far]), 'slab', outer_...  2.58 us
    ppermute x3, starting transfers between devices, exchange_and_relax(): lax.ppermute(replies[d], 'patch', patch_pairs(d))  2.22 us
  transfers between devices with their start and end apart: 11, of which 4 were waited for; matrix products, arithmetic and copies ran while one was open for 0% of the time, Pallas kernels for 3%

profile of v10, /device:TPU:1, one launch (start us, length us, event | category | flops | bytes accessed | tf_op | source)
XLA Modules:
  0.0 51.9 jit_solution(9941797544113090616)
XLA Ops:
  0.6 0.0 copy-start.4
  0.6 0.0 copy-start.5
  0.7 0.0 copy-start.6
  0.7 1.2 %near.1 = (bf16[64,256]{1,0:T(8,128)(2,1)S(1)}, bf16[200,256]{1,0:T(8,128)(2,1)S(1)}, bf16[64,256]{1,0:T(8,128)(2,1)S(1)}, bf16[24,256]{1,0:T(8,128)(2,1)S(1)}, bf16[24,256]{1,0:T(8,128)(2,1)S(1)}) custom-call(f32[2,64,256]{2,1,0:T(8,128)} %state_ref.1, f32[2,64,256]{2,1,0:T(8,128)} %rhs_ref.1, f32[2,64]{1,0:T(2,128)} %scale_ref.1, f32[3,64,128]{2,1,0:T(8,128)} %disp_ref.3), custom_call_target="tpu_custom_call" | custom-call | tf_op jit(solution)/shard_map/near/pallas_call | solution.py:476
  1.9 1.5 %collective-permute-start = (bf16[24,256]{1,0:T(8,128)(2,1)S(1)}, bf16[24,256]{1,0:T(8,128)(2,1)S(1)}, u32[]{:S(2)}, u32[]{:S(2)}) collective-permute-start(bf16[24,256]{1,0:T(8,128)(2,1)S(1)} %get-tuple-element.18), channel_id=1, source_target_pairs={{0,1},{1,0},{2,3},{3,2},{4,5},{5,4},{6,7},{7,6},{8,9},{9,8},{10,11... | collective-permute-start | bytes 36872 | tf_op jit(solution)/shard_map/ppermute | solution.py:533
  3.4 1.3 %collective-permute-start.1 = (bf16[24,256]{1,0:T(8,128)(2,1)S(1)}, bf16[24,256]{1,0:T(8,128)(2,1)S(1)}, u32[]{:S(2)}, u32[]{:S(2)}) collective-permute-start(bf16[24,256]{1,0:T(8,128)(2,1)S(1)} %get-tuple-element.19), channel_id=1, source_target_pairs={{0,3},{1,2},{2,1},{3,0},{4,7},{5,6},{6,5},{7,4},{8,11},{9,10},{10,... | collective-permute-start | bytes 36872 | tf_op jit(solution)/shard_map/ppermute | solution.py:532
  4.7 1.6 %collective-permute-start.2 = (bf16[64,256]{1,0:T(8,128)(2,1)S(1)}, bf16[64,256]{1,0:T(8,128)(2,1)S(1)}, u32[]{:S(2)}, u32[]{:S(2)}) collective-permute-start(bf16[64,256]{1,0:T(8,128)(2,1)S(1)} %get-tuple-element.20), channel_id=1, source_target_pairs={{0,4},{4,0},{8,12},{12,8},{16,20},{20,16},{24,28},{28,24},{32,36},... | collective-permute-start | bytes 98312 | tf_op jit(solution)/shard_map/ppermute | solution.py:531
  6.3 6.9 %collective-permute-start.4 = (bf16[200,256]{1,0:T(8,128)(2,1)S(1)}, bf16[200,256]{1,0:T(8,128)(2,1)S(1)}, u32[]{:S(2)}, u32[]{:S(2)}) collective-permute-start(bf16[200,256]{1,0:T(8,128)(2,1)S(1)} %get-tuple-element.21), channel_id=1, source_target_pairs={{4,8},{12,16},{20,24},{28,32},{36,40},{44,48},{52,56},{60,64},{68,... | collective-permute-start | bytes 307208 | tf_op jit(solution)/shard_map/ppermute | solution.py:530
  13.2 0.0 collective-permute-done.one_ref
  13.2 0.0 copy-start.8
  13.2 0.0 copy-start.9
  13.2 0.0 copy-start.1
  13.3 0.0 copy-start.2
  13.3 0.0 collective-permute-done.1.three_ref
  13.3 0.0 collective-permute-done.2.near_ref
  13.3 0.1 collective-permute-start.3
  13.4 0.0 copy-start.10
  13.4 0.0 copy-start.11
  13.5 0.0 copy-start.12
  13.5 2.6 %collective-permute-start.5 = (bf16[144,256]{1,0:T(8,128)(2,1)S(1)}, bf16[144,256]{1,0:T(8,128)(2,1)S(1)}, u32[]{:S(2)}, u32[]{:S(2)}) collective-permute-start(bf16[144,256]{1,0:T(8,128)(2,1)S(1)} %pad_maximum_fusion), channel_id=1, source_target_pairs={{4,8},{12,16},{20,24},{28,32},{36,40},{44,48},{52,56},{60,64},{68,... | collective-permute-start | bytes 221192 | tf_op jit(solution)/shard_map/ppermute | solution.py:536
  16.1 0.0 collective-permute-done.4.outer_ref
  16.1 0.0 collective-permute-start.6
  16.1 6.4 %collective-permute-done.5.rest_ref = bf16[144,256]{1,0:T(8,128)(2,1)S(1)} collective-permute-done((bf16[144,256]{1,0:T(8,128)(2,1)S(1)}, bf16[144,256]{1,0:T(8,128)(2,1)S(1)}, u32[]{:S(2)}, u32[]{:S(2)}) %collective-permute-start.5) | collective-permute-done | bytes 73760 | tf_op jit(solution)/shard_map/ppermute | solution.py:536
  22.5 0.0 collective-permute-done.6.relay_ref
  22.5 0.0 collective-permute-done.3.inner_ref
  22.5 0.0 copy-done.4
  22.5 0.0 copy-done.5
  22.5 0.0 copy-done.6
  22.5 0.0 copy-done.3
  22.5 0.0 copy-done.8
  22.5 0.0 copy-done.9
  22.5 0.0 copy-done.1
  22.5 0.0 copy-done.2
  22.6 2.4 %sweep.1 = (f32[2,64,256]{2,1,0:T(8,128)S(1)}, bf16[32,4,8,128]{3,2,1,0:T(8,128)(2,1)}) custom-call(f32[2,64,256]{2,1,0:T(8,128)S(1)} %copy-done.1, f32[2,64,256]{2,1,0:T(8,128)S(1)} %copy-done.2, f32[2,64]{1,0:T(2,128)S(1)} %copy-done.10, bf16[64,256]{1,0:T(8,128)(2,1)S(1)} %collective-permute-done.2.near_ref, ...), custom_call_target="tpu_custom_call" | custom-call | tf_op jit(solution)/shard_map/sweep/pallas_call | solution.py:476
  25.0 0.0 copy-start
  25.0 0.0 copy-start.7
  25.0 6.9 %all-to-all-start = ((bf16[128,8,128]{2,1,0:T(8,128)(2,1)}), bf16[128,8,128]{2,1,0:T(8,128)(2,1)S(1)}, u32[]{:S(2)}, u32[]{:S(2)}) async-start(bf16[128,8,128]{2,1,0:T(8,128)(2,1)} %bitcast), calls=%async_computation | async-start | bytes 524288 | tf_op jit(solution)/shard_map/all_to_all | solution.py:201
  31.9 0.7 %shell.1 = (f32[3,64,128]{2,1,0:T(8,128)S(1)}, f32[2,64,256]{2,1,0:T(8,128)}) custom-call(bf16[8,256]{1,0:T(8,128)(2,1)S(1)} %get-tuple-element.34.one_ref, bf16[8,256]{1,0:T(8,128)(2,1)S(1)} %get-tuple-element.36.three_ref, f32[3,64,128]{2,1,0:T(8,128)S(1)} %copy-done, f32[64,128]{1,0:T(8,128)S(1)} %copy-done.7, f32[2,64,256]{2,1,0:T(8,128)S(1)} %get-tuple-element.24.state_ref), custom_call_target="tpu_custom_call" | custom-call | tf_op jit(solution)/shard_map/shell/pallas_call | solution.py:476
  32.5 10.7 %all-to-all-done.got_ref = bf16[128,8,128]{2,1,0:T(8,128)(2,1)S(1)} async-done(((bf16[128,8,128]{2,1,0:T(8,128)(2,1)}), bf16[128,8,128]{2,1,0:T(8,128)(2,1)S(1)}, u32[]{:S(2)}, u32[]{:S(2)}) %all-to-all-start) | async-done | bytes 262176 | tf_op jit(solution)/shard_map/all_to_all | solution.py:201
  43.2 4.1 %owner.1 = (f32[3,64,128]{2,1,0:T(8,128)S(1)}, f32[8,256]{1,0:T(8,128)S(1)}, f32[8,256]{1,0:T(8,128)S(1)}, f32[8,256]{1,0:T(8,128)S(1)}, f32[8,256]{1,0:T(8,128)S(1)}) custom-call(bf16[128,8,128]{2,1,0:T(8,128)(2,1)S(1)} %all-to-all-done.got_ref, f32[3,64,128]{2,1,0:T(8,128)S(1)} %copy-done, f32[64,128]{1,0:T(8,128)S(1)} %copy-done.7, ...), custom_call_target="tpu_custom_call" | custom-call | tf_op jit(solution)/shard_map/owner/pallas_call | solution.py:205
  47.4 0.5 collective-permute-start.7
  47.9 0.3 collective-permute-start.8
  48.2 1.4 %collective-permute-start.9 = (f32[8,256]{1,0:T(8,128)S(1)}, f32[8,256]{1,0:T(8,128)S(1)}, u32[]{:S(2)}, u32[]{:S(2)}) collective-permute-start(f32[8,256]{1,0:T(8,128)S(1)} %get-tuple-element.32), channel_id=1, source_target_pairs={{0,3},{1,2},{2,1},{3,0},{4,7},{5,6},{6,5},{7,4},{8,11},{9,10},{10,... | collective-permute-start | bytes 24584 | tf_op jit(solution)/shard_map/ppermute | solution.py:215
  49.6 0.6 %store_shell.1 = f32[3,64,128]{2,1,0:T(8,128)} custom-call(f32[3,64,128]{2,1,0:T(8,128)S(1)} %get-tuple-element.28.value_ref), custom_call_target="tpu_custom_call" | custom-call | tf_op jit(solution)/shard_map/store_shell/pallas_call | solution.py:122
  50.2 0.0 collective-permute-done.7.r1
  50.3 0.1 collective-permute-done.8.r2
  50.4 0.9 %collective-permute-done.9.r3 = f32[8,256]{1,0:T(8,128)S(1)} collective-permute-done((f32[8,256]{1,0:T(8,128)S(1)}, f32[8,256]{1,0:T(8,128)S(1)}, u32[]{:S(2)}, u32[]{:S(2)}) %collective-permute-start.9) | collective-permute-done | bytes 8224 | tf_op jit(solution)/shard_map/ppermute | solution.py:215
  51.3 0.6 %finish.1 = f32[3,1,1,1024]{3,2,1,0:T(1,128)} custom-call(f32[8,256]{1,0:T(8,128)S(1)} %get-tuple-element.29.r0, f32[8,256]{1,0:T(8,128)S(1)} %collective-permute-done.7.r1, f32[8,256]{1,0:T(8,128)S(1)} %collective-permute-done.8.r2, f32[8,256]{1,0:T(8,128)S(1)} %collective-permute-done.9.r3), custom_call_target="tpu_custom_call" | custom-call | tf_op jit(solution)/shard_map/finish/pallas_call | solution.py:217
  (15 shorter events, 0.0 us)
Async XLA Ops:
  0.6 21.9 %copy-start.4 = (bf16[256,256]{1,0:T(8,128)(2,1)S(1)}, bf16[256,256]{1,0:T(8,128)(2,1)}, u32[]{:S(2)}) copy-start(bf16[256,256]{1,0:T(8,128)(2,1)} %x_ref.1) | copy-start | bytes 393220
  0.6 21.8 %copy-start.5 = (bf16[256,256]{1,0:T(8,128)(2,1)S(1)}, bf16[256,256]{1,0:T(8,128)(2,1)}, u32[]{:S(2)}) copy-start(bf16[256,256]{1,0:T(8,128)(2,1)} %y_ref.1) | copy-start | bytes 393220
  0.7 21.8 %copy-start.6 = (bf16[256,256]{1,0:T(8,128)(2,1)S(1)}, bf16[256,256]{1,0:T(8,128)(2,1)}, u32[]{:S(2)}) copy-start(bf16[256,256]{1,0:T(8,128)(2,1)} %inverse_ref.1) | copy-start | bytes 393220
  1.9 11.3 %collective-permute-start = (bf16[24,256]{1,0:T(8,128)(2,1)S(1)}, bf16[24,256]{1,0:T(8,128)(2,1)S(1)}, u32[]{:S(2)}, u32[]{:S(2)}) collective-permute-start(bf16[24,256]{1,0:T(8,128)(2,1)S(1)} %get-tuple-element.18), channel_id=1, source_target_pairs={{0,1},{1,0},{2,3},{3,2},{4,5},{5,4},{6,7},{7,6},{8,9},{9,8},{10,11... | collective-permute-start | bytes 36872 | tf_op jit(solution)/shard_map/ppermute | solution.py:533
  3.4 9.9 %collective-permute-start.1 = (bf16[24,256]{1,0:T(8,128)(2,1)S(1)}, bf16[24,256]{1,0:T(8,128)(2,1)S(1)}, u32[]{:S(2)}, u32[]{:S(2)}) collective-permute-start(bf16[24,256]{1,0:T(8,128)(2,1)S(1)} %get-tuple-element.19), channel_id=1, source_target_pairs={{0,3},{1,2},{2,1},{3,0},{4,7},{5,6},{6,5},{7,4},{8,11},{9,10},{10,... | collective-permute-start | bytes 36872 | tf_op jit(solution)/shard_map/ppermute | solution.py:532
  4.7 8.6 %collective-permute-start.2 = (bf16[64,256]{1,0:T(8,128)(2,1)S(1)}, bf16[64,256]{1,0:T(8,128)(2,1)S(1)}, u32[]{:S(2)}, u32[]{:S(2)}) collective-permute-start(bf16[64,256]{1,0:T(8,128)(2,1)S(1)} %get-tuple-element.20), channel_id=1, source_target_pairs={{0,4},{4,0},{8,12},{12,8},{16,20},{20,16},{24,28},{28,24},{32,36},... | collective-permute-start | bytes 98312 | tf_op jit(solution)/shard_map/ppermute | solution.py:531
  6.3 9.7 %collective-permute-start.4 = (bf16[200,256]{1,0:T(8,128)(2,1)S(1)}, bf16[200,256]{1,0:T(8,128)(2,1)S(1)}, u32[]{:S(2)}, u32[]{:S(2)}) collective-permute-start(bf16[200,256]{1,0:T(8,128)(2,1)S(1)} %get-tuple-element.21), channel_id=1, source_target_pairs={{4,8},{12,16},{20,24},{28,32},{36,40},{44,48},{52,56},{60,64},{68,... | collective-permute-start | bytes 307208 | tf_op jit(solution)/shard_map/ppermute | solution.py:530
  13.2 9.3 %copy-start.3 = (bf16[256,256]{1,0:T(8,128)(2,1)S(1)}, bf16[256,256]{1,0:T(8,128)(2,1)}, u32[]{:S(2)}) copy-start(bf16[256,256]{1,0:T(8,128)(2,1)} %matrix_ref.1) | copy-start | bytes 393220
  13.2 9.3 %copy-start.8 = (s32[1,1,1024]{2,1,0:T(1,128)S(1)}, s32[1,1,1024]{2,1,0:T(1,128)}, u32[]{:S(2)}) copy-start(s32[1,1,1024]{2,1,0:T(1,128)} %elem_hbm.1) | copy-start | bytes 12292
  13.2 9.3 %copy-start.9 = (s32[1,1,1024]{2,1,0:T(1,128)S(1)}, s32[1,1,1024]{2,1,0:T(1,128)}, u32[]{:S(2)}) copy-start(s32[1,1,1024]{2,1,0:T(1,128)} %point_hbm.1) | copy-start | bytes 12292
  13.2 9.3 %copy-start.1 = (f32[2,64,256]{2,1,0:T(8,128)S(1)}, f32[2,64,256]{2,1,0:T(8,128)}, u32[]{:S(2)}) copy-start(f32[2,64,256]{2,1,0:T(8,128)} %state_ref.1) | copy-start | bytes 393220
  13.3 9.3 %copy-start.2 = (f32[2,64,256]{2,1,0:T(8,128)S(1)}, f32[2,64,256]{2,1,0:T(8,128)}, u32[]{:S(2)}) copy-start(f32[2,64,256]{2,1,0:T(8,128)} %rhs_ref.1) | copy-start | bytes 393220
  13.3 9.2 %collective-permute-start.3 = (bf16[232,256]{1,0:T(8,128)(2,1)S(1)}, bf16[232,256]{1,0:T(8,128)(2,1)S(1)}, u32[]{:S(2)}, u32[]{:S(2)}) collective-permute-start(bf16[232,256]{1,0:T(8,128)(2,1)S(1)} %constant_dynamic-update-slice_fusion), channel_id=1, source_target_pairs={{0,4},{4,0},{8,12},{12,8},{16,20},{20,16},{24,28},{28,24},{32,36},... | collective-permute-start | bytes 356360 | tf_op jit(solution)/shard_map/ppermute | solution.py:539
  13.4 9.1 %copy-start.10 = (f32[2,64]{1,0:T(2,128)S(1)}, f32[2,64]{1,0:T(2,128)}, u32[]{:S(2)}) copy-start(f32[2,64]{1,0:T(2,128)} %scale_ref.1) | copy-start | bytes 1540
  13.4 9.1 %copy-start.11 = (bf16[3,256]{1,0:T(4,128)(2,1)S(1)}, bf16[3,256]{1,0:T(4,128)(2,1)}, u32[]{:S(2)}) copy-start(bf16[3,256]{1,0:T(4,128)(2,1)} %tmap_ref.1) | copy-start | bytes 4612
  13.5 9.1 %copy-start.12 = (s32[1,1,4]{2,1,0:T(1,128)S(1)}, s32[1,1,4]{2,1,0:T(1,128)}, u32[]{:S(2)}) copy-start(s32[1,1,4]{2,1,0:T(1,128)} %count_hbm.1) | copy-start | bytes 52
  13.5 9.0 %collective-permute-start.5 = (bf16[144,256]{1,0:T(8,128)(2,1)S(1)}, bf16[144,256]{1,0:T(8,128)(2,1)S(1)}, u32[]{:S(2)}, u32[]{:S(2)}) collective-permute-start(bf16[144,256]{1,0:T(8,128)(2,1)S(1)} %pad_maximum_fusion), channel_id=1, source_target_pairs={{4,8},{12,16},{20,24},{28,32},{36,40},{44,48},{52,56},{60,64},{68,... | collective-permute-start | bytes 221192 | tf_op jit(solution)/shard_map/ppermute | solution.py:536
  16.1 6.4 %collective-permute-start.6 = (bf16[64,256]{1,0:T(8,128)(2,1)S(1)}, bf16[64,256]{1,0:T(8,128)(2,1)S(1)}, u32[]{:S(2)}, u32[]{:S(2)}) collective-permute-start(bf16[64,256]{1,0:T(8,128)(2,1)S(1)} %slice.42), channel_id=1, source_target_pairs={{0,4},{4,0},{8,12},{12,8},{16,20},{20,16},{24,28},{28,24},{32,36},... | collective-permute-start | bytes 98312 | tf_op jit(solution)/shard_map/ppermute | solution.py:540
  25.0 6.9 %copy-start = (f32[3,64,128]{2,1,0:T(8,128)S(1)}, f32[3,64,128]{2,1,0:T(8,128)}, u32[]{:S(2)}) copy-start(f32[3,64,128]{2,1,0:T(8,128)} %disp_ref.3) | copy-start | bytes 294916
  25.0 6.9 %copy-start.7 = (f32[64,128]{1,0:T(8,128)S(1)}, f32[64,128]{1,0:T(8,128)}, u32[]{:S(2)}) copy-start(f32[64,128]{1,0:T(8,128)} %stiff_ref.3) | copy-start | bytes 98308
  25.0 18.2 %all-to-all-start = ((bf16[128,8,128]{2,1,0:T(8,128)(2,1)}), bf16[128,8,128]{2,1,0:T(8,128)(2,1)S(1)}, u32[]{:S(2)}, u32[]{:S(2)}) async-start(bf16[128,8,128]{2,1,0:T(8,128)(2,1)} %bitcast), calls=%async_computation | async-start | bytes 524288 | tf_op jit(solution)/shard_map/all_to_all | solution.py:201
  47.4 2.9 %collective-permute-start.7 = (f32[8,256]{1,0:T(8,128)S(1)}, f32[8,256]{1,0:T(8,128)S(1)}, u32[]{:S(2)}, u32[]{:S(2)}) collective-permute-start(f32[8,256]{1,0:T(8,128)S(1)} %get-tuple-element.30), channel_id=1, source_target_pairs={{0,1},{1,0},{2,3},{3,2},{4,5},{5,4},{6,7},{7,6},{8,9},{9,8},{10,11... | collective-permute-start | bytes 24584 | tf_op jit(solution)/shard_map/ppermute | solution.py:215
  47.9 2.5 %collective-permute-start.8 = (f32[8,256]{1,0:T(8,128)S(1)}, f32[8,256]{1,0:T(8,128)S(1)}, u32[]{:S(2)}, u32[]{:S(2)}) collective-permute-start(f32[8,256]{1,0:T(8,128)S(1)} %get-tuple-element.31), channel_id=1, source_target_pairs={{0,2},{1,3},{2,0},{3,1},{4,6},{5,7},{6,4},{7,5},{8,10},{9,11},{10,... | collective-permute-start | bytes 24584 | tf_op jit(solution)/shard_map/ppermute | solution.py:215
  48.2 3.1 %collective-permute-start.9 = (f32[8,256]{1,0:T(8,128)S(1)}, f32[8,256]{1,0:T(8,128)S(1)}, u32[]{:S(2)}, u32[]{:S(2)}) collective-permute-start(f32[8,256]{1,0:T(8,128)S(1)} %get-tuple-element.32), channel_id=1, source_target_pairs={{0,3},{1,2},{2,1},{3,0},{4,7},{5,6},{6,5},{7,4},{8,11},{9,10},{10,... | collective-permute-start | bytes 24584 | tf_op jit(solution)/shard_map/ppermute | solution.py:215

commit v11 on v10

--- a/solution.py
+++ b/solution.py
@@ -130,7 +130,7 @@
     )(value)
 
 
-def finish_kernel(r0, r1, r2, r3, out_ref):
+def finish_kernel(r3, r2, r1, r0, out_ref):
     cap = r0.shape[1]
     patch = lax.axis_index("patch")
     for d, reply in enumerate((r0, r1, r2, r3)):
@@ -211,9 +211,8 @@
         compiler_params=params(),
         name="owner",
     )(got, displacement, stiffness, kd)
-    back = [replies[0]] + [
-        lax.ppermute(replies[d], "patch", patch_pairs(d)) for d in (1, 2, 3)
-    ]
+    back = [lax.ppermute(replies[d], "patch", patch_pairs(d)) for d in (3, 2, 1)]
+    back.append(replies[0])
     wall = pl.pallas_call(
         finish_kernel,
         out_shape=jax.ShapeDtypeStruct((3, 1, 1, owners * 256), F32),
@@ -415,6 +414,12 @@
     for r in range(6):
         s_ref[r] = jnp.broadcast_to(columns[:wide, r : r + 1], (wide, width))
         i_ref[r] = jnp.broadcast_to(inverses[:wide, r : r + 1], (wide, width))
+    for copy in copies:
+        copy.wait()
+    elem = elem_ref[0]
+    owners = rows_ref.shape[0]
+    live, code = slot_codes(point_ref[0], count_ref.at[0], owners)
+    hot = ((iota((2 * cols, elem.shape[1]), 0) == elem) & live).astype(F32).astype(BF)
     for sweep in range(SWEEPS):
         a, b = 1 + sweep, 7 - sweep
         value = relaxed(
@@ -431,12 +436,6 @@
     out_ref[odd] = v_ref[3, 8 : 8 + cols, :]
     out_ref[1 - odd] = v_ref[4, 8 : 8 + cols, :]
     final = out_ref[...].astype(BF).reshape(2 * cols, width)
-    for copy in copies:
-        copy.wait()
-    elem = elem_ref[0]
-    owners = rows_ref.shape[0]
-    live, code = slot_codes(point_ref[0], count_ref.at[0], owners)
-    hot = ((iota((2 * cols, elem.shape[1]), 0) == elem) & live).astype(F32).astype(BF)
     pull = jnp.dot(nt(tmap_ref[...], final).astype(BF), hot, preferred_element_type=F32)
     for k in range(owners):
         for j in range(4):
@@ -464,8 +463,9 @@
     nx = (up + down).astype(BF)
     ny = (pltpu.roll(mid, 1, 1) + pltpu.roll(mid, wide - 1, 1)).astype(BF)
     own = jnp.dot(mid.astype(BF).reshape(flat), matrix_ref[...], preferred_element_type=F32)
-    side = jnp.dot(nx.reshape(flat), x_ref[...], preferred_element_type=F32)
-    side += jnp.dot(ny.reshape(flat), y_ref[...], preferred_element_type=F32)
+    both = jnp.concatenate([nx.reshape(flat), ny.reshape(flat)], axis=1)
+    couple = jnp.concatenate([x_ref[...], y_ref[...]], axis=0)
+    side = jnp.dot(both, couple, preferred_element_type=F32)
     residue = (rhs.reshape(flat) - (scale.reshape(flat) * own - side)).astype(BF)
     update = jnp.dot(residue, inverse_ref[...], preferred_element_type=F32)
     update = update * inverse_scale.reshape(flat)

time: 52.1 us -> 51.8 us (level)
  waiting for transfers between devices: 18.1 us -> 17.5 us
    ppermute x3, waiting for transfers between devices: 1.04 us -> 0.37 us  [exchange_and_relax(): lax.ppermute(replies[d], 'patch', patch_pairs(d))]
  transfers between devices with their start and end apart: 11 -> 11, of which waited for: 4 -> 3; matrix products, arithmetic and copies ran while one was open for 0% -> 0% of each run, Pallas kernels for 3% -> 3%
where the time goes in v11:
time: 51.8 us; the launch traced here: 51.6 us
  starting transfers between devices  23 us (44%)
  waiting for transfers between devices  17.5 us (34%)
  Pallas kernels  10 us (19%)
  between operations  0.97 us (2%)
    all_to_all x1, waiting for transfers between devices, exchange_and_relax(): lax.all_to_all(message.reshape(sources, 8, 128), ('slab', 'patch'), 0, 0,...  10.7 us
    ppermute x1, starting transfers between devices, shards(): outer = lax.ppermute(own, 'slab', outer_pairs)  6.86 us
    all_to_all x1, starting transfers between devices, exchange_and_relax(): lax.all_to_all(message.reshape(sources, 8, 128), ('slab', 'patch'), 0, 0,...  6.85 us
    ppermute x1, waiting for transfers between devices, shards(): lax.ppermute(jnp.concatenate([inner_near] + thin + [far]), 'slab', outer_...  6.41 us
    pallas_call x3, Pallas kernels, call(): pl.pallas_call(kernel, out_shape=out_shape, in_specs=in_specs or vmem(len...  4.64 us
    pallas_call x1, Pallas kernels, exchange_and_relax(): pl.pallas_call(owner_kernel, out_shape=(jax.ShapeDtypeStruct(displacement...  4.13 us
    ppermute x1, starting transfers between devices, shards(): lax.ppermute(jnp.concatenate([inner_near] + thin + [far]), 'slab', outer_...  2.58 us
    ppermute x3, starting transfers between devices, exchange_and_relax(): lax.ppermute(replies[d], 'patch', patch_pairs(d))  2.22 us
  transfers between devices with their start and end apart: 11, of which 3 were waited for; matrix products, arithmetic and copies ran while one was open for 0% of the time, Pallas kernels for 3%

profile of v11, /device:TPU:1, one launch (start us, length us, event | category | flops | bytes accessed | tf_op | source)
XLA Modules:
  0.0 51.6 jit_solution(11543946792089647462)
XLA Ops:
  0.6 0.0 copy-start.4
  0.6 0.0 copy-start.5
  0.7 0.0 copy-start.6
  0.7 1.2 %near.1 = (bf16[64,256]{1,0:T(8,128)(2,1)S(1)}, bf16[200,256]{1,0:T(8,128)(2,1)S(1)}, bf16[64,256]{1,0:T(8,128)(2,1)S(1)}, bf16[24,256]{1,0:T(8,128)(2,1)S(1)}, bf16[24,256]{1,0:T(8,128)(2,1)S(1)}) custom-call(f32[2,64,256]{2,1,0:T(8,128)} %state_ref.1, f32[2,64,256]{2,1,0:T(8,128)} %rhs_ref.1, f32[2,64]{1,0:T(2,128)} %scale_ref.1, f32[3,64,128]{2,1,0:T(8,128)} %disp_ref.3), custom_call_target="tpu_custom_call" | custom-call | tf_op jit(solution)/shard_map/near/pallas_call | solution.py:476
  1.9 1.5 %collective-permute-start = (bf16[24,256]{1,0:T(8,128)(2,1)S(1)}, bf16[24,256]{1,0:T(8,128)(2,1)S(1)}, u32[]{:S(2)}, u32[]{:S(2)}) collective-permute-start(bf16[24,256]{1,0:T(8,128)(2,1)S(1)} %get-tuple-element.18), channel_id=1, source_target_pairs={{0,1},{1,0},{2,3},{3,2},{4,5},{5,4},{6,7},{7,6},{8,9},{9,8},{10,11... | collective-permute-start | bytes 36872 | tf_op jit(solution)/shard_map/ppermute | solution.py:533
  3.4 1.3 %collective-permute-start.1 = (bf16[24,256]{1,0:T(8,128)(2,1)S(1)}, bf16[24,256]{1,0:T(8,128)(2,1)S(1)}, u32[]{:S(2)}, u32[]{:S(2)}) collective-permute-start(bf16[24,256]{1,0:T(8,128)(2,1)S(1)} %get-tuple-element.19), channel_id=1, source_target_pairs={{0,3},{1,2},{2,1},{3,0},{4,7},{5,6},{6,5},{7,4},{8,11},{9,10},{10,... | collective-permute-start | bytes 36872 | tf_op jit(solution)/shard_map/ppermute | solution.py:532
  4.7 1.6 %collective-permute-start.2 = (bf16[64,256]{1,0:T(8,128)(2,1)S(1)}, bf16[64,256]{1,0:T(8,128)(2,1)S(1)}, u32[]{:S(2)}, u32[]{:S(2)}) collective-permute-start(bf16[64,256]{1,0:T(8,128)(2,1)S(1)} %get-tuple-element.20), channel_id=1, source_target_pairs={{0,4},{4,0},{8,12},{12,8},{16,20},{20,16},{24,28},{28,24},{32,36},... | collective-permute-start | bytes 98312 | tf_op jit(solution)/shard_map/ppermute | solution.py:531
  6.3 6.9 %collective-permute-start.4 = (bf16[200,256]{1,0:T(8,128)(2,1)S(1)}, bf16[200,256]{1,0:T(8,128)(2,1)S(1)}, u32[]{:S(2)}, u32[]{:S(2)}) collective-permute-start(bf16[200,256]{1,0:T(8,128)(2,1)S(1)} %get-tuple-element.21), channel_id=1, source_target_pairs={{4,8},{12,16},{20,24},{28,32},{36,40},{44,48},{52,56},{60,64},{68,... | collective-permute-start | bytes 307208 | tf_op jit(solution)/shard_map/ppermute | solution.py:530
  13.2 0.0 collective-permute-done.one_ref
  13.2 0.0 copy-start.8
  13.2 0.0 copy-start.9
  13.2 0.0 copy-start.1
  13.3 0.0 copy-start.2
  13.3 0.0 collective-permute-done.1.three_ref
  13.3 0.0 collective-permute-done.2.near_ref
  13.3 0.1 collective-permute-start.3
  13.4 0.0 copy-start.10
  13.4 0.0 copy-start.11
  13.5 0.0 copy-start.12
  13.5 2.6 %collective-permute-start.5 = (bf16[144,256]{1,0:T(8,128)(2,1)S(1)}, bf16[144,256]{1,0:T(8,128)(2,1)S(1)}, u32[]{:S(2)}, u32[]{:S(2)}) collective-permute-start(bf16[144,256]{1,0:T(8,128)(2,1)S(1)} %pad_maximum_fusion), channel_id=1, source_target_pairs={{4,8},{12,16},{20,24},{28,32},{36,40},{44,48},{52,56},{60,64},{68,... | collective-permute-start | bytes 221192 | tf_op jit(solution)/shard_map/ppermute | solution.py:536
  16.1 0.0 collective-permute-done.4.outer_ref
  16.1 0.0 collective-permute-start.6
  16.1 6.4 %collective-permute-done.5.rest_ref = bf16[144,256]{1,0:T(8,128)(2,1)S(1)} collective-permute-done((bf16[144,256]{1,0:T(8,128)(2,1)S(1)}, bf16[144,256]{1,0:T(8,128)(2,1)S(1)}, u32[]{:S(2)}, u32[]{:S(2)}) %collective-permute-start.5) | collective-permute-done | bytes 73760 | tf_op jit(solution)/shard_map/ppermute | solution.py:536
  22.5 0.0 collective-permute-done.6.relay_ref
  22.5 0.0 collective-permute-done.3.inner_ref
  22.5 0.0 copy-done.4
  22.5 0.0 copy-done.5
  22.5 0.0 copy-done.6
  22.5 0.0 copy-done.3
  22.5 0.0 copy-done.8
  22.5 0.0 copy-done.9
  22.5 0.0 copy-done.1
  22.5 0.0 copy-done.2
  22.6 2.7 %sweep.1 = (f32[2,64,256]{2,1,0:T(8,128)S(1)}, bf16[32,4,8,128]{3,2,1,0:T(8,128)(2,1)}) custom-call(f32[2,64,256]{2,1,0:T(8,128)S(1)} %copy-done.1, f32[2,64,256]{2,1,0:T(8,128)S(1)} %copy-done.2, f32[2,64]{1,0:T(2,128)S(1)} %copy-done.10, bf16[64,256]{1,0:T(8,128)(2,1)S(1)} %collective-permute-done.2.near_ref, ...), custom_call_target="tpu_custom_call" | custom-call | tf_op jit(solution)/shard_map/sweep/pallas_call | solution.py:476
  25.3 0.0 copy-start
  25.3 0.0 copy-start.7
  25.4 6.9 %all-to-all-start = ((bf16[128,8,128]{2,1,0:T(8,128)(2,1)}), bf16[128,8,128]{2,1,0:T(8,128)(2,1)S(1)}, u32[]{:S(2)}, u32[]{:S(2)}) async-start(bf16[128,8,128]{2,1,0:T(8,128)(2,1)} %bitcast), calls=%async_computation | async-start | bytes 524288 | tf_op jit(solution)/shard_map/all_to_all | solution.py:201
  32.2 0.7 %shell.1 = (f32[3,64,128]{2,1,0:T(8,128)S(1)}, f32[2,64,256]{2,1,0:T(8,128)}) custom-call(bf16[8,256]{1,0:T(8,128)(2,1)S(1)} %get-tuple-element.34.one_ref, bf16[8,256]{1,0:T(8,128)(2,1)S(1)} %get-tuple-element.36.three_ref, f32[3,64,128]{2,1,0:T(8,128)S(1)} %copy-done, f32[64,128]{1,0:T(8,128)S(1)} %copy-done.7, f32[2,64,256]{2,1,0:T(8,128)S(1)} %get-tuple-element.24.state_ref), custom_call_target="tpu_custom_call" | custom-call | tf_op jit(solution)/shard_map/shell/pallas_call | solution.py:476
  32.9 10.7 %all-to-all-done.got_ref = bf16[128,8,128]{2,1,0:T(8,128)(2,1)S(1)} async-done(((bf16[128,8,128]{2,1,0:T(8,128)(2,1)}), bf16[128,8,128]{2,1,0:T(8,128)(2,1)S(1)}, u32[]{:S(2)}, u32[]{:S(2)}) %all-to-all-start) | async-done | bytes 262176 | tf_op jit(solution)/shard_map/all_to_all | solution.py:201
  43.6 4.1 %owner.1 = (f32[3,64,128]{2,1,0:T(8,128)S(1)}, f32[8,256]{1,0:T(8,128)S(1)}, f32[8,256]{1,0:T(8,128)S(1)}, f32[8,256]{1,0:T(8,128)S(1)}, f32[8,256]{1,0:T(8,128)S(1)}) custom-call(bf16[128,8,128]{2,1,0:T(8,128)(2,1)S(1)} %all-to-all-done.got_ref, f32[3,64,128]{2,1,0:T(8,128)S(1)} %copy-done, f32[64,128]{1,0:T(8,128)S(1)} %copy-done.7, ...), custom_call_target="tpu_custom_call" | custom-call | tf_op jit(solution)/shard_map/owner/pallas_call | solution.py:205
  47.7 0.7 %collective-permute-start.7 = (f32[8,256]{1,0:T(8,128)S(1)}, f32[8,256]{1,0:T(8,128)S(1)}, u32[]{:S(2)}, u32[]{:S(2)}) collective-permute-start(f32[8,256]{1,0:T(8,128)S(1)} %get-tuple-element.29), channel_id=1, source_target_pairs={{0,3},{1,2},{2,1},{3,0},{4,7},{5,6},{6,5},{7,4},{8,11},{9,10},{10,... | collective-permute-start | bytes 24584 | tf_op jit(solution)/shard_map/ppermute | solution.py:214
  48.4 1.2 %collective-permute-start.8 = (f32[8,256]{1,0:T(8,128)S(1)}, f32[8,256]{1,0:T(8,128)S(1)}, u32[]{:S(2)}, u32[]{:S(2)}) collective-permute-start(f32[8,256]{1,0:T(8,128)S(1)} %get-tuple-element.30), channel_id=1, source_target_pairs={{0,2},{1,3},{2,0},{3,1},{4,6},{5,7},{6,4},{7,5},{8,10},{9,11},{10,... | collective-permute-start | bytes 24584 | tf_op jit(solution)/shard_map/ppermute | solution.py:214
  49.6 0.4 collective-permute-start.9
  50.0 0.6 %store_shell.1 = f32[3,64,128]{2,1,0:T(8,128)} custom-call(f32[3,64,128]{2,1,0:T(8,128)S(1)} %get-tuple-element.28.value_ref), custom_call_target="tpu_custom_call" | custom-call | tf_op jit(solution)/shard_map/store_shell/pallas_call | solution.py:122
  50.6 0.3 collective-permute-done.7.r3
  51.0 0.0 collective-permute-done.8.r2
  51.0 0.0 collective-permute-done.9.r1
  51.0 0.6 %finish.1 = f32[3,1,1,1024]{3,2,1,0:T(1,128)} custom-call(f32[8,256]{1,0:T(8,128)S(1)} %collective-permute-done.7.r3, f32[8,256]{1,0:T(8,128)S(1)} %collective-permute-done.8.r2, f32[8,256]{1,0:T(8,128)S(1)} %collective-permute-done.9.r1, f32[8,256]{1,0:T(8,128)S(1)} %get-tuple-element.32.r0), custom_call_target="tpu_custom_call" | custom-call | tf_op jit(solution)/shard_map/finish/pallas_call | solution.py:216
  (15 shorter events, 0.0 us)
Async XLA Ops:
  0.6 21.9 %copy-start.4 = (bf16[256,256]{1,0:T(8,128)(2,1)S(1)}, bf16[256,256]{1,0:T(8,128)(2,1)}, u32[]{:S(2)}) copy-start(bf16[256,256]{1,0:T(8,128)(2,1)} %x_ref.1) | copy-start | bytes 393220
  0.6 21.8 %copy-start.5 = (bf16[256,256]{1,0:T(8,128)(2,1)S(1)}, bf16[256,256]{1,0:T(8,128)(2,1)}, u32[]{:S(2)}) copy-start(bf16[256,256]{1,0:T(8,128)(2,1)} %y_ref.1) | copy-start | bytes 393220
  0.7 21.8 %copy-start.6 = (bf16[256,256]{1,0:T(8,128)(2,1)S(1)}, bf16[256,256]{1,0:T(8,128)(2,1)}, u32[]{:S(2)}) copy-start(bf16[256,256]{1,0:T(8,128)(2,1)} %inverse_ref.1) | copy-start | bytes 393220
  1.9 11.3 %collective-permute-start = (bf16[24,256]{1,0:T(8,128)(2,1)S(1)}, bf16[24,256]{1,0:T(8,128)(2,1)S(1)}, u32[]{:S(2)}, u32[]{:S(2)}) collective-permute-start(bf16[24,256]{1,0:T(8,128)(2,1)S(1)} %get-tuple-element.18), channel_id=1, source_target_pairs={{0,1},{1,0},{2,3},{3,2},{4,5},{5,4},{6,7},{7,6},{8,9},{9,8},{10,11... | collective-permute-start | bytes 36872 | tf_op jit(solution)/shard_map/ppermute | solution.py:533
  3.4 9.9 %collective-permute-start.1 = (bf16[24,256]{1,0:T(8,128)(2,1)S(1)}, bf16[24,256]{1,0:T(8,128)(2,1)S(1)}, u32[]{:S(2)}, u32[]{:S(2)}) collective-permute-start(bf16[24,256]{1,0:T(8,128)(2,1)S(1)} %get-tuple-element.19), channel_id=1, source_target_pairs={{0,3},{1,2},{2,1},{3,0},{4,7},{5,6},{6,5},{7,4},{8,11},{9,10},{10,... | collective-permute-start | bytes 36872 | tf_op jit(solution)/shard_map/ppermute | solution.py:532
  4.7 8.6 %collective-permute-start.2 = (bf16[64,256]{1,0:T(8,128)(2,1)S(1)}, bf16[64,256]{1,0:T(8,128)(2,1)S(1)}, u32[]{:S(2)}, u32[]{:S(2)}) collective-permute-start(bf16[64,256]{1,0:T(8,128)(2,1)S(1)} %get-tuple-element.20), channel_id=1, source_target_pairs={{0,4},{4,0},{8,12},{12,8},{16,20},{20,16},{24,28},{28,24},{32,36},... | collective-permute-start | bytes 98312 | tf_op jit(solution)/shard_map/ppermute | solution.py:531
  6.3 9.7 %collective-permute-start.4 = (bf16[200,256]{1,0:T(8,128)(2,1)S(1)}, bf16[200,256]{1,0:T(8,128)(2,1)S(1)}, u32[]{:S(2)}, u32[]{:S(2)}) collective-permute-start(bf16[200,256]{1,0:T(8,128)(2,1)S(1)} %get-tuple-element.21), channel_id=1, source_target_pairs={{4,8},{12,16},{20,24},{28,32},{36,40},{44,48},{52,56},{60,64},{68,... | collective-permute-start | bytes 307208 | tf_op jit(solution)/shard_map/ppermute | solution.py:530
  13.2 9.3 %copy-start.3 = (bf16[256,256]{1,0:T(8,128)(2,1)S(1)}, bf16[256,256]{1,0:T(8,128)(2,1)}, u32[]{:S(2)}) copy-start(bf16[256,256]{1,0:T(8,128)(2,1)} %matrix_ref.1) | copy-start | bytes 393220
  13.2 9.3 %copy-start.8 = (s32[1,1,1024]{2,1,0:T(1,128)S(1)}, s32[1,1,1024]{2,1,0:T(1,128)}, u32[]{:S(2)}) copy-start(s32[1,1,1024]{2,1,0:T(1,128)} %elem_hbm.1) | copy-start | bytes 12292
  13.2 9.3 %copy-start.9 = (s32[1,1,1024]{2,1,0:T(1,128)S(1)}, s32[1,1,1024]{2,1,0:T(1,128)}, u32[]{:S(2)}) copy-start(s32[1,1,1024]{2,1,0:T(1,128)} %point_hbm.1) | copy-start | bytes 12292
  13.2 9.3 %copy-start.1 = (f32[2,64,256]{2,1,0:T(8,128)S(1)}, f32[2,64,256]{2,1,0:T(8,128)}, u32[]{:S(2)}) copy-start(f32[2,64,256]{2,1,0:T(8,128)} %state_ref.1) | copy-start | bytes 393220
  13.3 9.3 %copy-start.2 = (f32[2,64,256]{2,1,0:T(8,128)S(1)}, f32[2,64,256]{2,1,0:T(8,128)}, u32[]{:S(2)}) copy-start(f32[2,64,256]{2,1,0:T(8,128)} %rhs_ref.1) | copy-start | bytes 393220
  13.3 9.2 %collective-permute-start.3 = (bf16[232,256]{1,0:T(8,128)(2,1)S(1)}, bf16[232,256]{1,0:T(8,128)(2,1)S(1)}, u32[]{:S(2)}, u32[]{:S(2)}) collective-permute-start(bf16[232,256]{1,0:T(8,128)(2,1)S(1)} %constant_dynamic-update-slice_fusion), channel_id=1, source_target_pairs={{0,4},{4,0},{8,12},{12,8},{16,20},{20,16},{24,28},{28,24},{32,36},... | collective-permute-start | bytes 356360 | tf_op jit(solution)/shard_map/ppermute | solution.py:539
  13.4 9.1 %copy-start.10 = (f32[2,64]{1,0:T(2,128)S(1)}, f32[2,64]{1,0:T(2,128)}, u32[]{:S(2)}) copy-start(f32[2,64]{1,0:T(2,128)} %scale_ref.1) | copy-start | bytes 1540
  13.4 9.1 %copy-start.11 = (bf16[3,256]{1,0:T(4,128)(2,1)S(1)}, bf16[3,256]{1,0:T(4,128)(2,1)}, u32[]{:S(2)}) copy-start(bf16[3,256]{1,0:T(4,128)(2,1)} %tmap_ref.1) | copy-start | bytes 4612
  13.5 9.1 %copy-start.12 = (s32[1,1,4]{2,1,0:T(1,128)S(1)}, s32[1,1,4]{2,1,0:T(1,128)}, u32[]{:S(2)}) copy-start(s32[1,1,4]{2,1,0:T(1,128)} %count_hbm.1) | copy-start | bytes 52
  13.5 9.0 %collective-permute-start.5 = (bf16[144,256]{1,0:T(8,128)(2,1)S(1)}, bf16[144,256]{1,0:T(8,128)(2,1)S(1)}, u32[]{:S(2)}, u32[]{:S(2)}) collective-permute-start(bf16[144,256]{1,0:T(8,128)(2,1)S(1)} %pad_maximum_fusion), channel_id=1, source_target_pairs={{4,8},{12,16},{20,24},{28,32},{36,40},{44,48},{52,56},{60,64},{68,... | collective-permute-start | bytes 221192 | tf_op jit(solution)/shard_map/ppermute | solution.py:536
  16.1 6.4 %collective-permute-start.6 = (bf16[64,256]{1,0:T(8,128)(2,1)S(1)}, bf16[64,256]{1,0:T(8,128)(2,1)S(1)}, u32[]{:S(2)}, u32[]{:S(2)}) collective-permute-start(bf16[64,256]{1,0:T(8,128)(2,1)S(1)} %slice.42), channel_id=1, source_target_pairs={{0,4},{4,0},{8,12},{12,8},{16,20},{20,16},{24,28},{28,24},{32,36},... | collective-permute-start | bytes 98312 | tf_op jit(solution)/shard_map/ppermute | solution.py:540
  25.3 6.9 %copy-start = (f32[3,64,128]{2,1,0:T(8,128)S(1)}, f32[3,64,128]{2,1,0:T(8,128)}, u32[]{:S(2)}) copy-start(f32[3,64,128]{2,1,0:T(8,128)} %disp_ref.3) | copy-start | bytes 294916
  25.3 6.9 %copy-start.7 = (f32[64,128]{1,0:T(8,128)S(1)}, f32[64,128]{1,0:T(8,128)}, u32[]{:S(2)}) copy-start(f32[64,128]{1,0:T(8,128)} %stiff_ref.3) | copy-start | bytes 98308
  25.4 18.2 %all-to-all-start = ((bf16[128,8,128]{2,1,0:T(8,128)(2,1)}), bf16[128,8,128]{2,1,0:T(8,128)(2,1)S(1)}, u32[]{:S(2)}, u32[]{:S(2)}) async-start(bf16[128,8,128]{2,1,0:T(8,128)(2,1)} %bitcast), calls=%async_computation | async-start | bytes 524288 | tf_op jit(solution)/shard_map/all_to_all | solution.py:201
  47.7 3.2 %collective-permute-start.7 = (f32[8,256]{1,0:T(8,128)S(1)}, f32[8,256]{1,0:T(8,128)S(1)}, u32[]{:S(2)}, u32[]{:S(2)}) collective-permute-start(f32[8,256]{1,0:T(8,128)S(1)} %get-tuple-element.29), channel_id=1, source_target_pairs={{0,3},{1,2},{2,1},{3,0},{4,7},{5,6},{6,5},{7,4},{8,11},{9,10},{10,... | collective-permute-start | bytes 24584 | tf_op jit(solution)/shard_map/ppermute | solution.py:214
  48.4 2.6 %collective-permute-start.8 = (f32[8,256]{1,0:T(8,128)S(1)}, f32[8,256]{1,0:T(8,128)S(1)}, u32[]{:S(2)}, u32[]{:S(2)}) collective-permute-start(f32[8,256]{1,0:T(8,128)S(1)} %get-tuple-element.30), channel_id=1, source_target_pairs={{0,2},{1,3},{2,0},{3,1},{4,6},{5,7},{6,4},{7,5},{8,10},{9,11},{10,... | collective-permute-start | bytes 24584 | tf_op jit(solution)/shard_map/ppermute | solution.py:214
  49.6 1.4 %collective-permute-start.9 = (f32[8,256]{1,0:T(8,128)S(1)}, f32[8,256]{1,0:T(8,128)S(1)}, u32[]{:S(2)}, u32[]{:S(2)}) collective-permute-start(f32[8,256]{1,0:T(8,128)S(1)} %get-tuple-element.31), channel_id=1, source_target_pairs={{0,1},{1,0},{2,3},{3,2},{4,5},{5,4},{6,7},{7,6},{8,9},{9,8},{10,11... | collective-permute-start | bytes 24584 | tf_op jit(solution)/shard_map/ppermute | solution.py:214

commit v12 on v10

--- a/solution.py
+++ b/solution.py
@@ -130,7 +130,7 @@
     )(value)
 
 
-def finish_kernel(r0, r1, r2, r3, out_ref):
+def finish_kernel(r3, r2, r1, r0, out_ref):
     cap = r0.shape[1]
     patch = lax.axis_index("patch")
     for d, reply in enumerate((r0, r1, r2, r3)):
@@ -211,9 +211,8 @@
         compiler_params=params(),
         name="owner",
     )(got, displacement, stiffness, kd)
-    back = [replies[0]] + [
-        lax.ppermute(replies[d], "patch", patch_pairs(d)) for d in (1, 2, 3)
-    ]
+    back = [lax.ppermute(replies[d], "patch", patch_pairs(d)) for d in (3, 2, 1)]
+    back.append(replies[0])
     wall = pl.pallas_call(
         finish_kernel,
         out_shape=jax.ShapeDtypeStruct((3, 1, 1, owners * 256), F32),

time: 52.1 us -> 51.4 us (0.987)
  waiting for transfers between devices: 18.1 us -> 17.5 us
    ppermute x3, waiting for transfers between devices: 1.04 us -> 0.37 us  [exchange_and_relax(): lax.ppermute(replies[d], 'patch', patch_pairs(d))]
  transfers between devices with their start and end apart: 11 -> 11, of which waited for: 4 -> 3; matrix products, arithmetic and copies ran while one was open for 0% -> 0% of each run, Pallas kernels for 3% -> 3%
where the time goes in v12:
time: 51.4 us; the launch traced here: 51.2 us
  starting transfers between devices  23 us (45%)
  waiting for transfers between devices  17.5 us (34%)
  Pallas kernels  9.66 us (19%)
  between operations  0.97 us (2%)
    all_to_all x1, waiting for transfers between devices, exchange_and_relax(): lax.all_to_all(message.reshape(sources, 8, 128), ('slab', 'patch'), 0, 0,...  10.7 us
    ppermute x1, starting transfers between devices, shards(): outer = lax.ppermute(own, 'slab', outer_pairs)  6.86 us
    all_to_all x1, starting transfers between devices, exchange_and_relax(): lax.all_to_all(message.reshape(sources, 8, 128), ('slab', 'patch'), 0, 0,...  6.85 us
    ppermute x1, waiting for transfers between devices, shards(): lax.ppermute(jnp.concatenate([inner_near] + thin + [far]), 'slab', outer_...  6.41 us
    pallas_call x3, Pallas kernels, call(): pl.pallas_call(kernel, out_shape=out_shape, in_specs=in_specs or vmem(len...  4.27 us
    pallas_call x1, Pallas kernels, exchange_and_relax(): pl.pallas_call(owner_kernel, out_shape=(jax.ShapeDtypeStruct(displacement...  4.13 us
    ppermute x1, starting transfers between devices, shards(): lax.ppermute(jnp.concatenate([inner_near] + thin + [far]), 'slab', outer_...  2.58 us
    ppermute x3, starting transfers between devices, exchange_and_relax(): lax.ppermute(replies[d], 'patch', patch_pairs(d))  2.22 us
  transfers between devices with their start and end apart: 11, of which 3 were waited for; matrix products, arithmetic and copies ran while one was open for 0% of the time, Pallas kernels for 3%

profile of v12, /device:TPU:1, one launch (start us, length us, event | category | flops | bytes accessed | tf_op | source)
XLA Modules:
  0.0 51.2 jit_solution(17342067525034044220)
XLA Ops:
  0.6 0.0 copy-start.4
  0.6 0.0 copy-start.5
  0.7 0.0 copy-start.6
  0.7 1.2 %near.1 = (bf16[64,256]{1,0:T(8,128)(2,1)S(1)}, bf16[200,256]{1,0:T(8,128)(2,1)S(1)}, bf16[64,256]{1,0:T(8,128)(2,1)S(1)}, bf16[24,256]{1,0:T(8,128)(2,1)S(1)}, bf16[24,256]{1,0:T(8,128)(2,1)S(1)}) custom-call(f32[2,64,256]{2,1,0:T(8,128)} %state_ref.1, f32[2,64,256]{2,1,0:T(8,128)} %rhs_ref.1, f32[2,64]{1,0:T(2,128)} %scale_ref.1, f32[3,64,128]{2,1,0:T(8,128)} %disp_ref.3), custom_call_target="tpu_custom_call" | custom-call | tf_op jit(solution)/shard_map/near/pallas_call | solution.py:475
  1.9 1.5 %collective-permute-start = (bf16[24,256]{1,0:T(8,128)(2,1)S(1)}, bf16[24,256]{1,0:T(8,128)(2,1)S(1)}, u32[]{:S(2)}, u32[]{:S(2)}) collective-permute-start(bf16[24,256]{1,0:T(8,128)(2,1)S(1)} %get-tuple-element.18), channel_id=1, source_target_pairs={{0,1},{1,0},{2,3},{3,2},{4,5},{5,4},{6,7},{7,6},{8,9},{9,8},{10,11... | collective-permute-start | bytes 36872 | tf_op jit(solution)/shard_map/ppermute | solution.py:532
  3.4 1.3 %collective-permute-start.1 = (bf16[24,256]{1,0:T(8,128)(2,1)S(1)}, bf16[24,256]{1,0:T(8,128)(2,1)S(1)}, u32[]{:S(2)}, u32[]{:S(2)}) collective-permute-start(bf16[24,256]{1,0:T(8,128)(2,1)S(1)} %get-tuple-element.19), channel_id=1, source_target_pairs={{0,3},{1,2},{2,1},{3,0},{4,7},{5,6},{6,5},{7,4},{8,11},{9,10},{10,... | collective-permute-start | bytes 36872 | tf_op jit(solution)/shard_map/ppermute | solution.py:531
  4.7 1.6 %collective-permute-start.2 = (bf16[64,256]{1,0:T(8,128)(2,1)S(1)}, bf16[64,256]{1,0:T(8,128)(2,1)S(1)}, u32[]{:S(2)}, u32[]{:S(2)}) collective-permute-start(bf16[64,256]{1,0:T(8,128)(2,1)S(1)} %get-tuple-element.20), channel_id=1, source_target_pairs={{0,4},{4,0},{8,12},{12,8},{16,20},{20,16},{24,28},{28,24},{32,36},... | collective-permute-start | bytes 98312 | tf_op jit(solution)/shard_map/ppermute | solution.py:530
  6.3 6.9 %collective-permute-start.4 = (bf16[200,256]{1,0:T(8,128)(2,1)S(1)}, bf16[200,256]{1,0:T(8,128)(2,1)S(1)}, u32[]{:S(2)}, u32[]{:S(2)}) collective-permute-start(bf16[200,256]{1,0:T(8,128)(2,1)S(1)} %get-tuple-element.21), channel_id=1, source_target_pairs={{4,8},{12,16},{20,24},{28,32},{36,40},{44,48},{52,56},{60,64},{68,... | collective-permute-start | bytes 307208 | tf_op jit(solution)/shard_map/ppermute | solution.py:529
  13.2 0.0 collective-permute-done.one_ref
  13.2 0.0 copy-start.8
  13.2 0.0 copy-start.9
  13.2 0.0 copy-start.1
  13.3 0.0 copy-start.2
  13.3 0.0 collective-permute-done.1.three_ref
  13.3 0.0 collective-permute-done.2.near_ref
  13.3 0.1 collective-permute-start.3
  13.4 0.0 copy-start.10
  13.4 0.0 copy-start.11
  13.5 0.0 copy-start.12
  13.5 2.6 %collective-permute-start.5 = (bf16[144,256]{1,0:T(8,128)(2,1)S(1)}, bf16[144,256]{1,0:T(8,128)(2,1)S(1)}, u32[]{:S(2)}, u32[]{:S(2)}) collective-permute-start(bf16[144,256]{1,0:T(8,128)(2,1)S(1)} %pad_maximum_fusion), channel_id=1, source_target_pairs={{4,8},{12,16},{20,24},{28,32},{36,40},{44,48},{52,56},{60,64},{68,... | collective-permute-start | bytes 221192 | tf_op jit(solution)/shard_map/ppermute | solution.py:535
  16.1 0.0 collective-permute-done.4.outer_ref
  16.1 0.0 collective-permute-start.6
  16.1 6.4 %collective-permute-done.5.rest_ref = bf16[144,256]{1,0:T(8,128)(2,1)S(1)} collective-permute-done((bf16[144,256]{1,0:T(8,128)(2,1)S(1)}, bf16[144,256]{1,0:T(8,128)(2,1)S(1)}, u32[]{:S(2)}, u32[]{:S(2)}) %collective-permute-start.5) | collective-permute-done | bytes 73760 | tf_op jit(solution)/shard_map/ppermute | solution.py:535
  22.5 0.0 collective-permute-done.6.relay_ref
  22.5 0.0 collective-permute-done.3.inner_ref
  22.5 0.0 copy-done.4
  22.5 0.0 copy-done.5
  22.5 0.0 copy-done.6
  22.5 0.0 copy-done.3
  22.5 0.0 copy-done.8
  22.5 0.0 copy-done.9
  22.5 0.0 copy-done.1
  22.5 0.0 copy-done.2
  22.6 2.4 %sweep.1 = (f32[2,64,256]{2,1,0:T(8,128)S(1)}, bf16[32,4,8,128]{3,2,1,0:T(8,128)(2,1)}) custom-call(f32[2,64,256]{2,1,0:T(8,128)S(1)} %copy-done.1, f32[2,64,256]{2,1,0:T(8,128)S(1)} %copy-done.2, f32[2,64]{1,0:T(2,128)S(1)} %copy-done.10, bf16[64,256]{1,0:T(8,128)(2,1)S(1)} %collective-permute-done.2.near_ref, ...), custom_call_target="tpu_custom_call" | custom-call | tf_op jit(solution)/shard_map/sweep/pallas_call | solution.py:475
  25.0 0.0 copy-start
  25.0 0.0 copy-start.7
  25.0 6.9 %all-to-all-start = ((bf16[128,8,128]{2,1,0:T(8,128)(2,1)}), bf16[128,8,128]{2,1,0:T(8,128)(2,1)S(1)}, u32[]{:S(2)}, u32[]{:S(2)}) async-start(bf16[128,8,128]{2,1,0:T(8,128)(2,1)} %bitcast), calls=%async_computation | async-start | bytes 524288 | tf_op jit(solution)/shard_map/all_to_all | solution.py:201
  31.9 0.7 %shell.1 = (f32[3,64,128]{2,1,0:T(8,128)S(1)}, f32[2,64,256]{2,1,0:T(8,128)}) custom-call(bf16[8,256]{1,0:T(8,128)(2,1)S(1)} %get-tuple-element.34.one_ref, bf16[8,256]{1,0:T(8,128)(2,1)S(1)} %get-tuple-element.36.three_ref, f32[3,64,128]{2,1,0:T(8,128)S(1)} %copy-done, f32[64,128]{1,0:T(8,128)S(1)} %copy-done.7, f32[2,64,256]{2,1,0:T(8,128)S(1)} %get-tuple-element.24.state_ref), custom_call_target="tpu_custom_call" | custom-call | tf_op jit(solution)/shard_map/shell/pallas_call | solution.py:475
  32.5 10.7 %all-to-all-done.got_ref = bf16[128,8,128]{2,1,0:T(8,128)(2,1)S(1)} async-done(((bf16[128,8,128]{2,1,0:T(8,128)(2,1)}), bf16[128,8,128]{2,1,0:T(8,128)(2,1)S(1)}, u32[]{:S(2)}, u32[]{:S(2)}) %all-to-all-start) | async-done | bytes 262176 | tf_op jit(solution)/shard_map/all_to_all | solution.py:201
  43.2 4.1 %owner.1 = (f32[3,64,128]{2,1,0:T(8,128)S(1)}, f32[8,256]{1,0:T(8,128)S(1)}, f32[8,256]{1,0:T(8,128)S(1)}, f32[8,256]{1,0:T(8,128)S(1)}, f32[8,256]{1,0:T(8,128)S(1)}) custom-call(bf16[128,8,128]{2,1,0:T(8,128)(2,1)S(1)} %all-to-all-done.got_ref, f32[3,64,128]{2,1,0:T(8,128)S(1)} %copy-done, f32[64,128]{1,0:T(8,128)S(1)} %copy-done.7, ...), custom_call_target="tpu_custom_call" | custom-call | tf_op jit(solution)/shard_map/owner/pallas_call | solution.py:205
  47.4 0.7 %collective-permute-start.7 = (f32[8,256]{1,0:T(8,128)S(1)}, f32[8,256]{1,0:T(8,128)S(1)}, u32[]{:S(2)}, u32[]{:S(2)}) collective-permute-start(f32[8,256]{1,0:T(8,128)S(1)} %get-tuple-element.29), channel_id=1, source_target_pairs={{0,3},{1,2},{2,1},{3,0},{4,7},{5,6},{6,5},{7,4},{8,11},{9,10},{10,... | collective-permute-start | bytes 24584 | tf_op jit(solution)/shard_map/ppermute | solution.py:214
  48.0 1.2 %collective-permute-start.8 = (f32[8,256]{1,0:T(8,128)S(1)}, f32[8,256]{1,0:T(8,128)S(1)}, u32[]{:S(2)}, u32[]{:S(2)}) collective-permute-start(f32[8,256]{1,0:T(8,128)S(1)} %get-tuple-element.30), channel_id=1, source_target_pairs={{0,2},{1,3},{2,0},{3,1},{4,6},{5,7},{6,4},{7,5},{8,10},{9,11},{10,... | collective-permute-start | bytes 24584 | tf_op jit(solution)/shard_map/ppermute | solution.py:214
  49.2 0.4 collective-permute-start.9
  49.6 0.6 %store_shell.1 = f32[3,64,128]{2,1,0:T(8,128)} custom-call(f32[3,64,128]{2,1,0:T(8,128)S(1)} %get-tuple-element.28.value_ref), custom_call_target="tpu_custom_call" | custom-call | tf_op jit(solution)/shard_map/store_shell/pallas_call | solution.py:122
  50.2 0.4 collective-permute-done.7.r3
  50.6 0.0 collective-permute-done.8.r2
  50.6 0.0 collective-permute-done.9.r1
  50.6 0.6 %finish.1 = f32[3,1,1,1024]{3,2,1,0:T(1,128)} custom-call(f32[8,256]{1,0:T(8,128)S(1)} %collective-permute-done.7.r3, f32[8,256]{1,0:T(8,128)S(1)} %collective-permute-done.8.r2, f32[8,256]{1,0:T(8,128)S(1)} %collective-permute-done.9.r1, f32[8,256]{1,0:T(8,128)S(1)} %get-tuple-element.32.r0), custom_call_target="tpu_custom_call" | custom-call | tf_op jit(solution)/shard_map/finish/pallas_call | solution.py:216
  (15 shorter events, 0.0 us)
Async XLA Ops:
  0.6 21.9 %copy-start.4 = (bf16[256,256]{1,0:T(8,128)(2,1)S(1)}, bf16[256,256]{1,0:T(8,128)(2,1)}, u32[]{:S(2)}) copy-start(bf16[256,256]{1,0:T(8,128)(2,1)} %x_ref.1) | copy-start | bytes 393220
  0.6 21.8 %copy-start.5 = (bf16[256,256]{1,0:T(8,128)(2,1)S(1)}, bf16[256,256]{1,0:T(8,128)(2,1)}, u32[]{:S(2)}) copy-start(bf16[256,256]{1,0:T(8,128)(2,1)} %y_ref.1) | copy-start | bytes 393220
  0.7 21.8 %copy-start.6 = (bf16[256,256]{1,0:T(8,128)(2,1)S(1)}, bf16[256,256]{1,0:T(8,128)(2,1)}, u32[]{:S(2)}) copy-start(bf16[256,256]{1,0:T(8,128)(2,1)} %inverse_ref.1) | copy-start | bytes 393220
  1.9 11.3 %collective-permute-start = (bf16[24,256]{1,0:T(8,128)(2,1)S(1)}, bf16[24,256]{1,0:T(8,128)(2,1)S(1)}, u32[]{:S(2)}, u32[]{:S(2)}) collective-permute-start(bf16[24,256]{1,0:T(8,128)(2,1)S(1)} %get-tuple-element.18), channel_id=1, source_target_pairs={{0,1},{1,0},{2,3},{3,2},{4,5},{5,4},{6,7},{7,6},{8,9},{9,8},{10,11... | collective-permute-start | bytes 36872 | tf_op jit(solution)/shard_map/ppermute | solution.py:532
  3.4 9.9 %collective-permute-start.1 = (bf16[24,256]{1,0:T(8,128)(2,1)S(1)}, bf16[24,256]{1,0:T(8,128)(2,1)S(1)}, u32[]{:S(2)}, u32[]{:S(2)}) collective-permute-start(bf16[24,256]{1,0:T(8,128)(2,1)S(1)} %get-tuple-element.19), channel_id=1, source_target_pairs={{0,3},{1,2},{2,1},{3,0},{4,7},{5,6},{6,5},{7,4},{8,11},{9,10},{10,... | collective-permute-start | bytes 36872 | tf_op jit(solution)/shard_map/ppermute | solution.py:531
  4.7 8.6 %collective-permute-start.2 = (bf16[64,256]{1,0:T(8,128)(2,1)S(1)}, bf16[64,256]{1,0:T(8,128)(2,1)S(1)}, u32[]{:S(2)}, u32[]{:S(2)}) collective-permute-start(bf16[64,256]{1,0:T(8,128)(2,1)S(1)} %get-tuple-element.20), channel_id=1, source_target_pairs={{0,4},{4,0},{8,12},{12,8},{16,20},{20,16},{24,28},{28,24},{32,36},... | collective-permute-start | bytes 98312 | tf_op jit(solution)/shard_map/ppermute | solution.py:530
  6.3 9.7 %collective-permute-start.4 = (bf16[200,256]{1,0:T(8,128)(2,1)S(1)}, bf16[200,256]{1,0:T(8,128)(2,1)S(1)}, u32[]{:S(2)}, u32[]{:S(2)}) collective-permute-start(bf16[200,256]{1,0:T(8,128)(2,1)S(1)} %get-tuple-element.21), channel_id=1, source_target_pairs={{4,8},{12,16},{20,24},{28,32},{36,40},{44,48},{52,56},{60,64},{68,... | collective-permute-start | bytes 307208 | tf_op jit(solution)/shard_map/ppermute | solution.py:529
  13.2 9.3 %copy-start.3 = (bf16[256,256]{1,0:T(8,128)(2,1)S(1)}, bf16[256,256]{1,0:T(8,128)(2,1)}, u32[]{:S(2)}) copy-start(bf16[256,256]{1,0:T(8,128)(2,1)} %matrix_ref.1) | copy-start | bytes 393220
  13.2 9.3 %copy-start.8 = (s32[1,1,1024]{2,1,0:T(1,128)S(1)}, s32[1,1,1024]{2,1,0:T(1,128)}, u32[]{:S(2)}) copy-start(s32[1,1,1024]{2,1,0:T(1,128)} %elem_hbm.1) | copy-start | bytes 12292
  13.2 9.3 %copy-start.9 = (s32[1,1,1024]{2,1,0:T(1,128)S(1)}, s32[1,1,1024]{2,1,0:T(1,128)}, u32[]{:S(2)}) copy-start(s32[1,1,1024]{2,1,0:T(1,128)} %point_hbm.1) | copy-start | bytes 12292
  13.2 9.3 %copy-start.1 = (f32[2,64,256]{2,1,0:T(8,128)S(1)}, f32[2,64,256]{2,1,0:T(8,128)}, u32[]{:S(2)}) copy-start(f32[2,64,256]{2,1,0:T(8,128)} %state_ref.1) | copy-start | bytes 393220
  13.3 9.3 %copy-start.2 = (f32[2,64,256]{2,1,0:T(8,128)S(1)}, f32[2,64,256]{2,1,0:T(8,128)}, u32[]{:S(2)}) copy-start(f32[2,64,256]{2,1,0:T(8,128)} %rhs_ref.1) | copy-start | bytes 393220
  13.3 9.2 %collective-permute-start.3 = (bf16[232,256]{1,0:T(8,128)(2,1)S(1)}, bf16[232,256]{1,0:T(8,128)(2,1)S(1)}, u32[]{:S(2)}, u32[]{:S(2)}) collective-permute-start(bf16[232,256]{1,0:T(8,128)(2,1)S(1)} %constant_dynamic-update-slice_fusion), channel_id=1, source_target_pairs={{0,4},{4,0},{8,12},{12,8},{16,20},{20,16},{24,28},{28,24},{32,36},... | collective-permute-start | bytes 356360 | tf_op jit(solution)/shard_map/ppermute | solution.py:538
  13.4 9.1 %copy-start.10 = (f32[2,64]{1,0:T(2,128)S(1)}, f32[2,64]{1,0:T(2,128)}, u32[]{:S(2)}) copy-start(f32[2,64]{1,0:T(2,128)} %scale_ref.1) | copy-start | bytes 1540
  13.4 9.1 %copy-start.11 = (bf16[3,256]{1,0:T(4,128)(2,1)S(1)}, bf16[3,256]{1,0:T(4,128)(2,1)}, u32[]{:S(2)}) copy-start(bf16[3,256]{1,0:T(4,128)(2,1)} %tmap_ref.1) | copy-start | bytes 4612
  13.5 9.1 %copy-start.12 = (s32[1,1,4]{2,1,0:T(1,128)S(1)}, s32[1,1,4]{2,1,0:T(1,128)}, u32[]{:S(2)}) copy-start(s32[1,1,4]{2,1,0:T(1,128)} %count_hbm.1) | copy-start | bytes 52
  13.5 9.0 %collective-permute-start.5 = (bf16[144,256]{1,0:T(8,128)(2,1)S(1)}, bf16[144,256]{1,0:T(8,128)(2,1)S(1)}, u32[]{:S(2)}, u32[]{:S(2)}) collective-permute-start(bf16[144,256]{1,0:T(8,128)(2,1)S(1)} %pad_maximum_fusion), channel_id=1, source_target_pairs={{4,8},{12,16},{20,24},{28,32},{36,40},{44,48},{52,56},{60,64},{68,... | collective-permute-start | bytes 221192 | tf_op jit(solution)/shard_map/ppermute | solution.py:535
  16.1 6.4 %collective-permute-start.6 = (bf16[64,256]{1,0:T(8,128)(2,1)S(1)}, bf16[64,256]{1,0:T(8,128)(2,1)S(1)}, u32[]{:S(2)}, u32[]{:S(2)}) collective-permute-start(bf16[64,256]{1,0:T(8,128)(2,1)S(1)} %slice.42), channel_id=1, source_target_pairs={{0,4},{4,0},{8,12},{12,8},{16,20},{20,16},{24,28},{28,24},{32,36},... | collective-permute-start | bytes 98312 | tf_op jit(solution)/shard_map/ppermute | solution.py:539
  25.0 6.9 %copy-start = (f32[3,64,128]{2,1,0:T(8,128)S(1)}, f32[3,64,128]{2,1,0:T(8,128)}, u32[]{:S(2)}) copy-start(f32[3,64,128]{2,1,0:T(8,128)} %disp_ref.3) | copy-start | bytes 294916
  25.0 6.9 %copy-start.7 = (f32[64,128]{1,0:T(8,128)S(1)}, f32[64,128]{1,0:T(8,128)}, u32[]{:S(2)}) copy-start(f32[64,128]{1,0:T(8,128)} %stiff_ref.3) | copy-start | bytes 98308
  25.0 18.2 %all-to-all-start = ((bf16[128,8,128]{2,1,0:T(8,128)(2,1)}), bf16[128,8,128]{2,1,0:T(8,128)(2,1)S(1)}, u32[]{:S(2)}, u32[]{:S(2)}) async-start(bf16[128,8,128]{2,1,0:T(8,128)(2,1)} %bitcast), calls=%async_computation | async-start | bytes 524288 | tf_op jit(solution)/shard_map/all_to_all | solution.py:201
  47.4 3.2 %collective-permute-start.7 = (f32[8,256]{1,0:T(8,128)S(1)}, f32[8,256]{1,0:T(8,128)S(1)}, u32[]{:S(2)}, u32[]{:S(2)}) collective-permute-start(f32[8,256]{1,0:T(8,128)S(1)} %get-tuple-element.29), channel_id=1, source_target_pairs={{0,3},{1,2},{2,1},{3,0},{4,7},{5,6},{6,5},{7,4},{8,11},{9,10},{10,... | collective-permute-start | bytes 24584 | tf_op jit(solution)/shard_map/ppermute | solution.py:214
  48.0 2.6 %collective-permute-start.8 = (f32[8,256]{1,0:T(8,128)S(1)}, f32[8,256]{1,0:T(8,128)S(1)}, u32[]{:S(2)}, u32[]{:S(2)}) collective-permute-start(f32[8,256]{1,0:T(8,128)S(1)} %get-tuple-element.30), channel_id=1, source_target_pairs={{0,2},{1,3},{2,0},{3,1},{4,6},{5,7},{6,4},{7,5},{8,10},{9,11},{10,... | collective-permute-start | bytes 24584 | tf_op jit(solution)/shard_map/ppermute | solution.py:214
  49.2 1.4 %collective-permute-start.9 = (f32[8,256]{1,0:T(8,128)S(1)}, f32[8,256]{1,0:T(8,128)S(1)}, u32[]{:S(2)}, u32[]{:S(2)}) collective-permute-start(f32[8,256]{1,0:T(8,128)S(1)} %get-tuple-element.31), channel_id=1, source_target_pairs={{0,1},{1,0},{2,3},{3,2},{4,5},{5,4},{6,7},{7,6},{8,9},{9,8},{10,11... | collective-permute-start | bytes 24584 | tf_op jit(solution)/shard_map/ppermute | solution.py:214

commit v13 on v12

--- a/solution.py
+++ b/solution.py
@@ -240,6 +240,7 @@
     state_hbm, rhs_hbm, scale_hbm, disp_hbm, near_ref, own_ref, far_ref, one_ref, three_ref,
     state_ref, rhs_ref, scale_ref, disp_ref, pad_ref, build_ref, sems,
 ):
+    rows = disp_hbm.shape[1]
     copies = [
         pltpu.make_async_copy(a, b, sems.at[i])
         for i, (a, b) in enumerate(
@@ -247,7 +248,8 @@
                 (scale_hbm, scale_ref),
                 (state_hbm, state_ref),
                 (rhs_hbm, rhs_ref),
-                (disp_hbm, disp_ref),
+                (disp_hbm.at[:, 0:8], disp_ref.at[:, 0:8]),
+                (disp_hbm.at[:, rows - 8 : rows], disp_ref.at[:, 8:16]),
             )
         )
     ]
@@ -256,10 +258,19 @@
     odd = lax.axis_index("slab") % 2
     even = lax.axis_index("patch") % 2 == 0
     cols = state_ref.shape[1]
-    for copy in copies:
-        copy.wait()
     for e in range(2):
         build_ref[e] = jnp.zeros((EDGE + 8, 256), F32)
+    copies[0].wait()
+    lines = lines_of(scale_ref, pad_ref)
+    flip = odd == 1
+    first = jnp.where(flip, lines[1:2], lines[0:1])
+    second = jnp.where(flip, lines[0:1], lines[1:2])
+    pair = jnp.concatenate([halves(first), halves(second), jnp.zeros((6, 256), F32)], axis=0)
+    own_ref[3 * cols :, :] = pair.astype(BF)
+    for e in range(2):
+        build_ref[e, 6:8, :] = pair[0:2]
+    copies[1].wait()
+    copies[2].wait()
     for i, row in enumerate((odd, 1 - odd)):
         for part, ref, at, third in (
             (0, state_ref, 2 * i, 8 + i),
@@ -279,18 +290,11 @@
                 build_ref[0, third : third + 1, :] = jnp.where(even, high, low)
                 build_ref[1, third : third + 1, :] = jnp.where(even, low, high)
     near_ref[...] = state_ref[1 - odd].astype(BF)
-    lines = lines_of(scale_ref, pad_ref)
-    flip = odd == 1
-    first = jnp.where(flip, lines[1:2], lines[0:1])
-    second = jnp.where(flip, lines[0:1], lines[1:2])
-    pair = jnp.concatenate([halves(first), halves(second), jnp.zeros((6, 256), F32)], axis=0)
-    own_ref[3 * cols :, :] = pair.astype(BF)
-    for e in range(2):
-        build_ref[e, 6:8, :] = pair[0:2]
-    rows = disp_ref.shape[1]
+    copies[3].wait()
+    copies[4].wait()
     for c in range(3):
         top = halves(disp_ref[c, 0:2, :])
-        bottom = halves(disp_ref[c, rows - 2 : rows, :])
+        bottom = halves(disp_ref[c, 14:16, :])
         at = EDGE + 2 * c
         build_ref[0, at : at + 2, :] = jnp.where(even, bottom, top)
         build_ref[1, at : at + 2, :] = jnp.where(even, top, bottom)
@@ -519,10 +523,10 @@
             pltpu.VMEM(fluid_state.shape, F32),
             pltpu.VMEM(fluid_rhs.shape, F32),
             pltpu.VMEM(element_scale.shape, F32),
-            pltpu.VMEM(displacement.shape, F32),
+            pltpu.VMEM((displacement.shape[0], 16, displacement.shape[2]), F32),
             pltpu.VMEM((8, 128), F32),
             pltpu.VMEM((2, EDGE + 8, width), F32),
-            pltpu.SemaphoreType.DMA((4,)),
+            pltpu.SemaphoreType.DMA((5,)),
         ],
         in_specs=hbm(4),
     )

time: 51.4 us -> 51.3 us (level)
  no operation moved by 1% of the time
where the time goes in v13:
time: 51.3 us; the launch traced here: 51.1 us
  starting transfers between devices  23 us (45%)
  waiting for transfers between devices  17.5 us (34%)
  Pallas kernels  9.54 us (19%)
  between operations  0.97 us (2%)
    all_to_all x1, waiting for transfers between devices, exchange_and_relax(): lax.all_to_all(message.reshape(sources, 8, 128), ('slab', 'patch'), 0, 0,...  10.7 us
    ppermute x1, starting transfers between devices, shards(): outer = lax.ppermute(own, 'slab', outer_pairs)  6.86 us
    all_to_all x1, starting transfers between devices, exchange_and_relax(): lax.all_to_all(message.reshape(sources, 8, 128), ('slab', 'patch'), 0, 0,...  6.85 us
    ppermute x1, waiting for transfers between devices, shards(): lax.ppermute(jnp.concatenate([inner_near] + thin + [far]), 'slab', outer_...  6.41 us
    pallas_call x3, Pallas kernels, call(): pl.pallas_call(kernel, out_shape=out_shape, in_specs=in_specs or vmem(len...  4.15 us
    pallas_call x1, Pallas kernels, exchange_and_relax(): pl.pallas_call(owner_kernel, out_shape=(jax.ShapeDtypeStruct(displacement...  4.13 us
    ppermute x1, starting transfers between devices, shards(): lax.ppermute(jnp.concatenate([inner_near] + thin + [far]), 'slab', outer_...  2.58 us
    ppermute x3, starting transfers between devices, exchange_and_relax(): lax.ppermute(replies[d], 'patch', patch_pairs(d))  2.22 us
  transfers between devices with their start and end apart: 11, of which 3 were waited for; matrix products, arithmetic and copies ran while one was open for 0% of the time, Pallas kernels for 3%

profile of v13, /device:TPU:1, one launch (start us, length us, event | category | flops | bytes accessed | tf_op | source)
XLA Modules:
  0.0 51.1 jit_solution(1098881542892954712)
XLA Ops:
  0.6 0.0 copy-start.4
  0.6 0.0 copy-start.5
  0.7 0.0 copy-start.6
  0.7 1.1 %near.1 = (bf16[64,256]{1,0:T(8,128)(2,1)S(1)}, bf16[200,256]{1,0:T(8,128)(2,1)S(1)}, bf16[64,256]{1,0:T(8,128)(2,1)S(1)}, bf16[24,256]{1,0:T(8,128)(2,1)S(1)}, bf16[24,256]{1,0:T(8,128)(2,1)S(1)}) custom-call(f32[2,64,256]{2,1,0:T(8,128)} %state_ref.1, f32[2,64,256]{2,1,0:T(8,128)} %rhs_ref.1, f32[2,64]{1,0:T(2,128)} %scale_ref.1, f32[3,64,128]{2,1,0:T(8,128)} %disp_ref.3), custom_call_target="tpu_custom_call" | custom-call | tf_op jit(solution)/shard_map/near/pallas_call | solution.py:479
  1.8 1.5 %collective-permute-start = (bf16[24,256]{1,0:T(8,128)(2,1)S(1)}, bf16[24,256]{1,0:T(8,128)(2,1)S(1)}, u32[]{:S(2)}, u32[]{:S(2)}) collective-permute-start(bf16[24,256]{1,0:T(8,128)(2,1)S(1)} %get-tuple-element.18), channel_id=1, source_target_pairs={{0,1},{1,0},{2,3},{3,2},{4,5},{5,4},{6,7},{7,6},{8,9},{9,8},{10,11... | collective-permute-start | bytes 36872 | tf_op jit(solution)/shard_map/ppermute | solution.py:536
  3.3 1.3 %collective-permute-start.1 = (bf16[24,256]{1,0:T(8,128)(2,1)S(1)}, bf16[24,256]{1,0:T(8,128)(2,1)S(1)}, u32[]{:S(2)}, u32[]{:S(2)}) collective-permute-start(bf16[24,256]{1,0:T(8,128)(2,1)S(1)} %get-tuple-element.19), channel_id=1, source_target_pairs={{0,3},{1,2},{2,1},{3,0},{4,7},{5,6},{6,5},{7,4},{8,11},{9,10},{10,... | collective-permute-start | bytes 36872 | tf_op jit(solution)/shard_map/ppermute | solution.py:535
  4.6 1.6 %collective-permute-start.2 = (bf16[64,256]{1,0:T(8,128)(2,1)S(1)}, bf16[64,256]{1,0:T(8,128)(2,1)S(1)}, u32[]{:S(2)}, u32[]{:S(2)}) collective-permute-start(bf16[64,256]{1,0:T(8,128)(2,1)S(1)} %get-tuple-element.20), channel_id=1, source_target_pairs={{0,4},{4,0},{8,12},{12,8},{16,20},{20,16},{24,28},{28,24},{32,36},... | collective-permute-start | bytes 98312 | tf_op jit(solution)/shard_map/ppermute | solution.py:534
  6.2 6.9 %collective-permute-start.4 = (bf16[200,256]{1,0:T(8,128)(2,1)S(1)}, bf16[200,256]{1,0:T(8,128)(2,1)S(1)}, u32[]{:S(2)}, u32[]{:S(2)}) collective-permute-start(bf16[200,256]{1,0:T(8,128)(2,1)S(1)} %get-tuple-element.21), channel_id=1, source_target_pairs={{4,8},{12,16},{20,24},{28,32},{36,40},{44,48},{52,56},{60,64},{68,... | collective-permute-start | bytes 307208 | tf_op jit(solution)/shard_map/ppermute | solution.py:533
  13.1 0.0 collective-permute-done.one_ref
  13.1 0.0 copy-start.8
  13.1 0.0 copy-start.9
  13.1 0.0 copy-start.1
  13.1 0.0 copy-start.2
  13.2 0.0 collective-permute-done.1.three_ref
  13.2 0.0 collective-permute-done.2.near_ref
  13.2 0.1 collective-permute-start.3
  13.3 0.0 copy-start.10
  13.3 0.0 copy-start.11
  13.3 0.0 copy-start.12
  13.4 2.6 %collective-permute-start.5 = (bf16[144,256]{1,0:T(8,128)(2,1)S(1)}, bf16[144,256]{1,0:T(8,128)(2,1)S(1)}, u32[]{:S(2)}, u32[]{:S(2)}) collective-permute-start(bf16[144,256]{1,0:T(8,128)(2,1)S(1)} %pad_maximum_fusion), channel_id=1, source_target_pairs={{4,8},{12,16},{20,24},{28,32},{36,40},{44,48},{52,56},{60,64},{68,... | collective-permute-start | bytes 221192 | tf_op jit(solution)/shard_map/ppermute | solution.py:539
  15.9 0.0 collective-permute-done.4.outer_ref
  15.9 0.0 collective-permute-start.6
  16.0 6.4 %collective-permute-done.5.rest_ref = bf16[144,256]{1,0:T(8,128)(2,1)S(1)} collective-permute-done((bf16[144,256]{1,0:T(8,128)(2,1)S(1)}, bf16[144,256]{1,0:T(8,128)(2,1)S(1)}, u32[]{:S(2)}, u32[]{:S(2)}) %collective-permute-start.5) | collective-permute-done | bytes 73760 | tf_op jit(solution)/shard_map/ppermute | solution.py:539
  22.4 0.0 collective-permute-done.6.relay_ref
  22.4 0.0 collective-permute-done.3.inner_ref
  22.4 0.0 copy-done.4
  22.4 0.0 copy-done.5
  22.4 0.0 copy-done.6
  22.4 0.0 copy-done.3
  22.4 0.0 copy-done.8
  22.4 0.0 copy-done.9
  22.4 0.0 copy-done.1
  22.4 0.0 copy-done.2
  22.5 2.4 %sweep.1 = (f32[2,64,256]{2,1,0:T(8,128)S(1)}, bf16[32,4,8,128]{3,2,1,0:T(8,128)(2,1)}) custom-call(f32[2,64,256]{2,1,0:T(8,128)S(1)} %copy-done.1, f32[2,64,256]{2,1,0:T(8,128)S(1)} %copy-done.2, f32[2,64]{1,0:T(2,128)S(1)} %copy-done.10, bf16[64,256]{1,0:T(8,128)(2,1)S(1)} %collective-permute-done.2.near_ref, ...), custom_call_target="tpu_custom_call" | custom-call | tf_op jit(solution)/shard_map/sweep/pallas_call | solution.py:479
  24.9 0.0 copy-start
  24.9 0.0 copy-start.7
  24.9 6.9 %all-to-all-start = ((bf16[128,8,128]{2,1,0:T(8,128)(2,1)}), bf16[128,8,128]{2,1,0:T(8,128)(2,1)S(1)}, u32[]{:S(2)}, u32[]{:S(2)}) async-start(bf16[128,8,128]{2,1,0:T(8,128)(2,1)} %bitcast), calls=%async_computation | async-start | bytes 524288 | tf_op jit(solution)/shard_map/all_to_all | solution.py:201
  31.8 0.7 %shell.1 = (f32[3,64,128]{2,1,0:T(8,128)S(1)}, f32[2,64,256]{2,1,0:T(8,128)}) custom-call(bf16[8,256]{1,0:T(8,128)(2,1)S(1)} %get-tuple-element.34.one_ref, bf16[8,256]{1,0:T(8,128)(2,1)S(1)} %get-tuple-element.36.three_ref, f32[3,64,128]{2,1,0:T(8,128)S(1)} %copy-done, f32[64,128]{1,0:T(8,128)S(1)} %copy-done.7, f32[2,64,256]{2,1,0:T(8,128)S(1)} %get-tuple-element.24.state_ref), custom_call_target="tpu_custom_call" | custom-call | tf_op jit(solution)/shard_map/shell/pallas_call | solution.py:479
  32.4 10.7 %all-to-all-done.got_ref = bf16[128,8,128]{2,1,0:T(8,128)(2,1)S(1)} async-done(((bf16[128,8,128]{2,1,0:T(8,128)(2,1)}), bf16[128,8,128]{2,1,0:T(8,128)(2,1)S(1)}, u32[]{:S(2)}, u32[]{:S(2)}) %all-to-all-start) | async-done | bytes 262176 | tf_op jit(solution)/shard_map/all_to_all | solution.py:201
  43.1 4.1 %owner.1 = (f32[3,64,128]{2,1,0:T(8,128)S(1)}, f32[8,256]{1,0:T(8,128)S(1)}, f32[8,256]{1,0:T(8,128)S(1)}, f32[8,256]{1,0:T(8,128)S(1)}, f32[8,256]{1,0:T(8,128)S(1)}) custom-call(bf16[128,8,128]{2,1,0:T(8,128)(2,1)S(1)} %all-to-all-done.got_ref, f32[3,64,128]{2,1,0:T(8,128)S(1)} %copy-done, f32[64,128]{1,0:T(8,128)S(1)} %copy-done.7, ...), custom_call_target="tpu_custom_call" | custom-call | tf_op jit(solution)/shard_map/owner/pallas_call | solution.py:205
  47.3 0.7 %collective-permute-start.7 = (f32[8,256]{1,0:T(8,128)S(1)}, f32[8,256]{1,0:T(8,128)S(1)}, u32[]{:S(2)}, u32[]{:S(2)}) collective-permute-start(f32[8,256]{1,0:T(8,128)S(1)} %get-tuple-element.29), channel_id=1, source_target_pairs={{0,3},{1,2},{2,1},{3,0},{4,7},{5,6},{6,5},{7,4},{8,11},{9,10},{10,... | collective-permute-start | bytes 24584 | tf_op jit(solution)/shard_map/ppermute | solution.py:214
  47.9 1.2 %collective-permute-start.8 = (f32[8,256]{1,0:T(8,128)S(1)}, f32[8,256]{1,0:T(8,128)S(1)}, u32[]{:S(2)}, u32[]{:S(2)}) collective-permute-start(f32[8,256]{1,0:T(8,128)S(1)} %get-tuple-element.30), channel_id=1, source_target_pairs={{0,2},{1,3},{2,0},{3,1},{4,6},{5,7},{6,4},{7,5},{8,10},{9,11},{10,... | collective-permute-start | bytes 24584 | tf_op jit(solution)/shard_map/ppermute | solution.py:214
  49.1 0.4 collective-permute-start.9
  49.5 0.6 %store_shell.1 = f32[3,64,128]{2,1,0:T(8,128)} custom-call(f32[3,64,128]{2,1,0:T(8,128)S(1)} %get-tuple-element.28.value_ref), custom_call_target="tpu_custom_call" | custom-call | tf_op jit(solution)/shard_map/store_shell/pallas_call | solution.py:122
  50.1 0.3 collective-permute-done.7.r3
  50.5 0.0 collective-permute-done.8.r2
  50.5 0.0 collective-permute-done.9.r1
  50.5 0.6 %finish.1 = f32[3,1,1,1024]{3,2,1,0:T(1,128)} custom-call(f32[8,256]{1,0:T(8,128)S(1)} %collective-permute-done.7.r3, f32[8,256]{1,0:T(8,128)S(1)} %collective-permute-done.8.r2, f32[8,256]{1,0:T(8,128)S(1)} %collective-permute-done.9.r1, f32[8,256]{1,0:T(8,128)S(1)} %get-tuple-element.32.r0), custom_call_target="tpu_custom_call" | custom-call | tf_op jit(solution)/shard_map/finish/pallas_call | solution.py:216
  (15 shorter events, 0.0 us)
Async XLA Ops:
  0.6 21.7 %copy-start.4 = (bf16[256,256]{1,0:T(8,128)(2,1)S(1)}, bf16[256,256]{1,0:T(8,128)(2,1)}, u32[]{:S(2)}) copy-start(bf16[256,256]{1,0:T(8,128)(2,1)} %x_ref.1) | copy-start | bytes 393220
  0.6 21.7 %copy-start.5 = (bf16[256,256]{1,0:T(8,128)(2,1)S(1)}, bf16[256,256]{1,0:T(8,128)(2,1)}, u32[]{:S(2)}) copy-start(bf16[256,256]{1,0:T(8,128)(2,1)} %y_ref.1) | copy-start | bytes 393220
  0.7 21.7 %copy-start.6 = (bf16[256,256]{1,0:T(8,128)(2,1)S(1)}, bf16[256,256]{1,0:T(8,128)(2,1)}, u32[]{:S(2)}) copy-start(bf16[256,256]{1,0:T(8,128)(2,1)} %inverse_ref.1) | copy-start | bytes 393220
  1.8 11.3 %collective-permute-start = (bf16[24,256]{1,0:T(8,128)(2,1)S(1)}, bf16[24,256]{1,0:T(8,128)(2,1)S(1)}, u32[]{:S(2)}, u32[]{:S(2)}) collective-permute-start(bf16[24,256]{1,0:T(8,128)(2,1)S(1)} %get-tuple-element.18), channel_id=1, source_target_pairs={{0,1},{1,0},{2,3},{3,2},{4,5},{5,4},{6,7},{7,6},{8,9},{9,8},{10,11... | collective-permute-start | bytes 36872 | tf_op jit(solution)/shard_map/ppermute | solution.py:536
  3.3 9.9 %collective-permute-start.1 = (bf16[24,256]{1,0:T(8,128)(2,1)S(1)}, bf16[24,256]{1,0:T(8,128)(2,1)S(1)}, u32[]{:S(2)}, u32[]{:S(2)}) collective-permute-start(bf16[24,256]{1,0:T(8,128)(2,1)S(1)} %get-tuple-element.19), channel_id=1, source_target_pairs={{0,3},{1,2},{2,1},{3,0},{4,7},{5,6},{6,5},{7,4},{8,11},{9,10},{10,... | collective-permute-start | bytes 36872 | tf_op jit(solution)/shard_map/ppermute | solution.py:535
  4.6 8.6 %collective-permute-start.2 = (bf16[64,256]{1,0:T(8,128)(2,1)S(1)}, bf16[64,256]{1,0:T(8,128)(2,1)S(1)}, u32[]{:S(2)}, u32[]{:S(2)}) collective-permute-start(bf16[64,256]{1,0:T(8,128)(2,1)S(1)} %get-tuple-element.20), channel_id=1, source_target_pairs={{0,4},{4,0},{8,12},{12,8},{16,20},{20,16},{24,28},{28,24},{32,36},... | collective-permute-start | bytes 98312 | tf_op jit(solution)/shard_map/ppermute | solution.py:534
  6.2 9.7 %collective-permute-start.4 = (bf16[200,256]{1,0:T(8,128)(2,1)S(1)}, bf16[200,256]{1,0:T(8,128)(2,1)S(1)}, u32[]{:S(2)}, u32[]{:S(2)}) collective-permute-start(bf16[200,256]{1,0:T(8,128)(2,1)S(1)} %get-tuple-element.21), channel_id=1, source_target_pairs={{4,8},{12,16},{20,24},{28,32},{36,40},{44,48},{52,56},{60,64},{68,... | collective-permute-start | bytes 307208 | tf_op jit(solution)/shard_map/ppermute | solution.py:533
  13.1 9.3 %copy-start.3 = (bf16[256,256]{1,0:T(8,128)(2,1)S(1)}, bf16[256,256]{1,0:T(8,128)(2,1)}, u32[]{:S(2)}) copy-start(bf16[256,256]{1,0:T(8,128)(2,1)} %matrix_ref.1) | copy-start | bytes 393220
  13.1 9.3 %copy-start.8 = (s32[1,1,1024]{2,1,0:T(1,128)S(1)}, s32[1,1,1024]{2,1,0:T(1,128)}, u32[]{:S(2)}) copy-start(s32[1,1,1024]{2,1,0:T(1,128)} %elem_hbm.1) | copy-start | bytes 12292
  13.1 9.3 %copy-start.9 = (s32[1,1,1024]{2,1,0:T(1,128)S(1)}, s32[1,1,1024]{2,1,0:T(1,128)}, u32[]{:S(2)}) copy-start(s32[1,1,1024]{2,1,0:T(1,128)} %point_hbm.1) | copy-start | bytes 12292
  13.1 9.3 %copy-start.1 = (f32[2,64,256]{2,1,0:T(8,128)S(1)}, f32[2,64,256]{2,1,0:T(8,128)}, u32[]{:S(2)}) copy-start(f32[2,64,256]{2,1,0:T(8,128)} %state_ref.1) | copy-start | bytes 393220
  13.1 9.3 %copy-start.2 = (f32[2,64,256]{2,1,0:T(8,128)S(1)}, f32[2,64,256]{2,1,0:T(8,128)}, u32[]{:S(2)}) copy-start(f32[2,64,256]{2,1,0:T(8,128)} %rhs_ref.1) | copy-start | bytes 393220
  13.2 9.2 %collective-permute-start.3 = (bf16[232,256]{1,0:T(8,128)(2,1)S(1)}, bf16[232,256]{1,0:T(8,128)(2,1)S(1)}, u32[]{:S(2)}, u32[]{:S(2)}) collective-permute-start(bf16[232,256]{1,0:T(8,128)(2,1)S(1)} %constant_dynamic-update-slice_fusion), channel_id=1, source_target_pairs={{0,4},{4,0},{8,12},{12,8},{16,20},{20,16},{24,28},{28,24},{32,36},... | collective-permute-start | bytes 356360 | tf_op jit(solution)/shard_map/ppermute | solution.py:542
  13.3 9.1 %copy-start.10 = (f32[2,64]{1,0:T(2,128)S(1)}, f32[2,64]{1,0:T(2,128)}, u32[]{:S(2)}) copy-start(f32[2,64]{1,0:T(2,128)} %scale_ref.1) | copy-start | bytes 1540
  13.3 9.1 %copy-start.11 = (bf16[3,256]{1,0:T(4,128)(2,1)S(1)}, bf16[3,256]{1,0:T(4,128)(2,1)}, u32[]{:S(2)}) copy-start(bf16[3,256]{1,0:T(4,128)(2,1)} %tmap_ref.1) | copy-start | bytes 4612
  13.3 9.1 %copy-start.12 = (s32[1,1,4]{2,1,0:T(1,128)S(1)}, s32[1,1,4]{2,1,0:T(1,128)}, u32[]{:S(2)}) copy-start(s32[1,1,4]{2,1,0:T(1,128)} %count_hbm.1) | copy-start | bytes 52
  13.4 9.0 %collective-permute-start.5 = (bf16[144,256]{1,0:T(8,128)(2,1)S(1)}, bf16[144,256]{1,0:T(8,128)(2,1)S(1)}, u32[]{:S(2)}, u32[]{:S(2)}) collective-permute-start(bf16[144,256]{1,0:T(8,128)(2,1)S(1)} %pad_maximum_fusion), channel_id=1, source_target_pairs={{4,8},{12,16},{20,24},{28,32},{36,40},{44,48},{52,56},{60,64},{68,... | collective-permute-start | bytes 221192 | tf_op jit(solution)/shard_map/ppermute | solution.py:539
  15.9 6.4 %collective-permute-start.6 = (bf16[64,256]{1,0:T(8,128)(2,1)S(1)}, bf16[64,256]{1,0:T(8,128)(2,1)S(1)}, u32[]{:S(2)}, u32[]{:S(2)}) collective-permute-start(bf16[64,256]{1,0:T(8,128)(2,1)S(1)} %slice.42), channel_id=1, source_target_pairs={{0,4},{4,0},{8,12},{12,8},{16,20},{20,16},{24,28},{28,24},{32,36},... | collective-permute-start | bytes 98312 | tf_op jit(solution)/shard_map/ppermute | solution.py:543
  24.9 6.9 %copy-start = (f32[3,64,128]{2,1,0:T(8,128)S(1)}, f32[3,64,128]{2,1,0:T(8,128)}, u32[]{:S(2)}) copy-start(f32[3,64,128]{2,1,0:T(8,128)} %disp_ref.3) | copy-start | bytes 294916
  24.9 6.9 %copy-start.7 = (f32[64,128]{1,0:T(8,128)S(1)}, f32[64,128]{1,0:T(8,128)}, u32[]{:S(2)}) copy-start(f32[64,128]{1,0:T(8,128)} %stiff_ref.3) | copy-start | bytes 98308
  24.9 18.2 %all-to-all-start = ((bf16[128,8,128]{2,1,0:T(8,128)(2,1)}), bf16[128,8,128]{2,1,0:T(8,128)(2,1)S(1)}, u32[]{:S(2)}, u32[]{:S(2)}) async-start(bf16[128,8,128]{2,1,0:T(8,128)(2,1)} %bitcast), calls=%async_computation | async-start | bytes 524288 | tf_op jit(solution)/shard_map/all_to_all | solution.py:201
  47.3 3.2 %collective-permute-start.7 = (f32[8,256]{1,0:T(8,128)S(1)}, f32[8,256]{1,0:T(8,128)S(1)}, u32[]{:S(2)}, u32[]{:S(2)}) collective-permute-start(f32[8,256]{1,0:T(8,128)S(1)} %get-tuple-element.29), channel_id=1, source_target_pairs={{0,3},{1,2},{2,1},{3,0},{4,7},{5,6},{6,5},{7,4},{8,11},{9,10},{10,... | collective-permute-start | bytes 24584 | tf_op jit(solution)/shard_map/ppermute | solution.py:214
  47.9 2.6 %collective-permute-start.8 = (f32[8,256]{1,0:T(8,128)S(1)}, f32[8,256]{1,0:T(8,128)S(1)}, u32[]{:S(2)}, u32[]{:S(2)}) collective-permute-start(f32[8,256]{1,0:T(8,128)S(1)} %get-tuple-element.30), channel_id=1, source_target_pairs={{0,2},{1,3},{2,0},{3,1},{4,6},{5,7},{6,4},{7,5},{8,10},{9,11},{10,... | collective-permute-start | bytes 24584 | tf_op jit(solution)/shard_map/ppermute | solution.py:214
  49.1 1.4 %collective-permute-start.9 = (f32[8,256]{1,0:T(8,128)S(1)}, f32[8,256]{1,0:T(8,128)S(1)}, u32[]{:S(2)}, u32[]{:S(2)}) collective-permute-start(f32[8,256]{1,0:T(8,128)S(1)} %get-tuple-element.31), channel_id=1, source_target_pairs={{0,1},{1,0},{2,3},{3,2},{4,5},{5,4},{6,7},{7,6},{8,9},{9,8},{10,11... | collective-permute-start | bytes 24584 | tf_op jit(solution)/shard_map/ppermute | solution.py:214

commit v14 on v13

--- a/solution.py
+++ b/solution.py
@@ -439,7 +439,9 @@
     elem = elem_ref[0]
     owners = rows_ref.shape[0]
     live, code = slot_codes(point_ref[0], count_ref.at[0], owners)
-    hot = ((iota((2 * cols, elem.shape[1]), 0) == elem) & live).astype(F32).astype(BF)
+    chosen = jnp.where(live, elem, -1).astype(F32).astype(BF)
+    place = iota((2 * cols, elem.shape[1]), 0).astype(F32).astype(BF)
+    hot = jnp.where(place == chosen, jnp.ones(place.shape, BF), jnp.zeros(place.shape, BF))
     pull = jnp.dot(nt(tmap_ref[...], final).astype(BF), hot, preferred_element_type=F32)
     for k in range(owners):
         for j in range(4):
@@ -467,8 +469,9 @@
     nx = (up + down).astype(BF)
     ny = (pltpu.roll(mid, 1, 1) + pltpu.roll(mid, wide - 1, 1)).astype(BF)
     own = jnp.dot(mid.astype(BF).reshape(flat), matrix_ref[...], preferred_element_type=F32)
-    side = jnp.dot(nx.reshape(flat), x_ref[...], preferred_element_type=F32)
-    side += jnp.dot(ny.reshape(flat), y_ref[...], preferred_element_type=F32)
+    both = jnp.concatenate([nx.reshape(flat), ny.reshape(flat)], axis=1)
+    couple = jnp.concatenate([x_ref[...], y_ref[...]], axis=0)
+    side = jnp.dot(both, couple, preferred_element_type=F32)
     residue = (rhs.reshape(flat) - (scale.reshape(flat) * own - side)).astype(BF)
     update = jnp.dot(residue, inverse_ref[...], preferred_element_type=F32)
     update = update * inverse_scale.reshape(flat)

time: 51.3 us -> 51.3 us (level)
  no operation moved by 1% of the time
where the time goes in v14:
time: 51.3 us; the launch traced here: 51.2 us
  starting transfers between devices  23 us (45%)
  waiting for transfers between devices  17.5 us (34%)
  Pallas kernels  9.59 us (19%)
  between operations  0.97 us (2%)
    all_to_all x1, waiting for transfers between devices, exchange_and_relax(): lax.all_to_all(message.reshape(sources, 8, 128), ('slab', 'patch'), 0, 0,...  10.7 us
    ppermute x1, starting transfers between devices, shards(): outer = lax.ppermute(own, 'slab', outer_pairs)  6.86 us
    all_to_all x1, starting transfers between devices, exchange_and_relax(): lax.all_to_all(message.reshape(sources, 8, 128), ('slab', 'patch'), 0, 0,...  6.85 us
    ppermute x1, waiting for transfers between devices, shards(): lax.ppermute(jnp.concatenate([inner_near] + thin + [far]), 'slab', outer_...  6.41 us
    pallas_call x3, Pallas kernels, call(): pl.pallas_call(kernel, out_shape=out_shape, in_specs=in_specs or vmem(len...  4.2 us
    pallas_call x1, Pallas kernels, exchange_and_relax(): pl.pallas_call(owner_kernel, out_shape=(jax.ShapeDtypeStruct(displacement...  4.13 us
    ppermute x1, starting transfers between devices, shards(): lax.ppermute(jnp.concatenate([inner_near] + thin + [far]), 'slab', outer_...  2.58 us
    ppermute x3, starting transfers between devices, exchange_and_relax(): lax.ppermute(replies[d], 'patch', patch_pairs(d))  2.22 us
  transfers between devices with their start and end apart: 11, of which 3 were waited for; matrix products, arithmetic and copies ran while one was open for 0% of the time, Pallas kernels for 3%

profile of v14, /device:TPU:1, one launch (start us, length us, event | category | flops | bytes accessed | tf_op | source)
XLA Modules:
  0.0 51.2 jit_solution(11596246125962242924)
XLA Ops:
  0.6 0.0 copy-start.4
  0.6 0.0 copy-start.5
  0.7 0.0 copy-start.6
  0.7 1.1 %near.1 = (bf16[64,256]{1,0:T(8,128)(2,1)S(1)}, bf16[200,256]{1,0:T(8,128)(2,1)S(1)}, bf16[64,256]{1,0:T(8,128)(2,1)S(1)}, bf16[24,256]{1,0:T(8,128)(2,1)S(1)}, bf16[24,256]{1,0:T(8,128)(2,1)S(1)}) custom-call(f32[2,64,256]{2,1,0:T(8,128)} %state_ref.1, f32[2,64,256]{2,1,0:T(8,128)} %rhs_ref.1, f32[2,64]{1,0:T(2,128)} %scale_ref.1, f32[3,64,128]{2,1,0:T(8,128)} %disp_ref.3), custom_call_target="tpu_custom_call" | custom-call | tf_op jit(solution)/shard_map/near/pallas_call | solution.py:482
  1.8 1.5 %collective-permute-start = (bf16[24,256]{1,0:T(8,128)(2,1)S(1)}, bf16[24,256]{1,0:T(8,128)(2,1)S(1)}, u32[]{:S(2)}, u32[]{:S(2)}) collective-permute-start(bf16[24,256]{1,0:T(8,128)(2,1)S(1)} %get-tuple-element.18), channel_id=1, source_target_pairs={{0,1},{1,0},{2,3},{3,2},{4,5},{5,4},{6,7},{7,6},{8,9},{9,8},{10,11... | collective-permute-start | bytes 36872 | tf_op jit(solution)/shard_map/ppermute | solution.py:539
  3.3 1.3 %collective-permute-start.1 = (bf16[24,256]{1,0:T(8,128)(2,1)S(1)}, bf16[24,256]{1,0:T(8,128)(2,1)S(1)}, u32[]{:S(2)}, u32[]{:S(2)}) collective-permute-start(bf16[24,256]{1,0:T(8,128)(2,1)S(1)} %get-tuple-element.19), channel_id=1, source_target_pairs={{0,3},{1,2},{2,1},{3,0},{4,7},{5,6},{6,5},{7,4},{8,11},{9,10},{10,... | collective-permute-start | bytes 36872 | tf_op jit(solution)/shard_map/ppermute | solution.py:538
  4.6 1.6 %collective-permute-start.2 = (bf16[64,256]{1,0:T(8,128)(2,1)S(1)}, bf16[64,256]{1,0:T(8,128)(2,1)S(1)}, u32[]{:S(2)}, u32[]{:S(2)}) collective-permute-start(bf16[64,256]{1,0:T(8,128)(2,1)S(1)} %get-tuple-element.20), channel_id=1, source_target_pairs={{0,4},{4,0},{8,12},{12,8},{16,20},{20,16},{24,28},{28,24},{32,36},... | collective-permute-start | bytes 98312 | tf_op jit(solution)/shard_map/ppermute | solution.py:537
  6.2 6.9 %collective-permute-start.4 = (bf16[200,256]{1,0:T(8,128)(2,1)S(1)}, bf16[200,256]{1,0:T(8,128)(2,1)S(1)}, u32[]{:S(2)}, u32[]{:S(2)}) collective-permute-start(bf16[200,256]{1,0:T(8,128)(2,1)S(1)} %get-tuple-element.21), channel_id=1, source_target_pairs={{4,8},{12,16},{20,24},{28,32},{36,40},{44,48},{52,56},{60,64},{68,... | collective-permute-start | bytes 307208 | tf_op jit(solution)/shard_map/ppermute | solution.py:536
  13.1 0.0 collective-permute-done.one_ref
  13.1 0.0 copy-start.8
  13.1 0.0 copy-start.9
  13.1 0.0 copy-start.1
  13.1 0.0 copy-start.2
  13.2 0.0 collective-permute-done.1.three_ref
  13.2 0.0 collective-permute-done.2.near_ref
  13.2 0.1 collective-permute-start.3
  13.3 0.0 copy-start.10
  13.3 0.0 copy-start.11
  13.3 0.0 copy-start.12
  13.4 2.6 %collective-permute-start.5 = (bf16[144,256]{1,0:T(8,128)(2,1)S(1)}, bf16[144,256]{1,0:T(8,128)(2,1)S(1)}, u32[]{:S(2)}, u32[]{:S(2)}) collective-permute-start(bf16[144,256]{1,0:T(8,128)(2,1)S(1)} %pad_maximum_fusion), channel_id=1, source_target_pairs={{4,8},{12,16},{20,24},{28,32},{36,40},{44,48},{52,56},{60,64},{68,... | collective-permute-start | bytes 221192 | tf_op jit(solution)/shard_map/ppermute | solution.py:542
  15.9 0.0 collective-permute-done.4.outer_ref
  15.9 0.0 collective-permute-start.6
  16.0 6.4 %collective-permute-done.5.rest_ref = bf16[144,256]{1,0:T(8,128)(2,1)S(1)} collective-permute-done((bf16[144,256]{1,0:T(8,128)(2,1)S(1)}, bf16[144,256]{1,0:T(8,128)(2,1)S(1)}, u32[]{:S(2)}, u32[]{:S(2)}) %collective-permute-start.5) | collective-permute-done | bytes 73760 | tf_op jit(solution)/shard_map/ppermute | solution.py:542
  22.4 0.0 collective-permute-done.6.relay_ref
  22.4 0.0 collective-permute-done.3.inner_ref
  22.4 0.0 copy-done.4
  22.4 0.0 copy-done.5
  22.4 0.0 copy-done.6
  22.4 0.0 copy-done.3
  22.4 0.0 copy-done.8
  22.4 0.0 copy-done.9
  22.5 2.4 %sweep.1 = (f32[2,64,256]{2,1,0:T(8,128)S(1)}, bf16[32,4,8,128]{3,2,1,0:T(8,128)(2,1)}) custom-call(f32[2,64,256]{2,1,0:T(8,128)S(1)} %copy-done.1, f32[2,64,256]{2,1,0:T(8,128)S(1)} %copy-done.2, f32[2,64]{1,0:T(2,128)S(1)} %copy-done.10, bf16[64,256]{1,0:T(8,128)(2,1)S(1)} %collective-permute-done.2.near_ref, ...), custom_call_target="tpu_custom_call" | custom-call | tf_op jit(solution)/shard_map/sweep/pallas_call | solution.py:482
  24.9 0.0 copy-start
  24.9 0.0 copy-start.7
  24.9 6.9 %all-to-all-start = ((bf16[128,8,128]{2,1,0:T(8,128)(2,1)}), bf16[128,8,128]{2,1,0:T(8,128)(2,1)S(1)}, u32[]{:S(2)}, u32[]{:S(2)}) async-start(bf16[128,8,128]{2,1,0:T(8,128)(2,1)} %bitcast), calls=%async_computation | async-start | bytes 524288 | tf_op jit(solution)/shard_map/all_to_all | solution.py:201
  31.8 0.0 copy-done
  31.8 0.0 copy-done.7
  31.8 0.7 %shell.1 = (f32[3,64,128]{2,1,0:T(8,128)S(1)}, f32[2,64,256]{2,1,0:T(8,128)}) custom-call(bf16[8,256]{1,0:T(8,128)(2,1)S(1)} %get-tuple-element.34.one_ref, bf16[8,256]{1,0:T(8,128)(2,1)S(1)} %get-tuple-element.36.three_ref, f32[3,64,128]{2,1,0:T(8,128)S(1)} %copy-done, f32[64,128]{1,0:T(8,128)S(1)} %copy-done.7, f32[2,64,256]{2,1,0:T(8,128)S(1)} %get-tuple-element.24.state_ref), custom_call_target="tpu_custom_call" | custom-call | tf_op jit(solution)/shard_map/shell/pallas_call | solution.py:482
  32.5 10.7 %all-to-all-done.got_ref = bf16[128,8,128]{2,1,0:T(8,128)(2,1)S(1)} async-done(((bf16[128,8,128]{2,1,0:T(8,128)(2,1)}), bf16[128,8,128]{2,1,0:T(8,128)(2,1)S(1)}, u32[]{:S(2)}, u32[]{:S(2)}) %all-to-all-start) | async-done | bytes 262176 | tf_op jit(solution)/shard_map/all_to_all | solution.py:201
  43.2 4.1 %owner.1 = (f32[3,64,128]{2,1,0:T(8,128)S(1)}, f32[8,256]{1,0:T(8,128)S(1)}, f32[8,256]{1,0:T(8,128)S(1)}, f32[8,256]{1,0:T(8,128)S(1)}, f32[8,256]{1,0:T(8,128)S(1)}) custom-call(bf16[128,8,128]{2,1,0:T(8,128)(2,1)S(1)} %all-to-all-done.got_ref, f32[3,64,128]{2,1,0:T(8,128)S(1)} %copy-done, f32[64,128]{1,0:T(8,128)S(1)} %copy-done.7, ...), custom_call_target="tpu_custom_call" | custom-call | tf_op jit(solution)/shard_map/owner/pallas_call | solution.py:205
  47.3 0.7 %collective-permute-start.7 = (f32[8,256]{1,0:T(8,128)S(1)}, f32[8,256]{1,0:T(8,128)S(1)}, u32[]{:S(2)}, u32[]{:S(2)}) collective-permute-start(f32[8,256]{1,0:T(8,128)S(1)} %get-tuple-element.29), channel_id=1, source_target_pairs={{0,3},{1,2},{2,1},{3,0},{4,7},{5,6},{6,5},{7,4},{8,11},{9,10},{10,... | collective-permute-start | bytes 24584 | tf_op jit(solution)/shard_map/ppermute | solution.py:214
  48.0 1.2 %collective-permute-start.8 = (f32[8,256]{1,0:T(8,128)S(1)}, f32[8,256]{1,0:T(8,128)S(1)}, u32[]{:S(2)}, u32[]{:S(2)}) collective-permute-start(f32[8,256]{1,0:T(8,128)S(1)} %get-tuple-element.30), channel_id=1, source_target_pairs={{0,2},{1,3},{2,0},{3,1},{4,6},{5,7},{6,4},{7,5},{8,10},{9,11},{10,... | collective-permute-start | bytes 24584 | tf_op jit(solution)/shard_map/ppermute | solution.py:214
  49.2 0.4 collective-permute-start.9
  49.5 0.6 %store_shell.1 = f32[3,64,128]{2,1,0:T(8,128)} custom-call(f32[3,64,128]{2,1,0:T(8,128)S(1)} %get-tuple-element.28.value_ref), custom_call_target="tpu_custom_call" | custom-call | tf_op jit(solution)/shard_map/store_shell/pallas_call | solution.py:122
  50.2 0.4 collective-permute-done.7.r3
  50.5 0.0 collective-permute-done.8.r2
  50.5 0.0 collective-permute-done.9.r1
  50.5 0.6 %finish.1 = f32[3,1,1,1024]{3,2,1,0:T(1,128)} custom-call(f32[8,256]{1,0:T(8,128)S(1)} %collective-permute-done.7.r3, f32[8,256]{1,0:T(8,128)S(1)} %collective-permute-done.8.r2, f32[8,256]{1,0:T(8,128)S(1)} %collective-permute-done.9.r1, f32[8,256]{1,0:T(8,128)S(1)} %get-tuple-element.32.r0), custom_call_target="tpu_custom_call" | custom-call | tf_op jit(solution)/shard_map/finish/pallas_call | solution.py:216
  (15 shorter events, 0.0 us)
Async XLA Ops:
  0.6 21.7 %copy-start.4 = (bf16[256,256]{1,0:T(8,128)(2,1)S(1)}, bf16[256,256]{1,0:T(8,128)(2,1)}, u32[]{:S(2)}) copy-start(bf16[256,256]{1,0:T(8,128)(2,1)} %x_ref.1) | copy-start | bytes 393220
  0.6 21.7 %copy-start.5 = (bf16[256,256]{1,0:T(8,128)(2,1)S(1)}, bf16[256,256]{1,0:T(8,128)(2,1)}, u32[]{:S(2)}) copy-start(bf16[256,256]{1,0:T(8,128)(2,1)} %y_ref.1) | copy-start | bytes 393220
  0.7 21.7 %copy-start.6 = (bf16[256,256]{1,0:T(8,128)(2,1)S(1)}, bf16[256,256]{1,0:T(8,128)(2,1)}, u32[]{:S(2)}) copy-start(bf16[256,256]{1,0:T(8,128)(2,1)} %inverse_ref.1) | copy-start | bytes 393220
  1.8 11.3 %collective-permute-start = (bf16[24,256]{1,0:T(8,128)(2,1)S(1)}, bf16[24,256]{1,0:T(8,128)(2,1)S(1)}, u32[]{:S(2)}, u32[]{:S(2)}) collective-permute-start(bf16[24,256]{1,0:T(8,128)(2,1)S(1)} %get-tuple-element.18), channel_id=1, source_target_pairs={{0,1},{1,0},{2,3},{3,2},{4,5},{5,4},{6,7},{7,6},{8,9},{9,8},{10,11... | collective-permute-start | bytes 36872 | tf_op jit(solution)/shard_map/ppermute | solution.py:539
  3.3 9.9 %collective-permute-start.1 = (bf16[24,256]{1,0:T(8,128)(2,1)S(1)}, bf16[24,256]{1,0:T(8,128)(2,1)S(1)}, u32[]{:S(2)}, u32[]{:S(2)}) collective-permute-start(bf16[24,256]{1,0:T(8,128)(2,1)S(1)} %get-tuple-element.19), channel_id=1, source_target_pairs={{0,3},{1,2},{2,1},{3,0},{4,7},{5,6},{6,5},{7,4},{8,11},{9,10},{10,... | collective-permute-start | bytes 36872 | tf_op jit(solution)/shard_map/ppermute | solution.py:538
  4.6 8.6 %collective-permute-start.2 = (bf16[64,256]{1,0:T(8,128)(2,1)S(1)}, bf16[64,256]{1,0:T(8,128)(2,1)S(1)}, u32[]{:S(2)}, u32[]{:S(2)}) collective-permute-start(bf16[64,256]{1,0:T(8,128)(2,1)S(1)} %get-tuple-element.20), channel_id=1, source_target_pairs={{0,4},{4,0},{8,12},{12,8},{16,20},{20,16},{24,28},{28,24},{32,36},... | collective-permute-start | bytes 98312 | tf_op jit(solution)/shard_map/ppermute | solution.py:537
  6.2 9.7 %collective-permute-start.4 = (bf16[200,256]{1,0:T(8,128)(2,1)S(1)}, bf16[200,256]{1,0:T(8,128)(2,1)S(1)}, u32[]{:S(2)}, u32[]{:S(2)}) collective-permute-start(bf16[200,256]{1,0:T(8,128)(2,1)S(1)} %get-tuple-element.21), channel_id=1, source_target_pairs={{4,8},{12,16},{20,24},{28,32},{36,40},{44,48},{52,56},{60,64},{68,... | collective-permute-start | bytes 307208 | tf_op jit(solution)/shard_map/ppermute | solution.py:536
  13.1 9.3 %copy-start.3 = (bf16[256,256]{1,0:T(8,128)(2,1)S(1)}, bf16[256,256]{1,0:T(8,128)(2,1)}, u32[]{:S(2)}) copy-start(bf16[256,256]{1,0:T(8,128)(2,1)} %matrix_ref.1) | copy-start | bytes 393220
  13.1 9.3 %copy-start.8 = (s32[1,1,1024]{2,1,0:T(1,128)S(1)}, s32[1,1,1024]{2,1,0:T(1,128)}, u32[]{:S(2)}) copy-start(s32[1,1,1024]{2,1,0:T(1,128)} %elem_hbm.1) | copy-start | bytes 12292
  13.1 9.3 %copy-start.9 = (s32[1,1,1024]{2,1,0:T(1,128)S(1)}, s32[1,1,1024]{2,1,0:T(1,128)}, u32[]{:S(2)}) copy-start(s32[1,1,1024]{2,1,0:T(1,128)} %point_hbm.1) | copy-start | bytes 12292
  13.1 9.3 %copy-start.1 = (f32[2,64,256]{2,1,0:T(8,128)S(1)}, f32[2,64,256]{2,1,0:T(8,128)}, u32[]{:S(2)}) copy-start(f32[2,64,256]{2,1,0:T(8,128)} %state_ref.1) | copy-start | bytes 393220
  13.1 9.3 %copy-start.2 = (f32[2,64,256]{2,1,0:T(8,128)S(1)}, f32[2,64,256]{2,1,0:T(8,128)}, u32[]{:S(2)}) copy-start(f32[2,64,256]{2,1,0:T(8,128)} %rhs_ref.1) | copy-start | bytes 393220
  13.2 9.2 %collective-permute-start.3 = (bf16[232,256]{1,0:T(8,128)(2,1)S(1)}, bf16[232,256]{1,0:T(8,128)(2,1)S(1)}, u32[]{:S(2)}, u32[]{:S(2)}) collective-permute-start(bf16[232,256]{1,0:T(8,128)(2,1)S(1)} %constant_dynamic-update-slice_fusion), channel_id=1, source_target_pairs={{0,4},{4,0},{8,12},{12,8},{16,20},{20,16},{24,28},{28,24},{32,36},... | collective-permute-start | bytes 356360 | tf_op jit(solution)/shard_map/ppermute | solution.py:545
  13.3 9.1 %copy-start.10 = (f32[2,64]{1,0:T(2,128)S(1)}, f32[2,64]{1,0:T(2,128)}, u32[]{:S(2)}) copy-start(f32[2,64]{1,0:T(2,128)} %scale_ref.1) | copy-start | bytes 1540
  13.3 9.1 %copy-start.11 = (bf16[3,256]{1,0:T(4,128)(2,1)S(1)}, bf16[3,256]{1,0:T(4,128)(2,1)}, u32[]{:S(2)}) copy-start(bf16[3,256]{1,0:T(4,128)(2,1)} %tmap_ref.1) | copy-start | bytes 4612
  13.3 9.1 %copy-start.12 = (s32[1,1,4]{2,1,0:T(1,128)S(1)}, s32[1,1,4]{2,1,0:T(1,128)}, u32[]{:S(2)}) copy-start(s32[1,1,4]{2,1,0:T(1,128)} %count_hbm.1) | copy-start | bytes 52
  13.4 9.0 %collective-permute-start.5 = (bf16[144,256]{1,0:T(8,128)(2,1)S(1)}, bf16[144,256]{1,0:T(8,128)(2,1)S(1)}, u32[]{:S(2)}, u32[]{:S(2)}) collective-permute-start(bf16[144,256]{1,0:T(8,128)(2,1)S(1)} %pad_maximum_fusion), channel_id=1, source_target_pairs={{4,8},{12,16},{20,24},{28,32},{36,40},{44,48},{52,56},{60,64},{68,... | collective-permute-start | bytes 221192 | tf_op jit(solution)/shard_map/ppermute | solution.py:542
  15.9 6.4 %collective-permute-start.6 = (bf16[64,256]{1,0:T(8,128)(2,1)S(1)}, bf16[64,256]{1,0:T(8,128)(2,1)S(1)}, u32[]{:S(2)}, u32[]{:S(2)}) collective-permute-start(bf16[64,256]{1,0:T(8,128)(2,1)S(1)} %slice.42), channel_id=1, source_target_pairs={{0,4},{4,0},{8,12},{12,8},{16,20},{20,16},{24,28},{28,24},{32,36},... | collective-permute-start | bytes 98312 | tf_op jit(solution)/shard_map/ppermute | solution.py:546
  24.9 6.9 %copy-start = (f32[3,64,128]{2,1,0:T(8,128)S(1)}, f32[3,64,128]{2,1,0:T(8,128)}, u32[]{:S(2)}) copy-start(f32[3,64,128]{2,1,0:T(8,128)} %disp_ref.3) | copy-start | bytes 294916
  24.9 6.9 %copy-start.7 = (f32[64,128]{1,0:T(8,128)S(1)}, f32[64,128]{1,0:T(8,128)}, u32[]{:S(2)}) copy-start(f32[64,128]{1,0:T(8,128)} %stiff_ref.3) | copy-start | bytes 98308
  24.9 18.2 %all-to-all-start = ((bf16[128,8,128]{2,1,0:T(8,128)(2,1)}), bf16[128,8,128]{2,1,0:T(8,128)(2,1)S(1)}, u32[]{:S(2)}, u32[]{:S(2)}) async-start(bf16[128,8,128]{2,1,0:T(8,128)(2,1)} %bitcast), calls=%async_computation | async-start | bytes 524288 | tf_op jit(solution)/shard_map/all_to_all | solution.py:201
  47.3 3.2 %collective-permute-start.7 = (f32[8,256]{1,0:T(8,128)S(1)}, f32[8,256]{1,0:T(8,128)S(1)}, u32[]{:S(2)}, u32[]{:S(2)}) collective-permute-start(f32[8,256]{1,0:T(8,128)S(1)} %get-tuple-element.29), channel_id=1, source_target_pairs={{0,3},{1,2},{2,1},{3,0},{4,7},{5,6},{6,5},{7,4},{8,11},{9,10},{10,... | collective-permute-start | bytes 24584 | tf_op jit(solution)/shard_map/ppermute | solution.py:214
  48.0 2.6 %collective-permute-start.8 = (f32[8,256]{1,0:T(8,128)S(1)}, f32[8,256]{1,0:T(8,128)S(1)}, u32[]{:S(2)}, u32[]{:S(2)}) collective-permute-start(f32[8,256]{1,0:T(8,128)S(1)} %get-tuple-element.30), channel_id=1, source_target_pairs={{0,2},{1,3},{2,0},{3,1},{4,6},{5,7},{6,4},{7,5},{8,10},{9,11},{10,... | collective-permute-start | bytes 24584 | tf_op jit(solution)/shard_map/ppermute | solution.py:214
  49.2 1.4 %collective-permute-start.9 = (f32[8,256]{1,0:T(8,128)S(1)}, f32[8,256]{1,0:T(8,128)S(1)}, u32[]{:S(2)}, u32[]{:S(2)}) collective-permute-start(f32[8,256]{1,0:T(8,128)S(1)} %get-tuple-element.31), channel_id=1, source_target_pairs={{0,1},{1,0},{2,3},{3,2},{4,5},{5,4},{6,7},{7,6},{8,9},{9,8},{10,11... | collective-permute-start | bytes 24584 | tf_op jit(solution)/shard_map/ppermute | solution.py:214
